TPU v7x, 32 devices: a whole 2x2x4 slice. The times are simulated.
32 devices in a mesh: fsdp: 4 (over z), ctx: 4 (over x, core), tp: 2 (over y).
Axes of the slice: x: 2, y: 2, z: 4, core: 2. Of those that a mesh axis runs over, the one named last changes fastest.
Arguments:
- layer_input: bfloat16 [4, 8, 512, 768], P(None, 'fsdp', 'ctx'), may hold values from -6 to 6
- doc_ids: int32 [4, 8, 512], P(None, 'fsdp', 'ctx'), may hold values from 0 to 3, never falling along the last dimension, each value on 1 to 256 neighbouring positions
- w_qkv: bfloat16 [3, 768, 768], P(None, 'fsdp', 'tp'), may hold values from -0.21875 to 0.21875
- b_qv: float32 [2, 768], P(None, 'tp'), may hold values from -3 to 3
- w_out: bfloat16 [768, 768], P('tp', 'fsdp'), may hold values from -0.625 to 0.625
- b_out: float32 [768], replicated, may hold values from -2 to 2
- ln1_gain: float32 [768], replicated, may hold values from 0.1 to 1.9
- ln1_bias: float32 [768], replicated, may hold values from -2 to 2
- w_up: bfloat16 [768, 3072], P('fsdp', 'tp'), may hold values from -0.21875 to 0.21875
- b_up: float32 [3072], P('tp'), may hold values from -3 to 3
- w_down: bfloat16 [3072, 768], P('tp', 'fsdp'), may hold values from -0.109375 to 0.109375
- b_down: float32 [768], replicated, may hold values from -2 to 2
- ln2_gain: float32 [768], replicated, may hold values from 0.1 to 1.9
- ln2_bias: float32 [768], replicated, may hold values from -2 to 2
- out_grad: bfloat16 [4, 8, 512, 768], P(None, 'fsdp', 'ctx'), may hold values from -6 to 6
Outputs:
- layer_output: bfloat16 [4, 8, 512, 768], P(None, 'fsdp', 'ctx')
- grad_x: bfloat16 [4, 8, 512, 768], P(None, 'fsdp', 'ctx')
- grad_w_qkv: float32 [3, 768, 768], P(None, 'fsdp', 'tp')
- grad_b_qv: float32 [2, 768], P(None, 'tp')
- grad_w_out: float32 [768, 768], P('tp', 'fsdp')
- grad_b_out: float32 [768], replicated
- grad_ln1_gain: float32 [768], replicated
- grad_ln1_bias: float32 [768], replicated
- grad_w_up: float32 [768, 3072], P('fsdp', 'tp')
- grad_b_up: float32 [3072], P('tp')
- grad_w_down: float32 [3072, 768], P('tp', 'fsdp')
- grad_b_down: float32 [768], replicated
- grad_ln2_gain: float32 [768], replicated
- grad_ln2_bias: float32 [768], replicated
Inputs may be any that keep to these rules, and one draw needn't show every extreme that they name: `doc_ids`: within each sequence of 512 tokens the ids never fall and each of the 4 ids marks one run of 1 to 256 tokens.
All inputs are finite; a program needn't handle non-finite values.
Results may differ from a plain program's by a relative error of at most 0.02.
Values may be sent and summed in bfloat16 or wider, within the bound.
No kernel may reach another device: no remote copies, remote signals or barrier semaphores. Data moves between devices by JAX's collectives and lax.ppermute only.
A program may use at most 128 MiB of HBM per device.

v0:
```python
import jax
import jax.numpy as jnp
from jax import lax
from jax.sharding import PartitionSpec as P

HEAD_DIM = 64


def normalize_rows(values_in):
    mean = jnp.mean(values_in, axis=-1, keepdims=True)
    centred = values_in - mean
    var = jnp.mean(centred * centred, axis=-1, keepdims=True)
    scale = lax.rsqrt(var + 1e-12)
    return (centred * scale, scale)


def normalize_back(grad_hat, normed, scale):
    first_mean = jnp.mean(grad_hat, axis=-1, keepdims=True)
    second_mean = jnp.mean(grad_hat * normed, axis=-1, keepdims=True)
    return scale * (grad_hat - first_mean - normed * second_mean)


def collect_weights(weights):
    return (
        lax.all_gather(weights[0], "fsdp", axis=1, tiled=True),
        lax.all_gather(weights[1], "fsdp", axis=1, tiled=True),
        lax.all_gather(weights[2], "fsdp", axis=0, tiled=True),
        lax.all_gather(weights[3], "fsdp", axis=1, tiled=True),
    )


def spread_grads(grads):
    return (
        lax.psum_scatter(
            grads[0].astype(jnp.bfloat16), "fsdp", scatter_dimension=1, tiled=True
        ).astype(jnp.float32),
        lax.psum_scatter(
            grads[1].astype(jnp.bfloat16), "fsdp", scatter_dimension=1, tiled=True
        ).astype(jnp.float32),
        lax.psum_scatter(
            grads[2].astype(jnp.bfloat16), "fsdp", scatter_dimension=0, tiled=True
        ).astype(jnp.float32),
        lax.psum_scatter(
            grads[3].astype(jnp.bfloat16), "fsdp", scatter_dimension=1, tiled=True
        ).astype(jnp.float32),
    )


def attention_probs(query, keys, allowed, log_total):
    scores = jnp.einsum("sqhd,skhd->shqk", query, keys, preferred_element_type=jnp.float32) * 0.125
    masked = jnp.where(allowed, scores, -1e30)
    if log_total is None:
        top = jnp.max(masked, axis=-1, keepdims=True)
        log_total = top + jnp.log(jnp.sum(jnp.exp(masked - top), axis=-1, keepdims=True))
    return (jnp.exp(masked - log_total), log_total)


def body(
    layer_input,
    doc_ids,
    w_qkv,
    b_qv,
    w_out,
    b_out,
    ln1_gain,
    ln1_bias,
    w_up,
    b_up,
    w_down,
    b_down,
    ln2_gain,
    ln2_bias,
    out_grad,
):
    inputs_here, cot_here, ids_here = (layer_input, out_grad, doc_ids)
    key_ids = lax.all_gather(doc_ids, "ctx", axis=2, tiled=True)
    micro, seqs, local_len, width = inputs_here.shape
    full_len = key_ids.shape[2]
    shard_rows = width // lax.axis_size("fsdp")
    local_width = w_qkv.shape[2]
    local_units = w_up.shape[1]
    local_heads = local_width // HEAD_DIM
    rows_count = seqs * local_len
    bias_three = jnp.concatenate(
        [b_qv[0:1], jnp.zeros((1, local_width), jnp.float32), b_qv[1:2]], axis=0
    )[:, None, :]
    local_acc = (
        jnp.zeros((3, width, local_width), jnp.float32),
        jnp.zeros((local_width, width), jnp.float32),
        jnp.zeros((width, local_units), jnp.float32),
        jnp.zeros((local_units, width), jnp.float32),
    )
    shard_acc = (
        jnp.zeros((3, shard_rows, local_width), jnp.float32),
        jnp.zeros((local_width, shard_rows), jnp.float32),
        jnp.zeros((shard_rows, local_units), jnp.float32),
        jnp.zeros((local_units, shard_rows), jnp.float32),
    )
    zero_width = jnp.zeros((width,), jnp.float32)
    grad_bqv = jnp.zeros((2, local_width), jnp.float32)
    grad_bup = jnp.zeros((local_units,), jnp.float32)
    grad_bout, grad_gain1, grad_shift1 = (zero_width, zero_width, zero_width)
    grad_bdown, grad_gain2, grad_shift2 = (zero_width, zero_width, zero_width)
    outputs, input_grads = ([], [])
    for micro_step in range(micro):
        weights_now = collect_weights((w_qkv, w_out, w_up, w_down))
        wq_all, wo_all, wu_all, wd_all = weights_now
        rows_b = inputs_here[micro_step].reshape(rows_count, width)
        rows_f = rows_b.astype(jnp.float32)
        projected = (
            jnp.einsum("rd,cde->cre", rows_b, wq_all, preferred_element_type=jnp.float32)
            + bias_three
        )
        proj_b = projected.astype(jnp.bfloat16)
        query = proj_b[0].reshape(seqs, local_len, local_heads, HEAD_DIM)
        local_kv = proj_b[1:].reshape(2, seqs, local_len, local_width)
        full_kv = lax.all_gather(local_kv, "ctx", axis=2, tiled=True)
        keys = full_kv[0].reshape(seqs, full_len, local_heads, HEAD_DIM)
        values = full_kv[1].reshape(seqs, full_len, local_heads, HEAD_DIM)
        allowed = ids_here[micro_step][:, None, :, None] == key_ids[micro_step][:, None, None, :]
        probs, log_total = attention_probs(query, keys, allowed, None)
        probs_b = probs.astype(jnp.bfloat16)
        mixed = jnp.einsum("shqk,skhd->sqhd", probs_b, values, preferred_element_type=jnp.float32)
        mixed_b = mixed.reshape(rows_count, local_width).astype(jnp.bfloat16)
        branch = lax.psum(jnp.dot(mixed_b, wo_all, preferred_element_type=jnp.float32), "tp")
        normed1, scale1 = normalize_rows(rows_f + branch + b_out)
        first = normed1 * ln1_gain + ln1_bias
        first_b = first.astype(jnp.bfloat16)
        hidden = jnp.dot(first_b, wu_all, preferred_element_type=jnp.float32) + b_up
        activation, gelu_pull = jax.vjp(
            lambda hidden_in: jax.nn.gelu(hidden_in, approximate=False), hidden
        )
        act_b = activation.astype(jnp.bfloat16)
        second = lax.psum(
            jnp.dot(act_b, wd_all, preferred_element_type=jnp.float32).astype(jnp.bfloat16), "tp"
        ).astype(jnp.float32)
        normed2, scale2 = normalize_rows(first + second + b_down)
        result = normed2 * ln2_gain + ln2_bias
        outputs.append(result.astype(jnp.bfloat16).reshape(seqs, local_len, width))
        incoming = cot_here[micro_step].reshape(rows_count, width).astype(jnp.float32)
        grad_gain2 = grad_gain2 + jnp.sum(incoming * normed2, axis=0)
        grad_shift2 = grad_shift2 + jnp.sum(incoming, axis=0)
        grad_z2 = normalize_back(incoming * ln2_gain, normed2, scale2)
        grad_bdown = grad_bdown + jnp.sum(grad_z2, axis=0)
        grad_second_b = grad_z2.astype(jnp.bfloat16)
        step_wd = jnp.dot(act_b.T, grad_second_b, preferred_element_type=jnp.float32)
        grad_act = jnp.dot(grad_second_b, wd_all.T, preferred_element_type=jnp.float32)
        (grad_hidden,) = gelu_pull(grad_act)
        grad_hidden_b = grad_hidden.astype(jnp.bfloat16)
        grad_bup = grad_bup + jnp.sum(grad_hidden_b.astype(jnp.float32), axis=0)
        step_wu = jnp.dot(first_b.T, grad_hidden_b, preferred_element_type=jnp.float32)
        grad_first = grad_z2 + lax.psum(
            jnp.dot(grad_hidden_b, wu_all.T, preferred_element_type=jnp.float32).astype(
                jnp.bfloat16
            ),
            "tp",
        ).astype(jnp.float32)
        grad_gain1 = grad_gain1 + jnp.sum(grad_first * normed1, axis=0)
        grad_shift1 = grad_shift1 + jnp.sum(grad_first, axis=0)
        grad_z1 = normalize_back(grad_first * ln1_gain, normed1, scale1)
        grad_bout = grad_bout + jnp.sum(grad_z1, axis=0)
        grad_branch_b = grad_z1.astype(jnp.bfloat16)
        step_wo = jnp.dot(mixed_b.T, grad_branch_b, preferred_element_type=jnp.float32)
        grad_mixed_b = jnp.dot(grad_branch_b, wo_all.T, preferred_element_type=jnp.float32).astype(
            jnp.bfloat16
        )
        grad_mixed_b = grad_mixed_b.reshape(seqs, local_len, local_heads, HEAD_DIM)
        recomputed, unused_total = attention_probs(query, keys, allowed, log_total)
        recomputed_b = recomputed.astype(jnp.bfloat16)
        grad_probs = jnp.einsum(
            "sqhd,skhd->shqk", grad_mixed_b, values, preferred_element_type=jnp.float32
        )
        weighted = jnp.sum(recomputed * grad_probs, axis=-1, keepdims=True)
        grad_scores_b = (recomputed * (grad_probs - weighted)).astype(jnp.bfloat16)
        grad_query = (
            jnp.einsum("shqk,skhd->sqhd", grad_scores_b, keys, preferred_element_type=jnp.float32)
            * 0.125
        )
        grad_keys = (
            jnp.einsum("shqk,sqhd->skhd", grad_scores_b, query, preferred_element_type=jnp.float32)
            * 0.125
        )
        grad_values = jnp.einsum(
            "shqk,sqhd->skhd", recomputed_b, grad_mixed_b, preferred_element_type=jnp.float32
        )
        kv_terms = jnp.stack([grad_keys, grad_values]).reshape(2, seqs, full_len, local_width)
        kv_back = lax.psum_scatter(
            kv_terms.astype(jnp.bfloat16), "ctx", scatter_dimension=2, tiled=True
        ).astype(jnp.float32)
        grad_proj_b = jnp.concatenate(
            [
                grad_query.reshape(1, rows_count, local_width).astype(jnp.bfloat16),
                kv_back.reshape(2, rows_count, local_width).astype(jnp.bfloat16),
            ],
            axis=0,
        )
        grad_bqv = grad_bqv + jnp.sum(grad_proj_b[0::2].astype(jnp.float32), axis=1)
        step_wq = jnp.einsum("rd,cre->cde", rows_b, grad_proj_b, preferred_element_type=jnp.float32)
        back_rows = jnp.einsum(
            "cre,cde->rd", grad_proj_b, wq_all, preferred_element_type=jnp.float32
        )
        grad_rows = grad_z1 + lax.psum(back_rows.astype(jnp.bfloat16), "tp").astype(jnp.float32)
        input_grads.append(grad_rows.astype(jnp.bfloat16).reshape(seqs, local_len, width))
        step_grads = (step_wq, step_wo, step_wu, step_wd)
        local_acc = tuple((left + right for left, right in zip(local_acc, step_grads)))
    shard_acc = spread_grads(local_acc)
    small_sums = lax.psum(
        (
            grad_bqv,
            grad_bout,
            grad_gain1,
            grad_shift1,
            grad_bup,
            grad_bdown,
            grad_gain2,
            grad_shift2,
        ),
        "fsdp",
    )
    summed = (
        lax.psum(shard_acc[0].astype(jnp.bfloat16), "ctx").astype(jnp.float32),
        lax.psum(shard_acc[1].astype(jnp.bfloat16), "ctx").astype(jnp.float32),
        lax.psum(shard_acc[2].astype(jnp.bfloat16), "ctx").astype(jnp.float32),
        lax.psum(shard_acc[3].astype(jnp.bfloat16), "ctx").astype(jnp.float32),
        lax.psum(small_sums[0].astype(jnp.bfloat16), "ctx").astype(jnp.float32),
        lax.psum(small_sums[1].astype(jnp.bfloat16), "ctx").astype(jnp.float32),
        lax.psum(small_sums[2].astype(jnp.bfloat16), "ctx").astype(jnp.float32),
        lax.psum(small_sums[3].astype(jnp.bfloat16), "ctx").astype(jnp.float32),
        lax.psum(small_sums[4].astype(jnp.bfloat16), "ctx").astype(jnp.float32),
        lax.psum(small_sums[5].astype(jnp.bfloat16), "ctx").astype(jnp.float32),
        lax.psum(small_sums[6].astype(jnp.bfloat16), "ctx").astype(jnp.float32),
        lax.psum(small_sums[7].astype(jnp.bfloat16), "ctx").astype(jnp.float32),
    )
    stacked_out = jnp.stack(outputs)
    stacked_grad = jnp.stack(input_grads)
    return (
        stacked_out,
        stacked_grad,
        summed[0],
        summed[4],
        summed[1],
        summed[5],
        summed[6],
        summed[7],
        summed[2],
        summed[8],
        summed[3],
        summed[9],
        summed[10],
        summed[11],
    )


def solution(mesh):
    return jax.shard_map(
        body,
        mesh=mesh,
        in_specs=(
            P(None, "fsdp", "ctx", None),
            P(None, "fsdp", "ctx"),
            P(None, "fsdp", "tp"),
            P(None, "tp"),
            P("tp", "fsdp"),
            P(),
            P(),
            P(),
            P("fsdp", "tp"),
            P("tp"),
            P("tp", "fsdp"),
            P(),
            P(),
            P(),
            P(None, "fsdp", "ctx", None),
        ),
        out_specs=(
            P(None, "fsdp", "ctx", None),
            P(None, "fsdp", "ctx", None),
            P(None, "fsdp", "tp"),
            P(None, "tp"),
            P("tp", "fsdp"),
            P(),
            P(),
            P(),
            P("fsdp", "tp"),
            P("tp"),
            P("tp", "fsdp"),
            P(),
            P(),
            P(),
        ),
        check_vma=False,
    )
```

profile of v0, /device:TPU:0, one launch (start us, length us, event | category | flops | bytes accessed | tf_op | source)
XLA Modules:
  0.0 957.4 jit_solution(15539514754937439668)
XLA Ops:
  10.4 42.3 %all-gather.8.cloned.1.call-done = bf16[3,768,384]{2,1,0:T(8,128)(2,1)} async-done(((bf16[3,192,384]{2,1,0:T(8,128)(2,1)}), bf16[3,768,384]{2,1,0:T(8,128)(2,1)}) %all-gather.8.cloned.1.call-update) | async-done | bytes 1769488 | tf_op jit(solution)/shard_map/all_gather | solution.py:25
  52.6 2.2 fusion.45
  55.7 2.2 fusion.44
  58.8 2.2 fusion.42
  61.9 2.3 fusion.43
  65.2 5.2 all_gather.20
  70.3 17.5 %all_gather.42 = bf16[384,768]{0,1:T(8,128)(2,1)} all-gather(bf16[384,192]{0,1:T(8,128)(2,1)S(1)} %copy-done.144), channel_id=1, replica_groups=mesh['fsdp'=4,'ctx'=4,'tp'=2] {'fsdp'}, dimensions={1}, use_global_device_ids=true | all-gather | bytes 737280 | tf_op jit(solution)/shard_map/all_gather | solution.py:26
  98.8 18.0 %all-gather.20.cloned.1.call-done = bf16[2,2,512,384]{3,2,1,0:T(8,128)(2,1)} async-done(((bf16[2,2,128,384]{3,2,1,0:T(8,128)(2,1)}), bf16[2,2,512,384]{3,2,1,0:T(8,128)(2,1)}) %all-gather.20.cloned.1.call-update) | async-done | bytes 1572880 | tf_op jit(solution)/shard_map/all_gather | solution.py:117
  119.5 19.0 %all-gather.18.cloned.1.call-done = bf16[2,2,512,384]{3,2,1,0:T(8,128)(2,1)} async-done(((bf16[2,2,128,384]{3,2,1,0:T(8,128)(2,1)}), bf16[2,2,512,384]{3,2,1,0:T(8,128)(2,1)}) %all-gather.18.cloned.1.call-update) | async-done | bytes 1572880 | tf_op jit(solution)/shard_map/all_gather | solution.py:117
  138.4 2.4 fusion.212
  140.9 2.3 copy.127
  147.9 2.0 fusion.2
  171.0 84.9 %all-reduce.13.cloned.1.call-done = (f32[256,768]{1,0:T(8,128)}, f32[256,768]{1,0:T(8,128)}, f32[256,768]{1,0:T(8,128)}, f32[256,768]{1,0:T(8,128)}) async-done(((f32[256,768]{1,0:T(8,128)}, f32[256,768]{1,0:T(8,128)}, f32[256,768]{1,0:T(8,128)}, f32[256,768]{1,0:T(8,128)}), (f32[256,768]{1,0:T(8,128)}, f32[256,768]{1,0:T(8,128)}, f32[256,768]{1,0:T(8,128)}, ...) | async-done | bytes 3145744 | tf_op jit(solution)/shard_map/psum | solution.py:125
  255.9 2.7 fusion.201
  262.6 45.5 %all-gather.12.cloned.1.call-done = bf16[768,1536]{1,0:T(8,128)(2,1)} async-done(((bf16[192,1536]{1,0:T(8,128)(2,1)}), bf16[768,1536]{1,0:T(8,128)(2,1)}) %all-gather.12.cloned.1.call-update) | async-done | bytes 2359312 | tf_op jit(solution)/shard_map/all_gather | solution.py:27
  308.1 7.9 multiply_convert_fusion.10
  316.1 5.8 multiply_convert_fusion.9
  321.8 37.2 %all-gather.14.cloned.1.call-done = bf16[1536,768]{0,1:T(8,128)(2,1)} async-done(((bf16[1536,192]{0,1:T(8,128)(2,1)}), bf16[1536,768]{0,1:T(8,128)(2,1)}) %all-gather.14.cloned.1.call-update) | async-done | bytes 2359312 | tf_op jit(solution)/shard_map/all_gather | solution.py:28
  359.1 3.6 convolution_convert_fusion.10
  364.8 5.2 multiply_convert_fusion.8
  372.5 5.2 multiply_convert_fusion.11
  380.4 2.5 convert_reduce_fusion.6
  384.0 47.1 %all-reduce.21.cloned.1.call-done = (bf16[256,768]{1,0:T(8,128)(2,1)}, bf16[256,768]{1,0:T(8,128)(2,1)}, bf16[256,768]{1,0:T(8,128)(2,1)}, bf16[256,768]{1,0:T(8,128)(2,1)}) async-done(((bf16[256,768]{1,0:T(8,128)(2,1)}, bf16[256,768]{1,0:T(8,128)(2,1)}, bf16[256,768]{1,0:T(8,128)(2,1)}, bf16[256,768]{1,0:T(8,128)(2,1)}), (bf16[256,768]{1,0:T(8,128)(2,1)}, bf16[256,768]{1,0:T(8,128)(2,1)}, ...) | async-done | bytes 1572880 | tf_op jit(solution)/shard_map/psum | solution.py:134
  433.4 2.0 fusion.196
  436.8 2.6 fusion.64
  439.4 2.2 fusion.71
  461.9 52.0 %all-reduce.19.cloned.1.call-done = (bf16[256,768]{1,0:T(8,128)(2,1)}, bf16[256,768]{1,0:T(8,128)(2,1)}, bf16[256,768]{1,0:T(8,128)(2,1)}, bf16[256,768]{1,0:T(8,128)(2,1)}) async-done(((bf16[256,768]{1,0:T(8,128)(2,1)}, bf16[256,768]{1,0:T(8,128)(2,1)}, bf16[256,768]{1,0:T(8,128)(2,1)}, bf16[256,768]{1,0:T(8,128)(2,1)}), (bf16[256,768]{1,0:T(8,128)(2,1)}, bf16[256,768]{1,0:T(8,128)(2,1)}, ...) | async-done | bytes 1572880 | tf_op jit(solution)/shard_map/psum | solution.py:152
  514.0 3.7 multiply_reduce_fusion.7
  517.9 4.1 fusion.193
  522.0 2.1 fusion.192
  529.5 3.0 convolution_convert_fusion
  538.0 4.9 copy.178
  542.9 4.8 reshape.466
  548.2 2.3 convolution_convert_fusion.18
  554.0 4.1 multiply_reduce_fusion.2
  562.5 5.0 copy.174
  567.5 4.9 reshape.462
  572.5 2.3 convolution_convert_fusion.19
  578.2 3.7 multiply_reduce_fusion.3
  586.3 5.0 copy.172
  591.3 4.8 reshape.460
  597.8 2.4 fusion.194
  605.6 2.6 multiply_reduce_fusion.1
  611.4 2.2 copy.176
  613.6 1.9 reshape.464
  625.6 1.9 fusion.55
  630.6 7.0 reduce-scatter.25.cloned.1.call-done
  638.8 30.0 %reduce-scatter.29.cloned.1.call-done = bf16[128,1536]{1,0:T(8,128)(2,1)} async-done(((bf16[512,1536]{1,0:T(8,128)(2,1)}), bf16[128,1536]{1,0:T(8,128)(2,1)}) %reduce-scatter.29.cloned.1.call-update) | async-done | bytes 393232
  670.0 3.1 fusion.41
  681.0 1.9 fusion.32
  682.9 4.0 copy.180
  689.9 3.2 fusion.183
  697.9 2.2 fusion.180
  701.9 2.4 add_convert_fusion.1
  705.4 2.0 fusion.120
  710.3 2.4 add_convert_fusion
  717.7 19.4 %all-reduce = (bf16[2,384]{1,0:T(2,128)(2,1)S(1)}, bf16[768]{0:T(1024)(128)(2,1)S(1)}, bf16[768]{0:T(1024)(128)(2,1)S(1)}, bf16[768]{0:T(1024)(128)(2,1)S(1)}, b...) all-reduce(f32[2,384]{1,0:T(2,128)S(1)} %add_add_fusion.15, ...), channel_id=1, replica_groups=mesh['fsdp'=4,'ctx'=4,'tp'=2] {'fsdp'}, use_global_device_ids=true, to_apply=%region_70.71 | all-reduce | flops 6912 | bytes 41472 | tf_op jit(solution)/shard_map/psum | solution.py:207
  737.0 11.0 %all-reduce.2 = (bf16[2,384]{1,0:T(2,128)(2,1)S(1)}, bf16[768]{0:T(1024)(128)(2,1)S(1)}, bf16[768]{0:T(1024)(128)(2,1)S(1)}, bf16[768]{0:T(1024)(128)(2,1)S(1)},...) all-reduce(bf16[2,384]{1,0:T(2,128)(2,1)S(1)} %get-tuple-element.10, ...), channel_id=1, replica_groups=mesh['fsdp'=4,'ctx'=4,'tp'=2] {'ctx'}, use_global_device_ids=true, to_apply=%region_71.72 | all-reduce | flops 6912 | bytes 27648 | tf_op jit(solution)/shard_map/psum | solution.py:225
  753.9 16.5 %reduce-scatter.33.cloned.1.call-done = bf16[192,1152]{1,0:T(8,128)(2,1)} async-done(((bf16[768,1152]{1,0:T(8,128)(2,1)}), bf16[192,1152]{1,0:T(8,128)(2,1)}) %reduce-scatter.33.cloned.1.call-update) | async-done | bytes 442384
  773.1 21.2 %reduce-scatter.19.cloned.1.call-done = bf16[384,192]{0,1:T(8,128)(2,1)} async-done(((bf16[384,768]{0,1:T(8,128)(2,1)}), bf16[384,192]{0,1:T(8,128)(2,1)}) %reduce-scatter.19.cloned.1.call-update) | async-done | bytes 147472 | tf_op jit(solution)/shard_map/reduce_scatter | solution.py:37
  794.3 48.7 %reduce-scatter.21.cloned.1.call-done = bf16[192,1536]{1,0:T(8,128)(2,1)} async-done(((bf16[768,1536]{1,0:T(8,128)(2,1)}), bf16[192,1536]{1,0:T(8,128)(2,1)}) %reduce-scatter.21.cloned.1.call-update) | async-done | bytes 589840 | tf_op jit(solution)/shard_map/reduce_scatter | solution.py:40
  843.0 50.0 %reduce-scatter.23.cloned.1.call-done = bf16[1536,192]{0,1:T(8,128)(2,1)} async-done(((bf16[1536,768]{0,1:T(8,128)(2,1)}), bf16[1536,192]{0,1:T(8,128)(2,1)}) %reduce-scatter.23.cloned.1.call-update) | async-done | bytes 589840 | tf_op jit(solution)/shard_map/reduce_scatter | solution.py:43
  895.7 49.2 %all-reduce.15.cloned.1.call-done = (bf16[3,192,384]{1,2,0:T(8,128)(2,1)}, bf16[384,192]{0,1:T(8,128)(2,1)}, bf16[192,1536]{1,0:T(8,128)(2,1)}, bf16[1536,192]{0,1:T(8,128)(2,1)}) async-done(((bf16[3,192,384]{1,2,0:T(8,128)(2,1)}, bf16[384,192]{0,1:T(8,128)(2,1)}, bf16[192,1536]{1,0:T(8,128)(2,1)}, bf16[1536,192]{0,1:T(8,128)(2,1)}), (bf16[3,192,384]{1,2,0:T(8,128)(2,1)}, bf16[384,192]{0,1:T(8,128)(2,1)}, ...) | async-done | bytes 1769488 | tf_op jit(solution)/shard_map/psum | solution.py:221
  944.9 2.3 copy.167
  (731 shorter events, 173.8 us)
Async XLA Ops:
  7.2 45.5 %all-gather.8.cloned.1.call-start = ((), (), s32[]{:S(2)}) async-start(), calls=%async_computation.8 | async-start | bytes 2211840 | tf_op jit(solution)/shard_map/all_gather | solution.py:25
  7.9 85.4 %all-gather.10.cloned.1.call-start = ((), (), s32[]{:S(2)}) async-start(), calls=%async_computation.9 | async-start | bytes 1966080 | tf_op jit(solution)/shard_map/all_gather | solution.py:117
  10.3 44.5 %copy-start.60 = (bf16[1,2,128,768]{3,2,1,0:T(8,128)(2,1)}, bf16[1,2,128,768]{3,2,1,0:T(8,128)(2,1)S(1)}, u32[]{:S(2)}) copy-start(bf16[1,2,128,768]{3,2,1,0:T(8,128)(2,1)S(1)} %get-tuple-element.175) | copy-start | bytes 1179652
  10.3 45.3 %copy-start.58 = (bf16[1,2,128,768]{3,2,1,0:T(8,128)(2,1)}, bf16[1,2,128,768]{3,2,1,0:T(8,128)(2,1)S(1)}, u32[]{:S(2)}) copy-start(bf16[1,2,128,768]{3,2,1,0:T(8,128)(2,1)S(1)} %get-tuple-element.174) | copy-start | bytes 1179652
  10.4 51.5 %copy-start.62 = (bf16[1,2,128,768]{3,2,1,0:T(8,128)(2,1)}, bf16[1,2,128,768]{3,2,1,0:T(8,128)(2,1)S(1)}, u32[]{:S(2)}) copy-start(bf16[1,2,128,768]{3,2,1,0:T(8,128)(2,1)S(1)} %get-tuple-element.177) | copy-start | bytes 1179652
  55.6 40.4 %all-gather.16.cloned.1.call-start = ((), (), s32[]{:S(2)}) async-start(), calls=%async_computation.12 | async-start | bytes 1966080 | tf_op jit(solution)/shard_map/all_gather | solution.py:117
  57.8 31.9 %copy-start.132 = (bf16[3,256,384]{2,1,0:T(8,128)(2,1)}, bf16[3,256,384]{2,1,0:T(8,128)(2,1)S(1)}, u32[]{:S(2)}) copy-start(bf16[3,256,384]{2,1,0:T(8,128)(2,1)S(1)} %fusion.44) | copy-start | bytes 1769476
  58.7 58.0 %all-gather.20.cloned.1.call-start = ((), (), s32[]{:S(2)}) async-start(), calls=%async_computation.14 | async-start | bytes 1966080 | tf_op jit(solution)/shard_map/all_gather | solution.py:117
  60.9 28.8 %copy-start.131 = (bf16[3,256,384]{2,1,0:T(8,128)(2,1)}, bf16[3,256,384]{2,1,0:T(8,128)(2,1)S(1)}, u32[]{:S(2)}) copy-start(bf16[3,256,384]{2,1,0:T(8,128)(2,1)S(1)} %fusion.42) | copy-start | bytes 1769476
  61.8 76.6 %all-gather.18.cloned.1.call-start = ((), (), s32[]{:S(2)}) async-start(), calls=%async_computation.13 | async-start | bytes 1966080 | tf_op jit(solution)/shard_map/all_gather | solution.py:117
  61.9 8.4 copy-start.144
  64.2 25.5 %copy-start.130 = (bf16[3,256,384]{2,1,0:T(8,128)(2,1)}, bf16[3,256,384]{2,1,0:T(8,128)(2,1)S(1)}, u32[]{:S(2)}) copy-start(bf16[3,256,384]{2,1,0:T(8,128)(2,1)S(1)} %fusion.43) | copy-start | bytes 1769476
  65.1 190.8 %all-reduce.13.cloned.1.call-start = ((), (), s32[]{:S(2)}) async-start(), calls=%async_computation.23 | async-start | bytes 6291456 | tf_op jit(solution)/shard_map/psum | solution.py:125
  169.4 86.5 %copy-start.215 = (f32[768]{0:T(1024)S(1)}, f32[768]{0:T(1024)}, u32[]{:S(2)}) copy-start(f32[768]{0:T(1024)} %param.20) | copy-start | bytes 9220
  169.4 138.7 %all-gather.12.cloned.1.call-start = ((), (), s32[]{:S(2)}) async-start(), calls=%async_computation.10 | async-start | bytes 2949120 | tf_op jit(solution)/shard_map/all_gather | solution.py:27
  170.2 188.9 %all-gather.14.cloned.1.call-start = ((), (), s32[]{:S(2)}) async-start(), calls=%async_computation.11 | async-start | bytes 2949120 | tf_op jit(solution)/shard_map/all_gather | solution.py:28
  170.9 260.2 %all-reduce.21.cloned.1.call-start = ((), (), s32[]{:S(2)}) async-start(), calls=%async_computation.27 | async-start | bytes 3145728 | tf_op jit(solution)/shard_map/psum | solution.py:134
  258.7 49.4 %copy-start.119 = (f32[768]{0:T(1024)S(1)}, f32[768]{0:T(1024)}, u32[]{:S(2)}) copy-start(f32[768]{0:T(1024)} %param.21) | copy-start | bytes 9220
  258.7 49.4 %copy-start.120 = (f32[768]{0:T(1024)S(1)}, f32[768]{0:T(1024)}, u32[]{:S(2)}) copy-start(f32[768]{0:T(1024)} %param.22) | copy-start | bytes 9220
  308.1 8.0 copy-start.19
  308.1 8.0 copy-start.158
  308.1 7.9 copy-start.174
  308.1 7.9 copy-start.220
  308.1 7.9 copy-start.226
  380.2 133.7 %all-reduce.19.cloned.1.call-start = ((), (), s32[]{:S(2)}) async-start(), calls=%async_computation.26 | async-start | bytes 3145728 | tf_op jit(solution)/shard_map/psum | solution.py:152
  441.6 15.1 %copy-start.50 = (f32[256,768]{1,0:T(8,128)}, f32[256,768]{1,0:T(8,128)S(1)}, u32[]{:S(2)}) copy-start(f32[256,768]{1,0:T(8,128)S(1)} %get-tuple-element.171) | copy-start | bytes 2359300
  442.5 4.5 copy-start.36
  442.5 6.1 copy-start.53
  442.5 10.1 %copy-start.42 = (f32[256,768]{1,0:T(8,128)}, f32[256,768]{1,0:T(8,128)S(1)}, u32[]{:S(2)}) copy-start(f32[256,768]{1,0:T(8,128)S(1)} %get-tuple-element.168) | copy-start | bytes 2359300
  461.6 166.4 %reduce-scatter.31.cloned.1.call-start = ((), (), s32[]{:S(2)}) async-start(), calls=%async_computation.21 | async-start | bytes 1966080
  513.9 3.8 copy-start.155
  513.9 3.8 copy-start.160
  517.8 4.2 copy-start.16
  517.8 4.2 copy-start.43
  517.8 4.1 copy-start.113
  517.8 4.1 copy-start.114
  517.8 4.1 copy-start.164
  517.8 4.1 copy-start.179
  547.8 81.5 %reduce-scatter.27.cloned.1.call-start = ((), (), s32[]{:S(2)}) async-start(), calls=%async_computation.19 | async-start | bytes 1966080
  554.0 4.1 copy-start.3
  554.0 4.1 copy-start.77
  554.0 4.1 copy-start.148
  572.4 65.2 %reduce-scatter.25.cloned.1.call-start = ((), (), s32[]{:S(2)}) async-start(), calls=%async_computation.18 | async-start | bytes 1966080
  596.2 72.6 %reduce-scatter.29.cloned.1.call-start = ((), (), s32[]{:S(2)}) async-start(), calls=%async_computation.20 | async-start | bytes 1966080
  596.4 4.7 copy-start.8
  615.6 4.5 copy-start.30
  615.6 137.2 %all-reduce.17.cloned.1.call-start = ((), (), s32[]{:S(2)}) async-start(), calls=%async_computation.25 | async-start | bytes 3145728 | tf_op jit(solution)/shard_map/psum | solution.py:202
  625.6 49.0 %copy-start.98 = (bf16[1,256,384]{2,1,0:T(8,128)(2,1)}, bf16[1,256,384]{2,1,0:T(8,128)(2,1)S(1)}, u32[]{:S(2)}) copy-start(bf16[1,256,384]{2,1,0:T(8,128)(2,1)S(1)} %copy.141) | copy-start | bytes 589828
  628.1 49.8 %copy-start.101 = (bf16[1,256,384]{2,1,0:T(8,128)(2,1)}, bf16[1,256,384]{2,1,0:T(8,128)(2,1)S(1)}, u32[]{:S(2)}) copy-start(bf16[1,256,384]{2,1,0:T(8,128)(2,1)S(1)} %copy.155) | copy-start | bytes 589828
  629.3 51.7 %copy-start.64 = (bf16[2,2,128,384]{3,2,1,0:T(8,128)(2,1)}, bf16[2,2,128,384]{3,2,1,0:T(8,128)(2,1)S(1)}, u32[]{:S(2)}) copy-start(bf16[2,2,128,384]{3,2,1,0:T(8,128)(2,1)S(1)} %copy.161) | copy-start | bytes 1179652
  630.6 49.4 %copy-start.66 = (bf16[2,2,128,384]{3,2,1,0:T(8,128)(2,1)}, bf16[2,2,128,384]{3,2,1,0:T(8,128)(2,1)S(1)}, u32[]{:S(2)}) copy-start(bf16[2,2,128,384]{3,2,1,0:T(8,128)(2,1)S(1)} %copy.147) | copy-start | bytes 1179652
  630.6 39.3 %copy-start.111 = (bf16[1,256,384]{2,1,0:T(8,128)(2,1)S(1)}, bf16[1,256,384]{2,1,0:T(8,128)(2,1)}, u32[]{:S(2)}) copy-start(bf16[1,256,384]{2,1,0:T(8,128)(2,1)} %copy.162) | copy-start | bytes 589828
  638.8 40.5 %copy-start.68 = (bf16[2,2,128,384]{3,2,1,0:T(8,128)(2,1)}, bf16[2,2,128,384]{3,2,1,0:T(8,128)(2,1)S(1)}, u32[]{:S(2)}) copy-start(bf16[2,2,128,384]{3,2,1,0:T(8,128)(2,1)S(1)} %copy.140) | copy-start | bytes 1179652
  669.9 7.9 copy-start.70
  677.6 92.8 %reduce-scatter.33.cloned.1.call-start = ((), (), s32[]{:S(2)}) async-start(), calls=%async_computation.22 | async-start | bytes 2211840
  688.5 4.5 copy-start.48
  688.5 4.5 copy-start.108
  688.5 105.8 %reduce-scatter.19.cloned.1.call-start = ((), (), s32[]{:S(2)}) async-start(), calls=%async_computation.15 | async-start | bytes 737280 | tf_op jit(solution)/shard_map/reduce_scatter | solution.py:37
  697.8 145.2 %reduce-scatter.21.cloned.1.call-start = ((), (), s32[]{:S(2)}) async-start(), calls=%async_computation.16 | async-start | bytes 2949120 | tf_op jit(solution)/shard_map/reduce_scatter | solution.py:40
  704.3 188.6 %reduce-scatter.23.cloned.1.call-start = ((), (), s32[]{:S(2)}) async-start(), calls=%async_computation.17 | async-start | bytes 2949120 | tf_op jit(solution)/shard_map/reduce_scatter | solution.py:43
  712.9 232.0 %all-reduce.15.cloned.1.call-start = ((), (), s32[]{:S(2)}) async-start(), calls=%async_computation.24 | async-start | bytes 3833856 | tf_op jit(solution)/shard_map/psum | solution.py:221
  717.2 35.6 %copy-start.49 = (f32[256,768]{1,0:T(8,128)S(1)}, f32[256,768]{1,0:T(8,128)}, u32[]{:S(2)}) copy-start(f32[256,768]{1,0:T(8,128)} %get-tuple-element.139) | copy-start | bytes 2359300
  771.8 121.2 %copy-start.142 = (bf16[256,768]{1,0:T(8,128)(2,1)S(1)}, bf16[256,768]{1,0:T(8,128)(2,1)}, u32[]{:S(2)}) copy-start(bf16[256,768]{1,0:T(8,128)(2,1)} %get-tuple-element.126) | copy-start | bytes 1179652
  944.9 4.2 copy-start.137
  (197 other events, 371.4 us)
Sparse Core Ops, SparseCore 0:
  9.6 43.0 all-gather.7
  55.7 18.6 all-gather.9
  76.0 19.6 all-gather.15
  97.1 19.6 all-gather.19
  118.7 19.6 all-gather.17
  169.6 86.3 all-reduce.12
  257.6 50.4 all-gather.11
  309.7 49.2 all-gather.13
  380.3 50.8 all-reduce.20
  461.8 52.0 all-reduce.18
  547.9 28.1 reduce-scatter.30
  578.5 28.1 reduce-scatter.26
  609.4 28.1 reduce-scatter.24
  640.6 28.1 reduce-scatter.28
  677.7 52.0 all-reduce.16
  732.0 38.3 reduce-scatter.32
  773.2 21.0 reduce-scatter.18
  796.6 46.3 reduce-scatter.20
  845.4 47.5 reduce-scatter.22
  896.2 48.6 all-reduce.14
where the time goes:
time: 963 us; the launch traced here: 957 us
  waiting for transfers between devices  571 us (59%)
  matrix products  130 us (13%)
  local copies, waits for them, and re-layouts  124 us (13%)
  other arithmetic  59.6 us (6%)
  blocking collectives  53.1 us (6%)
  between operations  17.5 us (2%)
    psum x1, waiting for transfers between devices, body(): lax.psum(jnp.dot(mixed_b, wo_all, preferred_element_type=jnp.float32), 'tp')  84.9 us
    unnamed x493, local copies, waits for them, and re-layouts  79.3 us
    unnamed x25, waiting for transfers between devices  55.9 us
    psum x1, waiting for transfers between devices, body(): lax.psum(jnp.dot(grad_hidden_b, wu_all.T, preferred_element_type=jnp.floa...  52 us
    reduce_scatter x1, waiting for transfers between devices, spread_grads(): lax.psum_scatter(grads[3].astype(jnp.bfloat16), 'fsdp', scatter_dimension...  50 us
    psum x1, waiting for transfers between devices, body(): lax.psum(shard_acc[0].astype(jnp.bfloat16), 'ctx').astype(jnp.float32)  49.2 us
    reduce_scatter x1, waiting for transfers between devices, spread_grads(): lax.psum_scatter(grads[2].astype(jnp.bfloat16), 'fsdp', scatter_dimension...  48.7 us
    psum x1, waiting for transfers between devices, body(): lax.psum(jnp.dot(act_b, wd_all, preferred_element_type=jnp.float32).astyp...  47.1 us
  transfers between devices with their start and end apart: 20, of which 15 were waited for; matrix products, arithmetic and copies ran while one was open for 17% of the time, Pallas kernels for 0%

commit v1 on v0

v1 whole, which is shorter than its diff:
```python
import functools
import jax
import jax.numpy as jnp
from jax import lax
from jax.experimental import pallas as pl
from jax.experimental.pallas import tpu as pltpu
from jax.sharding import PartitionSpec as P

HEAD_DIM = 64
AXES = ("fsdp", "ctx", "tp")
F32 = jnp.float32
BF16 = jnp.bfloat16
NEG = -1e30


def normalize_rows(values_in):
    mean = jnp.mean(values_in, axis=-1, keepdims=True)
    centred = values_in - mean
    var = jnp.mean(centred * centred, axis=-1, keepdims=True)
    scale = lax.rsqrt(var + 1e-12)
    return (centred * scale, scale)


def normalize_back(grad_hat, normed, scale):
    first_mean = jnp.mean(grad_hat, axis=-1, keepdims=True)
    second_mean = jnp.mean(grad_hat * normed, axis=-1, keepdims=True)
    return scale * (grad_hat - first_mean - normed * second_mean)


def partner(dim, z, c, t):
    if dim == "core":
        return z, c ^ 1, t
    if dim == "x":
        return z, c ^ 2, t
    if dim == "y":
        return z, c, t ^ 1
    return z ^ int(dim[1:]), c, t


def exchange(value, dims, sizes):
    nz, nc, nt = sizes
    pairs = []
    for z in range(nz):
        for c in range(nc):
            for t in range(nt):
                tz, tc, tt = partner(dims[c & 1], z, c, t)
                pairs.append(((z * nc + c) * nt + t, (tz * nc + tc) * nt + tt))
    return lax.ppermute(value, AXES, pairs)


GATHER_ORDER = (("z1", "z2", "y", "x"), ("z1", "z2", "x", "y"))
SCATTER_ORDER = (("x", "y", "z1", "z2"), ("y", "z1", "z2", "x"))
PACK_ORDER = tuple(order[::-1] for order in SCATTER_ORDER)


def piece_place(order, core, here, index):
    z, x, t = here
    for bit, dim in enumerate(order):
        flip = (index >> bit) & 1
        if dim == "x":
            x = x ^ flip
        elif dim == "y":
            t = t ^ flip
        else:
            z = z ^ (flip * int(dim[1:]))
    return z * 4 + x * 2 + core, t


def position():
    c = lax.axis_index("ctx")
    return lax.axis_index("fsdp"), lax.div(c, 2), lax.rem(c, 2), lax.axis_index("tp")


def places(orders):
    z, x, k, t = position()
    rows = []
    for mine in (0, 1):
        core = k if mine == 0 else 1 - k
        for i in range(16):
            r0, t0 = piece_place(orders[0], core, (z, x, t), i)
            r1, t1 = piece_place(orders[1], core, (z, x, t), i)
            rows.append(jnp.where(core == 0, r0, r1))
            rows.append(jnp.where(core == 0, t0, t1))
    return jnp.stack(rows).astype(jnp.int32)


def unpack_kernel(place_ref, own_ref, sib_ref, out_ref, sem):
    rows, cols = own_ref.shape[1:]
    copies = []
    for half, ref in ((0, own_ref), (1, sib_ref)):
        for i in range(16):
            at = (half * 16 + i) * 2
            row = pl.multiple_of(place_ref[at] * rows, rows)
            col = pl.multiple_of(place_ref[at + 1] * cols, cols)
            copy = pltpu.make_async_copy(
                ref.at[i], out_ref.at[pl.ds(row, rows), pl.ds(col, cols)], sem.at[half * 16 + i]
            )
            copy.start()
            copies.append(copy)
    for copy in copies:
        copy.wait()


def unpack(place, own, sib):
    _, rows, cols = own.shape
    return pl.pallas_call(
        unpack_kernel,
        out_shape=jax.ShapeDtypeStruct((16 * rows, 2 * cols), own.dtype),
        in_specs=[
            pl.BlockSpec(memory_space=pltpu.SMEM),
            pl.BlockSpec(memory_space=pl.ANY),
            pl.BlockSpec(memory_space=pl.ANY),
        ],
        out_specs=pl.BlockSpec(memory_space=pltpu.VMEM),
        scratch_shapes=[pltpu.SemaphoreType.DMA((32,))],
        cost_estimate=pl.CostEstimate(flops=0, transcendentals=0, bytes_accessed=4 * own.size * 2 * 2),
    )(place, own, sib)


def gather_weight(shard, place, sizes):
    rows, cols = shard.shape
    part = rows // 4
    mine = lax.dynamic_slice_in_dim(shard, lax.axis_index("ctx") * part, part, 0)[None]
    for step in range(4):
        got = exchange(mine, (GATHER_ORDER[0][step], GATHER_ORDER[1][step]), sizes)
        mine = jnp.concatenate([mine, got], axis=0)
    return unpack(place, mine, exchange(mine, ("core", "core"), sizes))


def dw_kernel(place_ref, a_ref, b_ref, own_ref, sib_ref, full, sem):
    rows, cols = own_ref.shape[1:]
    a_t = a_ref[...].T
    for half in range(2):
        full[:, half * cols : (half + 1) * cols] = jnp.dot(
            a_t, b_ref[:, half * cols : (half + 1) * cols], preferred_element_type=F32
        ).astype(BF16)
    copies = []
    for half, ref in ((1, sib_ref), (0, own_ref)):
        for i in range(16):
            at = (half * 16 + i) * 2
            row = pl.multiple_of(place_ref[at] * rows, rows)
            col = pl.multiple_of(place_ref[at + 1] * cols, cols)
            copy = pltpu.make_async_copy(
                full.at[pl.ds(row, rows), pl.ds(col, cols)], ref.at[i], sem.at[half * 16 + i]
            )
            copy.start()
            copies.append(copy)
    for copy in copies:
        copy.wait()


def weight_pieces(place, a, b):
    tokens, width = a.shape
    wide = b.shape[1]
    shape = jax.ShapeDtypeStruct((16, width // 16, wide // 2), BF16)
    return pl.pallas_call(
        dw_kernel,
        out_shape=(shape, shape),
        in_specs=[
            pl.BlockSpec(memory_space=pltpu.SMEM),
            pl.BlockSpec(memory_space=pltpu.VMEM),
            pl.BlockSpec(memory_space=pltpu.VMEM),
        ],
        out_specs=(pl.BlockSpec(memory_space=pl.ANY), pl.BlockSpec(memory_space=pl.ANY)),
        scratch_shapes=[pltpu.VMEM((width, wide), BF16), pltpu.SemaphoreType.DMA((32,))],
        cost_estimate=pl.CostEstimate(
            flops=2 * tokens * width * wide,
            transcendentals=0,
            bytes_accessed=2 * (tokens * (width + wide) + width * wide),
        ),
    )(place, a, b)


def add_up(left, right):
    return (left.astype(F32) + right.astype(F32)).astype(BF16)


def reduce_grad(place, a, b, sizes):
    own, sib = weight_pieces(place, a, b)
    acc = add_up(own, exchange(sib, ("core", "core"), sizes))
    for step in range(4):
        half = acc.shape[0] // 2
        got = exchange(acc[half:], (SCATTER_ORDER[0][step], SCATTER_ORDER[1][step]), sizes)
        acc = add_up(acc[:half], got)
    return lax.all_gather(acc[0], "ctx", axis=0, tiled=True).astype(F32)


def attend_kernel(q_ref, k_ref, v_ref, idc_ref, idr_ref, o_ref, p_ref):
    length = q_ref.shape[0]
    lane = lax.broadcasted_iota(jnp.int32, (1, 128), 1)
    keys, values = k_ref[...], v_ref[...]
    block = 128
    for at in range(0, length, block):
        rows = pl.ds(at, block)
        query = q_ref[rows, :]
        allowed = idc_ref[rows, :] == idr_ref[...]
        outs = []
        for head in range(2):
            here = (lane >= 64 * head) & (lane < 64 * head + 64)
            one = jnp.where(here, query, jnp.zeros_like(query))
            scores = lax.dot_general(one, keys, (((1,), (1,)), ((), ())), preferred_element_type=F32)
            masked = jnp.where(allowed, scores * 0.125, NEG)
            top = jnp.max(masked, axis=-1, keepdims=True)
            raised = jnp.exp(masked - top)
            probs = (raised * (1.0 / jnp.sum(raised, axis=-1, keepdims=True))).astype(BF16)
            p_ref[head, rows, :] = probs
            outs.append(jnp.dot(probs, values, preferred_element_type=F32))
        o_ref[rows, :] = jnp.where(lane < 64, outs[0], outs[1]).astype(BF16)


def attend(proj, ids, heads):
    length = proj.shape[0]
    pairs = heads // 2
    half = pairs // 2
    spot = lambda which: pl.BlockSpec(
        (length, 128), lambda g: (0, (g // half) * 3 * half + which * half + g % half)
    )
    return pl.pallas_call(
        attend_kernel,
        grid=(pairs,),
        out_shape=(
            jax.ShapeDtypeStruct((length, heads * HEAD_DIM), BF16),
            jax.ShapeDtypeStruct((heads, length, length), BF16),
        ),
        in_specs=[
            spot(0),
            spot(1),
            spot(2),
            pl.BlockSpec((length, 1), lambda g: (0, 0)),
            pl.BlockSpec((1, length), lambda g: (0, 0)),
        ],
        out_specs=(
            pl.BlockSpec((length, 128), lambda g: (0, g)),
            pl.BlockSpec((2, length, length), lambda g: (g, 0, 0)),
        ),
        cost_estimate=pl.CostEstimate(
            flops=8 * heads * length * length * HEAD_DIM * 2,
            transcendentals=heads * length * length,
            bytes_accessed=2 * heads * length * length + 8 * length * heads * HEAD_DIM,
        ),
    )(proj, proj, proj, ids[:, None], ids[None, :])


def attend_back_kernel(q_ref, k_ref, v_ref, p_ref, g_ref, dq_ref, dk_ref, dv_ref):
    length = q_ref.shape[0]
    lane = lax.broadcasted_iota(jnp.int32, (1, 128), 1)
    query, keys, values, grad = q_ref[...], k_ref[...], v_ref[...], g_ref[...]
    block = 128
    dks, dvs = [], []
    dqs = [[], []]
    for head in range(2):
        here = (lane >= 64 * head) & (lane < 64 * head + 64)
        only = jnp.where(here, grad, jnp.zeros_like(grad))
        parts = []
        for at in range(0, length, block):
            probs = p_ref[head, at : at + block, :]
            wide = probs.astype(F32)
            gp = lax.dot_general(
                only[at : at + block], values, (((1,), (1,)), ((), ())), preferred_element_type=F32
            )
            weighted = jnp.sum(wide * gp, axis=-1, keepdims=True)
            gs = (wide * (gp - weighted)).astype(BF16)
            dqs[head].append(jnp.dot(gs, keys, preferred_element_type=F32))
            parts.append(gs)
        gs = jnp.concatenate(parts, axis=0)
        dks.append(lax.dot_general(gs, query, (((0,), (0,)), ((), ())), preferred_element_type=F32))
        dvs.append(
            lax.dot_general(p_ref[head], grad, (((0,), (0,)), ((), ())), preferred_element_type=F32)
        )
    low = lane < 64
    dq = jnp.where(low, jnp.concatenate(dqs[0], axis=0), jnp.concatenate(dqs[1], axis=0))
    dq_ref[...] = (dq * 0.125).astype(BF16)
    dk_ref[...] = (jnp.where(low, dks[0], dks[1]) * 0.125).astype(BF16)
    dv_ref[...] = jnp.where(low, dvs[0], dvs[1]).astype(BF16)


def attend_back(proj, probs, grad_mixed, heads):
    length = proj.shape[0]
    pairs = heads // 2
    half = pairs // 2
    spot = lambda which: pl.BlockSpec(
        (length, 128), lambda g: (0, (g // half) * 3 * half + which * half + g % half)
    )
    plain = pl.BlockSpec((length, 128), lambda g: (0, g))
    shape = jax.ShapeDtypeStruct((length, heads * HEAD_DIM), BF16)
    return pl.pallas_call(
        attend_back_kernel,
        grid=(pairs,),
        out_shape=(shape, shape, shape),
        in_specs=[
            spot(0),
            spot(1),
            spot(2),
            pl.BlockSpec((2, length, length), lambda g: (g, 0, 0)),
            plain,
        ],
        out_specs=(plain, plain, plain),
        cost_estimate=pl.CostEstimate(
            flops=16 * heads * length * length * HEAD_DIM * 2,
            transcendentals=0,
            bytes_accessed=2 * heads * length * length + 14 * length * heads * HEAD_DIM,
        ),
    )(proj, proj, proj, probs, grad_mixed)


def split_halves(value, parts):
    half = value[0].shape[1] // 2
    return jnp.concatenate(
        [part[:, y * half : (y + 1) * half] for y in range(2) for part in value], axis=1
    )


def body(
    layer_input,
    doc_ids,
    w_qkv,
    b_qv,
    w_out,
    b_out,
    ln1_gain,
    ln1_bias,
    w_up,
    b_up,
    w_down,
    b_down,
    ln2_gain,
    ln2_bias,
    out_grad,
):
    sizes = (lax.axis_size("fsdp"), lax.axis_size("ctx"), lax.axis_size("tp"))
    micro, seqs, local_len, width = layer_input.shape
    length = local_len * sizes[1]
    shard_rows, local_width = w_qkv.shape[1:]
    local_units = w_up.shape[1]
    heads = width // HEAD_DIM
    fast = sizes == (4, 4, 2)
    t = lax.axis_index("tp")
    c = lax.axis_index("ctx")

    def gather(shard):
        if fast:
            return gather_weight(shard, places(GATHER_ORDER), sizes)
        rows = lax.all_gather(shard, "fsdp", axis=0, tiled=True)
        return lax.all_gather(rows, "tp", axis=1, tiled=True)

    def reduce(a, b):
        if fast:
            return reduce_grad(places(PACK_ORDER), a, b, sizes)
        full = lax.dot_general(a, b, (((0,), (0,)), ((), ())), preferred_element_type=F32)
        part = lax.psum_scatter(full.astype(BF16), "tp", scatter_dimension=1, tiled=True)
        part = lax.psum_scatter(part, "fsdp", scatter_dimension=0, tiled=True)
        return lax.psum(part, "ctx").astype(F32)

    def whole_sequence(value):
        mine = lax.dynamic_index_in_dim(value, t, 1, keepdims=False)
        return lax.all_to_all(mine, "ctx", 0, 0, tiled=True).reshape(length, width)

    def spread_sequence(value):
        chunks = jnp.broadcast_to(
            value.reshape(sizes[1], 1, local_len, width), (sizes[1], sizes[2], local_len, width)
        ).reshape(sizes[1] * sizes[2], local_len, width)
        out = lax.all_to_all(chunks, ("ctx", "tp"), 0, 0, tiled=True)
        return out.reshape(micro, seqs, local_len, width)

    wq_shard = jnp.swapaxes(w_qkv, 0, 1).reshape(shard_rows, 3 * local_width)
    rows_b = whole_sequence(layer_input)
    wq = gather(wq_shard)
    all_ids = lax.all_gather(doc_ids, "ctx", axis=2, tiled=True)
    ids = lax.dynamic_index_in_dim(
        lax.dynamic_index_in_dim(all_ids, c, 0, keepdims=False), t, 0, keepdims=False
    )
    small = jnp.concatenate([b_qv.reshape(-1), b_up])
    small = lax.all_gather(small, "tp", axis=0, tiled=False)
    bias_qv = small[:, : 2 * local_width].reshape(2, 2, local_width)
    bias_three = jnp.stack(
        [bias_qv[:, 0], jnp.zeros_like(bias_qv[:, 0]), bias_qv[:, 1]], axis=1
    ).reshape(-1)
    bias_up = small[:, 2 * local_width :].reshape(-1)

    cot = whole_sequence(out_grad)
    wo_t = gather(w_out.T)
    wu = gather(w_up)
    wd_t = gather(w_down.T)

    rows_f = rows_b.astype(F32)
    proj = (jnp.dot(rows_b, wq, preferred_element_type=F32) + bias_three).astype(BF16)
    mixed, probs = attend(proj, ids, heads)
    nt = (((1,), (1,)), ((), ()))
    branch = lax.dot_general(mixed, wo_t, nt, preferred_element_type=F32)
    normed1, scale1 = normalize_rows(rows_f + branch + b_out)
    first = normed1 * ln1_gain + ln1_bias
    first_b = first.astype(BF16)
    hidden = jnp.dot(first_b, wu, preferred_element_type=F32) + bias_up
    activation, gelu_pull = jax.vjp(lambda value: jax.nn.gelu(value, approximate=False), hidden)
    act_b = activation.astype(BF16)
    second = lax.dot_general(act_b, wd_t, nt, preferred_element_type=F32)
    normed2, scale2 = normalize_rows(first + second + b_down)
    result = (normed2 * ln2_gain + ln2_bias).astype(BF16)
    layer_output = spread_sequence(result)

    incoming = cot.astype(F32)
    grad_gain2 = jnp.sum(incoming * normed2, axis=0)
    grad_shift2 = jnp.sum(incoming, axis=0)
    grad_z2 = normalize_back(incoming * ln2_gain, normed2, scale2)
    grad_bdown = jnp.sum(grad_z2, axis=0)
    grad_second = grad_z2.astype(BF16)
    grad_wdown = reduce(grad_second, act_b)
    grad_act = jnp.dot(grad_second, wd_t, preferred_element_type=F32)
    (grad_hidden,) = gelu_pull(grad_act)
    grad_hidden = grad_hidden.astype(BF16)
    grad_bup = jnp.sum(grad_hidden.astype(F32), axis=0)
    grad_wup = reduce(first_b, grad_hidden)
    grad_first = grad_z2 + lax.dot_general(grad_hidden, wu, nt, preferred_element_type=F32)
    grad_gain1 = jnp.sum(grad_first * normed1, axis=0)
    grad_shift1 = jnp.sum(grad_first, axis=0)
    grad_z1 = normalize_back(grad_first * ln1_gain, normed1, scale1)
    grad_bout = jnp.sum(grad_z1, axis=0)
    grad_branch = grad_z1.astype(BF16)
    grad_wout = reduce(grad_branch, mixed)
    grad_mixed = jnp.dot(grad_branch, wo_t, preferred_element_type=F32).astype(BF16)
    dq, dk, dv = attend_back(proj, probs, grad_mixed, heads)
    grad_bqv = jnp.stack([jnp.sum(dq.astype(F32), axis=0), jnp.sum(dv.astype(F32), axis=0)])
    grad_proj = split_halves((dq, dk, dv), 3)
    grad_wq = reduce(rows_b, grad_proj)
    back = lax.dot_general(grad_proj, wq, nt, preferred_element_type=F32)
    grad_x = spread_sequence((grad_z1 + back).astype(BF16))

    vectors = (
        grad_bqv.reshape(-1),
        grad_bout,
        grad_gain1,
        grad_shift1,
        grad_bup,
        grad_bdown,
        grad_gain2,
        grad_shift2,
    )
    flat = lax.psum(jnp.concatenate(vectors), AXES)
    cuts = []
    at = 0
    for vector in vectors:
        cuts.append(flat[at : at + vector.shape[0]])
        at += vector.shape[0]
    out_bqv = lax.dynamic_slice_in_dim(cuts[0].reshape(2, width), t * local_width, local_width, 1)
    out_bup = lax.dynamic_slice_in_dim(cuts[4], t * local_units, local_units, 0)
    return (
        layer_output,
        grad_x,
        jnp.swapaxes(grad_wq.reshape(shard_rows, 3, local_width), 0, 1),
        out_bqv,
        grad_wout.T,
        cuts[1],
        cuts[2],
        cuts[3],
        grad_wup,
        out_bup,
        grad_wdown.T,
        cuts[5],
        cuts[6],
        cuts[7],
    )


def solution(mesh):
    return jax.shard_map(
        body,
        mesh=mesh,
        in_specs=(
            P(None, "fsdp", "ctx", None),
            P(None, "fsdp", "ctx"),
            P(None, "fsdp", "tp"),
            P(None, "tp"),
            P("tp", "fsdp"),
            P(),
            P(),
            P(),
            P("fsdp", "tp"),
            P("tp"),
            P("tp", "fsdp"),
            P(),
            P(),
            P(),
            P(None, "fsdp", "ctx", None),
        ),
        out_specs=(
            P(None, "fsdp", "ctx", None),
            P(None, "fsdp", "ctx", None),
            P(None, "fsdp", "tp"),
            P(None, "tp"),
            P("tp", "fsdp"),
            P(),
            P(),
            P(),
            P("fsdp", "tp"),
            P("tp"),
            P("tp", "fsdp"),
            P(),
            P(),
            P(),
        ),
        check_vma=False,
    )
```

time: 963 us -> 480 us (0.50)
  waiting for transfers between devices: 571 us -> 95.9 us
  Pallas kernels: 0 us -> 83.5 us
  matrix products: 130 us -> 50.3 us
  local copies, waits for them, and re-layouts: 124 us -> 58 us
  starting transfers between devices: 2.25 us -> 60.8 us
  blocking collectives: 53.1 us -> 95.9 us
  other arithmetic: 59.6 us -> 28.7 us
  between operations: 17.5 us -> 1.97 us
    psum x5 -> x0, waiting for transfers between devices: 233 us -> none  [the longest x1 84.9 us: body(): lax.psum(jnp.dot(mixed_b, wo_all, preferred_element_type=jnp.float32), 'tp')]
    all_gather x7 -> x0, waiting for transfers between devices: 162 us -> none  [the longest x1 45.5 us: collect_weights(): lax.all_gather(weights[2], 'fsdp', axis=0, tiled=True)]
    reduce_scatter x3 -> x0, waiting for transfers between devices: 120 us -> none  [the longest x1 50 us: spread_grads(): lax.psum_scatter(grads[3].astype(jnp.bfloat16), 'fsdp', scatter_dimension...]
    ppermute x0 -> x40, waiting for transfers between devices: none -> 84.5 us  [exchange(): return lax.ppermute(value, AXES, pairs)]
    pallas_call x0 -> x10, Pallas kernels: none -> 83.5 us  [the longest x4 24.5 us: weight_pieces(): pl.pallas_call(dw_kernel, out_shape=(shape, shape), in_specs=[pl.BlockSpe...]
    dot_general x72 -> x8, matrix products: 130 us -> 50.3 us  [the longest x1 19.1 us: body(): hidden = jnp.dot(first_b, wu, preferred_element_type=F32) + bias_up]
    unnamed x25 -> x0, waiting for transfers between devices: 55.9 us -> none
    unnamed x493 -> x113, local copies, waits for them, and re-layouts: 79.3 us -> 33 us
  transfers between devices with their start and end apart: 20 -> 44, of which waited for: 15 -> 15; matrix products, arithmetic and copies ran while one was open for 17% -> 21% of each run, Pallas kernels for 0% -> 10%
where the time goes in v1:
time: 480 us; the launch traced here: 475 us
  blocking collectives  95.9 us (20%)
  waiting for transfers between devices  95.9 us (20%)
  Pallas kernels  83.5 us (17%)
  starting transfers between devices  60.8 us (13%)
  local copies, waits for them, and re-layouts  58 us (12%)
  matrix products  50.3 us (10%)
  other arithmetic  28.7 us (6%)
    ppermute x40, waiting for transfers between devices, exchange(): return lax.ppermute(value, AXES, pairs)  84.5 us
    all_gather x4, blocking collectives, reduce_grad(): return lax.all_gather(acc[0], 'ctx', axis=0, tiled=True).astype(F32)  46 us
    ppermute x40, starting transfers between devices, exchange(): return lax.ppermute(value, AXES, pairs)  43.9 us
    psum x1, blocking collectives, body(): flat = lax.psum(jnp.concatenate(vectors), AXES)  40.4 us
    unnamed x113, local copies, waits for them, and re-layouts  33 us
    pallas_call x4, Pallas kernels, weight_pieces(): pl.pallas_call(dw_kernel, out_shape=(shape, shape), in_specs=[pl.BlockSpe...  24.5 us
    pallas_call x1, Pallas kernels, attend(): pl.pallas_call(attend_kernel, grid=(pairs,), out_shape=(jax.ShapeDtypeStr...  20 us
    pallas_call x1, Pallas kernels, attend_back(): pl.pallas_call(attend_back_kernel, grid=(pairs,), out_shape=(shape, shape...  19.8 us
  transfers between devices with their start and end apart: 44, of which 15 were waited for; matrix products, arithmetic and copies ran while one was open for 21% of the time, Pallas kernels for 10%

profile of v1, /device:TPU:0, one launch (start us, length us, event | category | flops | bytes accessed | tf_op | source)
XLA Modules:
  0.0 475.1 jit_solution(14138029090333363602)
XLA Ops:
  2.2 3.0 collective-permute-start.5
  6.2 3.5 all-to-all-start.2
  12.0 2.0 collective-permute-start.10
  15.7 4.4 all-gather.5
  20.1 5.1 %all_gather.23 = s32[4,2,512]{2,1,0:T(2,128)S(1)} all-gather(s32[4,2,128]{2,1,0:T(2,128)S(1)} %copy-done.32), channel_id=1, replica_groups=mesh['fsdp'=4,'ctx'=4,'tp'=2] {'ctx'}, dimensions={2}, use_global_device_ids=true | all-gather | bytes 20480 | tf_op jit(solution)/shard_map/all_gather | solution.py:368
  25.3 2.1 dynamic-slice_bitcast_fusion.1
  31.0 3.1 collective-permute-start.6
  34.7 3.7 collective-permute-done.6
  42.6 1.9 collective-permute-start.11
  47.1 2.0 collective-permute-start.8
  49.8 17.0 %collective-permute-done.1 = bf16[2,48,1152]{2,1,0:T(8,128)(2,1)S(1)} collective-permute-done((bf16[2,48,1152]{2,1,0:T(8,128)(2,1)S(1)}, bf16[2,48,1152]{2,1,0:T(8,128)(2,1)S(1)}, u32[]{:S(2)}, u32[]{:S(2)}) %collective-permute-start.1) | collective-permute-done | bytes 221216 | tf_op jit(solution)/shard_map/ppermute | solution.py:48
  68.1 5.0 %collective-permute-done.11 = bf16[2,48,1536]{2,1,0:T(8,128)(2,1)S(1)} collective-permute-done((bf16[2,48,1536]{2,1,0:T(8,128)(2,1)S(1)}, bf16[2,48,1536]{2,1,0:T(8,128)(2,1)S(1)}, u32[]{:S(2)}, u32[]{:S(2)}) %collective-permute-start.11) | collective-permute-done | bytes 294944 | tf_op jit(solution)/shard_map/ppermute | solution.py:48
  73.7 4.7 collective-permute-done.16
  81.6 4.1 collective-permute-done.12
  86.8 9.3 %collective-permute-done.3 = bf16[8,48,1152]{2,1,0:T(8,128)(2,1)S(1)} collective-permute-done((bf16[8,48,1152]{2,1,0:T(8,128)(2,1)S(1)}, bf16[8,48,1152]{2,1,0:T(8,128)(2,1)S(1)}, u32[]{:S(2)}, u32[]{:S(2)}) %collective-permute-start.3) | collective-permute-done | bytes 884768 | tf_op jit(solution)/shard_map/ppermute | solution.py:48
  97.1 3.0 collective-permute-start.4
  102.0 4.7 all-to-all-start
  109.6 3.2 shard_map.256
  112.8 2.4 constant_dynamic-update-slice_fusion.10.own_ref
  115.7 10.0 %collective-permute-done.18 = bf16[8,48,1536]{2,1,0:T(8,128)(2,1)} collective-permute-done((bf16[8,48,1536]{2,1,0:T(8,128)(2,1)}, bf16[8,48,1536]{2,1,0:T(8,128)(2,1)}, u32[]{:S(2)}, u32[]{:S(2)}) %collective-permute-start.18) | collective-permute-done | bytes 1179680 | tf_op jit(solution)/shard_map/ppermute | solution.py:48
  125.7 2.4 constant_dynamic-update-slice_fusion.15.own_ref
  128.0 4.8 %shard_map.254 = bf16[768,2304]{1,0:T(8,128)(2,1)} custom-call(s32[64]{0:T(128)} %stack.182.place_ref, bf16[16,48,1152]{2,1,0:T(8,128)(2,1)} %constant_dynamic-update-slice_fusion.own_ref, bf16[16,48,1152]{2,1,0:T(8,128)(2,1)} %collective-permute-done.4.sib_ref), custom_call_target="tpu_custom_call" | custom-call | bytes 14155776 | tf_op jit(solution)/shard_map/pallas_call | solution.py:106
  132.8 5.7 %fusion.6.q_ref.k_ref.v_ref = bf16[512,2304]{1,0:T(8,128)(2,1)} fusion(bf16[512,768]{1,0:T(8,128)(2,1)} %bitcast.1.a_ref, bf16[768,2304]{1,0:T(8,128)(2,1)} %shard_map.254, f32[2304]{0:T(1024)S(1)} %add.197), kind=kOutput, calls=%fused_computation.21 | convolution fusion | flops 1814298624 | bytes 6693888 | tf_op jit(solution)/shard_map/dot_general | solution.py:386
  138.5 20.0 %shard_map.255 = (bf16[512,768]{1,0:T(8,128)(2,1)}, bf16[12,512,512]{2,1,0:T(8,128)(2,1)}) custom-call(bf16[512,2304]{1,0:T(8,128)(2,1)} %fusion.6.q_ref.k_ref.v_ref, bf16[512,2304]{1,0:T(8,128)(2,1)} %fusion.6.q_ref.k_ref.v_ref, bf16[512,2304]{1,0:T(8,128)(2,1)} %fusion.6.q_ref.k_ref.v_ref, s32[512,1]{1,0:T(8,128)} %copy.34.idc_ref, ...), custom_call_target="tpu_custom_call" | custom-call | flops 3221225472 | bytes 9437184 | tf_op jit(solution)/shard_map/pallas_call | solution.py:218
  158.6 2.3 fusion.23
  161.5 5.6 %shard_map.257 = bf16[768,3072]{1,0:T(8,128)(2,1)} custom-call(s32[64]{0:T(128)} %stack.182.place_ref, bf16[16,48,1536]{2,1,0:T(8,128)(2,1)} %constant_dynamic-update-slice_fusion.10.own_ref, bf16[16,48,1536]{2,1,0:T(8,128)(2,1)} %collective-permute-done.14.sib_ref), custom_call_target="tpu_custom_call" | custom-call | bytes 18874368 | tf_op jit(solution)/shard_map/pallas_call | solution.py:106
  167.2 19.1 %multiply_convert_fusion = (bf16[512,3072]{1,0:T(8,128)(2,1)}, f32[512,3072]{1,0:T(8,128)}, f32[512,3072]{1,0:T(8,128)}) fusion(f32[3072]{0:T(1024)S(1)} %copy-done.28, bf16[512,768]{1,0:T(8,128)(2,1)S(1)} %fusion.14.a_ref, bf16[768,3072]{1,0:T(8,128)(2,1)} %shard_map.257), kind=kOutput, calls=%fused_computation.4 | convolution fusion | flops 2519728128 | bytes 21245952 | tf_op jit(solution)/shard_map/dot_general | solution.py:393
  186.3 5.5 %shard_map.258 = bf16[768,3072]{1,0:T(8,128)(2,1)} custom-call(s32[64]{0:T(128)} %stack.182.place_ref, bf16[16,48,1536]{2,1,0:T(8,128)(2,1)} %constant_dynamic-update-slice_fusion.15.own_ref, bf16[16,48,1536]{2,1,0:T(8,128)(2,1)} %collective-permute-done.19.sib_ref), custom_call_target="tpu_custom_call" | custom-call | bytes 18874368 | tf_op jit(solution)/shard_map/pallas_call | solution.py:106
  191.9 6.1 %fusion.24 = (f32[512]{0:T(512)S(1)}, f32[512,768]{1,0:T(8,128)S(1)}) fusion(f32[768]{0:T(1024)S(1)} %copy-done.35, bf16[512,3072]{1,0:T(8,128)(2,1)} %get-tuple-element.84.b_ref, bf16[768,3072]{1,0:T(8,128)(2,1)} %shard_map.258, f32[768]{0:T(1024)S(1)} %copy-done.31, f32[768]{0:T(1024)S(1)} %copy-done.27, f32[512]{0:T(512)S(1)} %add_rsqrt_fusion.1, ...), kind=kOutput, calls=%fused_computation.145 | convolution fusion | flops 2418671104 | bytes 11025408 | tf_op jit(solution)/shard_map/dot_general | solution.py:396
  201.0 1.8 copy-done.4
  202.8 6.8 %convert_reduce_fusion = (f32[3072]{0:T(1024)S(1)}, bf16[512,3072]{1,0:T(8,128)(2,1)S(1)}) fusion(f32[512,3072]{1,0:T(8,128)S(1)} %copy-done.37, f32[512,3072]{1,0:T(8,128)} %get-tuple-element.105, f32[3072]{0:T(1024)S(1)} %copy-done.28, bf16[512,768]{1,0:T(8,128)(2,1)S(1)} %convert_element_type.243.a_ref, bf16[768,3072]{1,0:T(8,128)(2,1)S(1)} %copy-done.4), kind=kOutput, calls=%fused_computation.2 | convolution fusion | flops 2442654720 | bytes 21258240 | tf_op jit(solution)/shard_map/dot_general | solution.py:408
  209.7 3.1 multiply_reduce_fusion
  216.2 19.8 %shard_map.259 = (bf16[512,768]{1,0:T(8,128)(2,1)}, bf16[512,768]{1,0:T(8,128)(2,1)}, bf16[512,768]{1,0:T(8,128)(2,1)}) custom-call(bf16[512,2304]{1,0:T(8,128)(2,1)} %fusion.6.q_ref.k_ref.v_ref, bf16[512,2304]{1,0:T(8,128)(2,1)} %fusion.6.q_ref.k_ref.v_ref, bf16[512,2304]{1,0:T(8,128)(2,1)} %fusion.6.q_ref.k_ref.v_ref, ...), custom_call_target="tpu_custom_call" | custom-call | flops 6442450944 | bytes 11796480 | tf_op jit(solution)/shard_map/pallas_call | solution.py:286
  237.3 1.8 slice_dynamic-update-slice_fusion.5
  239.1 3.7 shard_map.261
  242.8 7.3 %shard_map.262 = (bf16[16,48,1536]{2,1,0:T(8,128)(2,1)}, bf16[16,48,1536]{2,1,0:T(8,128)(2,1)}) custom-call(s32[64]{0:T(128)} %stack.212.place_ref, bf16[512,768]{1,0:T(8,128)(2,1)} %copy-done.14, bf16[512,3072]{1,0:T(8,128)(2,1)} %copy-done.36), custom_call_target="tpu_custom_call" | custom-call | flops 2415919104 | bytes 8650752 | tf_op jit(solution)/shard_map/pallas_call | solution.py:156
  250.9 1.8 slice_dynamic-update-slice_fusion.4
  256.1 6.2 %shard_map.260 = (bf16[16,48,1152]{2,1,0:T(8,128)(2,1)}, bf16[16,48,1152]{2,1,0:T(8,128)(2,1)}) custom-call(s32[64]{0:T(128)} %stack.212.place_ref, bf16[512,768]{1,0:T(8,128)(2,1)} %bitcast.1.a_ref, bf16[512,2304]{1,0:T(8,128)(2,1)} %slice_dynamic-update-slice_fusion.b_ref), custom_call_target="tpu_custom_call" | custom-call | flops 1811939328 | bytes 6684672 | tf_op jit(solution)/shard_map/pallas_call | solution.py:156
  263.0 5.7 %add_convert_fusion.7 = bf16[512,768]{1,0:T(8,128)(2,1)} fusion(f32[512,768]{1,0:T(8,128)S(1)} %get-tuple-element.81, bf16[512,2304]{1,0:T(8,128)(2,1)} %slice_dynamic-update-slice_fusion.b_ref, bf16[768,2304]{1,0:T(8,128)(2,1)} %shard_map.254), kind=kOutput, calls=%fused_computation.40 | convolution fusion | flops 1812725760 | bytes 8257536 | tf_op jit(solution)/shard_map/dot_general | solution.py:425
  270.3 40.4 %psum.7 = f32[9216]{0:T(1024)} all-reduce(f32[9216]{0:T(1024)S(1)} %constant_dynamic-update-slice_fusion.22), channel_id=1, replica_groups=mesh['fsdp'=4,'ctx'=4,'tp'=2] {'fsdp','ctx','tp'}, use_global_device_ids=true, to_apply=%region_17.18 | all-reduce | flops 9216 | bytes 73728 | tf_op jit(solution)/shard_map/psum | solution.py:438
  310.7 7.4 %shard_map.263 = (bf16[16,48,1536]{2,1,0:T(8,128)(2,1)}, bf16[16,48,1536]{2,1,0:T(8,128)(2,1)}) custom-call(s32[64]{0:T(128)} %stack.212.place_ref, bf16[512,768]{1,0:T(8,128)(2,1)} %copy-done.13, bf16[512,3072]{1,0:T(8,128)(2,1)} %get-tuple-element.84.b_ref), custom_call_target="tpu_custom_call" | custom-call | flops 2415919104 | bytes 8650752 | tf_op jit(solution)/shard_map/pallas_call | solution.py:156
  318.2 2.3 collective-permute-start.27
  320.5 1.9 add_convert_fusion.3
  325.3 3.1 collective-permute-start.28
  330.4 4.4 all-to-all-start.1
  338.5 2.8 collective-permute-done.29
  341.3 18.8 %all-gather.2 = bf16[1,192,384]{2,1,0:T(8,128)(2,1)} all-gather(bf16[1,48,384]{2,1,0:T(8,128)(2,1)S(1)} %add_convert_fusion.22), channel_id=4, replica_groups=mesh['fsdp'=4,'ctx'=4,'tp'=2] {'ctx'}, dimensions={1}, use_global_device_ids=true | all-gather | bytes 184320 | tf_op jit(solution)/shard_map/all_gather | solution.py:185
  363.0 2.4 add_convert_fusion.2
  367.8 3.8 collective-permute-done.22
  371.8 2.4 broadcast_in_dim.26
  374.2 4.3 all-to-all-start.3
  378.5 3.1 add_convert_fusion.1
  384.1 1.9 collective-permute-start.36
  386.1 2.9 collective-permute-start.24
  389.7 11.4 %all-to-all-done.3 = bf16[8,128,768]{2,1,0:T(8,128)(2,1)} async-done(((bf16[8,128,768]{2,1,0:T(8,128)(2,1)}), bf16[8,128,768]{2,1,0:T(8,128)(2,1)}, u32[]{:S(2)}, u32[]{:S(2)}) %all-to-all-start.3) | async-done | bytes 1572896 | tf_op jit(solution)/shard_map/all_to_all | solution.py:362
  403.8 10.0 %collective-permute-done.36 = bf16[8,48,1536]{2,1,0:T(8,128)(2,1)} collective-permute-done((bf16[8,48,1536]{2,1,0:T(8,128)(2,1)}, bf16[8,48,1536]{2,1,0:T(8,128)(2,1)}, u32[]{:S(2)}, u32[]{:S(2)}) %collective-permute-start.36) | collective-permute-done | bytes 1179680 | tf_op jit(solution)/shard_map/ppermute | solution.py:48
  416.8 11.5 %all-gather.1 = bf16[1,192,1152]{2,1,0:T(8,128)(2,1)} all-gather(bf16[1,48,1152]{2,1,0:T(8,128)(2,1)S(1)} %add_convert_fusion.20), channel_id=3, replica_groups=mesh['fsdp'=4,'ctx'=4,'tp'=2] {'ctx'}, dimensions={1}, use_global_device_ids=true | all-gather | bytes 552960 | tf_op jit(solution)/shard_map/all_gather | solution.py:185
  435.3 6.1 %collective-permute-done.33 = bf16[2,48,1536]{2,1,0:T(8,128)(2,1)S(1)} collective-permute-done((bf16[2,48,1536]{2,1,0:T(8,128)(2,1)S(1)}, bf16[2,48,1536]{2,1,0:T(8,128)(2,1)S(1)}, u32[]{:S(2)}, u32[]{:S(2)}) %collective-permute-start.33) | collective-permute-done | bytes 294944 | tf_op jit(solution)/shard_map/ppermute | solution.py:48
  443.0 4.7 collective-permute-done.38
  448.9 2.4 collective-permute-done.34
  451.4 8.1 %all-gather.3 = bf16[1,192,1536]{2,1,0:T(8,128)(2,1)S(1)} all-gather(bf16[1,48,1536]{2,1,0:T(8,128)(2,1)S(1)} %add_convert_fusion.18), channel_id=5, replica_groups=mesh['fsdp'=4,'ctx'=4,'tp'=2] {'ctx'}, dimensions={1}, use_global_device_ids=true | all-gather | bytes 737280 | tf_op jit(solution)/shard_map/all_gather | solution.py:185
  460.7 7.7 %all-gather.4 = bf16[1,192,1536]{2,1,0:T(8,128)(2,1)S(1)} all-gather(bf16[1,48,1536]{2,1,0:T(8,128)(2,1)S(1)} %add_convert_fusion.17), channel_id=6, replica_groups=mesh['fsdp'=4,'ctx'=4,'tp'=2] {'ctx'}, dimensions={1}, use_global_device_ids=true | all-gather | bytes 737280 | tf_op jit(solution)/shard_map/all_gather | solution.py:185
  469.5 2.8 copy.71
  472.2 2.7 copy.72
  (270 shorter events, 80.5 us)
Async XLA Ops:
  0.7 9.0 %copy-start.23 = (bf16[3,192,384]{2,1,0:T(8,128)(2,1)S(1)}, bf16[3,192,384]{2,1,0:T(8,128)(2,1)}, u32[]{:S(2)}) copy-start(bf16[3,192,384]{2,1,0:T(8,128)(2,1)} %param.17) | copy-start | bytes 1327108
  2.2 28.8 %collective-permute-start.5 = (bf16[1,48,384]{2,1,0:T(8,128)(2,1)S(1)}, bf16[1,48,384]{2,1,0:T(8,128)(2,1)S(1)}, u32[]{:S(2)}, u32[]{:S(2)}) collective-permute-start(bf16[1,48,384]{2,1,0:T(8,128)(2,1)S(1)} %get-tuple-element.89), channel_id=1, source_target_pairs={{0,8},{1,9},{2,10},{3,11},{4,12},{5,13},{6,14},{7,15},{8,0},{9,1},... | collective-permute-start | bytes 110600 | tf_op jit(solution)/shard_map/ppermute | solution.py:48
  5.2 10.4 %copy-start.34 = (f32[2,384]{1,0:T(2,128)S(1)}, f32[2,384]{1,0:T(2,128)}, u32[]{:S(2)}) copy-start(f32[2,384]{1,0:T(2,128)} %param.18) | copy-start | bytes 9220
  5.2 10.4 %copy-start.29 = (f32[1536]{0:T(1024)S(1)}, f32[1536]{0:T(1024)}, u32[]{:S(2)}) copy-start(f32[1536]{0:T(1024)} %param.24) | copy-start | bytes 18436
  5.2 14.9 %copy-start.32 = (s32[4,2,128]{2,1,0:T(2,128)S(1)}, s32[4,2,128]{2,1,0:T(2,128)}, u32[]{:S(2)}) copy-start(s32[4,2,128]{2,1,0:T(2,128)} %param.16) | copy-start | bytes 12292
  6.2 95.8 %all-to-all-start.2 = ((bf16[4,128,768]{2,1,0:T(8,128)(2,1)}), bf16[4,128,768]{2,1,0:T(8,128)(2,1)S(1)}, u32[]{:S(2)}, u32[]{:S(2)}) async-start(bf16[4,128,768]{2,1,0:T(8,128)(2,1)} %dynamic-slice_bitcast_fusion), calls=%async_computation.2 | async-start | bytes 1572864 | tf_op jit(solution)/shard_map/all_to_all | solution.py:356
  10.4 29.7 %collective-permute-start = (bf16[1,48,1152]{2,1,0:T(8,128)(2,1)S(1)}, bf16[1,48,1152]{2,1,0:T(8,128)(2,1)S(1)}, u32[]{:S(2)}, u32[]{:S(2)}) collective-permute-start(bf16[1,48,1152]{2,1,0:T(8,128)(2,1)S(1)} %get-tuple-element.91), channel_id=1, source_target_pairs={{0,8},{1,9},{2,10},{3,11},{4,12},{5,13},{6,14},{7,15},{8,0},{9,1},... | collective-permute-start | bytes 331784 | tf_op jit(solution)/shard_map/ppermute | solution.py:48
  12.0 30.5 %collective-permute-start.10 = (bf16[1,48,1536]{2,1,0:T(8,128)(2,1)S(1)}, bf16[1,48,1536]{2,1,0:T(8,128)(2,1)S(1)}, u32[]{:S(2)}, u32[]{:S(2)}) collective-permute-start(bf16[1,48,1536]{2,1,0:T(8,128)(2,1)S(1)} %get-tuple-element.87), channel_id=1, source_target_pairs={{0,8},{1,9},{2,10},{3,11},{4,12},{5,13},{6,14},{7,15},{8,0},{9,1},... | collective-permute-start | bytes 442376 | tf_op jit(solution)/shard_map/ppermute | solution.py:48
  15.6 28.9 %collective-permute-start.15 = (bf16[1,48,1536]{2,1,0:T(8,128)(2,1)S(1)}, bf16[1,48,1536]{2,1,0:T(8,128)(2,1)S(1)}, u32[]{:S(2)}, u32[]{:S(2)}) collective-permute-start(bf16[1,48,1536]{2,1,0:T(8,128)(2,1)S(1)} %get-tuple-element.83), channel_id=1, source_target_pairs={{0,8},{1,9},{2,10},{3,11},{4,12},{5,13},{6,14},{7,15},{8,0},{9,1},... | collective-permute-start | bytes 442376 | tf_op jit(solution)/shard_map/ppermute | solution.py:48
  31.0 7.4 %collective-permute-start.6 = (bf16[2,48,384]{2,1,0:T(8,128)(2,1)S(1)}, bf16[2,48,384]{2,1,0:T(8,128)(2,1)S(1)}, u32[]{:S(2)}, u32[]{:S(2)}) collective-permute-start(bf16[2,48,384]{2,1,0:T(8,128)(2,1)S(1)} %pad_maximum_fusion.11), channel_id=1, source_target_pairs={{0,16},{1,17},{2,18},{3,19},{4,20},{5,21},{6,22},{7,23},{8,24},{9,... | collective-permute-start | bytes 221192 | tf_op jit(solution)/shard_map/ppermute | solution.py:48
  38.4 8.6 %collective-permute-start.7 = (bf16[4,48,384]{2,1,0:T(8,128)(2,1)S(1)}, bf16[4,48,384]{2,1,0:T(8,128)(2,1)S(1)}, u32[]{:S(2)}, u32[]{:S(2)}) collective-permute-start(bf16[4,48,384]{2,1,0:T(8,128)(2,1)S(1)} %pad_maximum_fusion.10), channel_id=1, source_target_pairs={{0,1},{1,0},{2,6},{3,7},{4,5},{5,4},{6,2},{7,3},{8,9},{9,8},{10,14... | collective-permute-start | bytes 442376 | tf_op jit(solution)/shard_map/ppermute | solution.py:48
  40.1 26.6 %collective-permute-start.1 = (bf16[2,48,1152]{2,1,0:T(8,128)(2,1)S(1)}, bf16[2,48,1152]{2,1,0:T(8,128)(2,1)S(1)}, u32[]{:S(2)}, u32[]{:S(2)}) collective-permute-start(bf16[2,48,1152]{2,1,0:T(8,128)(2,1)S(1)} %pad_maximum_fusion.9), channel_id=1, source_target_pairs={{0,16},{1,17},{2,18},{3,19},{4,20},{5,21},{6,22},{7,23},{8,24},{9,... | collective-permute-start | bytes 663560 | tf_op jit(solution)/shard_map/ppermute | solution.py:48
  42.6 30.5 %collective-permute-start.11 = (bf16[2,48,1536]{2,1,0:T(8,128)(2,1)S(1)}, bf16[2,48,1536]{2,1,0:T(8,128)(2,1)S(1)}, u32[]{:S(2)}, u32[]{:S(2)}) collective-permute-start(bf16[2,48,1536]{2,1,0:T(8,128)(2,1)S(1)} %pad_maximum_fusion.7), channel_id=1, source_target_pairs={{0,16},{1,17},{2,18},{3,19},{4,20},{5,21},{6,22},{7,23},{8,24},{9,... | collective-permute-start | bytes 884744 | tf_op jit(solution)/shard_map/ppermute | solution.py:48
  44.5 33.9 %collective-permute-start.16 = (bf16[2,48,1536]{2,1,0:T(8,128)(2,1)S(1)}, bf16[2,48,1536]{2,1,0:T(8,128)(2,1)S(1)}, u32[]{:S(2)}, u32[]{:S(2)}) collective-permute-start(bf16[2,48,1536]{2,1,0:T(8,128)(2,1)S(1)} %pad_maximum_fusion.8), channel_id=1, source_target_pairs={{0,16},{1,17},{2,18},{3,19},{4,20},{5,21},{6,22},{7,23},{8,24},{9,... | collective-permute-start | bytes 884744 | tf_op jit(solution)/shard_map/ppermute | solution.py:48
  47.1 54.7 %collective-permute-start.8 = (bf16[8,48,384]{2,1,0:T(8,128)(2,1)S(1)}, bf16[8,48,384]{2,1,0:T(8,128)(2,1)S(1)}, u32[]{:S(2)}, u32[]{:S(2)}) collective-permute-start(bf16[8,48,384]{2,1,0:T(8,128)(2,1)S(1)} %pad_maximum_fusion.6), channel_id=1, source_target_pairs={{0,4},{1,5},{2,3},{3,2},{4,0},{5,1},{6,7},{7,6},{8,12},{9,13},{10,... | collective-permute-start | bytes 884744 | tf_op jit(solution)/shard_map/ppermute | solution.py:48
  66.8 11.7 %collective-permute-start.2 = (bf16[4,48,1152]{2,1,0:T(8,128)(2,1)S(1)}, bf16[4,48,1152]{2,1,0:T(8,128)(2,1)S(1)}, u32[]{:S(2)}, u32[]{:S(2)}) collective-permute-start(bf16[4,48,1152]{2,1,0:T(8,128)(2,1)S(1)} %pad_maximum_fusion.5), channel_id=1, source_target_pairs={{0,1},{1,0},{2,6},{3,7},{4,5},{5,4},{6,2},{7,3},{8,9},{9,8},{10,14... | collective-permute-start | bytes 1327112 | tf_op jit(solution)/shard_map/ppermute | solution.py:48
  73.1 12.5 %collective-permute-start.12 = (bf16[4,48,1536]{2,1,0:T(8,128)(2,1)S(1)}, bf16[4,48,1536]{2,1,0:T(8,128)(2,1)S(1)}, u32[]{:S(2)}, u32[]{:S(2)}) collective-permute-start(bf16[4,48,1536]{2,1,0:T(8,128)(2,1)S(1)} %pad_maximum_fusion.3), channel_id=1, source_target_pairs={{0,1},{1,0},{2,6},{3,7},{4,5},{5,4},{6,2},{7,3},{8,9},{9,8},{10,14... | collective-permute-start | bytes 1769480 | tf_op jit(solution)/shard_map/ppermute | solution.py:48
  78.5 21.6 %collective-permute-start.17 = (bf16[4,48,1536]{2,1,0:T(8,128)(2,1)S(1)}, bf16[4,48,1536]{2,1,0:T(8,128)(2,1)S(1)}, u32[]{:S(2)}, u32[]{:S(2)}) collective-permute-start(bf16[4,48,1536]{2,1,0:T(8,128)(2,1)S(1)} %pad_maximum_fusion.4), channel_id=1, source_target_pairs={{0,1},{1,0},{2,6},{3,7},{4,5},{5,4},{6,2},{7,3},{8,9},{9,8},{10,14... | collective-permute-start | bytes 1769480 | tf_op jit(solution)/shard_map/ppermute | solution.py:48
  78.7 17.4 %collective-permute-start.3 = (bf16[8,48,1152]{2,1,0:T(8,128)(2,1)S(1)}, bf16[8,48,1152]{2,1,0:T(8,128)(2,1)S(1)}, u32[]{:S(2)}, u32[]{:S(2)}) collective-permute-start(bf16[8,48,1152]{2,1,0:T(8,128)(2,1)S(1)} %pad_maximum_fusion.2), channel_id=1, source_target_pairs={{0,4},{1,5},{2,3},{3,2},{4,0},{5,1},{6,7},{7,6},{8,12},{9,13},{10,... | collective-permute-start | bytes 2654216 | tf_op jit(solution)/shard_map/ppermute | solution.py:48
  86.8 15.1 %copy-start.16 = (bf16[16,48,384]{2,1,0:T(8,128)(2,1)S(1)}, bf16[16,48,384]{2,1,0:T(8,128)(2,1)}, u32[]{:S(2)}) copy-start(bf16[16,48,384]{2,1,0:T(8,128)(2,1)} %constant_dynamic-update-slice_fusion.6) | copy-start | bytes 1769476
  86.8 26.1 %collective-permute-start.13 = (bf16[8,48,1536]{2,1,0:T(8,128)(2,1)}, bf16[8,48,1536]{2,1,0:T(8,128)(2,1)}, u32[]{:S(2)}, u32[]{:S(2)}) collective-permute-start(bf16[8,48,1536]{2,1,0:T(8,128)(2,1)} %pad_maximum_fusion), channel_id=1, source_target_pairs={{0,4},{1,5},{2,3},{3,2},{4,0},{5,1},{6,7},{7,6},{8,12},{9,13},{10,... | collective-permute-start | bytes 3538952 | tf_op jit(solution)/shard_map/ppermute | solution.py:48
  97.1 9.6 %copy-start.26 = (f32[768]{0:T(1024)S(1)}, f32[768]{0:T(1024)}, u32[]{:S(2)}) copy-start(f32[768]{0:T(1024)} %param.27) | copy-start | bytes 9220
  97.1 31.0 %collective-permute-start.4 = (bf16[16,48,1152]{2,1,0:T(8,128)(2,1)}, bf16[16,48,1152]{2,1,0:T(8,128)(2,1)}, u32[]{:S(2)}, u32[]{:S(2)}) collective-permute-start(bf16[16,48,1152]{2,1,0:T(8,128)(2,1)} %constant_dynamic-update-slice_fusion.own_ref), channel_id=1, source_target_pairs={{0,2},{1,3},{2,0},{3,1},{4,6},{5,7},{6,4},{7,5},{8,10},{9,11},{10,... | collective-permute-start | bytes 5308424 | tf_op jit(solution)/shard_map/ppermute | solution.py:48
  101.2 24.4 %collective-permute-start.18 = (bf16[8,48,1536]{2,1,0:T(8,128)(2,1)}, bf16[8,48,1536]{2,1,0:T(8,128)(2,1)}, u32[]{:S(2)}, u32[]{:S(2)}) collective-permute-start(bf16[8,48,1536]{2,1,0:T(8,128)(2,1)} %pad_maximum_fusion.1), channel_id=1, source_target_pairs={{0,4},{1,5},{2,3},{3,2},{4,0},{5,1},{6,7},{7,6},{8,12},{9,13},{10,... | collective-permute-start | bytes 3538952 | tf_op jit(solution)/shard_map/ppermute | solution.py:48
  101.9 6.9 %copy-start.17 = (bf16[16,48,384]{2,1,0:T(8,128)(2,1)}, bf16[16,48,384]{2,1,0:T(8,128)(2,1)S(1)}, u32[]{:S(2)}) copy-start(bf16[16,48,384]{2,1,0:T(8,128)(2,1)S(1)} %constant_dynamic-update-slice_fusion.5.own_ref) | copy-start | bytes 1769476
  101.9 6.9 %collective-permute-start.9 = (bf16[16,48,384]{2,1,0:T(8,128)(2,1)S(1)}, bf16[16,48,384]{2,1,0:T(8,128)(2,1)S(1)}, u32[]{:S(2)}, u32[]{:S(2)}) collective-permute-start(bf16[16,48,384]{2,1,0:T(8,128)(2,1)S(1)} %constant_dynamic-update-slice_fusion.5.own_ref), channel_id=1, source_target_pairs={{0,2},{1,3},{2,0},{3,1},{4,6},{5,7},{6,4},{7,5},{8,10},{9,11},{10,... | collective-permute-start | bytes 1769480 | tf_op jit(solution)/shard_map/ppermute | solution.py:48
  102.0 30.9 %all-to-all-start = ((bf16[4,128,768]{2,1,0:T(8,128)(2,1)}), bf16[4,128,768]{2,1,0:T(8,128)(2,1)}, u32[]{:S(2)}, u32[]{:S(2)}) async-start(bf16[4,128,768]{2,1,0:T(8,128)(2,1)} %dynamic-slice_bitcast_fusion.1), calls=%async_computation | async-start | bytes 1572864 | tf_op jit(solution)/shard_map/all_to_all | solution.py:356
  115.2 46.3 %collective-permute-start.14 = (bf16[16,48,1536]{2,1,0:T(8,128)(2,1)}, bf16[16,48,1536]{2,1,0:T(8,128)(2,1)}, u32[]{:S(2)}, u32[]{:S(2)}) collective-permute-start(bf16[16,48,1536]{2,1,0:T(8,128)(2,1)} %constant_dynamic-update-slice_fusion.10.own_ref), channel_id=1, source_target_pairs={{0,2},{1,3},{2,0},{3,1},{4,6},{5,7},{6,4},{7,5},{8,10},{9,11},{10,... | collective-permute-start | bytes 7077896 | tf_op jit(solution)/shard_map/ppermute | solution.py:48
  128.0 58.3 %collective-permute-start.19 = (bf16[16,48,1536]{2,1,0:T(8,128)(2,1)}, bf16[16,48,1536]{2,1,0:T(8,128)(2,1)}, u32[]{:S(2)}, u32[]{:S(2)}) collective-permute-start(bf16[16,48,1536]{2,1,0:T(8,128)(2,1)} %constant_dynamic-update-slice_fusion.15.own_ref), channel_id=1, source_target_pairs={{0,2},{1,3},{2,0},{3,1},{4,6},{5,7},{6,4},{7,5},{8,10},{9,11},{10,... | collective-permute-start | bytes 7077896 | tf_op jit(solution)/shard_map/ppermute | solution.py:48
  138.5 20.0 %copy-start.10 = (bf16[768,768]{1,0:T(8,128)(2,1)S(1)}, bf16[768,768]{1,0:T(8,128)(2,1)}, u32[]{:S(2)}) copy-start(bf16[768,768]{1,0:T(8,128)(2,1)} %shard_map.256) | copy-start | bytes 3538948
  199.0 10.6 %slice-start = ((s8[4718592]{0:T(1024)(128)(4,1)}), s8[4194304]{0:T(1024)(128)(4,1)S(1)}, s32[]{:S(2)}) async-start(s8[4718592]{0:T(1024)(128)(4,1)} %bitcast.153), calls=%async_computation.4 | async-start | bytes 8388608
  200.7 8.9 %copy-start.13 = (bf16[512,768]{1,0:T(8,128)(2,1)}, bf16[512,768]{1,0:T(8,128)(2,1)S(1)}, u32[]{:S(2)}) copy-start(bf16[512,768]{1,0:T(8,128)(2,1)S(1)} %convert_element_type.243.a_ref) | copy-start | bytes 2359300
  202.8 6.9 %slice-start.1 = ((s8[4718592]{0:T(1024)(128)(4,1)}), s8[524288]{0:T(1024)(128)(4,1)S(1)}, s32[]{:S(2)}) async-start(s8[4718592]{0:T(1024)(128)(4,1)} %bitcast.153), calls=%async_computation.5 | async-start | bytes 1048576
  214.5 21.4 %copy-start.15 = (bf16[512,768]{1,0:T(8,128)(2,1)}, bf16[512,768]{1,0:T(8,128)(2,1)S(1)}, u32[]{:S(2)}) copy-start(bf16[512,768]{1,0:T(8,128)(2,1)S(1)} %convert_element_type.245.a_ref) | copy-start | bytes 2359300
  242.8 7.3 %copy-start.5 = (bf16[512,768]{1,0:T(8,128)(2,1)S(1)}, bf16[512,768]{1,0:T(8,128)(2,1)}, u32[]{:S(2)}) copy-start(bf16[512,768]{1,0:T(8,128)(2,1)} %get-tuple-element.31) | copy-start | bytes 2359300
  250.3 18.3 %collective-permute-start.25 = (bf16[16,48,384]{2,1,0:T(8,128)(2,1)}, bf16[16,48,384]{2,1,0:T(8,128)(2,1)}, u32[]{:S(2)}, u32[]{:S(2)}) collective-permute-start(bf16[16,48,384]{2,1,0:T(8,128)(2,1)} %get-tuple-element.35), channel_id=1, source_target_pairs={{0,2},{1,3},{2,0},{3,1},{4,6},{5,7},{6,4},{7,5},{8,10},{9,11},{10,... | collective-permute-start | bytes 1769480 | tf_op jit(solution)/shard_map/ppermute | solution.py:48
  256.1 6.8 %copy-start.25 = (f32[9216]{0:T(1024)S(1)}, f32[9216]{0:T(1024)}, u32[]{:S(2)}) copy-start(f32[9216]{0:T(1024)} %custom-call) | copy-start | bytes 110596
  262.3 58.2 %collective-permute-start.20 = (bf16[16,48,1152]{2,1,0:T(8,128)(2,1)}, bf16[16,48,1152]{2,1,0:T(8,128)(2,1)}, u32[]{:S(2)}, u32[]{:S(2)}) collective-permute-start(bf16[16,48,1152]{2,1,0:T(8,128)(2,1)} %get-tuple-element.33), channel_id=1, source_target_pairs={{0,2},{1,3},{2,0},{3,1},{4,6},{5,7},{6,4},{7,5},{8,10},{9,11},{10,... | collective-permute-start | bytes 5308424 | tf_op jit(solution)/shard_map/ppermute | solution.py:48
  262.4 100.6 %collective-permute-start.30 = (bf16[16,48,1536]{2,1,0:T(8,128)(2,1)}, bf16[16,48,1536]{2,1,0:T(8,128)(2,1)}, u32[]{:S(2)}, u32[]{:S(2)}) collective-permute-start(bf16[16,48,1536]{2,1,0:T(8,128)(2,1)} %get-tuple-element.37), channel_id=1, source_target_pairs={{0,2},{1,3},{2,0},{3,1},{4,6},{5,7},{6,4},{7,5},{8,10},{9,11},{10,... | collective-permute-start | bytes 7077896 | tf_op jit(solution)/shard_map/ppermute | solution.py:48
  269.9 48.2 %collective-permute-start.26 = (bf16[8,48,384]{2,1,0:T(8,128)(2,1)S(1)}, bf16[8,48,384]{2,1,0:T(8,128)(2,1)S(1)}, u32[]{:S(2)}, u32[]{:S(2)}) collective-permute-start(bf16[8,48,384]{2,1,0:T(8,128)(2,1)S(1)} %slice.225), channel_id=1, source_target_pairs={{0,4},{1,5},{2,3},{3,2},{4,0},{5,1},{6,7},{7,6},{8,12},{9,13},{10,... | collective-permute-start | bytes 884744 | tf_op jit(solution)/shard_map/ppermute | solution.py:48
  310.7 9.8 %copy-start.9 = (bf16[16,48,1152]{2,1,0:T(8,128)(2,1)S(1)}, bf16[16,48,1152]{2,1,0:T(8,128)(2,1)}, u32[]{:S(2)}) copy-start(bf16[16,48,1152]{2,1,0:T(8,128)(2,1)} %get-tuple-element.32) | copy-start | bytes 5308420
  318.2 5.8 %collective-permute-start.27 = (bf16[4,48,384]{2,1,0:T(8,128)(2,1)S(1)}, bf16[4,48,384]{2,1,0:T(8,128)(2,1)S(1)}, u32[]{:S(2)}, u32[]{:S(2)}) collective-permute-start(bf16[4,48,384]{2,1,0:T(8,128)(2,1)S(1)} %slice.227), channel_id=1, source_target_pairs={{0,1},{1,0},{2,10},{3,11},{4,5},{5,4},{6,14},{7,15},{8,9},{9,8},{1... | collective-permute-start | bytes 442376 | tf_op jit(solution)/shard_map/ppermute | solution.py:48
  322.4 6.1 %copy-start.24 = (f32[9216]{0:T(1024)S(1)}, f32[9216]{0:T(1024)}, u32[]{:S(2)}) copy-start(f32[9216]{0:T(1024)} %psum.7) | copy-start | bytes 110596
  322.4 6.7 %slice-start.2 = ((f32[9216]{0:T(1024)}), f32[1536]{0:T(1024)S(1)}, s32[]{:S(2)}) async-start(f32[9216]{0:T(1024)} %psum.7), calls=%async_computation.6 | async-start | bytes 16384 | tf_op jit(solution)/shard_map/slice | solution.py:442
  322.4 6.7 %copy-start.7 = (bf16[512,768]{1,0:T(8,128)(2,1)S(1)}, bf16[512,768]{1,0:T(8,128)(2,1)}, u32[]{:S(2)}) copy-start(bf16[512,768]{1,0:T(8,128)(2,1)} %get-tuple-element.92) | copy-start | bytes 2359300
  322.5 37.5 %collective-permute-start.21 = (bf16[8,48,1152]{2,1,0:T(8,128)(2,1)S(1)}, bf16[8,48,1152]{2,1,0:T(8,128)(2,1)}, u32[]{:S(2)}, u32[]{:S(2)}) collective-permute-start(bf16[8,48,1152]{2,1,0:T(8,128)(2,1)S(1)} %slice.216), channel_id=1, source_target_pairs={{0,4},{1,5},{2,3},{3,2},{4,0},{5,1},{6,7},{7,6},{8,12},{9,13},{10,... | collective-permute-start | bytes 2654216 | tf_op jit(solution)/shard_map/ppermute | solution.py:48
  325.3 9.9 %collective-permute-start.28 = (bf16[2,48,384]{2,1,0:T(8,128)(2,1)}, bf16[2,48,384]{2,1,0:T(8,128)(2,1)}, u32[]{:S(2)}, u32[]{:S(2)}) collective-permute-start(bf16[2,48,384]{2,1,0:T(8,128)(2,1)} %slice.229), channel_id=1, source_target_pairs={{0,8},{1,9},{2,18},{3,19},{4,12},{5,13},{6,22},{7,23},{8,0},{9,1},... | collective-permute-start | bytes 221192 | tf_op jit(solution)/shard_map/ppermute | solution.py:48
  330.4 41.4 %all-to-all-start.1 = ((bf16[8,128,768]{2,1,0:T(8,128)(2,1)}), bf16[8,128,768]{2,1,0:T(8,128)(2,1)}, u32[]{:S(2)}, u32[]{:S(2)}) async-start(bf16[8,128,768]{2,1,0:T(8,128)(2,1)} %bitcast.52), calls=%async_computation.1 | async-start | bytes 3145728 | tf_op jit(solution)/shard_map/all_to_all | solution.py:362
  334.8 28.2 %copy-start.8 = (bf16[16,48,1536]{2,1,0:T(8,128)(2,1)S(1)}, bf16[16,48,1536]{2,1,0:T(8,128)(2,1)}, u32[]{:S(2)}) copy-start(bf16[16,48,1536]{2,1,0:T(8,128)(2,1)} %get-tuple-element.36) | copy-start | bytes 7077892
  334.8 43.7 %collective-permute-start.35 = (bf16[16,48,1536]{2,1,0:T(8,128)(2,1)}, bf16[16,48,1536]{2,1,0:T(8,128)(2,1)}, u32[]{:S(2)}, u32[]{:S(2)}) collective-permute-start(bf16[16,48,1536]{2,1,0:T(8,128)(2,1)} %get-tuple-element.39), channel_id=1, source_target_pairs={{0,2},{1,3},{2,0},{3,1},{4,6},{5,7},{6,4},{7,5},{8,10},{9,11},{10,... | collective-permute-start | bytes 7077896 | tf_op jit(solution)/shard_map/ppermute | solution.py:48
  336.3 4.9 %collective-permute-start.29 = (bf16[1,48,384]{2,1,0:T(8,128)(2,1)S(1)}, bf16[1,48,384]{2,1,0:T(8,128)(2,1)S(1)}, u32[]{:S(2)}, u32[]{:S(2)}) collective-permute-start(bf16[1,48,384]{2,1,0:T(8,128)(2,1)S(1)} %slice.231), channel_id=1, source_target_pairs={{0,16},{1,17},{2,6},{3,7},{4,20},{5,21},{6,2},{7,3},{8,24},{9,25},... | collective-permute-start | bytes 110600 | tf_op jit(solution)/shard_map/ppermute | solution.py:48
  361.5 10.1 %collective-permute-start.22 = (bf16[4,48,1152]{2,1,0:T(8,128)(2,1)S(1)}, bf16[4,48,1152]{2,1,0:T(8,128)(2,1)S(1)}, u32[]{:S(2)}, u32[]{:S(2)}) collective-permute-start(bf16[4,48,1152]{2,1,0:T(8,128)(2,1)S(1)} %slice.218), channel_id=1, source_target_pairs={{0,1},{1,0},{2,10},{3,11},{4,5},{5,4},{6,14},{7,15},{8,9},{9,8},{1... | collective-permute-start | bytes 1327112 | tf_op jit(solution)/shard_map/ppermute | solution.py:48
  366.5 34.7 %collective-permute-start.31 = (bf16[8,48,1536]{2,1,0:T(8,128)(2,1)}, bf16[8,48,1536]{2,1,0:T(8,128)(2,1)}, u32[]{:S(2)}, u32[]{:S(2)}) collective-permute-start(bf16[8,48,1536]{2,1,0:T(8,128)(2,1)} %slice.236), channel_id=1, source_target_pairs={{0,4},{1,5},{2,3},{3,2},{4,0},{5,1},{6,7},{7,6},{8,12},{9,13},{10,... | collective-permute-start | bytes 3538952 | tf_op jit(solution)/shard_map/ppermute | solution.py:48
  371.7 14.3 %collective-permute-start.23 = (bf16[2,48,1152]{2,1,0:T(8,128)(2,1)S(1)}, bf16[2,48,1152]{2,1,0:T(8,128)(2,1)S(1)}, u32[]{:S(2)}, u32[]{:S(2)}) collective-permute-start(bf16[2,48,1152]{2,1,0:T(8,128)(2,1)S(1)} %slice.220), channel_id=1, source_target_pairs={{0,8},{1,9},{2,18},{3,19},{4,12},{5,13},{6,22},{7,23},{8,0},{9,1},... | collective-permute-start | bytes 663560 | tf_op jit(solution)/shard_map/ppermute | solution.py:48
  374.2 26.9 %all-to-all-start.3 = ((bf16[8,128,768]{2,1,0:T(8,128)(2,1)}), bf16[8,128,768]{2,1,0:T(8,128)(2,1)}, u32[]{:S(2)}, u32[]{:S(2)}) async-start(bf16[8,128,768]{2,1,0:T(8,128)(2,1)} %bitcast.152), calls=%async_computation.3 | async-start | bytes 3145728 | tf_op jit(solution)/shard_map/all_to_all | solution.py:362
  384.1 29.7 %collective-permute-start.36 = (bf16[8,48,1536]{2,1,0:T(8,128)(2,1)}, bf16[8,48,1536]{2,1,0:T(8,128)(2,1)}, u32[]{:S(2)}, u32[]{:S(2)}) collective-permute-start(bf16[8,48,1536]{2,1,0:T(8,128)(2,1)} %slice.245), channel_id=1, source_target_pairs={{0,4},{1,5},{2,3},{3,2},{4,0},{5,1},{6,7},{7,6},{8,12},{9,13},{10,... | collective-permute-start | bytes 3538952 | tf_op jit(solution)/shard_map/ppermute | solution.py:48
  386.1 15.0 %collective-permute-start.24 = (bf16[1,48,1152]{2,1,0:T(8,128)(2,1)S(1)}, bf16[1,48,1152]{2,1,0:T(8,128)(2,1)S(1)}, u32[]{:S(2)}, u32[]{:S(2)}) collective-permute-start(bf16[1,48,1152]{2,1,0:T(8,128)(2,1)S(1)} %slice.222), channel_id=1, source_target_pairs={{0,16},{1,17},{2,6},{3,7},{4,20},{5,21},{6,2},{7,3},{8,24},{9,25},... | collective-permute-start | bytes 331784 | tf_op jit(solution)/shard_map/ppermute | solution.py:48
  401.2 12.6 %copy-start.3 = (bf16[16,48,1536]{2,1,0:T(8,128)(2,1)S(1)}, bf16[16,48,1536]{2,1,0:T(8,128)(2,1)}, u32[]{:S(2)}) copy-start(bf16[16,48,1536]{2,1,0:T(8,128)(2,1)} %copy-done.2) | copy-start | bytes 7077892
  403.8 26.9 %collective-permute-start.32 = (bf16[4,48,1536]{2,1,0:T(8,128)(2,1)}, bf16[4,48,1536]{2,1,0:T(8,128)(2,1)}, u32[]{:S(2)}, u32[]{:S(2)}) collective-permute-start(bf16[4,48,1536]{2,1,0:T(8,128)(2,1)} %slice.238), channel_id=1, source_target_pairs={{0,1},{1,0},{2,10},{3,11},{4,5},{5,4},{6,14},{7,15},{8,9},{9,8},{1... | collective-permute-start | bytes 1769480 | tf_op jit(solution)/shard_map/ppermute | solution.py:48
  416.2 16.0 %collective-permute-start.37 = (bf16[4,48,1536]{2,1,0:T(8,128)(2,1)}, bf16[4,48,1536]{2,1,0:T(8,128)(2,1)}, u32[]{:S(2)}, u32[]{:S(2)}) collective-permute-start(bf16[4,48,1536]{2,1,0:T(8,128)(2,1)} %slice.247), channel_id=1, source_target_pairs={{0,1},{1,0},{2,10},{3,11},{4,5},{5,4},{6,14},{7,15},{8,9},{9,8},{1... | collective-permute-start | bytes 1769480 | tf_op jit(solution)/shard_map/ppermute | solution.py:48
  431.9 9.5 %collective-permute-start.33 = (bf16[2,48,1536]{2,1,0:T(8,128)(2,1)S(1)}, bf16[2,48,1536]{2,1,0:T(8,128)(2,1)S(1)}, u32[]{:S(2)}, u32[]{:S(2)}) collective-permute-start(bf16[2,48,1536]{2,1,0:T(8,128)(2,1)S(1)} %slice.240), channel_id=1, source_target_pairs={{0,8},{1,9},{2,18},{3,19},{4,12},{5,13},{6,22},{7,23},{8,0},{9,1},... | collective-permute-start | bytes 884744 | tf_op jit(solution)/shard_map/ppermute | solution.py:48
  433.5 14.2 %collective-permute-start.38 = (bf16[2,48,1536]{2,1,0:T(8,128)(2,1)S(1)}, bf16[2,48,1536]{2,1,0:T(8,128)(2,1)S(1)}, u32[]{:S(2)}, u32[]{:S(2)}) collective-permute-start(bf16[2,48,1536]{2,1,0:T(8,128)(2,1)S(1)} %slice.249), channel_id=1, source_target_pairs={{0,8},{1,9},{2,18},{3,19},{4,12},{5,13},{6,22},{7,23},{8,0},{9,1},... | collective-permute-start | bytes 884744 | tf_op jit(solution)/shard_map/ppermute | solution.py:48
  441.5 9.9 %collective-permute-start.34 = (bf16[1,48,1536]{2,1,0:T(8,128)(2,1)S(1)}, bf16[1,48,1536]{2,1,0:T(8,128)(2,1)S(1)}, u32[]{:S(2)}, u32[]{:S(2)}) collective-permute-start(bf16[1,48,1536]{2,1,0:T(8,128)(2,1)S(1)} %slice.242), channel_id=1, source_target_pairs={{0,16},{1,17},{2,6},{3,7},{4,20},{5,21},{6,2},{7,3},{8,24},{9,25},... | collective-permute-start | bytes 442376 | tf_op jit(solution)/shard_map/ppermute | solution.py:48
  447.8 12.8 %collective-permute-start.39 = (bf16[1,48,1536]{2,1,0:T(8,128)(2,1)S(1)}, bf16[1,48,1536]{2,1,0:T(8,128)(2,1)S(1)}, u32[]{:S(2)}, u32[]{:S(2)}) collective-permute-start(bf16[1,48,1536]{2,1,0:T(8,128)(2,1)S(1)} %slice.251), channel_id=1, source_target_pairs={{0,16},{1,17},{2,6},{3,7},{4,20},{5,21},{6,2},{7,3},{8,24},{9,25},... | collective-permute-start | bytes 442376 | tf_op jit(solution)/shard_map/ppermute | solution.py:48
  (21 other events, 77.7 us)

commit v2 on v0

v2 whole, which is shorter than its diff:
```python
import jax
import jax.numpy as jnp
from jax import lax
from jax.experimental import pallas as pl
from jax.experimental.pallas import tpu as pltpu
from jax.sharding import PartitionSpec as P

HEAD_DIM = 64
AXES = ("fsdp", "ctx", "tp")
F32 = jnp.float32
BF16 = jnp.bfloat16
NEG = -1e30
NT = (((1,), (1,)), ((), ()))
VMEM = pl.BlockSpec(memory_space=pltpu.VMEM)
SMEM = pl.BlockSpec(memory_space=pltpu.SMEM)
ANY = pl.BlockSpec(memory_space=pl.ANY)


def partner(dim, z, c, t):
    if dim == "core":
        return z, c ^ 1, t
    if dim == "x":
        return z, c ^ 2, t
    if dim == "y":
        return z, c, t ^ 1
    return z ^ int(dim[1:]), c, t


def exchange(value, dims, sizes):
    nz, nc, nt = sizes
    pairs = []
    for z in range(nz):
        for c in range(nc):
            for t in range(nt):
                tz, tc, tt = partner(dims[c & 1], z, c, t)
                pairs.append(((z * nc + c) * nt + t, (tz * nc + tc) * nt + tt))
    return lax.ppermute(value, AXES, pairs)


GATHER_ORDER = (("z2", "z1", "y", "x"), ("z2", "z1", "x", "y"))
SCATTER_ORDER = (("x", "y", "z1", "z2"), ("y", "z1", "z2", "x"))
PACK_ORDER = tuple(order[::-1] for order in SCATTER_ORDER)
CORE = (("core", "core"),)
GATHER_STEPS = tuple(zip(*GATHER_ORDER)) + CORE
SCATTER_STEPS = CORE + tuple(zip(*SCATTER_ORDER))


def piece_place(order, core, here, index):
    z, x, t = here
    for bit, dim in enumerate(order):
        flip = (index >> bit) & 1
        if dim == "x":
            x = x ^ flip
        elif dim == "y":
            t = t ^ flip
        else:
            z = z ^ (flip * int(dim[1:]))
    return z * 4 + x * 2 + core, t


def places(orders):
    c = lax.axis_index("ctx")
    here = (lax.axis_index("fsdp"), lax.div(c, 2), lax.axis_index("tp"))
    k = lax.rem(c, 2)
    rows = []
    for core in (k, 1 - k):
        for i in range(16):
            r0, t0 = piece_place(orders[0], core, here, i)
            r1, t1 = piece_place(orders[1], core, here, i)
            rows.append(jnp.where(core == 0, r0, r1))
            rows.append(jnp.where(core == 0, t0, t1))
    return jnp.stack(rows + [here[2]]).astype(jnp.int32)


def plain_places():
    rows = [place for half in range(2) for i in range(16) for place in (i, half)]
    return jnp.stack([jnp.asarray(row) for row in rows] + [lax.axis_index("tp")]).astype(jnp.int32)


def after(value, *first):
    return lax.optimization_barrier((value, first))[0]


def piece_copies(info_ref, own_ref, sib_ref, sem, whole, low, cols, collect, base=0):
    rows = own_ref.shape[1]
    stride = whole.shape[1] // 2
    copies = []
    for half, ref in ((0, own_ref), (1, sib_ref)):
        for i in range(16):
            at = (half * 16 + i) * 2
            row = pl.multiple_of(info_ref[at] * rows, rows)
            col = pl.multiple_of(info_ref[at + 1] * stride, 128)
            one = ref.at[i, :, pl.ds(low, cols)]
            two = whole.at[pl.ds(row, rows), pl.ds(col, cols)]
            src, dst = (one, two) if collect else (two, one)
            copy = pltpu.make_async_copy(src, dst, sem.at[base + half * 16 + i])
            copy.start()
            copies.append(copy)
    return copies


def finish(copies):
    for copy in copies:
        copy.wait()


def tiles(count, step):
    def run(one):
        lax.fori_loop(0, count // step, lambda i, carry: (one(pl.multiple_of(i * step, step)), carry)[1], 0)

    return run


def row_mean(value):
    return jnp.mean(value, axis=-1, keepdims=True)


def struct(shape, dtype):
    return jax.ShapeDtypeStruct(shape, dtype)


def call(kernel, name, outs, specs, out_specs, scratch, time, room, args):
    return pl.pallas_call(
        kernel,
        name=name,
        out_shape=outs,
        in_specs=specs,
        out_specs=out_specs,
        scratch_shapes=scratch,
        compiler_params=pltpu.CompilerParams(vmem_limit_bytes=room << 20),
        cost_estimate=pl.CostEstimate(flops=time * 10**9, transcendentals=0, bytes_accessed=10**6),
    )(*args)


B_OUT, GAIN1, SHIFT1, B_DOWN, GAIN2, SHIFT2 = range(6)


def unpack_kernel(info_ref, own_ref, sib_ref, *refs):
    outs, sem = refs[:-1], refs[-1]
    copies = []
    low = 0
    for i, out in enumerate(outs):
        cols = out.shape[1] // 2
        copies += piece_copies(info_ref, own_ref, sib_ref, sem, out, low, cols, True, 32 * i)
        low += cols
    finish(copies)


def unpack(info, own, sib, widths):
    rows = own.shape[0] * own.shape[1]
    return call(
        unpack_kernel,
        "unpack",
        tuple(struct((rows, width), BF16) for width in widths),
        [SMEM, ANY, ANY],
        (VMEM,) * len(widths),
        [pltpu.SemaphoreType.DMA((32 * len(widths),))],
        5,
        16,
        (info, own, sib),
    )


def project_kernel(info_ref, weight_ref, given_ref, small_ref, proj_ref, x_ref, mask_ref):
    count, more = given_ref.shape[:2]
    block = more - 8
    for i in range(count):
        x_ref[i * block : (i + 1) * block, :] = given_ref[i, 0:block, :]
    ids = [given_ref[i, block : block + 8, 0:block].astype(F32)[0:1] for i in range(count)]
    for kb in range(count):
        column = jnp.broadcast_to(ids[kb], (block, block)).T
        for qb in range(count):
            mask_ref[kb * block : (kb + 1) * block, qb * block : (qb + 1) * block] = jnp.where(
                column == jnp.broadcast_to(ids[qb], (block, block)), 0.0, NEG
            )
    width = proj_ref.shape[1] // 6
    for y in range(2):
        row = pl.ds(info_ref[64] ^ y, 1)
        for which in range(3):
            at = (y * 3 + which) * width
            value = jnp.dot(x_ref[...], weight_ref[:, at : at + width], preferred_element_type=F32)
            if which != 1:
                low = 0 if which == 0 else width
                value = value + small_ref[row, low : low + width]
            proj_ref[:, at : at + width] = value.astype(BF16)


def project(info, weight, given, small):
    width, wide = weight.shape
    length = given.shape[0] * (given.shape[1] - 8)
    return call(
        project_kernel,
        "project",
        (struct((length, wide), BF16), struct((length, width), BF16), struct((length, length), F32)),
        [SMEM, VMEM, VMEM, VMEM],
        (VMEM,) * 3,
        [],
        5,
        16,
        (info, weight, given, small),
    )


def attend_kernel(proj_ref, mask_ref, o_ref, p_ref, *, y):
    length = proj_ref.shape[0]
    pairs = o_ref.shape[1] // 128
    lane = lax.broadcasted_iota(jnp.int32, (1, 128), 1)

    def pair(g, carry):
        take = lambda which: proj_ref[:, pl.ds(pl.multiple_of(((y * 3 + which) * pairs + g) * 128, 128), 128)]
        query = take(0) * jnp.asarray(0.125, BF16)
        keys = take(1)
        values_t = take(2).T
        outs = []
        for head in range(2):
            here = (lane >= 64 * head) & (lane < 64 * head + 64)
            only = jnp.where(here, keys, jnp.zeros_like(keys))
            row = []
            for at in range(0, length, 256):
                scores = lax.dot_general(only, query[at : at + 256], NT, preferred_element_type=F32)
                scores = scores + mask_ref[:, at : at + 256]
                top = jnp.max(scores, axis=0, keepdims=True)
                raised = jnp.exp(scores - top)
                total = jnp.sum(raised, axis=0, keepdims=True)
                probs = (raised * (1.0 / total)).astype(BF16)
                p_ref[2 * g + head, :, at : at + 256] = probs
                row.append(
                    jnp.dot(values_t[64 * head : 64 * head + 64], probs, preferred_element_type=F32)
                )
            outs.append(jnp.concatenate(row, axis=1))
        both = jnp.concatenate(outs, axis=0).astype(BF16)
        o_ref[:, pl.ds(pl.multiple_of(g * 128, 128), 128)] = both.T
        return carry

    lax.fori_loop(0, pairs, pair, 0)


def attend(proj, mask, y):
    length, wide = proj.shape
    half = wide // 6
    return call(
        lambda *refs: attend_kernel(*refs, y=y),
        "attend",
        (struct((length, half), BF16), struct((half // HEAD_DIM, length, length), BF16)),
        [VMEM, VMEM],
        (VMEM, VMEM),
        [],
        12,
        16,
        (proj, mask),
    )


def middle_kernel(
    info_ref, w_out, w_up, mixed0_ref, mixed1_ref, x_ref, table_ref, small_ref,
    normed_ref, scale_ref, first_ref, act_ref, slope_ref,
):
    length, units = act_ref.shape
    narrow, half = w_out.shape[1] // 2, units // 2
    normed_ref[...] = lax.dot_general(
        mixed0_ref[...], w_out[:, :narrow], NT, preferred_element_type=F32
    ) + lax.dot_general(mixed1_ref[...], w_out[:, narrow:], NT, preferred_element_type=F32)

    @tiles(length, 64)
    def _(at):
        here = pl.ds(at, 64)
        value = x_ref[here, :].astype(F32) + normed_ref[here, :] + table_ref[B_OUT : B_OUT + 1, :]
        centred = value - row_mean(value)
        scale = lax.rsqrt(row_mean(centred * centred) + 1e-12)
        unit = centred * scale
        normed_ref[here, :] = unit
        scale_ref[here, :] = scale
        first_ref[here, :] = (
            unit * table_ref[GAIN1 : GAIN1 + 1, :] + table_ref[SHIFT1 : SHIFT1 + 1, :]
        ).astype(BF16)

    for y in range(2):
        row = pl.ds(info_ref[64] ^ y, 1)

        @tiles(half, 256)
        def _(at):
            here = pl.ds(pl.multiple_of(y * half + at, 256), 256)
            bias = small_ref[row, pl.ds(pl.multiple_of(2 * narrow + at, 256), 256)]
            hidden = jnp.dot(first_ref[...], w_up[:, here], preferred_element_type=F32) + bias
            phi = 0.5 + 0.5 * lax.erf(hidden * 0.7071067811865476)
            act_ref[:, here] = (hidden * phi).astype(BF16)
            bell = jnp.exp(-0.5 * hidden * hidden) * 0.3989422804014327
            slope_ref[:, here] = (phi + hidden * bell).astype(BF16)


def middle(info, w_out, w_up, mixed0, mixed1, x, table, small):
    length, width = x.shape
    units = w_up.shape[1]
    return call(
        middle_kernel,
        "middle",
        (
            struct((length, width), F32),
            struct((length, 1), F32),
            struct((length, width), BF16),
            struct((length, units), BF16),
            struct((length, units), BF16),
        ),
        [SMEM] + [VMEM] * 7,
        (VMEM,) * 5,
        [],
        12,
        20,
        (info, w_out, w_up, mixed0, mixed1, x, table, small),
    )


def turn_kernel(
    pack_ref, weight_ref, act_ref, normed_ref, cot_ref, table_ref,
    chunks_ref, gz_ref, gzb_ref, sums_ref, down_own, down_sib, full, sem,
):
    length = act_ref.shape[0]
    block = chunks_ref.shape[1]
    gz_ref[...] = lax.dot_general(act_ref[...], weight_ref[...], NT, preferred_element_type=F32)
    sums_ref[...] = jnp.zeros_like(sums_ref)
    row = lambda which: table_ref[which : which + 1, :]

    @tiles(length, 64)
    def _(at):
        here = pl.ds(at, 64)
        value = normed_ref[here, :] * row(GAIN1) + row(SHIFT1) + gz_ref[here, :] + row(B_DOWN)
        centred = value - row_mean(value)
        scale = lax.rsqrt(row_mean(centred * centred) + 1e-12)
        unit = centred * scale
        result = (unit * row(GAIN2) + row(SHIFT2)).astype(BF16)
        chunk = lax.div(at, block)
        low = pl.multiple_of(lax.rem(at, block), 64)
        for copy in range(2):
            chunks_ref[2 * chunk + copy, pl.ds(low, 64), :] = result
        coming = cot_ref[here, :].astype(F32)
        raised = coming * row(GAIN2)
        back = scale * (raised - row_mean(raised) - unit * row_mean(raised * unit))
        gz_ref[here, :] = back
        gzb_ref[here, :] = back.astype(BF16)
        sums_ref[0:1, :] += jnp.sum(coming * unit, axis=0, keepdims=True)
        sums_ref[1:2, :] += jnp.sum(coming, axis=0, keepdims=True)
        sums_ref[2:3, :] += jnp.sum(back, axis=0, keepdims=True)

    back_t = gzb_ref[...].T

    @tiles(full.shape[1], 1024)
    def _(at):
        here = pl.ds(at, 1024)
        full[:, here] = jnp.dot(back_t, act_ref[:, here], preferred_element_type=F32).astype(BF16)

    finish(piece_copies(pack_ref, down_own, down_sib, sem, full, 0, down_own.shape[2], False))


def turn(pack, weight, act, normed, cot, table, chunk):
    length, units = act.shape
    width = normed.shape[1]
    piece = struct((16, width // 16, units // 2), BF16)
    return call(
        turn_kernel,
        "turn",
        (
            struct((2 * length // chunk, chunk, width), BF16),
            struct((length, width), F32),
            struct((length, width), BF16),
            struct((8, width), F32),
            piece,
            piece,
        ),
        [SMEM] + [VMEM] * 5,
        (VMEM, VMEM, VMEM, VMEM, ANY, ANY),
        [pltpu.VMEM((width, units), BF16), pltpu.SemaphoreType.DMA((32,))],
        14,
        24,
        (pack, weight, act, normed, cot, table),
    )


def hidden_back_kernel(weight_ref, gzb_ref, slope_ref, gh_ref, sum_ref):
    @tiles(gh_ref.shape[1], 512)
    def _(at):
        here = pl.ds(at, 512)
        back = jnp.dot(gzb_ref[...], weight_ref[:, here], preferred_element_type=F32)
        back = (back * slope_ref[:, here].astype(F32)).astype(BF16)
        gh_ref[:, here] = back
        sum_ref[:, here] = jnp.sum(back.astype(F32), axis=0, keepdims=True)


def hidden_back(weight, gzb, slope):
    length, units = slope.shape
    return call(
        hidden_back_kernel,
        "hidden_back",
        (struct((length, units), BF16), struct((1, units), F32)),
        [VMEM] * 3,
        (VMEM, VMEM),
        [],
        12,
        20,
        (weight, gzb, slope),
    )


def first_back_kernel(
    pack_ref, w_out, w_up, gh_ref, gz_ref, normed_ref, scale_ref, table_ref, first_ref, mixed0_ref, mixed1_ref,
    gz1_ref, gm_ref, sums_ref, pieces_own, pieces_sib, branch, d_out, d_up, sem,
):
    narrow = w_out.shape[1] // 2
    half = w_up.shape[1] // 2
    length = gh_ref.shape[0]
    first_t = first_ref[...].T

    @tiles(d_up.shape[1], 1024)
    def _(at):
        here = pl.ds(at, 1024)
        d_up[:, here] = jnp.dot(first_t, gh_ref[:, here], preferred_element_type=F32).astype(BF16)

    sent = piece_copies(pack_ref, pieces_own, pieces_sib, sem, d_up, narrow, half, False)
    gz1_ref[...] = lax.dot_general(gh_ref[...], w_up[...], NT, preferred_element_type=F32)
    sums_ref[...] = jnp.zeros_like(sums_ref)

    @tiles(length, 64)
    def _(at):
        here = pl.ds(at, 64)
        coming = gz_ref[here, :] + gz1_ref[here, :]
        unit = normed_ref[here, :]
        raised = coming * table_ref[GAIN1 : GAIN1 + 1, :]
        back = scale_ref[here, :] * (raised - row_mean(raised) - unit * row_mean(raised * unit))
        gz1_ref[here, :] = back
        branch[here, :] = back.astype(BF16)
        sums_ref[0:1, :] += jnp.sum(coming * unit, axis=0, keepdims=True)
        sums_ref[1:2, :] += jnp.sum(coming, axis=0, keepdims=True)
        sums_ref[2:3, :] += jnp.sum(back, axis=0, keepdims=True)

    branch_t = branch[...].T
    d_out[:, :narrow] = jnp.dot(branch_t, mixed0_ref[...], preferred_element_type=F32).astype(BF16)
    d_out[:, narrow:] = jnp.dot(branch_t, mixed1_ref[...], preferred_element_type=F32).astype(BF16)
    sent += piece_copies(pack_ref, pieces_own, pieces_sib, sem, d_out, 0, narrow, False, 32)
    gm_ref[...] = jnp.dot(branch[...], w_out[...], preferred_element_type=F32).astype(BF16)
    finish(sent)


def first_back(pack, w_out, w_up, gh, gz, normed, scale, table, first_b, mixed0, mixed1):
    length, units = gh.shape
    width = gz.shape[1]
    piece = struct((16, width // 16, (units + width) // 2), BF16)
    return call(
        first_back_kernel,
        "first_back",
        (
            struct((length, width), F32),
            struct((length, width), BF16),
            struct((8, width), F32),
            piece,
            piece,
        ),
        [SMEM] + [VMEM] * 10,
        (VMEM, VMEM, VMEM, ANY, ANY),
        [
            pltpu.VMEM((length, width), BF16),
            pltpu.VMEM((width, width), BF16),
            pltpu.VMEM((width, units), BF16),
            pltpu.SemaphoreType.DMA((64,)),
        ],
        20,
        30,
        (pack, w_out, w_up, gh, gz, normed, scale, table, first_b, mixed0, mixed1),
    )


def attend_back_kernel(proj_ref, p_ref, gm_ref, dq_ref, dk_ref, dv_ref, dst, dqt, *, y):
    length = proj_ref.shape[0]
    pairs = dq_ref.shape[1] // 128
    lane = lax.broadcasted_iota(jnp.int32, (1, 128), 1)
    low = lane < 64

    def pair(g, carry):
        take = lambda which: proj_ref[:, pl.ds(pl.multiple_of(((y * 3 + which) * pairs + g) * 128, 128), 128)]
        query, keys, values = take(0), take(1), take(2)
        grad = gm_ref[:, pl.ds(pl.multiple_of((y * pairs + g) * 128, 128), 128)]
        keys_t = keys.T
        dks, dvs = [], []
        for head in range(2):
            here = low if head == 0 else jnp.logical_not(low)
            only = jnp.where(here, values, jnp.zeros_like(values))
            for at in range(0, length, 256):
                cols = slice(at, at + 256)
                gp = lax.dot_general(only, grad[cols], NT, preferred_element_type=F32)
                probs = p_ref[2 * g + head, :, cols].astype(F32)
                weighted = jnp.sum(probs * gp, axis=0, keepdims=True)
                dst[:, cols] = (probs * (gp - weighted)).astype(BF16)
            dqt[64 * head : 64 * head + 64, :] = (
                jnp.dot(keys_t[64 * head : 64 * head + 64], dst[...], preferred_element_type=F32) * 0.125
            ).astype(BF16)
            dks.append(jnp.dot(dst[...], query, preferred_element_type=F32))
            dvs.append(jnp.dot(p_ref[2 * g + head], grad, preferred_element_type=F32))
        cols = pl.ds(pl.multiple_of(g * 128, 128), 128)
        dq_ref[:, cols] = dqt[...].T
        dk_ref[:, cols] = (jnp.where(low, dks[0], dks[1]) * 0.125).astype(BF16)
        dv_ref[:, cols] = jnp.where(low, dvs[0], dvs[1]).astype(BF16)
        return carry

    lax.fori_loop(0, pairs, pair, 0)


def attend_back(proj, probs, grad_mixed, y):
    length, wide = proj.shape
    shape = struct((length, wide // 6), BF16)
    return call(
        lambda *refs: attend_back_kernel(*refs, y=y),
        "attend_back",
        (shape, shape, shape),
        [VMEM] * 3,
        (VMEM,) * 3,
        [pltpu.VMEM((length, length), BF16), pltpu.VMEM((128, length), BF16)],
        14,
        16,
        (proj, probs, grad_mixed),
    )


def last_kernel(pack_ref, x_ref, *refs):
    parts, (sums_ref, pieces_own, pieces_sib, whole, sem) = refs[:6], refs[6:]
    half = parts[0].shape[1]
    sums_ref[...] = jnp.zeros_like(sums_ref)
    x_t = x_ref[...].T
    for y in range(2):
        for which in range(3):
            at = (y * 3 + which) * half
            value = parts[y * 3 + which][...]
            whole[:, at : at + half] = jnp.dot(x_t, value, preferred_element_type=F32).astype(BF16)
            if which != 1:
                r = which // 2
                sums_ref[r : r + 1, y * half : y * half + half] = jnp.sum(
                    value.astype(F32), axis=0, keepdims=True
                )
    finish(piece_copies(pack_ref, pieces_own, pieces_sib, sem, whole, 0, 3 * half, False))


def last(pack, x, parts):
    length, width = x.shape
    piece = struct((16, width // 16, 3 * width // 2), BF16)
    return call(
        last_kernel,
        "last",
        (struct((8, width), F32), piece, piece),
        [SMEM] + [VMEM] * 7,
        (VMEM, ANY, ANY),
        [pltpu.VMEM((width, 3 * width), BF16), pltpu.SemaphoreType.DMA((32,))],
        10,
        16,
        (pack, x) + tuple(parts),
    )


def input_back_kernel(weight_ref, gz1_ref, *refs):
    parts, chunks_ref = refs[:6], refs[6]
    half = parts[0].shape[1]
    total = gz1_ref[...]
    for i, part in enumerate(parts):
        total = total + lax.dot_general(
            part[...], weight_ref[:, i * half : (i + 1) * half], NT, preferred_element_type=F32
        )
    total = total.astype(BF16)
    count, block = chunks_ref.shape[:2]
    for i in range(count):
        at = i // 2 * block
        chunks_ref[i] = total[at : at + block]


def input_back(weight, gz1, parts, chunk):
    length, width = gz1.shape
    return call(
        input_back_kernel,
        "input_back",
        struct((2 * length // chunk, chunk, width), BF16),
        [VMEM] * 8,
        VMEM,
        [],
        8,
        20,
        (weight, gz1) + tuple(parts),
    )


def settle_kernel(owner_ref, pair_ref, got_ref, *refs, cuts):
    outs, four = refs[: len(cuts)], refs[len(cuts)]
    rows = pair_ref.shape[1]
    for i in range(4):
        ref = (pair_ref, got_ref)[i // 2]
        four[pl.ds(pl.multiple_of(owner_ref[i] * rows, 16), rows), :] = ref[i % 2].astype(F32)
    for out, (low, high, form) in zip(outs, cuts):
        if form == "plain":
            out[...] = four[:, low:high]
        else:
            step = (high - low) // 3
            for j in range(3):
                out[j] = four[:, low + j * step : low + (j + 1) * step]


def settle(owners, pair, got, cuts):
    _, rows, cols = pair.shape
    shapes = {"plain": lambda n: (4 * rows, n), "three": lambda n: (3, 4 * rows, n // 3)}
    return call(
        lambda *refs: settle_kernel(*refs, cuts=cuts),
        "settle",
        tuple(struct(shapes[form](high - low), F32) for low, high, form in cuts),
        [SMEM, VMEM, VMEM],
        (VMEM,) * len(cuts),
        [pltpu.VMEM((4 * rows, cols), F32)],
        3,
        10,
        (owners, pair, got),
    )


def add_up(terms, low, high):
    total = terms[0][low:high].astype(F32)
    for term in terms[1:]:
        total = total + term[low:high].astype(F32)
    return total.astype(BF16)


def cut(full):
    rows, cols = full.shape
    both = full.reshape(16, rows // 16, 2, cols // 2)
    return both[:, :, 0], both[:, :, 1]


def gather_plain(shard):
    rows = lax.all_gather(shard, "fsdp", axis=0, tiled=True)
    return lax.all_gather(rows, "tp", axis=1, tiled=True)


def reduce_plain(own, sib):
    rows = own.shape[0] * own.shape[1]
    full = jnp.concatenate([own.reshape(rows, -1), sib.reshape(rows, -1)], axis=1)
    part = lax.psum_scatter(full, "tp", scatter_dimension=1, tiled=True)
    part = lax.psum_scatter(part, "fsdp", scatter_dimension=0, tiled=True)
    return lax.psum(part, "ctx").astype(F32)


def body(
    layer_input,
    doc_ids,
    w_qkv,
    b_qv,
    w_out,
    b_out,
    ln1_gain,
    ln1_bias,
    w_up,
    b_up,
    w_down,
    b_down,
    ln2_gain,
    ln2_bias,
    out_grad,
):
    sizes = (lax.axis_size("fsdp"), lax.axis_size("ctx"), lax.axis_size("tp"))
    devices = sizes[0] * sizes[1] * sizes[2]
    micro, seqs, local_len, width = layer_input.shape
    length = local_len * sizes[1]
    shard_rows, local_width = w_qkv.shape[1:]
    local_units = w_up.shape[1]
    heads = width // HEAD_DIM
    fast = sizes == (4, 4, 2)
    t = lax.axis_index("tp")
    c = lax.axis_index("ctx")

    def mine(value):
        return lax.dynamic_index_in_dim(value, t, 1, keepdims=False)

    def to_owners(chunks):
        return lax.all_to_all(chunks, "ctx", 0, 0, tiled=True)

    def spread(chunks):
        out = lax.all_to_all(chunks, ("ctx", "tp"), 0, 0, tiled=True)
        return out.reshape(micro, seqs, local_len, width)

    shards = (
        jnp.swapaxes(w_qkv, 0, 1).reshape(shard_rows, 3 * local_width),
        jnp.concatenate([w_out.T, w_up], axis=1),
        w_down.T,
    )
    ids = mine(doc_ids).astype(BF16)[:, None, :]
    ids = jnp.pad(ids, ((0, 0), (0, 7), (0, width - local_len)))
    given = to_owners(jnp.concatenate([mine(layer_input), ids], axis=1))
    small = jnp.concatenate([b_qv.reshape(-1), b_up])[None]
    small = jnp.concatenate([small, exchange(small, ("y", "y"), sizes)], axis=0)
    table = jnp.stack([b_out, ln1_gain, ln1_bias, b_down, ln2_gain, ln2_bias, b_out, b_out])

    def swap(value, step):
        return exchange(value, GATHER_STEPS[step], sizes)

    def shed(value, step):
        return exchange(value, SCATTER_STEPS[step], sizes)

    def joined(*parts):
        return jnp.concatenate(parts, axis=0)

    if fast:
        place, pack = places(GATHER_ORDER), places(PACK_ORDER)
        part = shard_rows // 4
        h1, h2, h3 = [lax.dynamic_slice_in_dim(s, c * part, part, 0)[None] for s in shards]
        h1 = joined(h1, swap(h1, 0))
        h1 = joined(h1, swap(h1, 1))
        h1, given, small, table = lax.optimization_barrier((h1, given, small, table))
        h2 = after(h2, h1)
        g1, g2 = swap(h1, 2), swap(h2, 0)
        h1, h2 = joined(h1, g1), joined(h2, g2)
        h1, h2 = after(h1, h2), after(h2, h1)
        g1, g2 = swap(h1, 3), swap(h2, 1)
        h1, h2 = joined(h1, g1), joined(h2, g2)
        h1, h2, h3 = after(h1, h2), after(h2, h1), after(h3, h1)
        g1, g2, g3 = swap(h1, 4), swap(h2, 2), swap(h3, 0)
        (wq,) = unpack(place, after(h1, h2, h3), g1, (3 * width,))
        proj, rows_b, mask = project(place, wq, given, small)
        g2, g3, cot_from = after(g2, proj), after(g3, proj), after(out_grad, proj)
        h2, h3 = joined(h2, g2), joined(h3, g3)
        g2, g3 = swap(h2, 3), swap(h3, 1)
        mixed0, probs0 = attend(after(proj, h2, h3), mask, 0)
        g3 = after(g3, mixed0)
        h3 = joined(h3, g3)
        mixed1, probs1 = attend(after(proj, h3, mixed0), mask, 1)
        g2 = after(g2, mixed1)
        h2 = joined(h2, g2)
        h3 = after(h3, h2)
        g2, g3 = swap(h2, 4), swap(h3, 2)
        wo, wu = unpack(place, h2, g2, (width, 2 * local_units))
        h3 = joined(h3, after(g3, g2))
        g3 = swap(h3, 3)
        cot = to_owners(mine(after(cot_from, g2))).reshape(length, width)
    else:
        place = pack = plain_places()
        parts = (shards[0], w_out.T, w_up, w_down.T)
        pieces = [cut(gather_plain(s)) for s in parts]
        (wq,) = unpack(place, *pieces[0], (3 * width,))
        (wo,) = unpack(place, *pieces[1], (width,))
        (wu,) = unpack(place, *pieces[2], (2 * local_units,))
        (wd,) = unpack(place, *pieces[3], (2 * local_units,))
        cot = to_owners(mine(out_grad)).reshape(length, width)
        proj, rows_b, mask = project(place, wq, given, small)
        mixed0, probs0 = attend(proj, mask, 0)
        mixed1, probs1 = attend(proj, mask, 1)
        h3 = mixed0

    normed1, scale1, first_b, act, slope = middle(
        place, wo, wu, after(mixed0, h3), mixed1, rows_b, table, small
    )
    if fast:
        h3 = joined(h3, after(g3, act))
        (wd,) = unpack(place, h3, swap(h3, 4), (2 * local_units,))
    chunks, gz, gzb, sums2, down_own, down_sib = turn(pack, wd, act, normed1, cot, table, local_len)

    layer_output = spread(chunks)
    if fast:
        got = shed(down_sib, 0)
        gzb = after(gzb, down_sib, chunks)
    gh, sum_up = hidden_back(wd, gzb, slope)
    if fast:
        down = [down_own, after(got, gh)]
        send = add_up(down, 8, 16)
        got = shed(send, 1)
        gh = after(gh, send)
    gz1, grad_mixed, sums1, up_own, up_sib = first_back(
        pack, wo, wu, gh, gz, normed1, scale1, table, first_b, mixed0, mixed1
    )
    if fast:
        down = [v[:8] for v in down] + [after(got, grad_mixed)]
        send = add_up(down, 4, 8)
        got, got2 = shed(send, 2), shed(up_sib, 0)
        grad_mixed = after(grad_mixed, send, up_sib, layer_output)
    parts0 = attend_back(proj, probs0, grad_mixed, 0)
    if fast:
        down = [v[:4] for v in down] + [after(got, parts0[0])]
        up = [up_own, after(got2, parts0[0])]
        send, send2 = add_up(down, 2, 4), add_up(up, 8, 16)
        got, got2 = shed(send, 3), shed(send2, 1)
        grad_mixed = after(grad_mixed, send, send2)
    parts1 = attend_back(proj, probs1, grad_mixed, 1)
    if fast:
        down = [v[:2] for v in down] + [after(got, parts1[0])]
        send = add_up(down, 1, 2)
        got = shed(send, 4)
        parts1 = [after(parts1[0], send)] + list(parts1[1:])
    parts = list(parts0) + list(parts1)
    sums3, qkv_own, qkv_sib = last(pack, rows_b, parts)

    flat = jnp.concatenate(
        [sums3[:2].reshape(-1), sums1[:3].reshape(-1), sums2[:3].reshape(-1), sum_up.reshape(-1)]
    ).reshape(devices, 1, -1)
    if fast:
        down = [v[:1] for v in down] + [after(got, qkv_sib)]
        pair1 = add_up(down, 0, 1)
        got3 = shed(qkv_sib, 0)
        got = exchange(pair1, ("x", "x"), sizes)
        parts[0] = after(parts[0], qkv_sib, pair1, flat)
    chunks = grad_rows = input_back(wq, gz1, parts, local_len)
    part = lax.all_to_all(flat, AXES, 0, 0, tiled=True)
    part = jnp.sum(part, axis=0, keepdims=True)
    flat = lax.all_to_all(jnp.broadcast_to(part, (devices,) + part.shape[1:]), AXES, 0, 0, tiled=True)
    flat = flat.reshape(-1)
    if fast:
        owners = jnp.stack([c, c ^ 2, c ^ 1, c ^ 3]).astype(jnp.int32)
        got2, got3, got = after(got2, grad_rows), after(got3, grad_rows), after(got, grad_rows)
        up = [v[:8] for v in up] + [got2]
        qkv = [qkv_own, got3]
        send2, send3 = add_up(up, 4, 8), add_up(qkv, 8, 16)
        got3, got2 = shed(send3, 1), shed(send2, 2)
        pair1 = joined(pair1, got)
        got1 = exchange(pair1, ("core", "core"), sizes)
        grad_x = spread(after(chunks, send2, send3))
        up = [v[:4] for v in up] + [got2]
        send2 = add_up(up, 2, 4)
        got2 = shed(send2, 3)
        qkv = [v[:8] for v in qkv] + [got3]
        send3 = after(add_up(qkv, 4, 8), send2)
        got3 = shed(send3, 2)
        up = [v[:2] for v in up] + [got2]
        send2 = add_up(up, 1, 2)
        got2 = shed(send2, 4)
        qkv = [v[:4] for v in qkv] + [got3]
        send3 = add_up(qkv, 2, 4)
        got3 = shed(send3, 3)
        (grad_down,) = settle(owners, pair1, got1, ((0, local_units, "plain"),))
        up = [v[:1] for v in up] + [got2]
        pair2 = add_up(up, 0, 1)
        pair2 = joined(pair2, exchange(pair2, ("x", "x"), sizes))
        qkv = [v[:2] for v in qkv] + [got3]
        send3 = add_up(qkv, 1, 2)
        got3 = shed(send3, 4)
        got2 = exchange(pair2, ("core", "core"), sizes)
        grad_wout, grad_up = settle(
            owners, pair2, got2, ((0, local_width, "plain"), (local_width, local_width + local_units, "plain"))
        )
        qkv = [v[:1] for v in qkv] + [got3]
        pair3 = add_up(qkv, 0, 1)
        pair3 = joined(pair3, exchange(pair3, ("x", "x"), sizes))
        got3 = exchange(pair3, ("core", "core"), sizes)
        (grad_qkv,) = settle(owners, pair3, got3, ((0, 3 * local_width, "three"),))
    else:
        grad_x = spread(chunks)
        grad_down = reduce_plain(down_own, down_sib)
        both = reduce_plain(up_own, up_sib)
        grad_wout, grad_up = both[:, :local_width], both[:, local_width:]
        grad_qkv = reduce_plain(qkv_own, qkv_sib)
        grad_qkv = jnp.swapaxes(grad_qkv.reshape(shard_rows, 3, local_width), 0, 1)

    vector = lambda i: flat[i * width : (i + 1) * width]
    out_bqv = lax.dynamic_slice_in_dim(flat[: 2 * width].reshape(2, width), t * local_width, local_width, 1)
    out_bup = lax.dynamic_slice_in_dim(flat[8 * width :], t * local_units, local_units, 0)
    return (
        layer_output,
        grad_x,
        grad_qkv,
        out_bqv,
        grad_wout.T,
        vector(4),
        vector(2),
        vector(3),
        grad_up,
        out_bup,
        grad_down.T,
        vector(7),
        vector(5),
        vector(6),
    )


def solution(mesh):
    return jax.shard_map(
        body,
        mesh=mesh,
        in_specs=(
            P(None, "fsdp", "ctx", None),
            P(None, "fsdp", "ctx"),
            P(None, "fsdp", "tp"),
            P(None, "tp"),
            P("tp", "fsdp"),
            P(),
            P(),
            P(),
            P("fsdp", "tp"),
            P("tp"),
            P("tp", "fsdp"),
            P(),
            P(),
            P(),
            P(None, "fsdp", "ctx", None),
        ),
        out_specs=(
            P(None, "fsdp", "ctx", None),
            P(None, "fsdp", "ctx", None),
            P(None, "fsdp", "tp"),
            P(None, "tp"),
            P("tp", "fsdp"),
            P(),
            P(),
            P(),
            P("fsdp", "tp"),
            P("tp"),
            P("tp", "fsdp"),
            P(),
            P(),
            P(),
        ),
        check_vma=False,
    )
```

time: 963 us -> 334 us (0.35)
  waiting for transfers between devices: 571 us -> 99.8 us
  matrix products: 130 us -> 0 us
  Pallas kernels: 0 us -> 85.9 us
  local copies, waits for them, and re-layouts: 124 us -> 61 us
  blocking collectives: 53.1 us -> 0 us
  starting transfers between devices: 2.25 us -> 55.1 us
  other arithmetic: 59.6 us -> 28.2 us
  between operations: 17.5 us -> 2 us
    psum x5 -> x0, waiting for transfers between devices: 233 us -> none  [the longest x1 84.9 us: body(): lax.psum(jnp.dot(mixed_b, wo_all, preferred_element_type=jnp.float32), 'tp')]
    all_gather x7 -> x0, waiting for transfers between devices: 162 us -> none  [the longest x1 45.5 us: collect_weights(): lax.all_gather(weights[2], 'fsdp', axis=0, tiled=True)]
    dot_general x72 -> x0, matrix products: 130 us -> none  [the longest x4 24.1 us: body(): hidden = jnp.dot(first_b, wu_all, preferred_element_type=jnp.float32) + b_up]
    reduce_scatter x3 -> x0, waiting for transfers between devices: 120 us -> none  [the longest x1 50 us: spread_grads(): lax.psum_scatter(grads[3].astype(jnp.bfloat16), 'fsdp', scatter_dimension...]
    pallas_call x0 -> x17, Pallas kernels: none -> 85.9 us  [call(): pl.pallas_call(kernel, name=name, out_shape=outs, in_specs=specs, out_spe...]
    ppermute x0 -> x37, waiting for transfers between devices: none -> 79.1 us  [exchange(): return lax.ppermute(value, AXES, pairs)]
    unnamed x25 -> x0, waiting for transfers between devices: 55.9 us -> none
    ppermute x0 -> x37, starting transfers between devices: none -> 34.2 us  [exchange(): return lax.ppermute(value, AXES, pairs)]
  transfers between devices with their start and end apart: 20 -> 43, of which waited for: 15 -> 19; matrix products, arithmetic and copies ran while one was open for 17% -> 11% of each run, Pallas kernels for 0% -> 22%
where the time goes in v2:
time: 334 us; the launch traced here: 332 us
  waiting for transfers between devices  99.8 us (30%)
  Pallas kernels  85.9 us (26%)
  local copies, waits for them, and re-layouts  61 us (18%)
  starting transfers between devices  55.1 us (16%)
  other arithmetic  28.2 us (8%)
    pallas_call x17, Pallas kernels, call(): pl.pallas_call(kernel, name=name, out_shape=outs, in_specs=specs, out_spe...  85.9 us
    ppermute x37, waiting for transfers between devices, exchange(): return lax.ppermute(value, AXES, pairs)  79.1 us
    unnamed x158, local copies, waits for them, and re-layouts  53.3 us
    ppermute x37, starting transfers between devices, exchange(): return lax.ppermute(value, AXES, pairs)  34.2 us
    convert_element_type x15, other arithmetic, add_up(): return total.astype(BF16)  26.8 us
    all_to_all x2, starting transfers between devices, spread(): out = lax.all_to_all(chunks, ('ctx', 'tp'), 0, 0, tiled=True)  8.6 us
    all_to_all x2, waiting for transfers between devices, to_owners(): return lax.all_to_all(chunks, 'ctx', 0, 0, tiled=True)  8.5 us
    all_to_all x1, waiting for transfers between devices, body(): lax.all_to_all(jnp.broadcast_to(part, (devices,) + part.shape[1:]), AXES,...  7.4 us
  transfers between devices with their start and end apart: 43, of which 19 were waited for; matrix products, arithmetic and copies ran while one was open for 11% of the time, Pallas kernels for 22%

profile of v2, /device:TPU:0, one launch (start us, length us, event | category | flops | bytes accessed | tf_op | source)
XLA Modules:
  0.0 331.9 jit_solution(13154999179004980378)
XLA Ops:
  1.9 4.1 %collective-permute-start = (bf16[1,48,1152]{2,1,0:T(8,128)(2,1)S(1)}, bf16[1,48,1152]{2,1,0:T(8,128)(2,1)S(1)}, u32[]{:S(2)}, u32[]{:S(2)}) collective-permute-start(bf16[1,48,1152]{2,1,0:T(8,128)(2,1)S(1)} %dynamic-slice_bitcast_fusion.3), channel_id=1, source_target_pairs={{0,16},{1,17},{2,18},{3,19},{4,20},{5,21},{6,22},{7,23},{8,24},{9,... | collective-permute-start | bytes 331784 | tf_op jit(solution)/shard_map/ppermute | solution.py:37
  7.1 3.5 %all-to-all-start = ((bf16[4,136,768]{2,1,0:T(8,128)(2,1)}), bf16[4,136,768]{2,1,0:T(8,128)(2,1)S(1)}, u32[]{:S(2)}, u32[]{:S(2)}) async-start(bf16[4,136,768]{2,1,0:T(8,128)(2,1)} %fusion.1), calls=%async_computation | async-start | bytes 1671168 | tf_op jit(solution)/shard_map/all_to_all | solution.py:674
  12.6 1.6 collective-permute-start.1
  14.5 5.7 %collective-permute-done.1 = bf16[2,48,1152]{2,1,0:T(8,128)(2,1)S(1)} collective-permute-done((bf16[2,48,1152]{2,1,0:T(8,128)(2,1)S(1)}, bf16[2,48,1152]{2,1,0:T(8,128)(2,1)S(1)}, u32[]{:S(2)}, u32[]{:S(2)}) %collective-permute-start.1) | collective-permute-done | bytes 221216 | tf_op jit(solution)/shard_map/ppermute | solution.py:37
  20.2 2.6 all-to-all-done.given_ref
  24.8 9.5 %collective-permute-done.4 = bf16[1,48,1920]{2,1,0:T(8,128)(2,1)S(1)} collective-permute-done((bf16[1,48,1920]{2,1,0:T(8,128)(2,1)S(1)}, bf16[1,48,1920]{2,1,0:T(8,128)(2,1)S(1)}, u32[]{:S(2)}, u32[]{:S(2)}) %collective-permute-start.4) | collective-permute-done | bytes 184352 | tf_op jit(solution)/shard_map/ppermute | solution.py:37
  35.9 9.2 %collective-permute-done.7 = bf16[2,48,1920]{2,1,0:T(8,128)(2,1)S(1)} collective-permute-done((bf16[2,48,1920]{2,1,0:T(8,128)(2,1)S(1)}, bf16[2,48,1920]{2,1,0:T(8,128)(2,1)S(1)}, u32[]{:S(2)}, u32[]{:S(2)}) %collective-permute-start.7) | collective-permute-done | bytes 368672 | tf_op jit(solution)/shard_map/ppermute | solution.py:37
  45.1 2.3 collective-permute-done.5
  51.7 2.8 unpack.3.weight_ref
  54.5 3.2 project.1
  57.7 2.9 collective-permute-done.10
  62.4 6.7 %attend.2 = (bf16[512,384]{1,0:T(8,128)(2,1)S(1)}, bf16[6,512,512]{2,1,0:T(8,128)(2,1)S(1)}) custom-call(bf16[512,2304]{1,0:T(8,128)(2,1)S(1)} %get-tuple-element.109.refs_0_, f32[512,512]{1,0:T(8,128)S(1)} %get-tuple-element.106.refs_1_), custom_call_target="tpu_custom_call" | custom-call | flops 12000000000 | bytes 1000000 | tf_op jit(solution)/shard_map/attend/pallas_call | solution.py:123
  69.1 1.7 copy-done.31
  70.8 6.7 %attend.3 = (bf16[512,384]{1,0:T(8,128)(2,1)S(1)}, bf16[6,512,512]{2,1,0:T(8,128)(2,1)S(1)}) custom-call(bf16[512,2304]{1,0:T(8,128)(2,1)S(1)} %get-tuple-element.109.refs_0_, f32[512,512]{1,0:T(8,128)S(1)} %get-tuple-element.106.refs_1_), custom_call_target="tpu_custom_call" | custom-call | flops 12000000000 | bytes 1000000 | tf_op jit(solution)/shard_map/attend/pallas_call | solution.py:123
  77.5 1.6 copy-done.29
  82.3 8.3 %collective-permute-done.12 = bf16[4,48,1536]{2,1,0:T(8,128)(2,1)S(1)} collective-permute-done((bf16[4,48,1536]{2,1,0:T(8,128)(2,1)S(1)}, bf16[4,48,1536]{2,1,0:T(8,128)(2,1)S(1)}, u32[]{:S(2)}, u32[]{:S(2)}) %collective-permute-start.12) | collective-permute-done | bytes 589856 | tf_op jit(solution)/shard_map/ppermute | solution.py:37
  92.1 2.9 unpack.4
  95.1 9.3 %middle.1 = (f32[512,768]{1,0:T(8,128)S(1)}, f32[512,1]{1,0:T(8,128)S(1)}, bf16[512,768]{1,0:T(8,128)(2,1)S(1)}, bf16[512,3072]{1,0:T(8,128)(2,1)S(1)}, bf16[512,3072]{1,0:T(8,128)(2,1)S(1)}) custom-call(s32[65]{0:T(128)S(1)} %stack.361.info_ref, bf16[768,768]{1,0:T(8,128)(2,1)S(1)} %get-tuple-element.114.w_out, ...), custom_call_target="tpu_custom_call" | custom-call | flops 12000000000 | bytes 1000000 | tf_op jit(solution)/shard_map/middle/pallas_call | solution.py:123
  104.4 1.6 copy-done.25
  106.0 1.7 copy-done.27
  111.0 3.7 %all-to-all-start.1 = ((bf16[4,128,768]{2,1,0:T(8,128)(2,1)}), bf16[4,128,768]{2,1,0:T(8,128)(2,1)S(1)}, u32[]{:S(2)}, u32[]{:S(2)}) async-start(bf16[4,128,768]{2,1,0:T(8,128)(2,1)} %dynamic-slice_bitcast_fusion), calls=%async_computation.1 | async-start | bytes 1572864 | tf_op jit(solution)/shard_map/all_to_all | solution.py:674
  114.9 3.1 unpack.5.weight_ref
  118.0 2.2 copy-done.9
  120.2 5.9 %all-to-all-done.1 = bf16[4,128,768]{2,1,0:T(8,128)(2,1)S(1)} async-done(((bf16[4,128,768]{2,1,0:T(8,128)(2,1)}), bf16[4,128,768]{2,1,0:T(8,128)(2,1)S(1)}, u32[]{:S(2)}, u32[]{:S(2)}) %all-to-all-start.1) | async-done | bytes 786464 | tf_op jit(solution)/shard_map/all_to_all | solution.py:674
  126.1 2.3 copy-done.10
  128.4 1.9 copy-done.28
  131.7 11.4 %turn.1 = (bf16[8,128,768]{2,1,0:T(8,128)(2,1)S(1)}, f32[512,768]{1,0:T(8,128)S(1)}, bf16[512,768]{1,0:T(8,128)(2,1)S(1)}, f32[8,768]{1,0:T(8,128)S(1)}, bf16[16...) custom-call(s32[65]{0:T(128)S(1)} %stack.336.pack_ref, bf16[768,3072]{1,0:T(8,128)(2,1)S(1)} %copy-done.10, ...), custom_call_target="tpu_custom_call" | custom-call | flops 14000000000 | bytes 1000000 | tf_op jit(solution)/shard_map/turn/pallas_call | solution.py:123
  146.3 4.3 %all-to-all-start.2 = ((bf16[8,128,768]{2,1,0:T(8,128)(2,1)}), bf16[8,128,768]{2,1,0:T(8,128)(2,1)}, u32[]{:S(2)}, u32[]{:S(2)}) async-start(bf16[8,128,768]{2,1,0:T(8,128)(2,1)} %copy-done.7), calls=%async_computation.2 | async-start | bytes 3145728 | tf_op jit(solution)/shard_map/all_to_all | solution.py:677
  150.6 2.3 copy-done.11
  152.9 1.9 copy-done.26
  156.0 3.8 %hidden_back.1 = (bf16[512,3072]{1,0:T(8,128)(2,1)S(1)}, f32[1,3072]{1,0:T(1,128)S(1)}) custom-call(bf16[768,3072]{1,0:T(8,128)(2,1)S(1)} %copy-done.11, bf16[512,768]{1,0:T(8,128)(2,1)S(1)} %copy-done.51, bf16[512,3072]{1,0:T(8,128)(2,1)S(1)} %copy-done.26), custom_call_target="tpu_custom_call" | custom-call | flops 12000000000 | bytes 1000000 | tf_op jit(solution)/shard_map/hidden_back/pallas_call | solution.py:123
  159.8 2.7 add_convert_fusion.1
  162.5 1.9 collective-permute-start.17
  164.5 2.3 copy-done.13
  166.8 13.1 %first_back.1 = (f32[512,768]{1,0:T(8,128)S(1)}, bf16[512,768]{1,0:T(8,128)(2,1)S(1)}, f32[8,768]{1,0:T(8,128)S(1)}, bf16[16,48,1920]{2,1,0:T(8,128)(2,1)S(1)}, bf16[16,48,1920]{2,1,0:T(8,128)(2,1)}) custom-call(s32[65]{0:T(128)S(1)} %stack.336.pack_ref, bf16[768,768]{1,0:T(8,128)(2,1)S(1)} %copy-done.20, bf16[768,3072]{1,0:T(8,128)(2,1)S(1)} %copy-done.13, ...), custom_call_target="tpu_custom_call" | custom-call | flops 20000000000 | bytes 1000000 | tf_op jit(solution)/shard_map/first_back/pallas_call | solution.py:123
  183.4 2.4 add_convert_fusion.4
  187.3 1.7 copy-done.17
  189.0 1.9 copy-done.32
  192.0 5.3 %attend_back.2 = (bf16[512,384]{1,0:T(8,128)(2,1)S(1)}, bf16[512,384]{1,0:T(8,128)(2,1)S(1)}, bf16[512,384]{1,0:T(8,128)(2,1)S(1)}) custom-call(bf16[512,2304]{1,0:T(8,128)(2,1)S(1)} %copy-done.17, bf16[6,512,512]{2,1,0:T(8,128)(2,1)S(1)} %copy-done.32, bf16[512,768]{1,0:T(8,128)(2,1)S(1)} %copy-done.55), custom_call_target="tpu_custom_call" | custom-call | flops 14000000000 | bytes 1000000 | tf_op jit(solution)/shard_map/attend_back/pallas_call | solution.py:123
  197.4 1.8 add_convert_fusion.7
  199.2 2.1 collective-permute-start.20
  201.2 3.0 add_convert_fusion
  204.8 5.6 %attend_back.3 = (bf16[512,384]{1,0:T(8,128)(2,1)S(1)}, bf16[512,384]{1,0:T(8,128)(2,1)S(1)}, bf16[512,384]{1,0:T(8,128)(2,1)S(1)}) custom-call(bf16[512,2304]{1,0:T(8,128)(2,1)S(1)} %copy-done.18, bf16[6,512,512]{2,1,0:T(8,128)(2,1)S(1)} %copy-done.30, bf16[512,768]{1,0:T(8,128)(2,1)S(1)} %copy-done.55), custom_call_target="tpu_custom_call" | custom-call | flops 14000000000 | bytes 1000000 | tf_op jit(solution)/shard_map/attend_back/pallas_call | solution.py:123
  210.4 1.7 add_convert_fusion.12
  212.1 4.4 %last.1 = (f32[8,768]{1,0:T(8,128)S(1)}, bf16[16,48,1152]{2,1,0:T(8,128)(2,1)S(1)}, bf16[16,48,1152]{2,1,0:T(8,128)(2,1)S(1)}) custom-call(s32[65]{0:T(128)S(1)} %stack.336.pack_ref, bf16[512,768]{1,0:T(8,128)(2,1)S(1)} %copy-done.22, bf16[512,384]{1,0:T(8,128)(2,1)S(1)} %get-tuple-element.161.refs_0_, bf16[512,384]{1,0:T(8,128)(2,1)S(1)} %get-tuple-element.143.refs_1_, ...), custom_call_target="tpu_custom_call" | custom-call | flops 10000000000 | bytes 1000000 | tf_op jit(solution)/shard_map/last/pallas_call | solution.py:123
  219.8 2.5 all-to-all-start.4
  222.4 2.7 collective-permute-start.21
  225.1 4.8 %all-to-all-done.4 = f32[32,1,288]{2,1,0:T(1,128)S(1)} async-done(((f32[32,1,288]{2,1,0:T(1,128)}), f32[32,1,288]{2,1,0:T(1,128)S(1)}, u32[]{:S(2)}, u32[]{:S(2)}) %all-to-all-start.4) | async-done | bytes 36896 | tf_op jit(solution)/shard_map/all_to_all | solution.py:799
  230.6 2.5 all-to-all-start.5
  233.2 7.4 %all-to-all-done.5 = f32[32,1,288]{2,1,0:T(1,128)S(1)} async-done(((f32[32,1,288]{2,1,0:T(1,128)}), f32[32,1,288]{2,1,0:T(1,128)S(1)}, u32[]{:S(2)}, u32[]{:S(2)}) %all-to-all-start.5) | async-done | bytes 36896 | tf_op jit(solution)/shard_map/all_to_all | solution.py:801
  242.6 2.0 copy-done.15
  252.0 2.6 input_back.1
  254.6 3.1 add_convert_fusion.3
  258.4 2.3 add_convert_fusion.2
  264.2 4.3 %all-to-all-start.3 = ((bf16[8,128,768]{2,1,0:T(8,128)(2,1)}), bf16[8,128,768]{2,1,0:T(8,128)(2,1)}, u32[]{:S(2)}, u32[]{:S(2)}) async-start(bf16[8,128,768]{2,1,0:T(8,128)(2,1)} %copy-done.6), calls=%async_computation.3 | async-start | bytes 3145728 | tf_op jit(solution)/shard_map/all_to_all | solution.py:677
  268.5 10.7 %collective-permute-done.25 = bf16[4,48,1920]{2,1,0:T(8,128)(2,1)} collective-permute-done((bf16[4,48,1920]{2,1,0:T(8,128)(2,1)}, bf16[4,48,1920]{2,1,0:T(8,128)(2,1)}, u32[]{:S(2)}, u32[]{:S(2)}) %collective-permute-start.25) | collective-permute-done | bytes 737312 | tf_op jit(solution)/shard_map/ppermute | solution.py:37
  282.5 5.7 %collective-permute-done.31 = bf16[2,48,1920]{2,1,0:T(8,128)(2,1)S(1)} collective-permute-done((bf16[2,48,1920]{2,1,0:T(8,128)(2,1)S(1)}, bf16[2,48,1920]{2,1,0:T(8,128)(2,1)S(1)}, u32[]{:S(2)}, u32[]{:S(2)}) %collective-permute-start.31) | collective-permute-done | bytes 368672 | tf_op jit(solution)/shard_map/ppermute | solution.py:37
  290.3 10.2 %collective-permute-done.26 = bf16[4,48,1152]{2,1,0:T(8,128)(2,1)S(1)} collective-permute-done((bf16[4,48,1152]{2,1,0:T(8,128)(2,1)S(1)}, bf16[4,48,1152]{2,1,0:T(8,128)(2,1)S(1)}, u32[]{:S(2)}, u32[]{:S(2)}) %collective-permute-start.26) | collective-permute-done | bytes 442400 | tf_op jit(solution)/shard_map/ppermute | solution.py:37
  304.8 5.1 %collective-permute-done.27 = bf16[2,48,1152]{2,1,0:T(8,128)(2,1)S(1)} collective-permute-done((bf16[2,48,1152]{2,1,0:T(8,128)(2,1)S(1)}, bf16[2,48,1152]{2,1,0:T(8,128)(2,1)S(1)}, u32[]{:S(2)}, u32[]{:S(2)}) %collective-permute-start.27) | collective-permute-done | bytes 221216 | tf_op jit(solution)/shard_map/ppermute | solution.py:37
  312.1 5.1 %collective-permute-done.28 = bf16[1,48,1152]{2,1,0:T(8,128)(2,1)S(1)} collective-permute-done((bf16[1,48,1152]{2,1,0:T(8,128)(2,1)S(1)}, bf16[1,48,1152]{2,1,0:T(8,128)(2,1)S(1)}, u32[]{:S(2)}, u32[]{:S(2)}) %collective-permute-start.28) | collective-permute-done | bytes 110624 | tf_op jit(solution)/shard_map/ppermute | solution.py:37
  319.7 1.7 settle.5
  323.1 1.8 settle.4
  326.5 2.8 copy.51
  329.2 2.7 copy.52
  (266 shorter events, 69.4 us)
Async XLA Ops:
  1.9 10.6 %collective-permute-start = (bf16[1,48,1152]{2,1,0:T(8,128)(2,1)S(1)}, bf16[1,48,1152]{2,1,0:T(8,128)(2,1)S(1)}, u32[]{:S(2)}, u32[]{:S(2)}) collective-permute-start(bf16[1,48,1152]{2,1,0:T(8,128)(2,1)S(1)} %dynamic-slice_bitcast_fusion.3), channel_id=1, source_target_pairs={{0,16},{1,17},{2,18},{3,19},{4,20},{5,21},{6,22},{7,23},{8,24},{9,... | collective-permute-start | bytes 331784 | tf_op jit(solution)/shard_map/ppermute | solution.py:37
  6.2 6.3 %copy-start.71 = (f32[768]{0:T(1024)S(1)}, f32[768]{0:T(1024)}, u32[]{:S(2)}) copy-start(f32[768]{0:T(1024)} %param.28) | copy-start | bytes 9220
  7.1 15.7 %all-to-all-start = ((bf16[4,136,768]{2,1,0:T(8,128)(2,1)}), bf16[4,136,768]{2,1,0:T(8,128)(2,1)S(1)}, u32[]{:S(2)}, u32[]{:S(2)}) async-start(bf16[4,136,768]{2,1,0:T(8,128)(2,1)} %fusion.1), calls=%async_computation | async-start | bytes 1671168 | tf_op jit(solution)/shard_map/all_to_all | solution.py:674
  10.7 3.7 %collective-permute-start.2 = (f32[1,2304]{1,0:T(1,128)S(1)}, f32[1,2304]{1,0:T(1,128)S(1)}, u32[]{:S(2)}, u32[]{:S(2)}) collective-permute-start(f32[1,2304]{1,0:T(1,128)S(1)} %broadcast_in_dim.21), channel_id=1, source_target_pairs={{0,1},{1,0},{2,3},{3,2},{4,5},{5,4},{6,7},{7,6},{8,9},{9,8},{10,11... | collective-permute-start | bytes 27656 | tf_op jit(solution)/shard_map/ppermute | solution.py:37
  12.6 7.6 %collective-permute-start.1 = (bf16[2,48,1152]{2,1,0:T(8,128)(2,1)S(1)}, bf16[2,48,1152]{2,1,0:T(8,128)(2,1)S(1)}, u32[]{:S(2)}, u32[]{:S(2)}) collective-permute-start(bf16[2,48,1152]{2,1,0:T(8,128)(2,1)S(1)} %pad_maximum_fusion.3), channel_id=1, source_target_pairs={{0,8},{1,9},{2,10},{3,11},{4,12},{5,13},{6,14},{7,15},{8,0},{9,1},... | collective-permute-start | bytes 663560 | tf_op jit(solution)/shard_map/ppermute | solution.py:37
  22.8 11.5 %collective-permute-start.3 = (bf16[4,48,1152]{2,1,0:T(8,128)(2,1)S(1)}, bf16[4,48,1152]{2,1,0:T(8,128)(2,1)S(1)}, u32[]{:S(2)}, u32[]{:S(2)}) collective-permute-start(bf16[4,48,1152]{2,1,0:T(8,128)(2,1)S(1)} %pad_maximum_fusion), channel_id=1, source_target_pairs={{0,1},{1,0},{2,6},{3,7},{4,5},{5,4},{6,2},{7,3},{8,9},{9,8},{10,14... | collective-permute-start | bytes 1327112 | tf_op jit(solution)/shard_map/ppermute | solution.py:37
  24.4 9.9 %collective-permute-start.4 = (bf16[1,48,1920]{2,1,0:T(8,128)(2,1)S(1)}, bf16[1,48,1920]{2,1,0:T(8,128)(2,1)S(1)}, u32[]{:S(2)}, u32[]{:S(2)}) collective-permute-start(bf16[1,48,1920]{2,1,0:T(8,128)(2,1)S(1)} %fusion.3), channel_id=1, source_target_pairs={{0,16},{1,17},{2,18},{3,19},{4,20},{5,21},{6,22},{7,23},{8,24},{9,... | collective-permute-start | bytes 552968 | tf_op jit(solution)/shard_map/ppermute | solution.py:37
  34.4 13.1 %collective-permute-start.5 = (bf16[8,48,1152]{2,1,0:T(8,128)(2,1)S(1)}, bf16[8,48,1152]{2,1,0:T(8,128)(2,1)S(1)}, u32[]{:S(2)}, u32[]{:S(2)}) collective-permute-start(bf16[8,48,1152]{2,1,0:T(8,128)(2,1)S(1)} %constant_dynamic-update-slice_fusion), channel_id=1, source_target_pairs={{0,4},{1,5},{2,3},{3,2},{4,0},{5,1},{6,7},{7,6},{8,12},{9,13},{10,... | collective-permute-start | bytes 2654216 | tf_op jit(solution)/shard_map/ppermute | solution.py:37
  35.8 9.3 %collective-permute-start.7 = (bf16[2,48,1920]{2,1,0:T(8,128)(2,1)S(1)}, bf16[2,48,1920]{2,1,0:T(8,128)(2,1)S(1)}, u32[]{:S(2)}, u32[]{:S(2)}) collective-permute-start(bf16[2,48,1920]{2,1,0:T(8,128)(2,1)S(1)} %constant_dynamic-update-slice_fusion.2), channel_id=1, source_target_pairs={{0,8},{1,9},{2,10},{3,11},{4,12},{5,13},{6,14},{7,15},{8,0},{9,1},... | collective-permute-start | bytes 1105928 | tf_op jit(solution)/shard_map/ppermute | solution.py:37
  47.6 4.1 %collective-permute-start.8 = (bf16[16,48,1152]{2,1,0:T(8,128)(2,1)S(1)}, bf16[16,48,1152]{2,1,0:T(8,128)(2,1)}, u32[]{:S(2)}, u32[]{:S(2)}) collective-permute-start(bf16[16,48,1152]{2,1,0:T(8,128)(2,1)S(1)} %constant_dynamic-update-slice_fusion.4.own_ref), channel_id=1, source_target_pairs={{0,2},{1,3},{2,0},{3,1},{4,6},{5,7},{6,4},{7,5},{8,10},{9,11},{10,... | collective-permute-start | bytes 5308424 | tf_op jit(solution)/shard_map/ppermute | solution.py:37
  48.9 11.7 %collective-permute-start.10 = (bf16[4,48,1920]{2,1,0:T(8,128)(2,1)}, bf16[4,48,1920]{2,1,0:T(8,128)(2,1)S(1)}, u32[]{:S(2)}, u32[]{:S(2)}) collective-permute-start(bf16[4,48,1920]{2,1,0:T(8,128)(2,1)} %copy-done.60), channel_id=1, source_target_pairs={{0,1},{1,0},{2,6},{3,7},{4,5},{5,4},{6,2},{7,3},{8,9},{9,8},{10,14... | collective-permute-start | bytes 2211848 | tf_op jit(solution)/shard_map/ppermute | solution.py:37
  50.4 10.2 %collective-permute-start.6 = (bf16[1,48,1536]{2,1,0:T(8,128)(2,1)S(1)}, bf16[1,48,1536]{2,1,0:T(8,128)(2,1)S(1)}, u32[]{:S(2)}, u32[]{:S(2)}) collective-permute-start(bf16[1,48,1536]{2,1,0:T(8,128)(2,1)S(1)} %dynamic-slice_bitcast_fusion.2), channel_id=1, source_target_pairs={{0,16},{1,17},{2,18},{3,19},{4,20},{5,21},{6,22},{7,23},{8,24},{9,... | collective-permute-start | bytes 442376 | tf_op jit(solution)/shard_map/ppermute | solution.py:37
  57.7 13.0 %copy-start.16 = (bf16[512,2304]{1,0:T(8,128)(2,1)}, bf16[512,2304]{1,0:T(8,128)(2,1)S(1)}, u32[]{:S(2)}) copy-start(bf16[512,2304]{1,0:T(8,128)(2,1)S(1)} %get-tuple-element.109.refs_0_) | copy-start | bytes 7077892
  57.7 37.3 %copy-start.21 = (bf16[512,768]{1,0:T(8,128)(2,1)}, bf16[512,768]{1,0:T(8,128)(2,1)S(1)}, u32[]{:S(2)}) copy-start(bf16[512,768]{1,0:T(8,128)(2,1)S(1)} %get-tuple-element.117.x_ref) | copy-start | bytes 2359300
  60.6 10.1 %collective-permute-start.9 = (bf16[2,48,1536]{2,1,0:T(8,128)(2,1)S(1)}, bf16[2,48,1536]{2,1,0:T(8,128)(2,1)S(1)}, u32[]{:S(2)}, u32[]{:S(2)}) collective-permute-start(bf16[2,48,1536]{2,1,0:T(8,128)(2,1)S(1)} %get-tuple-element.178), channel_id=1, source_target_pairs={{0,8},{1,9},{2,10},{3,11},{4,12},{5,13},{6,14},{7,15},{8,0},{9,1},... | collective-permute-start | bytes 884744 | tf_op jit(solution)/shard_map/ppermute | solution.py:37
  60.9 19.4 %collective-permute-start.11 = (bf16[8,48,1920]{2,1,0:T(8,128)(2,1)S(1)}, bf16[8,48,1920]{2,1,0:T(8,128)(2,1)S(1)}, u32[]{:S(2)}, u32[]{:S(2)}) collective-permute-start(bf16[8,48,1920]{2,1,0:T(8,128)(2,1)S(1)} %get-tuple-element.171), channel_id=1, source_target_pairs={{0,4},{1,5},{2,3},{3,2},{4,0},{5,1},{6,7},{7,6},{8,12},{9,13},{10,... | collective-permute-start | bytes 4423688 | tf_op jit(solution)/shard_map/ppermute | solution.py:37
  70.7 24.3 %copy-start.56 = (bf16[512,384]{1,0:T(8,128)(2,1)}, bf16[512,384]{1,0:T(8,128)(2,1)S(1)}, u32[]{:S(2)}) copy-start(bf16[512,384]{1,0:T(8,128)(2,1)S(1)} %get-tuple-element.116.mixed0_ref) | copy-start | bytes 1179652
  79.1 16.0 %copy-start.58 = (bf16[512,384]{1,0:T(8,128)(2,1)}, bf16[512,384]{1,0:T(8,128)(2,1)S(1)}, u32[]{:S(2)}) copy-start(bf16[512,384]{1,0:T(8,128)(2,1)S(1)} %get-tuple-element.110.mixed1_ref) | copy-start | bytes 1179652
  80.5 10.0 %collective-permute-start.13 = (bf16[16,48,1920]{2,1,0:T(8,128)(2,1)S(1)}, bf16[16,48,1920]{2,1,0:T(8,128)(2,1)S(1)}, u32[]{:S(2)}, u32[]{:S(2)}) collective-permute-start(bf16[16,48,1920]{2,1,0:T(8,128)(2,1)S(1)} %constant_dynamic-update-slice_fusion.15.own_ref), channel_id=1, source_target_pairs={{0,2},{1,3},{2,0},{3,1},{4,6},{5,7},{6,4},{7,5},{8,10},{9,11},{10,... | collective-permute-start | bytes 8847368 | tf_op jit(solution)/shard_map/ppermute | solution.py:37
  80.6 9.9 %collective-permute-start.12 = (bf16[4,48,1536]{2,1,0:T(8,128)(2,1)S(1)}, bf16[4,48,1536]{2,1,0:T(8,128)(2,1)S(1)}, u32[]{:S(2)}, u32[]{:S(2)}) collective-permute-start(bf16[4,48,1536]{2,1,0:T(8,128)(2,1)S(1)} %constant_dynamic-update-slice_fusion.12), channel_id=1, source_target_pairs={{0,1},{1,0},{2,6},{3,7},{4,5},{5,4},{6,2},{7,3},{8,9},{9,8},{10,14... | collective-permute-start | bytes 1769480 | tf_op jit(solution)/shard_map/ppermute | solution.py:37
  90.7 17.1 %collective-permute-start.14 = (bf16[8,48,1536]{2,1,0:T(8,128)(2,1)S(1)}, bf16[8,48,1536]{2,1,0:T(8,128)(2,1)S(1)}, u32[]{:S(2)}, u32[]{:S(2)}) collective-permute-start(bf16[8,48,1536]{2,1,0:T(8,128)(2,1)S(1)} %get-tuple-element.174), channel_id=1, source_target_pairs={{0,4},{1,5},{2,3},{3,2},{4,0},{5,1},{6,7},{7,6},{8,12},{9,13},{10,... | collective-permute-start | bytes 3538952 | tf_op jit(solution)/shard_map/ppermute | solution.py:37
  95.0 9.3 %copy-start.12 = (bf16[768,3072]{1,0:T(8,128)(2,1)}, bf16[768,3072]{1,0:T(8,128)(2,1)S(1)}, u32[]{:S(2)}) copy-start(bf16[768,3072]{1,0:T(8,128)(2,1)S(1)} %get-tuple-element.115.w_up) | copy-start | bytes 14155780
  95.0 9.3 %copy-start.19 = (bf16[768,768]{1,0:T(8,128)(2,1)}, bf16[768,768]{1,0:T(8,128)(2,1)S(1)}, u32[]{:S(2)}) copy-start(bf16[768,768]{1,0:T(8,128)(2,1)S(1)} %get-tuple-element.114.w_out) | copy-start | bytes 3538948
  108.9 6.0 %collective-permute-start.15 = (bf16[16,48,1536]{2,1,0:T(8,128)(2,1)S(1)}, bf16[16,48,1536]{2,1,0:T(8,128)(2,1)}, u32[]{:S(2)}, u32[]{:S(2)}) collective-permute-start(bf16[16,48,1536]{2,1,0:T(8,128)(2,1)S(1)} %constant_dynamic-update-slice_fusion.20.own_ref), channel_id=1, source_target_pairs={{0,2},{1,3},{2,0},{3,1},{4,6},{5,7},{6,4},{7,5},{8,10},{9,11},{10,... | collective-permute-start | bytes 7077896 | tf_op jit(solution)/shard_map/ppermute | solution.py:37
  111.0 15.1 %all-to-all-start.1 = ((bf16[4,128,768]{2,1,0:T(8,128)(2,1)}), bf16[4,128,768]{2,1,0:T(8,128)(2,1)S(1)}, u32[]{:S(2)}, u32[]{:S(2)}) async-start(bf16[4,128,768]{2,1,0:T(8,128)(2,1)} %dynamic-slice_bitcast_fusion), calls=%async_computation.1 | async-start | bytes 1572864 | tf_op jit(solution)/shard_map/all_to_all | solution.py:674
  145.1 14.6 %copy-start.2 = (bf16[16,48,1536]{2,1,0:T(8,128)(2,1)}, bf16[16,48,1536]{2,1,0:T(8,128)(2,1)S(1)}, u32[]{:S(2)}) copy-start(bf16[16,48,1536]{2,1,0:T(8,128)(2,1)S(1)} %get-tuple-element.130) | copy-start | bytes 7077892
  145.1 14.6 %collective-permute-start.16 = (bf16[16,48,1536]{2,1,0:T(8,128)(2,1)}, bf16[16,48,1536]{2,1,0:T(8,128)(2,1)}, u32[]{:S(2)}, u32[]{:S(2)}) collective-permute-start(bf16[16,48,1536]{2,1,0:T(8,128)(2,1)} %get-tuple-element.126), channel_id=1, source_target_pairs={{0,2},{1,3},{2,0},{3,1},{4,6},{5,7},{6,4},{7,5},{8,10},{9,11},{10,... | collective-permute-start | bytes 7077896 | tf_op jit(solution)/shard_map/ppermute | solution.py:37
  146.3 41.0 %all-to-all-start.2 = ((bf16[8,128,768]{2,1,0:T(8,128)(2,1)}), bf16[8,128,768]{2,1,0:T(8,128)(2,1)}, u32[]{:S(2)}, u32[]{:S(2)}) async-start(bf16[8,128,768]{2,1,0:T(8,128)(2,1)} %copy-done.7), calls=%async_computation.2 | async-start | bytes 3145728 | tf_op jit(solution)/shard_map/all_to_all | solution.py:677
  155.9 8.5 %copy-start.49 = (f32[512,768]{1,0:T(8,128)S(1)}, f32[512,768]{1,0:T(8,128)}, u32[]{:S(2)}) copy-start(f32[512,768]{1,0:T(8,128)} %copy-done.48) | copy-start | bytes 4718596
  155.9 8.5 %copy-start.57 = (bf16[512,384]{1,0:T(8,128)(2,1)S(1)}, bf16[512,384]{1,0:T(8,128)(2,1)}, u32[]{:S(2)}) copy-start(bf16[512,384]{1,0:T(8,128)(2,1)} %copy-done.56) | copy-start | bytes 1179652
  156.0 8.5 %copy-start.59 = (bf16[512,384]{1,0:T(8,128)(2,1)S(1)}, bf16[512,384]{1,0:T(8,128)(2,1)}, u32[]{:S(2)}) copy-start(bf16[512,384]{1,0:T(8,128)(2,1)} %copy-done.58) | copy-start | bytes 1179652
  162.5 20.9 %collective-permute-start.17 = (bf16[8,48,1536]{2,1,0:T(8,128)(2,1)}, bf16[8,48,1536]{2,1,0:T(8,128)(2,1)}, u32[]{:S(2)}, u32[]{:S(2)}) collective-permute-start(bf16[8,48,1536]{2,1,0:T(8,128)(2,1)} %add_convert_fusion.1), channel_id=1, source_target_pairs={{0,4},{1,5},{2,3},{3,2},{4,0},{5,1},{6,7},{7,6},{8,12},{9,13},{10,... | collective-permute-start | bytes 3538952 | tf_op jit(solution)/shard_map/ppermute | solution.py:37
  182.0 19.3 %collective-permute-start.19 = (bf16[16,48,1920]{2,1,0:T(8,128)(2,1)}, bf16[16,48,1920]{2,1,0:T(8,128)(2,1)}, u32[]{:S(2)}, u32[]{:S(2)}) collective-permute-start(bf16[16,48,1920]{2,1,0:T(8,128)(2,1)} %get-tuple-element.140), channel_id=1, source_target_pairs={{0,2},{1,3},{2,0},{3,1},{4,6},{5,7},{6,4},{7,5},{8,10},{9,11},{10,... | collective-permute-start | bytes 8847368 | tf_op jit(solution)/shard_map/ppermute | solution.py:37
  185.8 11.5 %collective-permute-start.18 = (bf16[4,48,1536]{2,1,0:T(8,128)(2,1)}, bf16[4,48,1536]{2,1,0:T(8,128)(2,1)}, u32[]{:S(2)}, u32[]{:S(2)}) collective-permute-start(bf16[4,48,1536]{2,1,0:T(8,128)(2,1)} %add_convert_fusion.4), channel_id=1, source_target_pairs={{0,1},{1,0},{2,10},{3,11},{4,5},{5,4},{6,14},{7,15},{8,9},{9,8},{1... | collective-permute-start | bytes 1769480 | tf_op jit(solution)/shard_map/ppermute | solution.py:37
  197.3 14.8 %copy-start.36 = (bf16[512,384]{1,0:T(8,128)(2,1)}, bf16[512,384]{1,0:T(8,128)(2,1)S(1)}, u32[]{:S(2)}) copy-start(bf16[512,384]{1,0:T(8,128)(2,1)S(1)} %get-tuple-element.161.refs_0_) | copy-start | bytes 1179652
  197.3 14.8 %copy-start.38 = (bf16[512,384]{1,0:T(8,128)(2,1)}, bf16[512,384]{1,0:T(8,128)(2,1)S(1)}, u32[]{:S(2)}) copy-start(bf16[512,384]{1,0:T(8,128)(2,1)S(1)} %get-tuple-element.143.refs_1_) | copy-start | bytes 1179652
  197.3 14.8 %copy-start.40 = (bf16[512,384]{1,0:T(8,128)(2,1)}, bf16[512,384]{1,0:T(8,128)(2,1)S(1)}, u32[]{:S(2)}) copy-start(bf16[512,384]{1,0:T(8,128)(2,1)S(1)} %get-tuple-element.144.refs_2_) | copy-start | bytes 1179652
  197.4 7.4 %copy-start.30 = (bf16[6,512,512]{2,1,0:T(8,128)(2,1)S(1)}, bf16[6,512,512]{2,1,0:T(8,128)(2,1)}, u32[]{:S(2)}) copy-start(bf16[6,512,512]{2,1,0:T(8,128)(2,1)} %copy-done.29) | copy-start | bytes 9437188
  199.2 11.2 %collective-permute-start.20 = (bf16[2,48,1536]{2,1,0:T(8,128)(2,1)S(1)}, bf16[2,48,1536]{2,1,0:T(8,128)(2,1)S(1)}, u32[]{:S(2)}, u32[]{:S(2)}) collective-permute-start(bf16[2,48,1536]{2,1,0:T(8,128)(2,1)S(1)} %add_convert_fusion.7), channel_id=1, source_target_pairs={{0,8},{1,9},{2,18},{3,19},{4,12},{5,13},{6,22},{7,23},{8,0},{9,1},... | collective-permute-start | bytes 884744 | tf_op jit(solution)/shard_map/ppermute | solution.py:37
  204.2 50.4 %collective-permute-start.22 = (bf16[8,48,1920]{2,1,0:T(8,128)(2,1)}, bf16[8,48,1920]{2,1,0:T(8,128)(2,1)}, u32[]{:S(2)}, u32[]{:S(2)}) collective-permute-start(bf16[8,48,1920]{2,1,0:T(8,128)(2,1)} %add_convert_fusion), channel_id=1, source_target_pairs={{0,4},{1,5},{2,3},{3,2},{4,0},{5,1},{6,7},{7,6},{8,12},{9,13},{10,... | collective-permute-start | bytes 4423688 | tf_op jit(solution)/shard_map/ppermute | solution.py:37
  204.8 7.4 %copy-start.22 = (bf16[512,768]{1,0:T(8,128)(2,1)S(1)}, bf16[512,768]{1,0:T(8,128)(2,1)}, u32[]{:S(2)}) copy-start(bf16[512,768]{1,0:T(8,128)(2,1)} %copy-done.21) | copy-start | bytes 2359300
  210.3 6.3 %copy-start.42 = (bf16[512,384]{1,0:T(8,128)(2,1)}, bf16[512,384]{1,0:T(8,128)(2,1)S(1)}, u32[]{:S(2)}) copy-start(bf16[512,384]{1,0:T(8,128)(2,1)S(1)} %get-tuple-element.152.refs_3_) | copy-start | bytes 1179652
  210.3 6.3 %copy-start.44 = (bf16[512,384]{1,0:T(8,128)(2,1)}, bf16[512,384]{1,0:T(8,128)(2,1)S(1)}, u32[]{:S(2)}) copy-start(bf16[512,384]{1,0:T(8,128)(2,1)S(1)} %get-tuple-element.153.refs_4_) | copy-start | bytes 1179652
  210.4 6.3 %copy-start.46 = (bf16[512,384]{1,0:T(8,128)(2,1)}, bf16[512,384]{1,0:T(8,128)(2,1)S(1)}, u32[]{:S(2)}) copy-start(bf16[512,384]{1,0:T(8,128)(2,1)S(1)} %get-tuple-element.154.refs_5_) | copy-start | bytes 1179652
  210.4 6.2 %copy-start.63 = (bf16[2,48,1536]{2,1,0:T(8,128)(2,1)}, bf16[2,48,1536]{2,1,0:T(8,128)(2,1)S(1)}, u32[]{:S(2)}) copy-start(bf16[2,48,1536]{2,1,0:T(8,128)(2,1)S(1)} %collective-permute-done.20) | copy-start | bytes 884740
  219.8 10.0 %all-to-all-start.4 = ((f32[32,1,288]{2,1,0:T(1,128)}), f32[32,1,288]{2,1,0:T(1,128)S(1)}, u32[]{:S(2)}, u32[]{:S(2)}) async-start(f32[32,1,288]{2,1,0:T(1,128)} %reshape.77), calls=%async_computation.4 | async-start | bytes 98304 | tf_op jit(solution)/shard_map/all_to_all | solution.py:799
  222.4 18.4 %collective-permute-start.21 = (bf16[1,48,1536]{2,1,0:T(8,128)(2,1)S(1)}, bf16[1,48,1536]{2,1,0:T(8,128)(2,1)S(1)}, u32[]{:S(2)}, u32[]{:S(2)}) collective-permute-start(bf16[1,48,1536]{2,1,0:T(8,128)(2,1)S(1)} %add_convert_fusion.12), channel_id=1, source_target_pairs={{0,16},{1,17},{2,6},{3,7},{4,20},{5,21},{6,2},{7,3},{8,24},{9,25},... | collective-permute-start | bytes 442376 | tf_op jit(solution)/shard_map/ppermute | solution.py:37
  225.1 33.3 %collective-permute-start.23 = (bf16[16,48,1152]{2,1,0:T(8,128)(2,1)}, bf16[16,48,1152]{2,1,0:T(8,128)(2,1)}, u32[]{:S(2)}, u32[]{:S(2)}) collective-permute-start(bf16[16,48,1152]{2,1,0:T(8,128)(2,1)} %copy-done.8), channel_id=1, source_target_pairs={{0,2},{1,3},{2,0},{3,1},{4,6},{5,7},{6,4},{7,5},{8,10},{9,11},{10,... | collective-permute-start | bytes 5308424 | tf_op jit(solution)/shard_map/ppermute | solution.py:37
  230.6 10.0 %all-to-all-start.5 = ((f32[32,1,288]{2,1,0:T(1,128)}), f32[32,1,288]{2,1,0:T(1,128)S(1)}, u32[]{:S(2)}, u32[]{:S(2)}) async-start(f32[32,1,288]{2,1,0:T(1,128)} %broadcast_in_dim.23), calls=%async_computation.5 | async-start | bytes 98304 | tf_op jit(solution)/shard_map/all_to_all | solution.py:801
  242.2 21.9 %collective-permute-start.35 = (bf16[1,48,1536]{2,1,0:T(8,128)(2,1)S(1)}, bf16[1,48,1536]{2,1,0:T(8,128)(2,1)S(1)}, u32[]{:S(2)}, u32[]{:S(2)}) collective-permute-start(bf16[1,48,1536]{2,1,0:T(8,128)(2,1)S(1)} %add_convert_fusion.11), channel_id=1, source_target_pairs={{0,4},{1,5},{2,6},{3,7},{4,0},{5,1},{6,2},{7,3},{8,12},{9,13},{10,... | collective-permute-start | bytes 442376 | tf_op jit(solution)/shard_map/ppermute | solution.py:37
  257.7 21.6 %collective-permute-start.25 = (bf16[4,48,1920]{2,1,0:T(8,128)(2,1)}, bf16[4,48,1920]{2,1,0:T(8,128)(2,1)}, u32[]{:S(2)}, u32[]{:S(2)}) collective-permute-start(bf16[4,48,1920]{2,1,0:T(8,128)(2,1)} %add_convert_fusion.3), channel_id=1, source_target_pairs={{0,1},{1,0},{2,10},{3,11},{4,5},{5,4},{6,14},{7,15},{8,9},{9,8},{1... | collective-permute-start | bytes 2211848 | tf_op jit(solution)/shard_map/ppermute | solution.py:37
  260.7 20.0 %collective-permute-start.24 = (bf16[8,48,1152]{2,1,0:T(8,128)(2,1)}, bf16[8,48,1152]{2,1,0:T(8,128)(2,1)}, u32[]{:S(2)}, u32[]{:S(2)}) collective-permute-start(bf16[8,48,1152]{2,1,0:T(8,128)(2,1)} %add_convert_fusion.2), channel_id=1, source_target_pairs={{0,4},{1,5},{2,3},{3,2},{4,0},{5,1},{6,7},{7,6},{8,12},{9,13},{10,... | collective-permute-start | bytes 2654216 | tf_op jit(solution)/shard_map/ppermute | solution.py:37
  264.1 55.6 %collective-permute-start.36 = (bf16[2,48,1536]{2,1,0:T(8,128)(2,1)S(1)}, bf16[2,48,1536]{2,1,0:T(8,128)(2,1)S(1)}, u32[]{:S(2)}, u32[]{:S(2)}) collective-permute-start(bf16[2,48,1536]{2,1,0:T(8,128)(2,1)S(1)} %pad_maximum_fusion.2.refs_1_), channel_id=1, source_target_pairs={{0,2},{1,3},{2,0},{3,1},{4,6},{5,7},{6,4},{7,5},{8,10},{9,11},{10,... | collective-permute-start | bytes 884744 | tf_op jit(solution)/shard_map/ppermute | solution.py:37
  264.2 57.2 %all-to-all-start.3 = ((bf16[8,128,768]{2,1,0:T(8,128)(2,1)}), bf16[8,128,768]{2,1,0:T(8,128)(2,1)}, u32[]{:S(2)}, u32[]{:S(2)}) async-start(bf16[8,128,768]{2,1,0:T(8,128)(2,1)} %copy-done.6), calls=%async_computation.3 | async-start | bytes 3145728 | tf_op jit(solution)/shard_map/all_to_all | solution.py:677
  268.5 12.2 %copy-start.5 = (bf16[16,48,1152]{2,1,0:T(8,128)(2,1)S(1)}, bf16[16,48,1152]{2,1,0:T(8,128)(2,1)}, u32[]{:S(2)}) copy-start(bf16[16,48,1152]{2,1,0:T(8,128)(2,1)} %copy-done.3) | copy-start | bytes 5308420
  280.7 7.6 %collective-permute-start.31 = (bf16[2,48,1920]{2,1,0:T(8,128)(2,1)S(1)}, bf16[2,48,1920]{2,1,0:T(8,128)(2,1)S(1)}, u32[]{:S(2)}, u32[]{:S(2)}) collective-permute-start(bf16[2,48,1920]{2,1,0:T(8,128)(2,1)S(1)} %add_convert_fusion.6), channel_id=1, source_target_pairs={{0,8},{1,9},{2,18},{3,19},{4,12},{5,13},{6,22},{7,23},{8,0},{9,1},... | collective-permute-start | bytes 1105928 | tf_op jit(solution)/shard_map/ppermute | solution.py:37
  282.1 18.4 %collective-permute-start.26 = (bf16[4,48,1152]{2,1,0:T(8,128)(2,1)S(1)}, bf16[4,48,1152]{2,1,0:T(8,128)(2,1)S(1)}, u32[]{:S(2)}, u32[]{:S(2)}) collective-permute-start(bf16[4,48,1152]{2,1,0:T(8,128)(2,1)S(1)} %add_convert_fusion.5), channel_id=1, source_target_pairs={{0,1},{1,0},{2,10},{3,11},{4,5},{5,4},{6,14},{7,15},{8,9},{9,8},{1... | collective-permute-start | bytes 1327112 | tf_op jit(solution)/shard_map/ppermute | solution.py:37
  289.5 12.8 %collective-permute-start.32 = (bf16[1,48,1920]{2,1,0:T(8,128)(2,1)S(1)}, bf16[1,48,1920]{2,1,0:T(8,128)(2,1)S(1)}, u32[]{:S(2)}, u32[]{:S(2)}) collective-permute-start(bf16[1,48,1920]{2,1,0:T(8,128)(2,1)S(1)} %add_convert_fusion.10), channel_id=1, source_target_pairs={{0,16},{1,17},{2,6},{3,7},{4,20},{5,21},{6,2},{7,3},{8,24},{9,25},... | collective-permute-start | bytes 552968 | tf_op jit(solution)/shard_map/ppermute | solution.py:37
  301.6 8.4 %collective-permute-start.27 = (bf16[2,48,1152]{2,1,0:T(8,128)(2,1)S(1)}, bf16[2,48,1152]{2,1,0:T(8,128)(2,1)S(1)}, u32[]{:S(2)}, u32[]{:S(2)}) collective-permute-start(bf16[2,48,1152]{2,1,0:T(8,128)(2,1)S(1)} %add_convert_fusion.8), channel_id=1, source_target_pairs={{0,8},{1,9},{2,18},{3,19},{4,12},{5,13},{6,22},{7,23},{8,0},{9,1},... | collective-permute-start | bytes 663560 | tf_op jit(solution)/shard_map/ppermute | solution.py:37
  303.5 7.8 %collective-permute-start.33 = (bf16[1,48,1920]{2,1,0:T(8,128)(2,1)S(1)}, bf16[1,48,1920]{2,1,0:T(8,128)(2,1)S(1)}, u32[]{:S(2)}, u32[]{:S(2)}) collective-permute-start(bf16[1,48,1920]{2,1,0:T(8,128)(2,1)S(1)} %add_convert_fusion.9), channel_id=1, source_target_pairs={{0,4},{1,5},{2,6},{3,7},{4,0},{5,1},{6,2},{7,3},{8,12},{9,13},{10,... | collective-permute-start | bytes 552968 | tf_op jit(solution)/shard_map/ppermute | solution.py:37
  311.0 6.1 %collective-permute-start.28 = (bf16[1,48,1152]{2,1,0:T(8,128)(2,1)S(1)}, bf16[1,48,1152]{2,1,0:T(8,128)(2,1)S(1)}, u32[]{:S(2)}, u32[]{:S(2)}) collective-permute-start(bf16[1,48,1152]{2,1,0:T(8,128)(2,1)S(1)} %add_convert_fusion.14), channel_id=1, source_target_pairs={{0,16},{1,17},{2,6},{3,7},{4,20},{5,21},{6,2},{7,3},{8,24},{9,25},... | collective-permute-start | bytes 331784 | tf_op jit(solution)/shard_map/ppermute | solution.py:37
  311.4 11.7 %collective-permute-start.34 = (bf16[2,48,1920]{2,1,0:T(8,128)(2,1)S(1)}, bf16[2,48,1920]{2,1,0:T(8,128)(2,1)S(1)}, u32[]{:S(2)}, u32[]{:S(2)}) collective-permute-start(bf16[2,48,1920]{2,1,0:T(8,128)(2,1)S(1)} %pad_maximum_fusion.1.refs_1_), channel_id=1, source_target_pairs={{0,2},{1,3},{2,0},{3,1},{4,6},{5,7},{6,4},{7,5},{8,10},{9,11},{10,... | collective-permute-start | bytes 1105928 | tf_op jit(solution)/shard_map/ppermute | solution.py:37
  318.2 4.8 %collective-permute-start.29 = (bf16[1,48,1152]{2,1,0:T(8,128)(2,1)S(1)}, bf16[1,48,1152]{2,1,0:T(8,128)(2,1)S(1)}, u32[]{:S(2)}, u32[]{:S(2)}) collective-permute-start(bf16[1,48,1152]{2,1,0:T(8,128)(2,1)S(1)} %add_convert_fusion.13), channel_id=1, source_target_pairs={{0,4},{1,5},{2,6},{3,7},{4,0},{5,1},{6,2},{7,3},{8,12},{9,13},{10,... | collective-permute-start | bytes 331784 | tf_op jit(solution)/shard_map/ppermute | solution.py:37
  323.0 1.9 collective-permute-start.30
  (53 other events, 150.9 us)

commit v3 on v2

v3 whole, which is shorter than its diff:
```python
import jax
import jax.numpy as jnp
from jax import lax
from jax.experimental import pallas as pl
from jax.experimental.pallas import tpu as pltpu
from jax.sharding import PartitionSpec as P

HEAD_DIM = 64
AXES = ("fsdp", "ctx", "tp")
F32 = jnp.float32
BF16 = jnp.bfloat16
NEG = -1e30
NT = (((1,), (1,)), ((), ()))
VMEM = pl.BlockSpec(memory_space=pltpu.VMEM)
SMEM = pl.BlockSpec(memory_space=pltpu.SMEM)
ANY = pl.BlockSpec(memory_space=pl.ANY)


def partner(dim, z, c, t):
    if dim == "core":
        return z, c ^ 1, t
    if dim == "x":
        return z, c ^ 2, t
    if dim == "y":
        return z, c, t ^ 1
    return z ^ int(dim[1:]), c, t


def exchange(value, dims, sizes):
    nz, nc, nt = sizes
    pairs = []
    for z in range(nz):
        for c in range(nc):
            for t in range(nt):
                tz, tc, tt = partner(dims[c & 1], z, c, t)
                pairs.append(((z * nc + c) * nt + t, (tz * nc + tc) * nt + tt))
    return lax.ppermute(value, AXES, pairs)


GATHER = (
    (("z2", "z1", "y", "x"), ("z2", "z1", "x", "y")),
    (("z2", "z1", "y", "x"), ("z2", "z1", "x", "y")),
    (("z2", "z1", "x", "y"), ("y", "x", "z2", "z1")),
)
SCATTER = (
    (("x", "y", "z1", "z2"), ("y", "z1", "z2", "x")),
    (("x", "y", "z1", "z2"), ("z1", "z2", "y", "x")),
    (("y", "x", "z1", "z2"), ("z1", "z2", "x", "y")),
)
CORE = ("core", "core")
X = ("x", "x")
Y = ("y", "y")


def piece_place(order, core, here, index):
    z, x, t = here
    for bit, dim in enumerate(order):
        flip = (index >> bit) & 1
        if dim == "x":
            x = x ^ flip
        elif dim == "y":
            t = t ^ flip
        else:
            z = z ^ (flip * int(dim[1:]))
    return z * 4 + x * 2 + core, t


def places(orders):
    if orders is None:
        return [(i, half) for half in range(2) for i in range(16)]
    c = lax.axis_index("ctx")
    here = (lax.axis_index("fsdp"), c >> 1, lax.axis_index("tp"))
    spots = []
    for core in (c & 1, 1 - (c & 1)):
        for i in range(16):
            r0, t0 = piece_place(orders[0], core, here, i)
            r1, t1 = piece_place(orders[1], core, here, i)
            spots.append((jnp.where(core == 0, r0, r1), jnp.where(core == 0, t0, t1)))
    return spots


def packing(orders):
    return tuple(order[::-1] for order in orders)


def after(value, *first):
    return lax.optimization_barrier((value, first))[0]


def phase(*values):
    return lax.optimization_barrier(values)


def piece_copies(spots, own_ref, sib_ref, sem, whole, low, cols, collect, base=0):
    rows = whole.shape[0] // 16
    stride = whole.shape[1] // 2
    copies = []
    for half, ref in ((0, own_ref), (1, sib_ref)):
        for i in range(16):
            row, col = spots[half * 16 + i]
            row, col = row * rows, col * stride
            if not isinstance(row, int):
                row, col = pl.multiple_of(row, rows), pl.multiple_of(col, 128)
            one = ref.at[pl.ds(i * rows, rows), pl.ds(low, cols)]
            two = whole.at[pl.ds(row, rows), pl.ds(col, cols)]
            src, dst = (one, two) if collect else (two, one)
            copy = pltpu.make_async_copy(src, dst, sem.at[base + half * 16 + i])
            copy.start()
            copies.append(copy)
    return copies


def finish(copies):
    for copy in copies:
        copy.wait()


def tiles(count, step):
    def run(one):
        lax.fori_loop(0, count // step, lambda i, carry: (one(pl.multiple_of(i * step, step)), carry)[1], 0)

    return run


def row_mean(value):
    return jnp.mean(value, axis=-1, keepdims=True)


def struct(shape, dtype):
    return jax.ShapeDtypeStruct(shape, dtype)


def call(kernel, name, outs, specs, out_specs, scratch, time, room, args):
    return pl.pallas_call(
        kernel,
        name=name,
        out_shape=outs,
        in_specs=specs,
        out_specs=out_specs,
        scratch_shapes=scratch,
        compiler_params=pltpu.CompilerParams(vmem_limit_bytes=room << 20),
        cost_estimate=pl.CostEstimate(flops=time * 10**9, transcendentals=0, bytes_accessed=10**6),
    )(*args)


B_OUT, GAIN1, SHIFT1, B_DOWN, GAIN2, SHIFT2 = range(6)


def unpack_kernel(own_ref, sib_ref, *refs, orders):
    outs, sem = refs[:-1], refs[-1]
    copies = []
    spots = places(orders)
    low = 0
    for i, out in enumerate(outs):
        cols = out.shape[1] // 2
        copies += piece_copies(spots, own_ref, sib_ref, sem, out, low, cols, True, 32 * i)
        low += cols
    finish(copies)


def unpack(orders, own, sib, widths):
    rows = own.shape[0]
    return call(
        lambda *refs: unpack_kernel(*refs, orders=orders),
        "unpack",
        tuple(struct((rows, width), BF16) for width in widths),
        [ANY, ANY],
        (VMEM,) * len(widths),
        [pltpu.SemaphoreType.DMA((32 * len(widths),))],
        5,
        1,
        (own, sib),
    )


def sources(refs, fast):
    c = lax.axis_index("ctx") if fast else 0
    own, core, x = refs
    return [(c ^ 0, own, 0), (c ^ 1, core, 0), (c ^ 2, x, 0), (c ^ 3, x, 1)]


def project_kernel(weight_ref, own_ref, core_ref, far_ref, small_ref, proj_ref, x_ref, mask_ref, ids, *, fast):
    block = own_ref.shape[1] - 8
    count = 4
    for spot, ref, i in sources((own_ref, core_ref, far_ref), fast):
        x_ref[pl.ds(pl.multiple_of(spot * block, block), block), :] = ref[i, 0:block, :]
        ids[pl.ds(spot, 1), :] = ref[i, block:, 0:block].astype(F32)[0:1]
    for kb in range(count):
        column = jnp.broadcast_to(ids[kb : kb + 1], (block, block)).T
        for qb in range(count):
            mask_ref[kb * block : (kb + 1) * block, qb * block : (qb + 1) * block] = jnp.where(
                column == jnp.broadcast_to(ids[qb : qb + 1], (block, block)), 0.0, NEG
            )
    width = proj_ref.shape[1] // 6
    for y in range(2):
        row = pl.ds(lax.axis_index("tp") ^ y, 1)
        for which in range(3):
            at = (y * 3 + which) * width
            value = jnp.dot(x_ref[...], weight_ref[:, at : at + width], preferred_element_type=F32)
            if which != 1:
                low = 0 if which == 0 else width
                value = value + small_ref[row, low : low + width]
            proj_ref[:, at : at + width] = value.astype(BF16)


def project(weight, given, small, fast):
    width, wide = weight.shape
    block = given[0].shape[1] - 8
    length = 4 * block
    return call(
        lambda *refs: project_kernel(*refs, fast=fast),
        "project",
        (
            struct((length, wide), BF16),
            struct((length, width), BF16),
            struct((length, length), F32),
        ),
        [VMEM] * 5,
        (VMEM,) * 3,
        [pltpu.VMEM((8, block), F32)],
        5,
        6,
        (weight,) + tuple(given) + (small,),
    )


def attend_kernel(proj_ref, mask_ref, o_ref, p_ref, *, y):
    length = proj_ref.shape[0]
    pairs = o_ref.shape[1] // 128
    lane = lax.broadcasted_iota(jnp.int32, (1, 128), 1)

    def pair(g, carry):
        take = lambda which: proj_ref[:, pl.ds(pl.multiple_of(((y * 3 + which) * pairs + g) * 128, 128), 128)]
        query = take(0) * jnp.asarray(0.125, BF16)
        keys = take(1)
        values_t = take(2).T
        outs = []
        for head in range(2):
            here = (lane >= 64 * head) & (lane < 64 * head + 64)
            only = jnp.where(here, keys, jnp.zeros_like(keys))
            row = []
            for at in range(0, length, 256):
                scores = lax.dot_general(only, query[at : at + 256], NT, preferred_element_type=F32)
                scores = scores + mask_ref[:, at : at + 256]
                top = jnp.max(scores, axis=0, keepdims=True)
                raised = jnp.exp(scores - top)
                total = jnp.sum(raised, axis=0, keepdims=True)
                probs = (raised * (1.0 / total)).astype(BF16)
                p_ref[2 * g + head, :, at : at + 256] = probs
                row.append(
                    jnp.dot(values_t[64 * head : 64 * head + 64], probs, preferred_element_type=F32)
                )
            outs.append(jnp.concatenate(row, axis=1))
        both = jnp.concatenate(outs, axis=0).astype(BF16)
        o_ref[:, pl.ds(pl.multiple_of(g * 128, 128), 128)] = both.T
        return carry

    lax.fori_loop(0, pairs, pair, 0)


def attend(proj, mask, y):
    length, wide = proj.shape
    half = wide // 6
    return call(
        lambda *refs: attend_kernel(*refs, y=y),
        "attend",
        (struct((length, half), BF16), struct((half // HEAD_DIM, length, length), BF16)),
        [VMEM, VMEM],
        (VMEM, VMEM),
        [],
        12,
        6,
        (proj, mask),
    )


def middle_kernel(
    w_out, w_up, mixed0_ref, mixed1_ref, x_ref, table_ref, small_ref,
    normed_ref, scale_ref, first_ref, act_ref, slope_ref,
):
    length, units = act_ref.shape
    narrow, half = w_out.shape[1] // 2, units // 2
    normed_ref[...] = lax.dot_general(
        mixed0_ref[...], w_out[:, :narrow], NT, preferred_element_type=F32
    ) + lax.dot_general(mixed1_ref[...], w_out[:, narrow:], NT, preferred_element_type=F32)

    @tiles(length, 64)
    def _(at):
        here = pl.ds(at, 64)
        value = x_ref[here, :].astype(F32) + normed_ref[here, :] + table_ref[B_OUT : B_OUT + 1, :]
        centred = value - row_mean(value)
        scale = lax.rsqrt(row_mean(centred * centred) + 1e-12)
        unit = centred * scale
        normed_ref[here, :] = unit
        scale_ref[here, :] = scale
        first_ref[here, :] = (
            unit * table_ref[GAIN1 : GAIN1 + 1, :] + table_ref[SHIFT1 : SHIFT1 + 1, :]
        ).astype(BF16)

    for y in range(2):
        row = pl.ds(lax.axis_index("tp") ^ y, 1)

        @tiles(half, 256)
        def _(at):
            here = pl.ds(pl.multiple_of(y * half + at, 256), 256)
            bias = small_ref[row, pl.ds(pl.multiple_of(2 * narrow + at, 256), 256)]
            hidden = jnp.dot(first_ref[...], w_up[:, here], preferred_element_type=F32) + bias
            phi = 0.5 + 0.5 * lax.erf(hidden * 0.7071067811865476)
            act_ref[:, here] = (hidden * phi).astype(BF16)
            bell = jnp.exp(-0.5 * hidden * hidden) * 0.3989422804014327
            slope_ref[:, here] = (phi + hidden * bell).astype(BF16)


def middle(w_out, w_up, mixed0, mixed1, x, table, small):
    length, width = x.shape
    units = w_up.shape[1]
    return call(
        middle_kernel,
        "middle",
        (
            struct((length, width), F32),
            struct((length, 1), F32),
            struct((length, width), BF16),
            struct((length, units), BF16),
            struct((length, units), BF16),
        ),
        [VMEM] * 7,
        (VMEM,) * 5,
        [],
        12,
        6,
        (w_out, w_up, mixed0, mixed1, x, table, small),
    )


def turn_kernel(
    weight_ref, act_ref, normed_ref, own_ref, core_ref, far_ref, table_ref,
    chunks_ref, gz_ref, gzb_ref, sums_ref, down_own, down_sib, full, cot_ref, sem, *, orders,
):
    length = act_ref.shape[0]
    block = chunks_ref.shape[1]
    for spot, ref, i in sources((own_ref, core_ref, far_ref), orders is not None):
        cot_ref[pl.ds(pl.multiple_of(spot * block, block), block), :] = ref[i]
    gz_ref[...] = lax.dot_general(act_ref[...], weight_ref[...], NT, preferred_element_type=F32)
    sums_ref[...] = jnp.zeros_like(sums_ref)
    row = lambda which: table_ref[which : which + 1, :]

    @tiles(length, 64)
    def _(at):
        here = pl.ds(at, 64)
        value = normed_ref[here, :] * row(GAIN1) + row(SHIFT1) + gz_ref[here, :] + row(B_DOWN)
        centred = value - row_mean(value)
        scale = lax.rsqrt(row_mean(centred * centred) + 1e-12)
        unit = centred * scale
        result = (unit * row(GAIN2) + row(SHIFT2)).astype(BF16)
        chunk = lax.div(at, block)
        if orders is not None:
            c = lax.axis_index("ctx") ^ chunk
            chunk = (c & 1) * 2 + (c >> 1)
        chunks_ref[chunk, pl.ds(pl.multiple_of(lax.rem(at, block), 64), 64), :] = result
        coming = cot_ref[here, :].astype(F32)
        raised = coming * row(GAIN2)
        back = scale * (raised - row_mean(raised) - unit * row_mean(raised * unit))
        gz_ref[here, :] = back
        gzb_ref[here, :] = back.astype(BF16)
        sums_ref[0:1, :] += jnp.sum(coming * unit, axis=0, keepdims=True)
        sums_ref[1:2, :] += jnp.sum(coming, axis=0, keepdims=True)
        sums_ref[2:3, :] += jnp.sum(back, axis=0, keepdims=True)

    back_t = gzb_ref[...].T

    @tiles(full.shape[1], 1024)
    def _(at):
        here = pl.ds(at, 1024)
        full[:, here] = jnp.dot(back_t, act_ref[:, here], preferred_element_type=F32).astype(BF16)

    finish(piece_copies(places(orders), down_own, down_sib, sem, full, 0, down_own.shape[1], False))


def turn(orders, weight, act, normed, cot, table, chunk):
    length, units = act.shape
    width = normed.shape[1]
    piece = struct((width, units // 2), BF16)
    return call(
        lambda *refs: turn_kernel(*refs, orders=orders),
        "turn",
        (
            struct((length // chunk, chunk, width), BF16),
            struct((length, width), F32),
            struct((length, width), BF16),
            struct((8, width), F32),
            piece,
            piece,
        ),
        [VMEM] * 7,
        (VMEM, VMEM, VMEM, VMEM, ANY, ANY),
        [pltpu.VMEM((width, units), BF16), pltpu.VMEM((length, width), BF16), pltpu.SemaphoreType.DMA((32,))],
        14,
        10,
        (weight, act, normed) + tuple(cot) + (table,),
    )


def hidden_back_kernel(weight_ref, gzb_ref, slope_ref, gh_ref, sum_ref):
    @tiles(gh_ref.shape[1], 512)
    def _(at):
        here = pl.ds(at, 512)
        back = jnp.dot(gzb_ref[...], weight_ref[:, here], preferred_element_type=F32)
        back = (back * slope_ref[:, here].astype(F32)).astype(BF16)
        gh_ref[:, here] = back
        sum_ref[:, here] = jnp.sum(back.astype(F32), axis=0, keepdims=True)


def hidden_back(weight, gzb, slope):
    length, units = slope.shape
    return call(
        hidden_back_kernel,
        "hidden_back",
        (struct((length, units), BF16), struct((1, units), F32)),
        [VMEM] * 3,
        (VMEM, VMEM),
        [],
        12,
        6,
        (weight, gzb, slope),
    )


def first_back_kernel(
    w_out, w_up, gh_ref, gz_ref, normed_ref, scale_ref, table_ref, first_ref, mixed0_ref, mixed1_ref,
    gz1_ref, gm_ref, sums_ref, pieces_own, pieces_sib, branch, d_out, d_up, sem, *, orders,
):
    narrow = w_out.shape[1] // 2
    half = w_up.shape[1] // 2
    length = gh_ref.shape[0]
    first_t = first_ref[...].T
    spots = places(orders)

    @tiles(d_up.shape[1], 1024)
    def _(at):
        here = pl.ds(at, 1024)
        d_up[:, here] = jnp.dot(first_t, gh_ref[:, here], preferred_element_type=F32).astype(BF16)

    sent = piece_copies(spots, pieces_own, pieces_sib, sem, d_up, narrow, half, False)
    gz1_ref[...] = lax.dot_general(gh_ref[...], w_up[...], NT, preferred_element_type=F32)
    sums_ref[...] = jnp.zeros_like(sums_ref)

    @tiles(length, 64)
    def _(at):
        here = pl.ds(at, 64)
        coming = gz_ref[here, :] + gz1_ref[here, :]
        unit = normed_ref[here, :]
        raised = coming * table_ref[GAIN1 : GAIN1 + 1, :]
        back = scale_ref[here, :] * (raised - row_mean(raised) - unit * row_mean(raised * unit))
        gz1_ref[here, :] = back
        branch[here, :] = back.astype(BF16)
        sums_ref[0:1, :] += jnp.sum(coming * unit, axis=0, keepdims=True)
        sums_ref[1:2, :] += jnp.sum(coming, axis=0, keepdims=True)
        sums_ref[2:3, :] += jnp.sum(back, axis=0, keepdims=True)

    branch_t = branch[...].T
    d_out[:, :narrow] = jnp.dot(branch_t, mixed0_ref[...], preferred_element_type=F32).astype(BF16)
    d_out[:, narrow:] = jnp.dot(branch_t, mixed1_ref[...], preferred_element_type=F32).astype(BF16)
    sent += piece_copies(spots, pieces_own, pieces_sib, sem, d_out, 0, narrow, False, 32)
    gm_ref[...] = jnp.dot(branch[...], w_out[...], preferred_element_type=F32).astype(BF16)
    finish(sent)


def first_back(orders, w_out, w_up, gh, gz, normed, scale, table, first_b, mixed0, mixed1):
    length, units = gh.shape
    width = gz.shape[1]
    piece = struct((width, (units + width) // 2), BF16)
    return call(
        lambda *refs: first_back_kernel(*refs, orders=orders),
        "first_back",
        (
            struct((length, width), F32),
            struct((length, width), BF16),
            struct((8, width), F32),
            piece,
            piece,
        ),
        [VMEM] * 10,
        (VMEM, VMEM, VMEM, ANY, ANY),
        [
            pltpu.VMEM((length, width), BF16),
            pltpu.VMEM((width, width), BF16),
            pltpu.VMEM((width, units), BF16),
            pltpu.SemaphoreType.DMA((64,)),
        ],
        20,
        14,
        (w_out, w_up, gh, gz, normed, scale, table, first_b, mixed0, mixed1),
    )


def attend_back_kernel(proj_ref, p_ref, gm_ref, dq_ref, dk_ref, dv_ref, dst, dqt, *, y):
    length = proj_ref.shape[0]
    pairs = dq_ref.shape[1] // 128
    lane = lax.broadcasted_iota(jnp.int32, (1, 128), 1)
    low = lane < 64

    def pair(g, carry):
        take = lambda which: proj_ref[:, pl.ds(pl.multiple_of(((y * 3 + which) * pairs + g) * 128, 128), 128)]
        query, keys, values = take(0), take(1), take(2)
        grad = gm_ref[:, pl.ds(pl.multiple_of((y * pairs + g) * 128, 128), 128)]
        keys_t = keys.T
        dks, dvs = [], []
        for head in range(2):
            here = low if head == 0 else jnp.logical_not(low)
            only = jnp.where(here, values, jnp.zeros_like(values))
            for at in range(0, length, 256):
                cols = slice(at, at + 256)
                gp = lax.dot_general(only, grad[cols], NT, preferred_element_type=F32)
                probs = p_ref[2 * g + head, :, cols].astype(F32)
                weighted = jnp.sum(probs * gp, axis=0, keepdims=True)
                dst[:, cols] = (probs * (gp - weighted)).astype(BF16)
            dqt[64 * head : 64 * head + 64, :] = (
                jnp.dot(keys_t[64 * head : 64 * head + 64], dst[...], preferred_element_type=F32) * 0.125
            ).astype(BF16)
            dks.append(jnp.dot(dst[...], query, preferred_element_type=F32))
            dvs.append(jnp.dot(p_ref[2 * g + head], grad, preferred_element_type=F32))
        cols = pl.ds(pl.multiple_of(g * 128, 128), 128)
        dq_ref[:, cols] = dqt[...].T
        dk_ref[:, cols] = (jnp.where(low, dks[0], dks[1]) * 0.125).astype(BF16)
        dv_ref[:, cols] = jnp.where(low, dvs[0], dvs[1]).astype(BF16)
        return carry

    lax.fori_loop(0, pairs, pair, 0)


def attend_back(proj, probs, grad_mixed, y):
    length, wide = proj.shape
    shape = struct((length, wide // 6), BF16)
    return call(
        lambda *refs: attend_back_kernel(*refs, y=y),
        "attend_back",
        (shape, shape, shape),
        [VMEM] * 3,
        (VMEM,) * 3,
        [pltpu.VMEM((length, length), BF16), pltpu.VMEM((128, length), BF16)],
        2,
        6,
        (proj, probs, grad_mixed),
    )


def last_kernel(x_ref, sums1_ref, sums2_ref, sum_up_ref, *refs, orders):
    parts, (pieces_own, pieces_sib, whole, vec, sem) = refs[:6], refs[6:]
    half = parts[0].shape[1]
    rows = whole.shape[0]
    x_t = x_ref[...].T
    sums = [[], []]
    for y in range(2):
        for which in range(3):
            at = (y * 3 + which) * half
            value = parts[y * 3 + which][...]
            whole[:, at : at + half] = jnp.dot(x_t, value, preferred_element_type=F32).astype(BF16)
            if which != 1:
                sums[which // 2].append(jnp.sum(value.astype(F32), axis=0, keepdims=True))
    sent = piece_copies(places(orders), pieces_own, pieces_sib, sem, whole, 0, 3 * half, False)
    vectors = sums[0] + sums[1] + [ref[i : i + 1, :] for ref in (sums1_ref, sums2_ref) for i in range(3)]
    at = 0
    across = vec.shape[1] // 128
    wide = []
    for vector in vectors + [sum_up_ref[...]]:
        for low in range(0, vector.shape[1], 128):
            wide.append(vector[:, low : low + 128])
    for row in range(8):
        vec[row : row + 1, :] = jnp.concatenate(wide[row * across : (row + 1) * across], axis=1)
    pieces_own[rows:, :] = vec[...].astype(BF16)
    pieces_sib[rows:, :] = vec[...].astype(BF16)
    finish(sent)


def last(orders, x, sums1, sums2, sum_up, parts):
    length, width = x.shape
    piece = struct((width + 8, 3 * width // 2), BF16)
    return call(
        lambda *refs: last_kernel(*refs, orders=orders),
        "last",
        (piece, piece),
        [VMEM] * 10,
        (VMEM, VMEM),
        [
            pltpu.VMEM((width, 3 * width), BF16),
            pltpu.VMEM((8, 3 * width // 2), F32),
            pltpu.SemaphoreType.DMA((32,)),
        ],
        1,
        8,
        (x, sums1, sums2, sum_up) + tuple(parts),
    )


def vectors_kernel(one_ref, two_ref, qv_ref, up_ref, *refs):
    t = lax.axis_index("tp")
    rows, cols = one_ref.shape
    across = cols // 128
    value = one_ref[rows - 8 :, :].astype(F32)
    if two_ref is not None:
        value = value + two_ref[rows - 8 :, :].astype(F32)

    def block(at):
        row, low = at // across, at % across * 128
        return value[row : row + 1, low : low + 128]

    def take(out, row, first, other, count):
        for i in range(count):
            one = block(first + i)
            if other != first:
                one = jnp.where(t == 0, one, block(other + i))
            if row is None:
                out[i * 128 : (i + 1) * 128] = one[0]
            else:
                out[row : row + 1, i * 128 : (i + 1) * 128] = one

    narrow, wide = qv_ref.shape[1] // 128, up_ref.shape[0] // 128
    for which in range(2):
        take(qv_ref, which, 2 * which * narrow, (2 * which + 1) * narrow, narrow)
    for i, ref in enumerate(refs):
        take(ref, None, (4 + 2 * i) * narrow, (4 + 2 * i) * narrow, 2 * narrow)
    base = (4 + 2 * len(refs)) * narrow
    take(up_ref, None, base, base + wide, wide)


def vectors(one, two, local_width, local_units):
    shapes = [(2, local_width), (local_units,)] + [(2 * local_width,)] * 6
    given = (one,) if two is None else (one, two)

    def kernel(*refs):
        if two is None:
            refs = (refs[0], None) + refs[1:]
        vectors_kernel(*refs)

    return call(
        kernel,
        "vectors",
        tuple(struct(shape, F32) for shape in shapes),
        [VMEM] * len(given),
        (VMEM,) * 8,
        [],
        1,
        4,
        given,
    )


def add_kernel(*refs, low, high, vec, count):
    terms, out = refs[:-1], refs[-1]
    total = terms[0][low:high, :].astype(F32)
    for term in terms[1:count]:
        total = total + term[low:high, :].astype(F32)
    out[: high - low, :] = total.astype(BF16)
    if vec:
        total = 0.0
        for i in vec:
            total = total + terms[i][terms[i].shape[0] - 8 :, :].astype(F32)
        out[high - low :, :] = total.astype(BF16)


def add_up(terms, low, high, vec=(), lone=()):
    count, terms = len(terms), list(terms) + list(lone)
    cols = terms[0].shape[1]
    return call(
        lambda *refs: add_kernel(*refs, low=low, high=high, vec=vec, count=count),
        "add",
        struct((high - low + (8 if vec else 0), cols), BF16),
        [VMEM] * len(terms),
        VMEM,
        [],
        1,
        4,
        tuple(terms),
    )


def deliver_kernel(own_ref, core_ref, x_ref, y_ref, out_ref):
    c, t = lax.axis_index("ctx"), lax.axis_index("tp")
    sources = [(own_ref, 0), (core_ref, 0), (x_ref, 0), (x_ref, 1)] + [(y_ref, i) for i in range(4)]
    for i, (ref, at) in enumerate(sources):
        ctx = c ^ ((i & 1) + (i & 2))
        out_ref[ctx * 2 + (t ^ (i >> 2))] = ref[at]


def deliver(own, core, x, y):
    return call(
        deliver_kernel,
        "deliver",
        struct((2 * own.shape[0],) + own.shape[1:], BF16),
        [VMEM] * 4,
        VMEM,
        [],
        3,
        6,
        (own, core, x, y),
    )


def input_back_kernel(weight_ref, gz1_ref, *refs, fast):
    parts, chunks_ref = refs[:6], refs[6]
    half = parts[0].shape[1]
    total = gz1_ref[...]
    for i, part in enumerate(parts):
        total = total + lax.dot_general(
            part[...], weight_ref[:, i * half : (i + 1) * half], NT, preferred_element_type=F32
        )
    total = total.astype(BF16)
    count, block = chunks_ref.shape[:2]
    for i in range(count):
        spot = i
        if fast:
            c = lax.axis_index("ctx") ^ i
            spot = (c & 1) * 2 + (c >> 1)
        chunks_ref[spot] = total[i * block : (i + 1) * block]


def input_back(weight, gz1, parts, chunk, fast):
    length, width = gz1.shape
    return call(
        lambda *refs: input_back_kernel(*refs, fast=fast),
        "input_back",
        struct((length // chunk, chunk, width), BF16),
        [VMEM] * 8,
        VMEM,
        [],
        1,
        6,
        (weight, gz1) + tuple(parts),
    )


def settle_kernel(pair_ref, got_ref, *refs, cuts):
    outs, four = refs[: len(cuts)], refs[len(cuts)]
    rows = pair_ref.shape[0] // 2
    for i in range(4):
        ref = (pair_ref, got_ref)[i // 2]
        owner = lax.axis_index("ctx") ^ ((i & 1) * 2 + (i >> 1))
        low = i % 2 * rows
        four[pl.ds(pl.multiple_of(owner * rows, 16), rows), :] = ref[low : low + rows, :].astype(F32)
    for out, (low, high, form) in zip(outs, cuts):
        if form == "plain":
            out[...] = four[:, low:high]
        else:
            step = (high - low) // 3
            for j in range(3):
                out[j] = four[:, low + j * step : low + (j + 1) * step]


def settle(pair, got, cuts):
    rows, cols = pair.shape[0] // 2, pair.shape[1]
    shapes = {"plain": lambda n: (4 * rows, n), "three": lambda n: (3, 4 * rows, n // 3)}
    return call(
        lambda *refs: settle_kernel(*refs, cuts=cuts),
        "settle",
        tuple(struct(shapes[form](high - low), F32) for low, high, form in cuts),
        [VMEM, VMEM],
        (VMEM,) * len(cuts),
        [pltpu.VMEM((4 * rows, cols), F32)],
        3,
        6,
        (pair, got),
    )


def cut(full):
    rows, cols = full.shape
    return full[:, : cols // 2], full[:, cols // 2 :]


def gather_plain(shard):
    rows = lax.all_gather(shard, "fsdp", axis=0, tiled=True)
    return lax.all_gather(rows, "tp", axis=1, tiled=True)


def reduce_plain(own, sib):
    full = jnp.concatenate([own, sib], axis=1)
    part = lax.psum_scatter(full, "tp", scatter_dimension=1, tiled=True)
    part = lax.psum_scatter(part, "fsdp", scatter_dimension=0, tiled=True)
    return lax.psum(part, "ctx").astype(F32)


def body(
    layer_input,
    doc_ids,
    w_qkv,
    b_qv,
    w_out,
    b_out,
    ln1_gain,
    ln1_bias,
    w_up,
    b_up,
    w_down,
    b_down,
    ln2_gain,
    ln2_bias,
    out_grad,
):
    sizes = (lax.axis_size("fsdp"), lax.axis_size("ctx"), lax.axis_size("tp"))
    micro, seqs, local_len, width = layer_input.shape
    length = local_len * sizes[1]
    shard_rows, local_width = w_qkv.shape[1:]
    local_units = w_up.shape[1]
    heads = width // HEAD_DIM
    fast = sizes == (4, 4, 2)
    t = lax.axis_index("tp")
    c = lax.axis_index("ctx")

    def mine(value):
        return lax.dynamic_index_in_dim(value, t, 1, keepdims=False)

    def to_owners(chunks):
        return lax.all_to_all(chunks, "ctx", 0, 0, tiled=True)

    def spread(chunks):
        out = lax.all_to_all(chunks, ("ctx", "tp"), 0, 0, tiled=True)
        return out.reshape(micro, seqs, local_len, width)

    shards = (
        jnp.swapaxes(w_qkv, 0, 1).reshape(shard_rows, 3 * local_width),
        jnp.concatenate([w_out.T, w_up], axis=1),
        w_down.T,
    )
    ids = mine(doc_ids).astype(BF16)[:, None, :]
    ids = jnp.pad(ids, ((0, 0), (0, 7), (0, width - local_len)))
    rows_in = jnp.concatenate([mine(layer_input), ids], axis=1)
    cot_in = mine(out_grad)
    small = jnp.concatenate([b_qv.reshape(-1), b_up])[None]
    table = jnp.stack([b_out, ln1_gain, ln1_bias, b_down, ln2_gain, ln2_bias, b_out, b_out])
    gathers = GATHER if fast else (None,) * 3
    packs = tuple(packing(order) for order in SCATTER) if fast else (None,) * 3

    def swap(value, group, step):
        order = tuple(zip(*GATHER[group])) + (CORE,)
        return exchange(value, order[step], sizes)

    def shed(value, group, step):
        order = (CORE,) + tuple(zip(*SCATTER[group]))
        return exchange(value, order[step], sizes)

    def joined(*parts):
        return jnp.concatenate(parts, axis=0)

    if fast:
        def seen(value):
            return [lax.dynamic_index_in_dim(value, c ^ i, 0, keepdims=True) for i in range(4)]

        part = shard_rows // 4
        h1, h2, h3 = [lax.dynamic_slice_in_dim(s, c * part, part, 0) for s in shards]
        x0, x1, x2, x3 = seen(rows_in)
        g1, xk = phase(swap(h1, 0, 0), exchange(joined(x1, x3), CORE, sizes))
        h1 = joined(h1, g1)
        g1, xx, table = phase(swap(h1, 0, 1), exchange(joined(x2, xk[1:]), X, sizes), table)
        given = (x0, xk, xx)
        h1 = joined(h1, g1)
        h1, h2, small, cot_in = phase(h1, h2, small, cot_in)
        c0, c1, c2, c3 = seen(cot_in)
        g1, g2, got, ck = phase(
            swap(h1, 0, 2), swap(h2, 1, 0), exchange(small, Y, sizes), exchange(joined(c1, c3), CORE, sizes)
        )
        small = joined(small, got)
        h1, h2 = phase(joined(h1, g1), joined(h2, g2))
        g1, g2 = phase(swap(h1, 0, 3), swap(h2, 1, 1))
        h1, h2, h3 = phase(joined(h1, g1), joined(h2, g2), h3)
        g1, g2, g3 = swap(h1, 0, 4), swap(h2, 1, 2), swap(h3, 2, 0)
        (wq,) = unpack(gathers[0], h1, g1, (3 * width,))
        proj, rows_b, mask = project(wq, given, small, fast)
        proj, g2, g3, c2, ck = phase(proj, g2, g3, c2, ck)
        h2, h3 = joined(h2, g2), joined(h3, g3)
        g2, g3 = swap(h2, 1, 3), swap(h3, 2, 1)
        mixed0, probs0 = attend(after(proj, h2, h3), mask, 0)
        mixed0, g3 = phase(mixed0, g3)
        h3 = joined(h3, g3)
        g3 = swap(h3, 2, 2)
        mixed1, probs1 = attend(after(proj, h3, mixed0), mask, 1)
        mixed1, g2, g3 = phase(mixed1, g2, g3)
        h2, h3, c_send = phase(joined(h2, g2), joined(h3, g3), joined(c2, ck[1:]))
        g2, g3, cx = swap(h2, 1, 4), swap(h3, 2, 3), exchange(c_send, X, sizes)
        cot = (c0, ck, cx)
        wo, wu = unpack(gathers[1], h2, g2, (width, 2 * local_units))
    else:
        parts = (shards[0], w_out.T, w_up, w_down.T)
        pieces = [cut(gather_plain(s)) for s in parts]
        (wq,) = unpack(None, *pieces[0], (3 * width,))
        (wo,) = unpack(None, *pieces[1], (width,))
        (wu,) = unpack(None, *pieces[2], (2 * local_units,))
        (wd,) = unpack(None, *pieces[3], (2 * local_units,))
        order = lambda value: (value[:1], value[1:3], value[2:])
        given, cot = order(to_owners(rows_in)), order(to_owners(cot_in))
        small = joined(small, exchange(small, Y, sizes))
        proj, rows_b, mask = project(wq, given, small, fast)
        mixed0, probs0 = attend(proj, mask, 0)
        mixed1, probs1 = attend(proj, mask, 1)

    normed1, scale1, first_b, act, slope = middle(wo, wu, mixed0, mixed1, rows_b, table, small)
    if fast:
        act, g3, cx = phase(act, g3, cx)
        cot = (c0, ck, cx)
        h3 = joined(h3, g3)
        (wd,) = unpack(gathers[2], h3, swap(h3, 2, 4), (2 * local_units,))
    chunks, gz, gzb, sums2, down_own, down_sib = turn(packs[2], wd, act, normed1, cot, table, local_len)

    rows = shard_rows // 4
    if fast:
        down_sib, chunks, gzb = phase(down_sib, chunks, gzb)
        got, core_out = shed(down_sib, 2, 0), exchange(chunks[2:], CORE, sizes)
    gh, sum_up = hidden_back(wd, gzb, slope)
    if fast:
        gh, got, core_out = phase(gh, got, core_out)
        down = [down_own, got]
        send, x_send, gh = phase(
            add_up(down, 8 * rows, 16 * rows), joined(chunks[1:2], core_out[1:2]), gh
        )
        got, x_out = shed(send, 2, 1), exchange(x_send, X, sizes)
    gz1, grad_mixed, sums1, up_own, up_sib = first_back(
        packs[1], wo, wu, gh, gz, normed1, scale1, table, first_b, mixed0, mixed1
    )
    if fast:
        grad_mixed, up_sib, got, x_out = phase(grad_mixed, up_sib, got, x_out)
        down = down + [got]
        send, y_send, grad_mixed = phase(
            add_up(down, 4 * rows, 8 * rows), joined(chunks[:1], core_out[:1], x_out), grad_mixed
        )
        got, got2 = shed(send, 2, 2), shed(up_sib, 1, 0)
    parts0 = attend_back(proj, probs0, grad_mixed, 0)
    if fast:
        head, got2, grad_mixed = phase(parts0[0], got2, grad_mixed)
        parts0 = (head,) + tuple(parts0[1:])
        up = [up_own, got2]
        send2, grad_mixed, y_send = phase(add_up(up, 8 * rows, 16 * rows), grad_mixed, y_send)
        got2, y_out = shed(send2, 1, 1), exchange(y_send, Y, sizes)
    parts1 = attend_back(proj, probs1, grad_mixed, 1)
    parts = list(parts0) + list(parts1)
    chunks2 = input_back(wq, gz1, parts, local_len, fast)
    parts[0] = after(parts[0], chunks2)
    qkv_own, qkv_sib = last(packs[0], rows_b, sums1, sums2, sum_up, parts)
    if fast:
        chunks2, qkv_sib, got, got2, y_out = phase(chunks2, qkv_sib, got, got2, y_out)
        down, up = down + [got], up + [got2]
        send = add_up(down, 2 * rows, 4 * rows)
        send2 = add_up(up, 4 * rows, 8 * rows)
        qkv_sib, send, send2, chunks2 = phase(qkv_sib, send, send2, chunks2)
        got3, got, got2, core_x = (
            shed(qkv_sib, 0, 0), shed(send, 2, 3), shed(send2, 1, 2), exchange(chunks2[2:], CORE, sizes)
        )
        got3, core_x = phase(got3, core_x)
        qkv = [qkv_own, got3]
        sent3 = add_up(qkv, 8 * rows, 16 * rows, (0, 1))
        x_send = joined(chunks2[1:2], core_x[1:2])
        got3 = shed(sent3, 0, 1)
        sent3, x_send, got = phase(sent3, x_send, got)
        down = down + [got]
        got = shed(add_up(down, rows, 2 * rows), 2, 4)
        got3, got2 = phase(got3, got2)
        up, qkv = up + [got2], qkv + [got3]
        send3 = add_up(qkv, 4 * rows, 8 * rows, (3, 2), [sent3])
        send2 = add_up(up, 2 * rows, 4 * rows)
        send3, send2, x_send, got = phase(send3, send2, x_send, got)
        got3, got2, x_x = shed(send3, 0, 2), shed(send2, 1, 3), exchange(x_send, X, sizes)
        pair1 = add_up(down + [got], 0, rows)
        pair1, send3 = phase(pair1, send3)
        got = exchange(pair1, X, sizes)
        got3, got2, got, x_x = phase(got3, got2, got, x_x)
        up, qkv = up + [got2], qkv + [got3]
        sent3 = add_up(qkv, 2 * rows, 4 * rows, (4, 3), [send3])
        send2 = add_up(up, rows, 2 * rows)
        pair1, y_send = joined(pair1, got), joined(chunks2[:1], core_x[:1], x_x)
        sent3, send2, pair1, y_send = phase(sent3, send2, pair1, y_send)
        got3, got2, got1 = shed(sent3, 0, 3), shed(send2, 1, 4), exchange(pair1, CORE, sizes)
        y_x = exchange(y_send, Y, sizes)
        layer_output = deliver(chunks, core_out, x_out, y_out)
        got3, got2, got1, layer_output = phase(got3, got2, got1, layer_output)
        up, qkv = up + [got2], qkv + [got3]
        send3 = add_up(qkv, rows, 2 * rows, (5, 4), [sent3])
        pair2 = add_up(up, 0, rows)
        send3, pair2, got1 = phase(send3, pair2, got1)
        got3, got2 = shed(send3, 0, 4), exchange(pair2, X, sizes)
        (grad_down,) = settle(pair1, got1, ((0, local_units, "plain"),))
        got3, got2, grad_down, y_x = phase(got3, got2, grad_down, y_x)
        qkv = qkv + [got3]
        pair3, pair2 = phase(add_up(qkv, 0, rows), joined(pair2, got2))
        got, got2 = exchange(pair3, X, sizes), exchange(pair2, CORE, sizes)
        vec = vectors(after(send3, pair3), got3, local_width, local_units)
        grad_wout, grad_up = settle(
            pair2, got2, ((0, local_width, "plain"), (local_width, local_width + local_units, "plain"))
        )
        got, grad_up, bup = phase(got, grad_up, vec[1])
        vec = (vec[0], bup) + tuple(vec[2:])
        pair3 = joined(pair3, got)
        got3 = exchange(pair3, CORE, sizes)
        grad_x = deliver(chunks2, core_x, x_x, y_x)
        (grad_qkv,) = settle(pair3, after(got3, grad_x), ((0, 3 * local_width, "three"),))
        layer_output = layer_output.reshape(micro, seqs, local_len, width)
        grad_x = grad_x.reshape(micro, seqs, local_len, width)
    else:
        layer_output = spread(jnp.repeat(chunks, 2, axis=0))
        grad_x = spread(jnp.repeat(chunks2, 2, axis=0))
        vec = lax.psum(qkv_own[width:].astype(F32), AXES)
        vec = vectors(vec, None, local_width, local_units)
        grad_down = reduce_plain(down_own, down_sib)
        both = reduce_plain(up_own, up_sib)
        grad_wout, grad_up = both[:, :local_width], both[:, local_width:]
        grad_qkv = reduce_plain(qkv_own[:width], qkv_sib[:width])
        grad_qkv = jnp.swapaxes(grad_qkv.reshape(shard_rows, 3, local_width), 0, 1)

    out_bqv, out_bup, g1, s1, bout, g2, s2, bdown = vec
    return (
        layer_output,
        grad_x,
        grad_qkv,
        out_bqv,
        grad_wout.T,
        bout,
        g1,
        s1,
        grad_up,
        out_bup,
        grad_down.T,
        bdown,
        g2,
        s2,
    )


def solution(mesh):
    return jax.shard_map(
        body,
        mesh=mesh,
        in_specs=(
            P(None, "fsdp", "ctx", None),
            P(None, "fsdp", "ctx"),
            P(None, "fsdp", "tp"),
            P(None, "tp"),
            P("tp", "fsdp"),
            P(),
            P(),
            P(),
            P("fsdp", "tp"),
            P("tp"),
            P("tp", "fsdp"),
            P(),
            P(),
            P(),
            P(None, "fsdp", "ctx", None),
        ),
        out_specs=(
            P(None, "fsdp", "ctx", None),
            P(None, "fsdp", "ctx", None),
            P(None, "fsdp", "tp"),
            P(None, "tp"),
            P("tp", "fsdp"),
            P(),
            P(),
            P(),
            P("fsdp", "tp"),
            P("tp"),
            P("tp", "fsdp"),
            P(),
            P(),
            P(),
        ),
        check_vma=False,
    )
```

time: 334 us -> 259 us (0.78)
  local copies, waits for them, and re-layouts: 61 us -> 9.94 us
  other arithmetic: 28.2 us -> 2.71 us
  waiting for transfers between devices: 99.8 us -> 121 us
  starting transfers between devices: 55.1 us -> 40.2 us
    unnamed x158 -> x40, local copies, waits for them, and re-layouts: 53.3 us -> 6.74 us
    ppermute x37 -> x47, waiting for transfers between devices: 79.1 us -> 121 us  [exchange(): return lax.ppermute(value, AXES, pairs)]
    convert_element_type x15 -> x0, other arithmetic: 26.8 us -> none  [add_up(): return total.astype(BF16)]
    all_to_all x6 -> x0, starting transfers between devices: 20.9 us -> none  [the longest x2 8.6 us: spread(): out = lax.all_to_all(chunks, ('ctx', 'tp'), 0, 0, tiled=True)]
    all_to_all x6 -> x0, waiting for transfers between devices: 20.7 us -> none  [the longest x2 8.5 us: to_owners(): return lax.all_to_all(chunks, 'ctx', 0, 0, tiled=True)]
    ppermute x37 -> x47, starting transfers between devices: 34.2 us -> 40.2 us  [exchange(): return lax.ppermute(value, AXES, pairs)]
    pallas_call x17 -> x35, Pallas kernels: 85.9 us -> 84.1 us  [call(): pl.pallas_call(kernel, name=name, out_shape=outs, in_specs=specs, out_spe...]
  transfers between devices with their start and end apart: 43 -> 47, of which waited for: 19 -> 23; matrix products, arithmetic and copies ran while one was open for 11% -> 1% of each run, Pallas kernels for 22% -> 27%
where the time goes in v3:
time: 259 us
  waiting for transfers between devices  121 us (47%)
  Pallas kernels  84.1 us (32%)
  starting transfers between devices  40.2 us (16%)
  local copies, waits for them, and re-layouts  9.94 us (4%)
  other arithmetic  2.71 us (1%)
    ppermute x47, waiting for transfers between devices, exchange(): return lax.ppermute(value, AXES, pairs)  121 us
    pallas_call x35, Pallas kernels, call(): pl.pallas_call(kernel, name=name, out_shape=outs, in_specs=specs, out_spe...  84.1 us
    ppermute x47, starting transfers between devices, exchange(): return lax.ppermute(value, AXES, pairs)  40.2 us
    unnamed x40, local copies, waits for them, and re-layouts  6.74 us
  transfers between devices with their start and end apart: 47, of which 23 were waited for; matrix products, arithmetic and copies ran while one was open for 1% of the time, Pallas kernels for 27%

profile of v3, /device:TPU:0, one launch (start us, length us, event | category | flops | bytes accessed | tf_op | source)
XLA Modules:
  0.0 259.1 jit_solution(16757201795761517941)
XLA Ops:
  1.4 1.5 dynamic-slice_bitcast_fusion
  4.5 1.1 copy.31
  5.6 3.6 %collective-permute-start = (bf16[48,1152]{1,0:T(8,128)(2,1)S(1)}, bf16[48,1152]{1,0:T(8,128)(2,1)S(1)}, u32[]{:S(2)}, u32[]{:S(2)}) collective-permute-start(bf16[48,1152]{1,0:T(8,128)(2,1)S(1)} %constant_dynamic-slice_fusion.9), channel_id=1, source_target_pairs={{0,16},{1,17},{2,18},{3,19},{4,20},{5,21},{6,22},{7,23},{8,24},{9,... | collective-permute-start | bytes 331784 | tf_op jit(solution)/shard_map/ppermute | solution.py:37
  9.4 5.9 %collective-permute-done = bf16[48,1152]{1,0:T(8,128)(2,1)S(1)} collective-permute-done((bf16[48,1152]{1,0:T(8,128)(2,1)S(1)}, bf16[48,1152]{1,0:T(8,128)(2,1)S(1)}, u32[]{:S(2)}, u32[]{:S(2)}) %collective-permute-start) | collective-permute-done | bytes 110624 | tf_op jit(solution)/shard_map/ppermute | solution.py:37
  15.3 1.6 collective-permute-start.3
  17.8 6.1 %collective-permute-done.2 = bf16[96,1152]{1,0:T(8,128)(2,1)S(1)} collective-permute-done((bf16[96,1152]{1,0:T(8,128)(2,1)S(1)}, bf16[96,1152]{1,0:T(8,128)(2,1)S(1)}, u32[]{:S(2)}, u32[]{:S(2)}) %collective-permute-start.2) | collective-permute-done | bytes 221216 | tf_op jit(solution)/shard_map/ppermute | solution.py:37
  23.8 3.1 %collective-permute-done.3.refs_3_ = bf16[2,136,768]{2,1,0:T(8,128)(2,1)S(1)} collective-permute-done((bf16[2,136,768]{2,1,0:T(8,128)(2,1)S(1)}, bf16[2,136,768]{2,1,0:T(8,128)(2,1)S(1)}, u32[]{:S(2)}, u32[]{:S(2)}) %collective-permute-start.3) | collective-permute-done | bytes 417824 | tf_op jit(solution)/shard_map/ppermute | solution.py:37
  27.0 1.4 collective-permute-start.4
  29.4 6.2 %collective-permute-done.6 = f32[1,2304]{1,0:T(1,128)S(1)} collective-permute-done((f32[1,2304]{1,0:T(1,128)S(1)}, f32[1,2304]{1,0:T(1,128)S(1)}, u32[]{:S(2)}, u32[]{:S(2)}) %collective-permute-start.6) | collective-permute-done | bytes 9248 | tf_op jit(solution)/shard_map/ppermute | solution.py:37
  35.6 4.9 %collective-permute-done.5 = bf16[48,1920]{1,0:T(8,128)(2,1)S(1)} collective-permute-done((bf16[48,1920]{1,0:T(8,128)(2,1)S(1)}, bf16[48,1920]{1,0:T(8,128)(2,1)S(1)}, u32[]{:S(2)}, u32[]{:S(2)}) %collective-permute-start.5) | collective-permute-done | bytes 184352 | tf_op jit(solution)/shard_map/ppermute | solution.py:37
  40.6 1.6 collective-permute-start.8
  42.1 9.0 %collective-permute-done.9 = bf16[96,1920]{1,0:T(8,128)(2,1)S(1)} collective-permute-done((bf16[96,1920]{1,0:T(8,128)(2,1)S(1)}, bf16[96,1920]{1,0:T(8,128)(2,1)S(1)}, u32[]{:S(2)}, u32[]{:S(2)}) %collective-permute-start.9) | collective-permute-done | bytes 368672 | tf_op jit(solution)/shard_map/ppermute | solution.py:37
  51.2 2.5 collective-permute-done.8
  54.9 2.8 %collective-permute-done.10.refs_1_ = bf16[768,1152]{1,0:T(8,128)(2,1)S(1)} collective-permute-done((bf16[768,1152]{1,0:T(8,128)(2,1)S(1)}, bf16[768,1152]{1,0:T(8,128)(2,1)S(1)}, u32[]{:S(2)}, u32[]{:S(2)}) %collective-permute-start.10) | collective-permute-done | bytes 1769504 | tf_op jit(solution)/shard_map/ppermute | solution.py:37
  57.6 1.3 unpack.3.refs_0_
  59.0 2.6 %project.1 = (bf16[512,2304]{1,0:T(8,128)(2,1)S(1)}, bf16[512,768]{1,0:T(8,128)(2,1)S(1)}, f32[512,512]{1,0:T(8,128)S(1)}) custom-call(bf16[768,2304]{1,0:T(8,128)(2,1)S(1)} %unpack.3.refs_0_, bf16[1,136,768]{2,1,0:T(8,128)(2,1)S(1)} %get-tuple-element.322.refs_1_, bf16[2,136,768]{2,1,0:T(8,128)(2,1)S(1)} %collective-permute-done.1.refs_2_, ...), custom_call_target="tpu_custom_call" | custom-call | flops 5000000000 | bytes 1000000 | tf_op jit(solution)/shard_map/project/pallas_call | solution.py:134
  61.6 5.0 %collective-permute-done.11 = bf16[192,1920]{1,0:T(8,128)(2,1)S(1)} collective-permute-done((bf16[192,1920]{1,0:T(8,128)(2,1)S(1)}, bf16[192,1920]{1,0:T(8,128)(2,1)S(1)}, u32[]{:S(2)}, u32[]{:S(2)}) %collective-permute-start.11) | collective-permute-done | bytes 737312 | tf_op jit(solution)/shard_map/ppermute | solution.py:37
  67.4 1.6 collective-permute-start.14
  69.1 6.7 %attend.2 = (bf16[512,384]{1,0:T(8,128)(2,1)S(1)}, bf16[6,512,512]{2,1,0:T(8,128)(2,1)S(1)}) custom-call(bf16[512,2304]{1,0:T(8,128)(2,1)S(1)} %get-tuple-element.197.refs_0_, f32[512,512]{1,0:T(8,128)S(1)} %get-tuple-element.193.refs_1_), custom_call_target="tpu_custom_call" | custom-call | flops 12000000000 | bytes 1000000 | tf_op jit(solution)/shard_map/attend/pallas_call | solution.py:134
  76.4 6.7 %attend.3 = (bf16[512,384]{1,0:T(8,128)(2,1)S(1)}, bf16[6,512,512]{2,1,0:T(8,128)(2,1)S(1)}) custom-call(bf16[512,2304]{1,0:T(8,128)(2,1)S(1)} %get-tuple-element.197.refs_0_, f32[512,512]{1,0:T(8,128)S(1)} %get-tuple-element.193.refs_1_), custom_call_target="tpu_custom_call" | custom-call | flops 12000000000 | bytes 1000000 | tf_op jit(solution)/shard_map/attend/pallas_call | solution.py:134
  83.0 10.5 %collective-permute-done.15 = bf16[192,1536]{1,0:T(8,128)(2,1)S(1)} collective-permute-done((bf16[192,1536]{1,0:T(8,128)(2,1)S(1)}, bf16[192,1536]{1,0:T(8,128)(2,1)S(1)}, u32[]{:S(2)}, u32[]{:S(2)}) %collective-permute-start.15) | collective-permute-done | bytes 589856 | tf_op jit(solution)/shard_map/ppermute | solution.py:37
  93.9 1.4 collective-permute-start.18
  95.3 1.5 collective-permute-start.17
  96.9 2.4 collective-permute-done.16.refs_1_
  99.3 2.3 unpack.4
  101.6 8.7 %middle.1 = (f32[512,768]{1,0:T(8,128)S(1)}, f32[512,1]{1,0:T(8,128)S(1)}, bf16[512,768]{1,0:T(8,128)(2,1)S(1)}, bf16[512,3072]{1,0:T(8,128)(2,1)S(1)}, bf16[512,3072]{1,0:T(8,128)(2,1)S(1)}) custom-call(bf16[768,768]{1,0:T(8,128)(2,1)S(1)} %get-tuple-element.204.w_out.refs_0_, bf16[768,3072]{1,0:T(8,128)(2,1)S(1)} %get-tuple-element.205.w_up.refs_1_, ...), custom_call_target="tpu_custom_call" | custom-call | flops 12000000000 | bytes 1000000 | tf_op jit(solution)/shard_map/middle/pallas_call | solution.py:134
  110.4 1.1 collective-permute-done.17
  111.7 4.5 %collective-permute-done.19.refs_1_ = bf16[768,1536]{1,0:T(8,128)(2,1)S(1)} collective-permute-done((bf16[768,1536]{1,0:T(8,128)(2,1)S(1)}, bf16[768,1536]{1,0:T(8,128)(2,1)S(1)}, u32[]{:S(2)}, u32[]{:S(2)}) %collective-permute-start.19) | collective-permute-done | bytes 2359328 | tf_op jit(solution)/shard_map/ppermute | solution.py:37
  116.2 1.6 unpack.5.refs_0_.weight_ref
  117.8 10.4 %turn.1 = (bf16[4,128,768]{2,1,0:T(8,128)(2,1)S(1)}, f32[512,768]{1,0:T(8,128)S(1)}, bf16[512,768]{1,0:T(8,128)(2,1)S(1)}, f32[8,768]{1,0:T(8,128)S(1)}, bf16[76...) custom-call(bf16[768,3072]{1,0:T(8,128)(2,1)S(1)} %unpack.5.refs_0_.weight_ref, ...), custom_call_target="tpu_custom_call" | custom-call | flops 14000000000 | bytes 1000000 | tf_op jit(solution)/shard_map/turn/pallas_call | solution.py:134
  128.9 2.3 copy-done.3
  131.3 3.8 %hidden_back.1 = (bf16[512,3072]{1,0:T(8,128)(2,1)S(1)}, f32[1,3072]{1,0:T(1,128)S(1)}) custom-call(bf16[768,3072]{1,0:T(8,128)(2,1)S(1)} %copy-done.3, bf16[512,768]{1,0:T(8,128)(2,1)S(1)} %get-tuple-element.219.gzb_ref, bf16[512,3072]{1,0:T(8,128)(2,1)S(1)} %get-tuple-element.220.slope_ref), custom_call_target="tpu_custom_call" | custom-call | flops 12000000000 | bytes 1000000 | tf_op jit(solution)/shard_map/hidden_back/pallas_call | solution.py:134
  135.0 1.7 copy-done.6
  137.9 1.4 collective-permute-start.22
  139.3 2.3 copy-done.5
  141.6 13.0 %first_back.1 = (f32[512,768]{1,0:T(8,128)S(1)}, bf16[512,768]{1,0:T(8,128)(2,1)S(1)}, f32[8,768]{1,0:T(8,128)S(1)}, bf16[768,1920]{1,0:T(8,128)(2,1)S(1)}, bf16[768,1920]{1,0:T(8,128)(2,1)S(1)}) custom-call(bf16[768,768]{1,0:T(8,128)(2,1)S(1)} %get-tuple-element.204.w_out.refs_0_, bf16[768,3072]{1,0:T(8,128)(2,1)S(1)} %copy-done.5, ...), custom_call_target="tpu_custom_call" | custom-call | flops 20000000000 | bytes 1000000 | tf_op jit(solution)/shard_map/first_back/pallas_call | solution.py:134
  155.0 5.4 %attend_back.2 = (bf16[512,384]{1,0:T(8,128)(2,1)S(1)}, bf16[512,384]{1,0:T(8,128)(2,1)S(1)}, bf16[512,384]{1,0:T(8,128)(2,1)S(1)}) custom-call(bf16[512,2304]{1,0:T(8,128)(2,1)S(1)} %get-tuple-element.197.refs_0_, bf16[6,512,512]{2,1,0:T(8,128)(2,1)S(1)} %get-tuple-element.234.refs_1_, bf16[512,768]{1,0:T(8,128)(2,1)S(1)} %get-tuple-element.254.refs_2_), custom_call_target="tpu_custom_call" | custom-call | flops 2000000000 | bytes 1000000 | tf_op jit(solution)/shard_map/attend_back/pallas_call | solution.py:134
  160.8 1.5 collective-permute-start.26
  164.0 5.6 %attend_back.3 = (bf16[512,384]{1,0:T(8,128)(2,1)S(1)}, bf16[512,384]{1,0:T(8,128)(2,1)S(1)}, bf16[512,384]{1,0:T(8,128)(2,1)S(1)}) custom-call(bf16[512,2304]{1,0:T(8,128)(2,1)S(1)} %get-tuple-element.197.refs_0_, bf16[6,512,512]{2,1,0:T(8,128)(2,1)S(1)} %get-tuple-element.249.refs_1_, bf16[512,768]{1,0:T(8,128)(2,1)S(1)} %get-tuple-element.254.refs_2_), custom_call_target="tpu_custom_call" | custom-call | flops 2000000000 | bytes 1000000 | tf_op jit(solution)/shard_map/attend_back/pallas_call | solution.py:134
  169.6 2.7 %input_back.1.own_ref = bf16[4,128,768]{2,1,0:T(8,128)(2,1)S(1)} custom-call(bf16[768,2304]{1,0:T(8,128)(2,1)S(1)} %unpack.3.refs_0_, f32[512,768]{1,0:T(8,128)S(1)} %get-tuple-element.246.refs_1_, bf16[512,384]{1,0:T(8,128)(2,1)S(1)} %get-tuple-element.258.refs_2_.refs_4_, bf16[512,384]{1,0:T(8,128)(2,1)S(1)} %get-tuple-element.247.refs_3_.refs_5_, ...), custom_call_target="tpu_custom_call" | custom-call | flops 1000000000 | bytes 1000000 | tf_op jit(solution)/shard_map/input_back/pallas_call | solution.py:134
  172.3 4.0 %last.1 = (bf16[776,1152]{1,0:T(8,128)(2,1)S(1)}, bf16[776,1152]{1,0:T(8,128)(2,1)S(1)}) custom-call(bf16[512,768]{1,0:T(8,128)(2,1)S(1)} %get-tuple-element.184.x_ref.refs_0_, f32[8,768]{1,0:T(8,128)S(1)} %get-tuple-element.231.refs_1_, f32[8,768]{1,0:T(8,128)S(1)} %get-tuple-element.232.refs_2_, f32[1,3072]{1,0:T(1,128)S(1)} %get-tuple-element.233.refs_3_, ...), custom_call_target="tpu_custom_call" | custom-call | flops 1000000000 | bytes 1000000 | tf_op jit(solution)/shard_map/last/pallas_call | solution.py:134
  176.3 10.2 %collective-permute-done.25.refs_3_ = bf16[192,1536]{1,0:T(8,128)(2,1)S(1)} collective-permute-done((bf16[192,1536]{1,0:T(8,128)(2,1)S(1)}, bf16[192,1536]{1,0:T(8,128)(2,1)S(1)}, u32[]{:S(2)}, u32[]{:S(2)}) %collective-permute-start.25) | collective-permute-done | bytes 589856 | tf_op jit(solution)/shard_map/ppermute | solution.py:37
  187.6 3.7 %collective-permute-done.29.core_ref = bf16[2,128,768]{2,1,0:T(8,128)(2,1)S(1)} collective-permute-done((bf16[2,128,768]{2,1,0:T(8,128)(2,1)S(1)}, bf16[2,128,768]{2,1,0:T(8,128)(2,1)S(1)}, u32[]{:S(2)}, u32[]{:S(2)}) %collective-permute-start.29) | collective-permute-done | bytes 393248 | tf_op jit(solution)/shard_map/ppermute | solution.py:37
  191.5 1.5 collective-permute-start.30
  193.9 0.9 collective-permute-start.32
  194.9 8.3 %collective-permute-done.32.refs_4_ = bf16[96,1536]{1,0:T(8,128)(2,1)S(1)} collective-permute-done((bf16[96,1536]{1,0:T(8,128)(2,1)S(1)}, bf16[96,1536]{1,0:T(8,128)(2,1)S(1)}, u32[]{:S(2)}, u32[]{:S(2)}) %collective-permute-start.32) | collective-permute-done | bytes 294944 | tf_op jit(solution)/shard_map/ppermute | solution.py:37
  203.3 1.7 collective-permute-start.33
  204.9 7.6 %collective-permute-done.31.refs_3_ = bf16[192,1920]{1,0:T(8,128)(2,1)S(1)} collective-permute-done((bf16[192,1920]{1,0:T(8,128)(2,1)S(1)}, bf16[192,1920]{1,0:T(8,128)(2,1)S(1)}, u32[]{:S(2)}, u32[]{:S(2)}) %collective-permute-start.31) | collective-permute-done | bytes 737312 | tf_op jit(solution)/shard_map/ppermute | solution.py:37
  215.3 1.6 collective-permute-start.36
  216.9 11.4 %collective-permute-done.36 = bf16[48,1536]{1,0:T(8,128)(2,1)S(1)} collective-permute-done((bf16[48,1536]{1,0:T(8,128)(2,1)S(1)}, bf16[48,1536]{1,0:T(8,128)(2,1)S(1)}, u32[]{:S(2)}, u32[]{:S(2)}) %collective-permute-start.36) | collective-permute-done | bytes 147488 | tf_op jit(solution)/shard_map/ppermute | solution.py:37
  228.7 1.6 collective-permute-start.43
  230.3 1.1 collective-permute-start.39
  231.4 1.6 collective-permute-start.38
  233.0 1.3 deliver.2
  234.2 8.5 %collective-permute-done.39.refs_5_ = bf16[48,1920]{1,0:T(8,128)(2,1)S(1)} collective-permute-done((bf16[48,1920]{1,0:T(8,128)(2,1)S(1)}, bf16[48,1920]{1,0:T(8,128)(2,1)S(1)}, u32[]{:S(2)}, u32[]{:S(2)}) %collective-permute-start.39) | collective-permute-done | bytes 184352 | tf_op jit(solution)/shard_map/ppermute | solution.py:37
  243.0 1.2 collective-permute-start.42
  244.3 1.2 settle.3
  245.4 3.6 %collective-permute-done.41.refs_5_.refs_1_ = bf16[56,1152]{1,0:T(8,128)(2,1)S(1)} collective-permute-done((bf16[56,1152]{1,0:T(8,128)(2,1)S(1)}, bf16[56,1152]{1,0:T(8,128)(2,1)S(1)}, u32[]{:S(2)}, u32[]{:S(2)}) %collective-permute-start.41) | collective-permute-done | bytes 129056 | tf_op jit(solution)/shard_map/ppermute | solution.py:37
  249.0 1.5 collective-permute-done.42
  251.3 1.2 collective-permute-start.44
  253.2 1.2 settle.4
  254.5 1.9 collective-permute-done.44
  256.5 1.3 deliver.3
  257.9 1.0 settle.5
  (156 shorter events, 19.3 us)
Async XLA Ops:
  0.6 41.5 %copy-start = (bf16[1536,192]{0,1:T(8,128)(2,1)S(1)}, bf16[1536,192]{0,1:T(8,128)(2,1)}, u32[]{:S(2)}) copy-start(bf16[1536,192]{0,1:T(8,128)(2,1)} %param.25) | copy-start | bytes 1769476
  3.0 6.2 %copy-start.11 = (f32[768]{0:T(1024)S(1)}, f32[768]{0:T(1024)}, u32[]{:S(2)}) copy-start(f32[768]{0:T(1024)} %param.20) | copy-start | bytes 9220
  3.0 6.2 %copy-start.12 = (f32[768]{0:T(1024)S(1)}, f32[768]{0:T(1024)}, u32[]{:S(2)}) copy-start(f32[768]{0:T(1024)} %param.21) | copy-start | bytes 9220
  3.0 6.2 %copy-start.13 = (f32[768]{0:T(1024)S(1)}, f32[768]{0:T(1024)}, u32[]{:S(2)}) copy-start(f32[768]{0:T(1024)} %param.22) | copy-start | bytes 9220
  3.0 6.2 %copy-start.14 = (f32[768]{0:T(1024)S(1)}, f32[768]{0:T(1024)}, u32[]{:S(2)}) copy-start(f32[768]{0:T(1024)} %param.26) | copy-start | bytes 9220
  3.0 6.2 %copy-start.15 = (f32[768]{0:T(1024)S(1)}, f32[768]{0:T(1024)}, u32[]{:S(2)}) copy-start(f32[768]{0:T(1024)} %param.27) | copy-start | bytes 9220
  3.0 6.2 %copy-start.16 = (f32[768]{0:T(1024)S(1)}, f32[768]{0:T(1024)}, u32[]{:S(2)}) copy-start(f32[768]{0:T(1024)} %param.28) | copy-start | bytes 9220
  3.1 6.2 %copy-start.17 = (f32[2,384]{1,0:T(2,128)S(1)}, f32[2,384]{1,0:T(2,128)}, u32[]{:S(2)}) copy-start(f32[2,384]{1,0:T(2,128)} %param.18) | copy-start | bytes 9220
  3.1 6.2 %copy-start.10 = (f32[1536]{0:T(1024)S(1)}, f32[1536]{0:T(1024)}, u32[]{:S(2)}) copy-start(f32[1536]{0:T(1024)} %param.24) | copy-start | bytes 18436
  3.2 14.6 %copy-start.8 = (bf16[192,1536]{1,0:T(8,128)(2,1)S(1)}, bf16[192,1536]{1,0:T(8,128)(2,1)}, u32[]{:S(2)}) copy-start(bf16[192,1536]{1,0:T(8,128)(2,1)} %param.23) | copy-start | bytes 1769476
  3.2 14.6 %copy-start.9 = (bf16[384,192]{0,1:T(8,128)(2,1)S(1)}, bf16[384,192]{0,1:T(8,128)(2,1)}, u32[]{:S(2)}) copy-start(bf16[384,192]{0,1:T(8,128)(2,1)} %param.19) | copy-start | bytes 442372
  4.0 11.3 %collective-permute-start.1 = (bf16[2,136,768]{2,1,0:T(8,128)(2,1)}, bf16[2,136,768]{2,1,0:T(8,128)(2,1)S(1)}, u32[]{:S(2)}, u32[]{:S(2)}) collective-permute-start(bf16[2,136,768]{2,1,0:T(8,128)(2,1)} %pad_maximum_fusion.8), channel_id=1, source_target_pairs={{0,2},{1,3},{2,0},{3,1},{4,6},{5,7},{6,4},{7,5},{8,10},{9,11},{10,... | collective-permute-start | bytes 1253384 | tf_op jit(solution)/shard_map/ppermute | solution.py:37
  5.6 9.7 %collective-permute-start = (bf16[48,1152]{1,0:T(8,128)(2,1)S(1)}, bf16[48,1152]{1,0:T(8,128)(2,1)S(1)}, u32[]{:S(2)}, u32[]{:S(2)}) collective-permute-start(bf16[48,1152]{1,0:T(8,128)(2,1)S(1)} %constant_dynamic-slice_fusion.9), channel_id=1, source_target_pairs={{0,16},{1,17},{2,18},{3,19},{4,20},{5,21},{6,22},{7,23},{8,24},{9,... | collective-permute-start | bytes 331784 | tf_op jit(solution)/shard_map/ppermute | solution.py:37
  15.3 11.5 %collective-permute-start.3 = (bf16[2,136,768]{2,1,0:T(8,128)(2,1)S(1)}, bf16[2,136,768]{2,1,0:T(8,128)(2,1)S(1)}, u32[]{:S(2)}, u32[]{:S(2)}) collective-permute-start(bf16[2,136,768]{2,1,0:T(8,128)(2,1)S(1)} %pad_maximum_fusion.9), channel_id=1, source_target_pairs={{0,4},{1,5},{2,6},{3,7},{4,0},{5,1},{6,2},{7,3},{8,12},{9,13},{10,... | collective-permute-start | bytes 1253384 | tf_op jit(solution)/shard_map/ppermute | solution.py:37
  17.0 6.8 %collective-permute-start.2 = (bf16[96,1152]{1,0:T(8,128)(2,1)S(1)}, bf16[96,1152]{1,0:T(8,128)(2,1)S(1)}, u32[]{:S(2)}, u32[]{:S(2)}) collective-permute-start(bf16[96,1152]{1,0:T(8,128)(2,1)S(1)} %pad_maximum_fusion.17), channel_id=1, source_target_pairs={{0,8},{1,9},{2,10},{3,11},{4,12},{5,13},{6,14},{7,15},{8,0},{9,1},... | collective-permute-start | bytes 663560 | tf_op jit(solution)/shard_map/ppermute | solution.py:37
  27.0 13.5 %collective-permute-start.4 = (bf16[192,1152]{1,0:T(8,128)(2,1)S(1)}, bf16[192,1152]{1,0:T(8,128)(2,1)S(1)}, u32[]{:S(2)}, u32[]{:S(2)}) collective-permute-start(bf16[192,1152]{1,0:T(8,128)(2,1)S(1)} %pad_maximum_fusion.7), channel_id=1, source_target_pairs={{0,1},{1,0},{2,6},{3,7},{4,5},{5,4},{6,2},{7,3},{8,9},{9,8},{10,14... | collective-permute-start | bytes 1327112 | tf_op jit(solution)/shard_map/ppermute | solution.py:37
  28.5 12.0 %collective-permute-start.7 = (bf16[2,128,768]{2,1,0:T(8,128)(2,1)S(1)}, bf16[2,128,768]{2,1,0:T(8,128)(2,1)S(1)}, u32[]{:S(2)}, u32[]{:S(2)}) collective-permute-start(bf16[2,128,768]{2,1,0:T(8,128)(2,1)S(1)} %pad_maximum_fusion.10), channel_id=1, source_target_pairs={{0,2},{1,3},{2,0},{3,1},{4,6},{5,7},{6,4},{7,5},{8,10},{9,11},{10,... | collective-permute-start | bytes 1179656 | tf_op jit(solution)/shard_map/ppermute | solution.py:37
  28.6 11.9 %collective-permute-start.5 = (bf16[48,1920]{1,0:T(8,128)(2,1)S(1)}, bf16[48,1920]{1,0:T(8,128)(2,1)S(1)}, u32[]{:S(2)}, u32[]{:S(2)}) collective-permute-start(bf16[48,1920]{1,0:T(8,128)(2,1)S(1)} %fusion.2), channel_id=1, source_target_pairs={{0,16},{1,17},{2,18},{3,19},{4,20},{5,21},{6,22},{7,23},{8,24},{9,... | collective-permute-start | bytes 552968 | tf_op jit(solution)/shard_map/ppermute | solution.py:37
  28.9 6.7 %collective-permute-start.6 = (f32[1,2304]{1,0:T(1,128)S(1)}, f32[1,2304]{1,0:T(1,128)S(1)}, u32[]{:S(2)}, u32[]{:S(2)}) collective-permute-start(f32[1,2304]{1,0:T(1,128)S(1)} %broadcast_in_dim.4), channel_id=1, source_target_pairs={{0,1},{1,0},{2,3},{3,2},{4,5},{5,4},{6,7},{7,6},{8,9},{9,8},{10,11... | collective-permute-start | bytes 27656 | tf_op jit(solution)/shard_map/ppermute | solution.py:37
  40.6 13.1 %collective-permute-start.8 = (bf16[384,1152]{1,0:T(8,128)(2,1)S(1)}, bf16[384,1152]{1,0:T(8,128)(2,1)S(1)}, u32[]{:S(2)}, u32[]{:S(2)}) collective-permute-start(bf16[384,1152]{1,0:T(8,128)(2,1)S(1)} %pad_maximum_fusion.3), channel_id=1, source_target_pairs={{0,4},{1,5},{2,3},{3,2},{4,0},{5,1},{6,7},{7,6},{8,12},{9,13},{10,... | collective-permute-start | bytes 2654216 | tf_op jit(solution)/shard_map/ppermute | solution.py:37
  42.1 9.0 %collective-permute-start.9 = (bf16[96,1920]{1,0:T(8,128)(2,1)S(1)}, bf16[96,1920]{1,0:T(8,128)(2,1)S(1)}, u32[]{:S(2)}, u32[]{:S(2)}) collective-permute-start(bf16[96,1920]{1,0:T(8,128)(2,1)S(1)} %pad_maximum_fusion.14), channel_id=1, source_target_pairs={{0,8},{1,9},{2,10},{3,11},{4,12},{5,13},{6,14},{7,15},{8,0},{9,1},... | collective-permute-start | bytes 1105928 | tf_op jit(solution)/shard_map/ppermute | solution.py:37
  53.9 3.8 %collective-permute-start.10 = (bf16[768,1152]{1,0:T(8,128)(2,1)S(1)}, bf16[768,1152]{1,0:T(8,128)(2,1)S(1)}, u32[]{:S(2)}, u32[]{:S(2)}) collective-permute-start(bf16[768,1152]{1,0:T(8,128)(2,1)S(1)} %pad_maximum_fusion.1.refs_0_), channel_id=1, source_target_pairs={{0,2},{1,3},{2,0},{3,1},{4,6},{5,7},{6,4},{7,5},{8,10},{9,11},{10,... | collective-permute-start | bytes 5308424 | tf_op jit(solution)/shard_map/ppermute | solution.py:37
  54.0 7.6 %collective-permute-start.12 = (bf16[48,1536]{1,0:T(8,128)(2,1)S(1)}, bf16[48,1536]{1,0:T(8,128)(2,1)S(1)}, u32[]{:S(2)}, u32[]{:S(2)}) collective-permute-start(bf16[48,1536]{1,0:T(8,128)(2,1)S(1)} %dynamic-slice_bitcast_fusion.2), channel_id=1, source_target_pairs={{0,16},{1,17},{2,3},{3,2},{4,20},{5,21},{6,7},{7,6},{8,24},{9,25},... | collective-permute-start | bytes 442376 | tf_op jit(solution)/shard_map/ppermute | solution.py:37
  54.1 12.6 %collective-permute-start.11 = (bf16[192,1920]{1,0:T(8,128)(2,1)S(1)}, bf16[192,1920]{1,0:T(8,128)(2,1)S(1)}, u32[]{:S(2)}, u32[]{:S(2)}) collective-permute-start(bf16[192,1920]{1,0:T(8,128)(2,1)S(1)} %pad_maximum_fusion.6), channel_id=1, source_target_pairs={{0,1},{1,0},{2,6},{3,7},{4,5},{5,4},{6,2},{7,3},{8,9},{9,8},{10,14... | collective-permute-start | bytes 2211848 | tf_op jit(solution)/shard_map/ppermute | solution.py:37
  66.7 9.1 %collective-permute-start.13 = (bf16[96,1536]{1,0:T(8,128)(2,1)S(1)}, bf16[96,1536]{1,0:T(8,128)(2,1)S(1)}, u32[]{:S(2)}, u32[]{:S(2)}) collective-permute-start(bf16[96,1536]{1,0:T(8,128)(2,1)S(1)} %get-tuple-element.338), channel_id=1, source_target_pairs={{0,8},{1,9},{2,6},{3,7},{4,12},{5,13},{6,2},{7,3},{8,0},{9,1},{10,... | collective-permute-start | bytes 884744 | tf_op jit(solution)/shard_map/ppermute | solution.py:37
  67.4 26.1 %collective-permute-start.14 = (bf16[384,1920]{1,0:T(8,128)(2,1)S(1)}, bf16[384,1920]{1,0:T(8,128)(2,1)S(1)}, u32[]{:S(2)}, u32[]{:S(2)}) collective-permute-start(bf16[384,1920]{1,0:T(8,128)(2,1)S(1)} %constant_dynamic-update-slice_fusion), channel_id=1, source_target_pairs={{0,4},{1,5},{2,3},{3,2},{4,0},{5,1},{6,7},{7,6},{8,12},{9,13},{10,... | collective-permute-start | bytes 4423688 | tf_op jit(solution)/shard_map/ppermute | solution.py:37
  75.8 17.7 %collective-permute-start.15 = (bf16[192,1536]{1,0:T(8,128)(2,1)S(1)}, bf16[192,1536]{1,0:T(8,128)(2,1)S(1)}, u32[]{:S(2)}, u32[]{:S(2)}) collective-permute-start(bf16[192,1536]{1,0:T(8,128)(2,1)S(1)} %constant_dynamic-update-slice_fusion.4), channel_id=1, source_target_pairs={{0,4},{1,5},{2,18},{3,19},{4,0},{5,1},{6,22},{7,23},{8,12},{9,13},... | collective-permute-start | bytes 1769480 | tf_op jit(solution)/shard_map/ppermute | solution.py:37
  93.8 5.4 %collective-permute-start.16 = (bf16[768,1920]{1,0:T(8,128)(2,1)S(1)}, bf16[768,1920]{1,0:T(8,128)(2,1)S(1)}, u32[]{:S(2)}, u32[]{:S(2)}) collective-permute-start(bf16[768,1920]{1,0:T(8,128)(2,1)S(1)} %pad_maximum_fusion.refs_0_), channel_id=1, source_target_pairs={{0,2},{1,3},{2,0},{3,1},{4,6},{5,7},{6,4},{7,5},{8,10},{9,11},{10,... | collective-permute-start | bytes 8847368 | tf_op jit(solution)/shard_map/ppermute | solution.py:37
  93.9 16.5 %collective-permute-start.18 = (bf16[2,128,768]{2,1,0:T(8,128)(2,1)S(1)}, bf16[2,128,768]{2,1,0:T(8,128)(2,1)S(1)}, u32[]{:S(2)}, u32[]{:S(2)}) collective-permute-start(bf16[2,128,768]{2,1,0:T(8,128)(2,1)S(1)} %pad_maximum_fusion.11), channel_id=1, source_target_pairs={{0,4},{1,5},{2,6},{3,7},{4,0},{5,1},{6,2},{7,3},{8,12},{9,13},{10,... | collective-permute-start | bytes 1179656 | tf_op jit(solution)/shard_map/ppermute | solution.py:37
  95.3 16.2 %collective-permute-start.17 = (bf16[384,1536]{1,0:T(8,128)(2,1)S(1)}, bf16[384,1536]{1,0:T(8,128)(2,1)S(1)}, u32[]{:S(2)}, u32[]{:S(2)}) collective-permute-start(bf16[384,1536]{1,0:T(8,128)(2,1)S(1)} %pad_maximum_fusion.2), channel_id=1, source_target_pairs={{0,1},{1,0},{2,10},{3,11},{4,5},{5,4},{6,14},{7,15},{8,9},{9,8},{1... | collective-permute-start | bytes 3538952 | tf_op jit(solution)/shard_map/ppermute | solution.py:37
  101.6 8.7 %copy-start.4 = (bf16[768,3072]{1,0:T(8,128)(2,1)}, bf16[768,3072]{1,0:T(8,128)(2,1)S(1)}, u32[]{:S(2)}) copy-start(bf16[768,3072]{1,0:T(8,128)(2,1)S(1)} %get-tuple-element.205.w_up.refs_1_) | copy-start | bytes 14155780
  111.6 4.6 %collective-permute-start.19 = (bf16[768,1536]{1,0:T(8,128)(2,1)S(1)}, bf16[768,1536]{1,0:T(8,128)(2,1)S(1)}, u32[]{:S(2)}, u32[]{:S(2)}) collective-permute-start(bf16[768,1536]{1,0:T(8,128)(2,1)S(1)} %constant_dynamic-update-slice_fusion.7.refs_0_), channel_id=1, source_target_pairs={{0,2},{1,3},{2,0},{3,1},{4,6},{5,7},{6,4},{7,5},{8,10},{9,11},{10,... | collective-permute-start | bytes 7077896 | tf_op jit(solution)/shard_map/ppermute | solution.py:37
  117.8 10.4 %copy-start.2 = (bf16[768,3072]{1,0:T(8,128)(2,1)}, bf16[768,3072]{1,0:T(8,128)(2,1)S(1)}, u32[]{:S(2)}) copy-start(bf16[768,3072]{1,0:T(8,128)(2,1)S(1)} %unpack.5.refs_0_.weight_ref) | copy-start | bytes 14155780
  128.3 8.5 %collective-permute-start.20 = (bf16[768,1536]{1,0:T(8,128)(2,1)S(1)}, bf16[768,1536]{1,0:T(8,128)(2,1)S(1)}, u32[]{:S(2)}, u32[]{:S(2)}) collective-permute-start(bf16[768,1536]{1,0:T(8,128)(2,1)S(1)} %get-tuple-element.222), channel_id=1, source_target_pairs={{0,2},{1,3},{2,0},{3,1},{4,6},{5,7},{6,4},{7,5},{8,10},{9,11},{10,... | collective-permute-start | bytes 7077896 | tf_op jit(solution)/shard_map/ppermute | solution.py:37
  128.5 8.3 %collective-permute-start.21 = (bf16[2,128,768]{2,1,0:T(8,128)(2,1)S(1)}, bf16[2,128,768]{2,1,0:T(8,128)(2,1)S(1)}, u32[]{:S(2)}, u32[]{:S(2)}) collective-permute-start(bf16[2,128,768]{2,1,0:T(8,128)(2,1)S(1)} %slice.38), channel_id=1, source_target_pairs={{0,2},{1,3},{2,0},{3,1},{4,6},{5,7},{6,4},{7,5},{8,10},{9,11},{10,... | collective-permute-start | bytes 1179656 | tf_op jit(solution)/shard_map/ppermute | solution.py:37
  128.9 2.3 copy-start.3
  135.0 1.7 copy-start.6
  136.9 2.4 copy-start.7
  137.2 17.5 %collective-permute-start.23 = (bf16[2,128,768]{2,1,0:T(8,128)(2,1)S(1)}, bf16[2,128,768]{2,1,0:T(8,128)(2,1)S(1)}, u32[]{:S(2)}, u32[]{:S(2)}) collective-permute-start(bf16[2,128,768]{2,1,0:T(8,128)(2,1)S(1)} %pad_maximum_fusion.12), channel_id=1, source_target_pairs={{0,4},{1,5},{2,6},{3,7},{4,0},{5,1},{6,2},{7,3},{8,12},{9,13},{10,... | collective-permute-start | bytes 1179656 | tf_op jit(solution)/shard_map/ppermute | solution.py:37
  137.9 16.7 %collective-permute-start.22 = (bf16[384,1536]{1,0:T(8,128)(2,1)S(1)}, bf16[384,1536]{1,0:T(8,128)(2,1)S(1)}, u32[]{:S(2)}, u32[]{:S(2)}) collective-permute-start(bf16[384,1536]{1,0:T(8,128)(2,1)S(1)} %add.53), channel_id=1, source_target_pairs={{0,1},{1,0},{2,10},{3,11},{4,5},{5,4},{6,14},{7,15},{8,9},{9,8},{1... | collective-permute-start | bytes 3538952 | tf_op jit(solution)/shard_map/ppermute | solution.py:37
  139.3 2.3 copy-start.5
  154.6 5.7 %collective-permute-start.24 = (bf16[768,1920]{1,0:T(8,128)(2,1)S(1)}, bf16[768,1920]{1,0:T(8,128)(2,1)S(1)}, u32[]{:S(2)}, u32[]{:S(2)}) collective-permute-start(bf16[768,1920]{1,0:T(8,128)(2,1)S(1)} %get-tuple-element.244), channel_id=1, source_target_pairs={{0,2},{1,3},{2,0},{3,1},{4,6},{5,7},{6,4},{7,5},{8,10},{9,11},{10,... | collective-permute-start | bytes 8847368 | tf_op jit(solution)/shard_map/ppermute | solution.py:37
  160.8 25.8 %collective-permute-start.26 = (bf16[384,1920]{1,0:T(8,128)(2,1)S(1)}, bf16[384,1920]{1,0:T(8,128)(2,1)S(1)}, u32[]{:S(2)}, u32[]{:S(2)}) collective-permute-start(bf16[384,1920]{1,0:T(8,128)(2,1)S(1)} %add.55), channel_id=1, source_target_pairs={{0,4},{1,5},{2,10},{3,11},{4,0},{5,1},{6,14},{7,15},{8,12},{9,13},... | collective-permute-start | bytes 4423688 | tf_op jit(solution)/shard_map/ppermute | solution.py:37
  162.3 24.2 %collective-permute-start.27 = (bf16[4,128,768]{2,1,0:T(8,128)(2,1)S(1)}, bf16[4,128,768]{2,1,0:T(8,128)(2,1)S(1)}, u32[]{:S(2)}, u32[]{:S(2)}) collective-permute-start(bf16[4,128,768]{2,1,0:T(8,128)(2,1)S(1)} %pad_maximum_fusion.4), channel_id=1, source_target_pairs={{0,1},{1,0},{2,3},{3,2},{4,5},{5,4},{6,7},{7,6},{8,9},{9,8},{10,11... | collective-permute-start | bytes 2359304 | tf_op jit(solution)/shard_map/ppermute | solution.py:37
  163.1 23.4 %collective-permute-start.25 = (bf16[192,1536]{1,0:T(8,128)(2,1)S(1)}, bf16[192,1536]{1,0:T(8,128)(2,1)S(1)}, u32[]{:S(2)}, u32[]{:S(2)}) collective-permute-start(bf16[192,1536]{1,0:T(8,128)(2,1)S(1)} %add.54), channel_id=1, source_target_pairs={{0,4},{1,5},{2,18},{3,19},{4,0},{5,1},{6,22},{7,23},{8,12},{9,13},... | collective-permute-start | bytes 1769480 | tf_op jit(solution)/shard_map/ppermute | solution.py:37
  186.9 4.3 %collective-permute-start.28 = (bf16[776,1152]{1,0:T(8,128)(2,1)S(1)}, bf16[776,1152]{1,0:T(8,128)(2,1)S(1)}, u32[]{:S(2)}, u32[]{:S(2)}) collective-permute-start(bf16[776,1152]{1,0:T(8,128)(2,1)S(1)} %get-tuple-element.268), channel_id=1, source_target_pairs={{0,2},{1,3},{2,0},{3,1},{4,6},{5,7},{6,4},{7,5},{8,10},{9,11},{10,... | collective-permute-start | bytes 5363720 | tf_op jit(solution)/shard_map/ppermute | solution.py:37
  187.0 4.2 %collective-permute-start.29 = (bf16[2,128,768]{2,1,0:T(8,128)(2,1)S(1)}, bf16[2,128,768]{2,1,0:T(8,128)(2,1)S(1)}, u32[]{:S(2)}, u32[]{:S(2)}) collective-permute-start(bf16[2,128,768]{2,1,0:T(8,128)(2,1)S(1)} %slice.43), channel_id=1, source_target_pairs={{0,2},{1,3},{2,0},{3,1},{4,6},{5,7},{6,4},{7,5},{8,10},{9,11},{10,... | collective-permute-start | bytes 1179656 | tf_op jit(solution)/shard_map/ppermute | solution.py:37
  191.5 21.0 %collective-permute-start.30 = (bf16[392,1152]{1,0:T(8,128)(2,1)S(1)}, bf16[392,1152]{1,0:T(8,128)(2,1)S(1)}, u32[]{:S(2)}, u32[]{:S(2)}) collective-permute-start(bf16[392,1152]{1,0:T(8,128)(2,1)S(1)} %add.58.refs_3_), channel_id=1, source_target_pairs={{0,4},{1,5},{2,3},{3,2},{4,0},{5,1},{6,7},{7,6},{8,12},{9,13},{10,... | collective-permute-start | bytes 2709512 | tf_op jit(solution)/shard_map/ppermute | solution.py:37
  193.1 19.4 %collective-permute-start.31 = (bf16[192,1920]{1,0:T(8,128)(2,1)S(1)}, bf16[192,1920]{1,0:T(8,128)(2,1)S(1)}, u32[]{:S(2)}, u32[]{:S(2)}) collective-permute-start(bf16[192,1920]{1,0:T(8,128)(2,1)S(1)} %add.57), channel_id=1, source_target_pairs={{0,1},{1,0},{2,18},{3,19},{4,5},{5,4},{6,22},{7,23},{8,9},{9,8},{1... | collective-permute-start | bytes 2211848 | tf_op jit(solution)/shard_map/ppermute | solution.py:37
  193.9 9.3 %collective-permute-start.32 = (bf16[96,1536]{1,0:T(8,128)(2,1)S(1)}, bf16[96,1536]{1,0:T(8,128)(2,1)S(1)}, u32[]{:S(2)}, u32[]{:S(2)}) collective-permute-start(bf16[96,1536]{1,0:T(8,128)(2,1)S(1)} %add.56), channel_id=1, source_target_pairs={{0,8},{1,9},{2,6},{3,7},{4,12},{5,13},{6,2},{7,3},{8,0},{9,1},{10,... | collective-permute-start | bytes 884744 | tf_op jit(solution)/shard_map/ppermute | solution.py:37
  203.3 9.6 %collective-permute-start.33 = (bf16[48,1536]{1,0:T(8,128)(2,1)S(1)}, bf16[48,1536]{1,0:T(8,128)(2,1)S(1)}, u32[]{:S(2)}, u32[]{:S(2)}) collective-permute-start(bf16[48,1536]{1,0:T(8,128)(2,1)S(1)} %add.61), channel_id=1, source_target_pairs={{0,16},{1,17},{2,3},{3,2},{4,20},{5,21},{6,7},{7,6},{8,24},{9,25},... | collective-permute-start | bytes 442376 | tf_op jit(solution)/shard_map/ppermute | solution.py:37
  212.9 15.4 %collective-permute-start.34 = (bf16[200,1152]{1,0:T(8,128)(2,1)S(1)}, bf16[200,1152]{1,0:T(8,128)(2,1)S(1)}, u32[]{:S(2)}, u32[]{:S(2)}) collective-permute-start(bf16[200,1152]{1,0:T(8,128)(2,1)S(1)} %add.59.refs_4_), channel_id=1, source_target_pairs={{0,1},{1,0},{2,10},{3,11},{4,5},{5,4},{6,14},{7,15},{8,9},{9,8},{1... | collective-permute-start | bytes 1382408 | tf_op jit(solution)/shard_map/ppermute | solution.py:37
  213.8 14.5 %collective-permute-start.37 = (bf16[2,128,768]{2,1,0:T(8,128)(2,1)S(1)}, bf16[2,128,768]{2,1,0:T(8,128)(2,1)S(1)}, u32[]{:S(2)}, u32[]{:S(2)}) collective-permute-start(bf16[2,128,768]{2,1,0:T(8,128)(2,1)S(1)} %pad_maximum_fusion.13), channel_id=1, source_target_pairs={{0,4},{1,5},{2,6},{3,7},{4,0},{5,1},{6,2},{7,3},{8,12},{9,13},{10,... | collective-permute-start | bytes 1179656 | tf_op jit(solution)/shard_map/ppermute | solution.py:37
  214.6 13.7 %collective-permute-start.35 = (bf16[96,1920]{1,0:T(8,128)(2,1)S(1)}, bf16[96,1920]{1,0:T(8,128)(2,1)S(1)}, u32[]{:S(2)}, u32[]{:S(2)}) collective-permute-start(bf16[96,1920]{1,0:T(8,128)(2,1)S(1)} %add.60), channel_id=1, source_target_pairs={{0,8},{1,9},{2,3},{3,2},{4,12},{5,13},{6,7},{7,6},{8,0},{9,1},{10,... | collective-permute-start | bytes 1105928 | tf_op jit(solution)/shard_map/ppermute | solution.py:37
  215.3 13.0 %collective-permute-start.36 = (bf16[48,1536]{1,0:T(8,128)(2,1)S(1)}, bf16[48,1536]{1,0:T(8,128)(2,1)S(1)}, u32[]{:S(2)}, u32[]{:S(2)}) collective-permute-start(bf16[48,1536]{1,0:T(8,128)(2,1)S(1)} %add.62), channel_id=1, source_target_pairs={{0,4},{1,5},{2,6},{3,7},{4,0},{5,1},{6,2},{7,3},{8,12},{9,13},{10,... | collective-permute-start | bytes 442376 | tf_op jit(solution)/shard_map/ppermute | solution.py:37
  228.7 21.9 %collective-permute-start.43 = (bf16[4,128,768]{2,1,0:T(8,128)(2,1)S(1)}, bf16[4,128,768]{2,1,0:T(8,128)(2,1)S(1)}, u32[]{:S(2)}, u32[]{:S(2)}) collective-permute-start(bf16[4,128,768]{2,1,0:T(8,128)(2,1)S(1)} %pad_maximum_fusion.5), channel_id=1, source_target_pairs={{0,1},{1,0},{2,3},{3,2},{4,5},{5,4},{6,7},{7,6},{8,9},{9,8},{10,11... | collective-permute-start | bytes 2359304 | tf_op jit(solution)/shard_map/ppermute | solution.py:37
  230.3 12.4 %collective-permute-start.40 = (bf16[96,1536]{1,0:T(8,128)(2,1)S(1)}, bf16[96,1536]{1,0:T(8,128)(2,1)S(1)}, u32[]{:S(2)}, u32[]{:S(2)}) collective-permute-start(bf16[96,1536]{1,0:T(8,128)(2,1)S(1)} %pad_maximum_fusion.16.refs_0_), channel_id=1, source_target_pairs={{0,2},{1,3},{2,0},{3,1},{4,6},{5,7},{6,4},{7,5},{8,10},{9,11},{10,... | collective-permute-start | bytes 884744 | tf_op jit(solution)/shard_map/ppermute | solution.py:37
  230.3 12.4 %collective-permute-start.39 = (bf16[48,1920]{1,0:T(8,128)(2,1)S(1)}, bf16[48,1920]{1,0:T(8,128)(2,1)S(1)}, u32[]{:S(2)}, u32[]{:S(2)}) collective-permute-start(bf16[48,1920]{1,0:T(8,128)(2,1)S(1)} %add.64), channel_id=1, source_target_pairs={{0,16},{1,17},{2,6},{3,7},{4,20},{5,21},{6,2},{7,3},{8,24},{9,25},... | collective-permute-start | bytes 552968 | tf_op jit(solution)/shard_map/ppermute | solution.py:37
  231.4 11.3 %collective-permute-start.38 = (bf16[104,1152]{1,0:T(8,128)(2,1)S(1)}, bf16[104,1152]{1,0:T(8,128)(2,1)S(1)}, u32[]{:S(2)}, u32[]{:S(2)}) collective-permute-start(bf16[104,1152]{1,0:T(8,128)(2,1)S(1)} %add.63.refs_5_), channel_id=1, source_target_pairs={{0,8},{1,9},{2,18},{3,19},{4,12},{5,13},{6,22},{7,23},{8,0},{9,1},... | collective-permute-start | bytes 718856 | tf_op jit(solution)/shard_map/ppermute | solution.py:37
  242.9 6.1 %collective-permute-start.41 = (bf16[56,1152]{1,0:T(8,128)(2,1)S(1)}, bf16[56,1152]{1,0:T(8,128)(2,1)S(1)}, u32[]{:S(2)}, u32[]{:S(2)}) collective-permute-start(bf16[56,1152]{1,0:T(8,128)(2,1)S(1)} %add.65.refs_0_), channel_id=1, source_target_pairs={{0,16},{1,17},{2,6},{3,7},{4,20},{5,21},{6,2},{7,3},{8,24},{9,25},... | collective-permute-start | bytes 387080 | tf_op jit(solution)/shard_map/ppermute | solution.py:37
  243.0 7.5 %collective-permute-start.42 = (bf16[48,1920]{1,0:T(8,128)(2,1)S(1)}, bf16[48,1920]{1,0:T(8,128)(2,1)S(1)}, u32[]{:S(2)}, u32[]{:S(2)}) collective-permute-start(bf16[48,1920]{1,0:T(8,128)(2,1)S(1)} %add.66), channel_id=1, source_target_pairs={{0,4},{1,5},{2,6},{3,7},{4,0},{5,1},{6,2},{7,3},{8,12},{9,13},{10,... | collective-permute-start | bytes 552968 | tf_op jit(solution)/shard_map/ppermute | solution.py:37
  250.7 2.5 collective-permute-start.45
  251.3 5.0 %collective-permute-start.44 = (bf16[48,1152]{1,0:T(8,128)(2,1)S(1)}, bf16[48,1152]{1,0:T(8,128)(2,1)S(1)}, u32[]{:S(2)}, u32[]{:S(2)}) collective-permute-start(bf16[48,1152]{1,0:T(8,128)(2,1)S(1)} %add.67), channel_id=1, source_target_pairs={{0,4},{1,5},{2,6},{3,7},{4,0},{5,1},{6,2},{7,3},{8,12},{9,13},{10,... | collective-permute-start | bytes 331784 | tf_op jit(solution)/shard_map/ppermute | solution.py:37
  256.4 1.5 collective-permute-start.46
  (1 other events, 1.2 us)

commit v4 on v3

--- a/solution.py
+++ b/solution.py
@@ -21,6 +21,8 @@
         return z, c ^ 1, t
     if dim == "x":
         return z, c ^ 2, t
+    if dim == "x+core":
+        return z, c ^ 3, t
     if dim == "y":
         return z, c, t ^ 1
     return z ^ int(dim[1:]), c, t
@@ -38,8 +40,8 @@
 
 
 GATHER = (
-    (("z2", "z1", "y", "x"), ("z2", "z1", "x", "y")),
-    (("z2", "z1", "y", "x"), ("z2", "z1", "x", "y")),
+    (("z2", "z1", "y", "x"), ("z1", "z2", "x", "y")),
+    (("z2", "z1", "y", "x"), ("z1", "z2", "x", "y")),
     (("z2", "z1", "x", "y"), ("y", "x", "z2", "z1")),
 )
 SCATTER = (
@@ -49,6 +51,7 @@
 )
 CORE = ("core", "core")
 X = ("x", "x")
+FAR = ("x+core", "x+core")
 Y = ("y", "y")
 
 
@@ -91,23 +94,33 @@
     return lax.optimization_barrier(values)
 
 
-def piece_copies(spots, own_ref, sib_ref, sem, whole, low, cols, collect, base=0):
+def at_rows(place, count, unit=0):
+    start = place * count
+    return pl.ds(start if isinstance(start, int) else pl.multiple_of(start, unit or count), count)
+
+
+def piece_copies(spots, own_ref, sib_ref, sem, whole, low, cols, base=0):
     rows = whole.shape[0] // 16
-    stride = whole.shape[1] // 2
     copies = []
     for half, ref in ((0, own_ref), (1, sib_ref)):
         for i in range(16):
             row, col = spots[half * 16 + i]
-            row, col = row * rows, col * stride
-            if not isinstance(row, int):
-                row, col = pl.multiple_of(row, rows), pl.multiple_of(col, 128)
-            one = ref.at[pl.ds(i * rows, rows), pl.ds(low, cols)]
-            two = whole.at[pl.ds(row, rows), pl.ds(col, cols)]
-            src, dst = (one, two) if collect else (two, one)
-            copy = pltpu.make_async_copy(src, dst, sem.at[base + half * 16 + i])
+            copy = pltpu.make_async_copy(
+                ref.at[pl.ds(i * rows, rows), pl.ds(low, cols)],
+                whole.at[at_rows(row, rows), at_rows(col, cols, 128)],
+                sem.at[base + half * 16 + i],
+            )
             copy.start()
             copies.append(copy)
     return copies
+
+
+def pack(spots, own_ref, sib_ref, whole, low, cols):
+    rows = whole.shape[0] // 16
+    for half, ref in ((0, own_ref), (1, sib_ref)):
+        for i in range(16):
+            row, col = spots[half * 16 + i]
+            ref[i * rows : (i + 1) * rows, low : low + cols] = whole[at_rows(row, rows), at_rows(col, cols, 128)]
 
 
 def finish(copies):
@@ -153,7 +166,7 @@
     low = 0
     for i, out in enumerate(outs):
         cols = out.shape[1] // 2
-        copies += piece_copies(spots, own_ref, sib_ref, sem, out, low, cols, True, 32 * i)
+        copies += piece_copies(spots, own_ref, sib_ref, sem, out, low, cols, 32 * i)
         low += cols
     finish(copies)
 
@@ -168,7 +181,7 @@
         (VMEM,) * len(widths),
         [pltpu.SemaphoreType.DMA((32 * len(widths),))],
         5,
-        1,
+        2,
         (own, sib),
     )
 
@@ -177,6 +190,31 @@
     c = lax.axis_index("ctx") if fast else 0
     own, core, x = refs
     return [(c ^ 0, own, 0), (c ^ 1, core, 0), (c ^ 2, x, 0), (c ^ 3, x, 1)]
+
+
+def tables_kernel(qv_ref, up_ref, *refs):
+    rows, (table_ref, small_ref) = refs[:-2], refs[-2:]
+    table_ref[...] = jnp.zeros_like(table_ref)
+    for i, ref in enumerate(rows):
+        table_ref[i : i + 1, :] = ref[...][None]
+    width = qv_ref.shape[1]
+    small_ref[:, :width] = qv_ref[0:1, :]
+    small_ref[:, width : 2 * width] = qv_ref[1:2, :]
+    small_ref[:, 2 * width :] = up_ref[...][None]
+
+
+def tables(b_qv, b_up, rows):
+    return call(
+        tables_kernel,
+        "tables",
+        (struct((8, rows[0].shape[0]), F32), struct((1, b_qv.size + b_up.size), F32)),
+        [VMEM] * (2 + len(rows)),
+        (VMEM, VMEM),
+        [],
+        1,
+        3,
+        (b_qv, b_up) + tuple(rows),
+    )
 
 
 def project_kernel(weight_ref, own_ref, core_ref, far_ref, small_ref, proj_ref, x_ref, mask_ref, ids, *, fast):
@@ -219,7 +257,7 @@
         (VMEM,) * 3,
         [pltpu.VMEM((8, block), F32)],
         5,
-        6,
+        3,
         (weight,) + tuple(given) + (small,),
     )
 
@@ -269,7 +307,7 @@
         (VMEM, VMEM),
         [],
         12,
-        6,
+        3,
         (proj, mask),
     )
 
@@ -328,14 +366,14 @@
         (VMEM,) * 5,
         [],
         12,
-        6,
+        3,
         (w_out, w_up, mixed0, mixed1, x, table, small),
     )
 
 
 def turn_kernel(
     weight_ref, act_ref, normed_ref, own_ref, core_ref, far_ref, table_ref,
-    chunks_ref, gz_ref, gzb_ref, sums_ref, down_own, down_sib, full, cot_ref, sem, *, orders,
+    chunks_ref, gz_ref, gzb_ref, sums_ref, down_own, down_sib, full, cot_ref, *, orders,
 ):
     length = act_ref.shape[0]
     block = chunks_ref.shape[1]
@@ -374,7 +412,7 @@
         here = pl.ds(at, 1024)
         full[:, here] = jnp.dot(back_t, act_ref[:, here], preferred_element_type=F32).astype(BF16)
 
-    finish(piece_copies(places(orders), down_own, down_sib, sem, full, 0, down_own.shape[1], False))
+    pack(places(orders), down_own, down_sib, full, 0, down_own.shape[1])
 
 
 def turn(orders, weight, act, normed, cot, table, chunk):
@@ -393,8 +431,8 @@
             piece,
         ),
         [VMEM] * 7,
-        (VMEM, VMEM, VMEM, VMEM, ANY, ANY),
-        [pltpu.VMEM((width, units), BF16), pltpu.VMEM((length, width), BF16), pltpu.SemaphoreType.DMA((32,))],
+        (VMEM,) * 6,
+        [pltpu.VMEM((width, units), BF16), pltpu.VMEM((length, width), BF16)],
         14,
         10,
         (weight, act, normed) + tuple(cot) + (table,),
@@ -421,14 +459,14 @@
         (VMEM, VMEM),
         [],
         12,
-        6,
+        3,
         (weight, gzb, slope),
     )
 
 
 def first_back_kernel(
     w_out, w_up, gh_ref, gz_ref, normed_ref, scale_ref, table_ref, first_ref, mixed0_ref, mixed1_ref,
-    gz1_ref, gm_ref, sums_ref, pieces_own, pieces_sib, branch, d_out, d_up, sem, *, orders,
+    gz1_ref, gm_ref, sums_ref, pieces_own, pieces_sib, branch, d_out, d_up, *, orders,
 ):
     narrow = w_out.shape[1] // 2
     half = w_up.shape[1] // 2
@@ -441,7 +479,7 @@
         here = pl.ds(at, 1024)
         d_up[:, here] = jnp.dot(first_t, gh_ref[:, here], preferred_element_type=F32).astype(BF16)
 
-    sent = piece_copies(spots, pieces_own, pieces_sib, sem, d_up, narrow, half, False)
+    pack(spots, pieces_own, pieces_sib, d_up, narrow, half)
     gz1_ref[...] = lax.dot_general(gh_ref[...], w_up[...], NT, preferred_element_type=F32)
     sums_ref[...] = jnp.zeros_like(sums_ref)
 
@@ -461,9 +499,8 @@
     branch_t = branch[...].T
     d_out[:, :narrow] = jnp.dot(branch_t, mixed0_ref[...], preferred_element_type=F32).astype(BF16)
     d_out[:, narrow:] = jnp.dot(branch_t, mixed1_ref[...], preferred_element_type=F32).astype(BF16)
-    sent += piece_copies(spots, pieces_own, pieces_sib, sem, d_out, 0, narrow, False, 32)
+    pack(spots, pieces_own, pieces_sib, d_out, 0, narrow)
     gm_ref[...] = jnp.dot(branch[...], w_out[...], preferred_element_type=F32).astype(BF16)
-    finish(sent)
 
 
 def first_back(orders, w_out, w_up, gh, gz, normed, scale, table, first_b, mixed0, mixed1):
@@ -481,15 +518,14 @@
             piece,
         ),
         [VMEM] * 10,
-        (VMEM, VMEM, VMEM, ANY, ANY),
+        (VMEM,) * 5,
         [
             pltpu.VMEM((length, width), BF16),
             pltpu.VMEM((width, width), BF16),
             pltpu.VMEM((width, units), BF16),
-            pltpu.SemaphoreType.DMA((64,)),
         ],
         20,
-        14,
+        12,
         (w_out, w_up, gh, gz, normed, scale, table, first_b, mixed0, mixed1),
     )
 
@@ -540,13 +576,13 @@
         (VMEM,) * 3,
         [pltpu.VMEM((length, length), BF16), pltpu.VMEM((128, length), BF16)],
         2,
-        6,
+        4,
         (proj, probs, grad_mixed),
     )
 
 
 def last_kernel(x_ref, sums1_ref, sums2_ref, sum_up_ref, *refs, orders):
-    parts, (pieces_own, pieces_sib, whole, vec, sem) = refs[:6], refs[6:]
+    parts, (pieces_own, pieces_sib, whole, vec) = refs[:6], refs[6:]
     half = parts[0].shape[1]
     rows = whole.shape[0]
     x_t = x_ref[...].T
@@ -558,7 +594,7 @@
             whole[:, at : at + half] = jnp.dot(x_t, value, preferred_element_type=F32).astype(BF16)
             if which != 1:
                 sums[which // 2].append(jnp.sum(value.astype(F32), axis=0, keepdims=True))
-    sent = piece_copies(places(orders), pieces_own, pieces_sib, sem, whole, 0, 3 * half, False)
+    pack(places(orders), pieces_own, pieces_sib, whole, 0, 3 * half)
     vectors = sums[0] + sums[1] + [ref[i : i + 1, :] for ref in (sums1_ref, sums2_ref) for i in range(3)]
     at = 0
     across = vec.shape[1] // 128
@@ -570,7 +606,6 @@
         vec[row : row + 1, :] = jnp.concatenate(wide[row * across : (row + 1) * across], axis=1)
     pieces_own[rows:, :] = vec[...].astype(BF16)
     pieces_sib[rows:, :] = vec[...].astype(BF16)
-    finish(sent)
 
 
 def last(orders, x, sums1, sums2, sum_up, parts):
@@ -585,10 +620,9 @@
         [
             pltpu.VMEM((width, 3 * width), BF16),
             pltpu.VMEM((8, 3 * width // 2), F32),
-            pltpu.SemaphoreType.DMA((32,)),
         ],
         1,
-        8,
+        7,
         (x, sums1, sums2, sum_up) + tuple(parts),
     )
 
@@ -692,7 +726,7 @@
         VMEM,
         [],
         3,
-        6,
+        7,
         (own, core, x, y),
     )
 
@@ -725,7 +759,7 @@
         VMEM,
         [],
         1,
-        6,
+        3,
         (weight, gz1) + tuple(parts),
     )
 
@@ -758,7 +792,7 @@
         (VMEM,) * len(cuts),
         [pltpu.VMEM((4 * rows, cols), F32)],
         3,
-        6,
+        7,
         (pair, got),
     )
 
@@ -826,8 +860,6 @@
     ids = jnp.pad(ids, ((0, 0), (0, 7), (0, width - local_len)))
     rows_in = jnp.concatenate([mine(layer_input), ids], axis=1)
     cot_in = mine(out_grad)
-    small = jnp.concatenate([b_qv.reshape(-1), b_up])[None]
-    table = jnp.stack([b_out, ln1_gain, ln1_bias, b_down, ln2_gain, ln2_bias, b_out, b_out])
     gathers = GATHER if fast else (None,) * 3
     packs = tuple(packing(order) for order in SCATTER) if fast else (None,) * 3
 
@@ -847,37 +879,43 @@
             return [lax.dynamic_index_in_dim(value, c ^ i, 0, keepdims=True) for i in range(4)]
 
         part = shard_rows // 4
-        h1, h2, h3 = [lax.dynamic_slice_in_dim(s, c * part, part, 0) for s in shards]
-        x0, x1, x2, x3 = seen(rows_in)
-        g1, xk = phase(swap(h1, 0, 0), exchange(joined(x1, x3), CORE, sizes))
+        h1 = lax.dynamic_slice_in_dim(w_qkv, c * part, part, 1)
+        h1 = jnp.swapaxes(h1, 0, 1).reshape(part, 3 * local_width)
+        h2, h3 = [lax.dynamic_slice_in_dim(s, c * part, part, 0) for s in shards[1:]]
+        g1 = swap(h1, 0, 0)
+        x0, x1, x2, x3 = seen(after(rows_in, h1))
+        g1, x1, x2, x3, h2, h3, cot_in, b_up = phase(g1, x1, x2, x3, h2, h3, cot_in, b_up)
         h1 = joined(h1, g1)
-        g1, xx, table = phase(swap(h1, 0, 1), exchange(joined(x2, xk[1:]), X, sizes), table)
-        given = (x0, xk, xx)
-        h1 = joined(h1, g1)
-        h1, h2, small, cot_in = phase(h1, h2, small, cot_in)
+        g1, g3, xk, xx, xd = phase(
+            swap(h1, 0, 1), swap(h3, 2, 0), exchange(x1, CORE, sizes), exchange(x2, X, sizes), exchange(x3, FAR, sizes)
+        )
+        given = (x0, xk, joined(xx, xd))
+        h1, h2, h3, cot_in, b_up = phase(joined(h1, g1), h2, joined(h3, g3), cot_in, b_up)
+        g1, g2, g3 = swap(h1, 0, 2), swap(h2, 1, 0), swap(h3, 2, 1)
         c0, c1, c2, c3 = seen(cot_in)
-        g1, g2, got, ck = phase(
-            swap(h1, 0, 2), swap(h2, 1, 0), exchange(small, Y, sizes), exchange(joined(c1, c3), CORE, sizes)
+        c_send = joined(c1, c3)
+        table, small = tables(b_qv, b_up, (b_out, ln1_gain, ln1_bias, b_down, ln2_gain, ln2_bias))
+        g1, g2, g3, c_send, small = phase(g1, g2, g3, c_send, small)
+        h1, h2, h3 = phase(joined(h1, g1), joined(h2, g2), joined(h3, g3))
+        g1, g2, ck, got = phase(
+            swap(h1, 0, 3), swap(h2, 1, 1), exchange(c_send, CORE, sizes), exchange(small, Y, sizes)
         )
         small = joined(small, got)
-        h1, h2 = phase(joined(h1, g1), joined(h2, g2))
-        g1, g2 = phase(swap(h1, 0, 3), swap(h2, 1, 1))
         h1, h2, h3 = phase(joined(h1, g1), joined(h2, g2), h3)
-        g1, g2, g3 = swap(h1, 0, 4), swap(h2, 1, 2), swap(h3, 2, 0)
+        g1, g2, g3 = swap(h1, 0, 4), swap(h2, 1, 2), swap(h3, 2, 2)
         (wq,) = unpack(gathers[0], h1, g1, (3 * width,))
         proj, rows_b, mask = project(wq, given, small, fast)
-        proj, g2, g3, c2, ck = phase(proj, g2, g3, c2, ck)
-        h2, h3 = joined(h2, g2), joined(h3, g3)
-        g2, g3 = swap(h2, 1, 3), swap(h3, 2, 1)
-        mixed0, probs0 = attend(after(proj, h2, h3), mask, 0)
+        proj, g2, c2, ck = phase(proj, g2, c2, ck)
+        h2 = joined(h2, g2)
+        g2 = swap(h2, 1, 3)
+        mixed0, probs0 = attend(after(proj, h2), mask, 0)
         mixed0, g3 = phase(mixed0, g3)
         h3 = joined(h3, g3)
-        g3 = swap(h3, 2, 2)
+        g3 = swap(h3, 2, 3)
         mixed1, probs1 = attend(after(proj, h3, mixed0), mask, 1)
-        mixed1, g2, g3 = phase(mixed1, g2, g3)
-        h2, h3, c_send = phase(joined(h2, g2), joined(h3, g3), joined(c2, ck[1:]))
-        g2, g3, cx = swap(h2, 1, 4), swap(h3, 2, 3), exchange(c_send, X, sizes)
-        cot = (c0, ck, cx)
+        mixed1, g2 = phase(mixed1, g2)
+        h2, c_send = phase(joined(h2, g2), joined(c2, ck[1:]))
+        g2, cx = swap(h2, 1, 4), exchange(c_send, X, sizes)
         wo, wu = unpack(gathers[1], h2, g2, (width, 2 * local_units))
     else:
         parts = (shards[0], w_out.T, w_up, w_down.T)
@@ -888,6 +926,7 @@
         (wd,) = unpack(None, *pieces[3], (2 * local_units,))
         order = lambda value: (value[:1], value[1:3], value[2:])
         given, cot = order(to_owners(rows_in)), order(to_owners(cot_in))
+        table, small = tables(b_qv, b_up, (b_out, ln1_gain, ln1_bias, b_down, ln2_gain, ln2_bias))
         small = joined(small, exchange(small, Y, sizes))
         proj, rows_b, mask = project(wq, given, small, fast)
         mixed0, probs0 = attend(proj, mask, 0)
@@ -949,47 +988,59 @@
         sent3 = add_up(qkv, 8 * rows, 16 * rows, (0, 1))
         x_send = joined(chunks2[1:2], core_x[1:2])
         got3 = shed(sent3, 0, 1)
-        sent3, x_send, got = phase(sent3, x_send, got)
+        got3, x_send = phase(got3, x_send)
+        qkv = qkv + [got3]
+        send3 = add_up(qkv, 4 * rows, 8 * rows, (3, 2), [sent3])
+        got3 = shed(send3, 0, 2)
+        send3, got, x_send = phase(send3, got, x_send)
         down = down + [got]
-        got = shed(add_up(down, rows, 2 * rows), 2, 4)
-        got3, got2 = phase(got3, got2)
-        up, qkv = up + [got2], qkv + [got3]
-        send3 = add_up(qkv, 4 * rows, 8 * rows, (3, 2), [sent3])
+        send = add_up(down, rows, 2 * rows)
+        got, x_x = shed(send, 2, 4), exchange(x_send, X, sizes)
+        send, got2 = phase(send, got2)
+        up = up + [got2]
         send2 = add_up(up, 2 * rows, 4 * rows)
-        send3, send2, x_send, got = phase(send3, send2, x_send, got)
-        got3, got2, x_x = shed(send3, 0, 2), shed(send2, 1, 3), exchange(x_send, X, sizes)
+        got2 = shed(send2, 1, 3)
+        got3, send2 = phase(got3, send2)
+        qkv = qkv + [got3]
+        sent3 = add_up(qkv, 2 * rows, 4 * rows, (4, 3), [send3])
+        got3 = shed(sent3, 0, 3)
+        sent3, got, x_x = phase(sent3, got, x_x)
         pair1 = add_up(down + [got], 0, rows)
-        pair1, send3 = phase(pair1, send3)
-        got = exchange(pair1, X, sizes)
-        got3, got2, got, x_x = phase(got3, got2, got, x_x)
-        up, qkv = up + [got2], qkv + [got3]
-        sent3 = add_up(qkv, 2 * rows, 4 * rows, (4, 3), [send3])
+        y_send = joined(chunks2[:1], core_x[:1], x_x)
+        got, y_x = exchange(pair1, X, sizes), exchange(y_send, Y, sizes)
+        pair1, got2 = phase(pair1, got2)
+        up = up + [got2]
         send2 = add_up(up, rows, 2 * rows)
-        pair1, y_send = joined(pair1, got), joined(chunks2[:1], core_x[:1], x_x)
-        sent3, send2, pair1, y_send = phase(sent3, send2, pair1, y_send)
-        got3, got2, got1 = shed(sent3, 0, 3), shed(send2, 1, 4), exchange(pair1, CORE, sizes)
-        y_x = exchange(y_send, Y, sizes)
-        layer_output = deliver(chunks, core_out, x_out, y_out)
-        got3, got2, got1, layer_output = phase(got3, got2, got1, layer_output)
-        up, qkv = up + [got2], qkv + [got3]
+        got2 = shed(send2, 1, 4)
+        layer_output = deliver(chunks, core_out, x_out, after(y_out, send2))
+        got3, layer_output = phase(got3, layer_output)
+        qkv = qkv + [got3]
         send3 = add_up(qkv, rows, 2 * rows, (5, 4), [sent3])
+        got3 = shed(send3, 0, 4)
+        send3, got, got2 = phase(send3, got, got2)
+        pair1 = joined(pair1, got)
+        up = up + [got2]
         pair2 = add_up(up, 0, rows)
-        send3, pair2, got1 = phase(send3, pair2, got1)
-        got3, got2 = shed(send3, 0, 4), exchange(pair2, X, sizes)
+        got1, got2 = exchange(pair1, CORE, sizes), exchange(pair2, X, sizes)
+        got3, pair1, pair2 = phase(got3, pair1, pair2)
+        qkv = qkv + [got3]
+        pair3 = add_up(qkv, 0, rows)
+        got = exchange(pair3, X, sizes)
+        vec = vectors(after(send3, pair3), got3, local_width, local_units)
+        pair3, got1, bup = phase(pair3, got1, vec[1])
+        vec = (vec[0], bup) + tuple(vec[2:])
         (grad_down,) = settle(pair1, got1, ((0, local_units, "plain"),))
-        got3, got2, grad_down, y_x = phase(got3, got2, grad_down, y_x)
-        qkv = qkv + [got3]
-        pair3, pair2 = phase(add_up(qkv, 0, rows), joined(pair2, got2))
-        got, got2 = exchange(pair3, X, sizes), exchange(pair2, CORE, sizes)
-        vec = vectors(after(send3, pair3), got3, local_width, local_units)
+        grad_down, got2 = phase(grad_down, got2)
+        pair2 = joined(pair2, got2)
+        got2 = exchange(pair2, CORE, sizes)
+        got, pair2 = phase(got, pair2)
+        pair3 = joined(pair3, got)
+        got3 = exchange(pair3, CORE, sizes)
+        pair3, got2 = phase(pair3, got2)
         grad_wout, grad_up = settle(
             pair2, got2, ((0, local_width, "plain"), (local_width, local_width + local_units, "plain"))
         )
-        got, grad_up, bup = phase(got, grad_up, vec[1])
-        vec = (vec[0], bup) + tuple(vec[2:])
-        pair3 = joined(pair3, got)
-        got3 = exchange(pair3, CORE, sizes)
-        grad_x = deliver(chunks2, core_x, x_x, y_x)
+        grad_x = deliver(chunks2, core_x, x_x, after(y_x, grad_up))
         (grad_qkv,) = settle(pair3, after(got3, grad_x), ((0, 3 * local_width, "three"),))
         layer_output = layer_output.reshape(micro, seqs, local_len, width)
         grad_x = grad_x.reshape(micro, seqs, local_len, width)

time: 259 us -> 243 us (0.938)
  waiting for transfers between devices: 121 us -> 103 us
  starting transfers between devices: 40.2 us -> 50.9 us
  Pallas kernels: 84.1 us -> 79.2 us
  local copies, waits for them, and re-layouts: 9.94 us -> 6.4 us
    ppermute x47 -> x48, waiting for transfers between devices: 121 us -> 103 us  [exchange(): return lax.ppermute(value, AXES, pairs)]
    ppermute x47 -> x48, starting transfers between devices: 40.2 us -> 50.9 us  [exchange(): return lax.ppermute(value, AXES, pairs)]
    pallas_call x35 -> x36, Pallas kernels: 84.1 us -> 79.2 us  [call(): pl.pallas_call(kernel, name=name, out_shape=outs, in_specs=specs, out_spe...]
    unnamed x40 -> x43, local copies, waits for them, and re-layouts: 6.74 us -> 3.71 us
  transfers between devices with their start and end apart: 47 -> 48, of which waited for: 23 -> 26; matrix products, arithmetic and copies ran while one was open for 1% -> 2% of each run, Pallas kernels for 27% -> 27%
where the time goes in v4:
time: 243 us; the launch traced here: 242 us
  waiting for transfers between devices  103 us (42%)
  Pallas kernels  79.2 us (33%)
  starting transfers between devices  50.9 us (21%)
  local copies, waits for them, and re-layouts  6.4 us (3%)
    ppermute x48, waiting for transfers between devices, exchange(): return lax.ppermute(value, AXES, pairs)  103 us
    pallas_call x36, Pallas kernels, call(): pl.pallas_call(kernel, name=name, out_shape=outs, in_specs=specs, out_spe...  79.2 us
    ppermute x48, starting transfers between devices, exchange(): return lax.ppermute(value, AXES, pairs)  50.9 us
  transfers between devices with their start and end apart: 48, of which 26 were waited for; matrix products, arithmetic and copies ran while one was open for 2% of the time, Pallas kernels for 27%

profile of v4, /device:TPU:0, one launch (start us, length us, event | category | flops | bytes accessed | tf_op | source)
XLA Modules:
  0.0 242.3 jit_solution(16727694590491744613)
XLA Ops:
  0.7 1.0 dynamic-slice_bitcast_fusion.3
  1.7 4.1 %collective-permute-start = (bf16[48,1152]{1,0:T(8,128)(2,1)S(1)}, bf16[48,1152]{1,0:T(8,128)(2,1)S(1)}, u32[]{:S(2)}, u32[]{:S(2)}) collective-permute-start(bf16[48,1152]{1,0:T(8,128)(2,1)S(1)} %bitcast.15), channel_id=1, source_target_pairs={{0,16},{1,17},{2,10},{3,11},{4,20},{5,21},{6,14},{7,15},{8,24},{9,... | collective-permute-start | bytes 331784 | tf_op jit(solution)/shard_map/ppermute | solution.py:39
  5.9 0.9 dynamic-slice_bitcast_fusion.2
  7.7 1.2 dynamic-slice_bitcast_fusion
  9.1 1.8 collective-permute-start.1
  10.9 1.5 collective-permute-start.4
  12.7 3.4 %collective-permute-start.2 = (bf16[48,1536]{1,0:T(8,128)(2,1)S(1)}, bf16[48,1536]{1,0:T(8,128)(2,1)S(1)}, u32[]{:S(2)}, u32[]{:S(2)}) collective-permute-start(bf16[48,1536]{1,0:T(8,128)(2,1)S(1)} %dynamic-slice_bitcast_fusion.2), channel_id=1, source_target_pairs={{0,16},{1,17},{2,3},{3,2},{4,20},{5,21},{6,7},{7,6},{8,24},{9,25},... | collective-permute-start | bytes 442376 | tf_op jit(solution)/shard_map/ppermute | solution.py:39
  16.1 4.6 %collective-permute-done.2 = bf16[48,1536]{1,0:T(8,128)(2,1)S(1)} collective-permute-done((bf16[48,1536]{1,0:T(8,128)(2,1)S(1)}, bf16[48,1536]{1,0:T(8,128)(2,1)S(1)}, u32[]{:S(2)}, u32[]{:S(2)}) %collective-permute-start.2) | collective-permute-done | bytes 147488 | tf_op jit(solution)/shard_map/ppermute | solution.py:39
  20.8 1.8 collective-permute-done.5
  22.6 1.6 collective-permute-start.6
  24.2 3.4 %collective-permute-start.7 = (bf16[48,1920]{1,0:T(8,128)(2,1)S(1)}, bf16[48,1920]{1,0:T(8,128)(2,1)S(1)}, u32[]{:S(2)}, u32[]{:S(2)}) collective-permute-start(bf16[48,1920]{1,0:T(8,128)(2,1)S(1)} %fusion.2), channel_id=1, source_target_pairs={{0,16},{1,17},{2,10},{3,11},{4,20},{5,21},{6,14},{7,15},{8,24},{9,... | collective-permute-start | bytes 552968 | tf_op jit(solution)/shard_map/ppermute | solution.py:39
  27.8 4.8 %collective-permute-done.7 = bf16[48,1920]{1,0:T(8,128)(2,1)S(1)} collective-permute-done((bf16[48,1920]{1,0:T(8,128)(2,1)S(1)}, bf16[48,1920]{1,0:T(8,128)(2,1)S(1)}, u32[]{:S(2)}, u32[]{:S(2)}) %collective-permute-start.7) | collective-permute-done | bytes 184352 | tf_op jit(solution)/shard_map/ppermute | solution.py:39
  32.6 2.8 %collective-permute-done.8 = bf16[96,1536]{1,0:T(8,128)(2,1)S(1)} collective-permute-done((bf16[96,1536]{1,0:T(8,128)(2,1)S(1)}, bf16[96,1536]{1,0:T(8,128)(2,1)S(1)}, u32[]{:S(2)}, u32[]{:S(2)}) %collective-permute-start.8) | collective-permute-done | bytes 294944 | tf_op jit(solution)/shard_map/ppermute | solution.py:39
  35.6 1.4 collective-permute-start.9
  37.0 1.1 collective-permute-start.10
  38.5 3.3 %collective-permute-done.12 = f32[1,2304]{1,0:T(1,128)S(1)} collective-permute-done((f32[1,2304]{1,0:T(1,128)S(1)}, f32[1,2304]{1,0:T(1,128)S(1)}, u32[]{:S(2)}, u32[]{:S(2)}) %collective-permute-start.12) | collective-permute-done | bytes 9248 | tf_op jit(solution)/shard_map/ppermute | solution.py:39
  41.9 6.6 %collective-permute-done.10 = bf16[96,1920]{1,0:T(8,128)(2,1)S(1)} collective-permute-done((bf16[96,1920]{1,0:T(8,128)(2,1)S(1)}, bf16[96,1920]{1,0:T(8,128)(2,1)S(1)}, u32[]{:S(2)}, u32[]{:S(2)}) %collective-permute-start.10) | collective-permute-done | bytes 368672 | tf_op jit(solution)/shard_map/ppermute | solution.py:39
  49.0 1.4 collective-permute-start.15
  51.2 0.9 constant_dynamic-update-slice_fusion.6
  52.7 1.3 unpack.3.refs_0_
  54.0 2.6 %project.1 = (bf16[512,2304]{1,0:T(8,128)(2,1)S(1)}, bf16[512,768]{1,0:T(8,128)(2,1)S(1)}, f32[512,512]{1,0:T(8,128)S(1)}) custom-call(bf16[768,2304]{1,0:T(8,128)(2,1)S(1)} %unpack.3.refs_0_, bf16[1,136,768]{2,1,0:T(8,128)(2,1)S(1)} %get-tuple-element.340.refs_1_, bf16[1,136,768]{2,1,0:T(8,128)(2,1)S(1)} %collective-permute-done.3.refs_2_, ...), custom_call_target="tpu_custom_call" | custom-call | flops 5000000000 | bytes 1000000 | tf_op jit(solution)/shard_map/project/pallas_call | solution.py:147
  56.7 5.2 %collective-permute-done.14 = bf16[192,1920]{1,0:T(8,128)(2,1)S(1)} collective-permute-done((bf16[192,1920]{1,0:T(8,128)(2,1)S(1)}, bf16[192,1920]{1,0:T(8,128)(2,1)S(1)}, u32[]{:S(2)}, u32[]{:S(2)}) %collective-permute-start.14) | collective-permute-done | bytes 737312 | tf_op jit(solution)/shard_map/ppermute | solution.py:39
  62.0 0.8 collective-permute-start.16
  62.8 6.7 %attend.2 = (bf16[512,384]{1,0:T(8,128)(2,1)S(1)}, bf16[6,512,512]{2,1,0:T(8,128)(2,1)S(1)}) custom-call(bf16[512,2304]{1,0:T(8,128)(2,1)S(1)} %get-tuple-element.221.refs_0_, f32[512,512]{1,0:T(8,128)S(1)} %get-tuple-element.217.refs_1_), custom_call_target="tpu_custom_call" | custom-call | flops 12000000000 | bytes 1000000 | tf_op jit(solution)/shard_map/attend/pallas_call | solution.py:147
  69.4 0.9 constant_dynamic-update-slice_fusion.5
  70.4 6.7 %attend.3 = (bf16[512,384]{1,0:T(8,128)(2,1)S(1)}, bf16[6,512,512]{2,1,0:T(8,128)(2,1)S(1)}) custom-call(bf16[512,2304]{1,0:T(8,128)(2,1)S(1)} %get-tuple-element.221.refs_0_, f32[512,512]{1,0:T(8,128)S(1)} %get-tuple-element.217.refs_1_), custom_call_target="tpu_custom_call" | custom-call | flops 12000000000 | bytes 1000000 | tf_op jit(solution)/shard_map/attend/pallas_call | solution.py:147
  77.1 5.6 %collective-permute-done.16 = bf16[384,1920]{1,0:T(8,128)(2,1)S(1)} collective-permute-done((bf16[384,1920]{1,0:T(8,128)(2,1)S(1)}, bf16[384,1920]{1,0:T(8,128)(2,1)S(1)}, u32[]{:S(2)}, u32[]{:S(2)}) %collective-permute-start.16) | collective-permute-done | bytes 1474592 | tf_op jit(solution)/shard_map/ppermute | solution.py:39
  82.9 4.0 %collective-permute-start.17 = (bf16[768,1920]{1,0:T(8,128)(2,1)S(1)}, bf16[768,1920]{1,0:T(8,128)(2,1)S(1)}, u32[]{:S(2)}, u32[]{:S(2)}) collective-permute-start(bf16[768,1920]{1,0:T(8,128)(2,1)S(1)} %pad_maximum_fusion.refs_0_), channel_id=1, source_target_pairs={{0,2},{1,3},{2,0},{3,1},{4,6},{5,7},{6,4},{7,5},{8,10},{9,11},{10,... | collective-permute-start | bytes 8847368 | tf_op jit(solution)/shard_map/ppermute | solution.py:39
  87.3 2.0 collective-permute-start.19
  89.3 2.6 %collective-permute-done.17.refs_1_ = bf16[768,1920]{1,0:T(8,128)(2,1)S(1)} collective-permute-done((bf16[768,1920]{1,0:T(8,128)(2,1)S(1)}, bf16[768,1920]{1,0:T(8,128)(2,1)S(1)}, u32[]{:S(2)}, u32[]{:S(2)}) %collective-permute-start.17) | collective-permute-done | bytes 2949152 | tf_op jit(solution)/shard_map/ppermute | solution.py:39
  91.9 2.3 unpack.4
  94.3 8.7 %middle.1 = (f32[512,768]{1,0:T(8,128)S(1)}, f32[512,1]{1,0:T(8,128)S(1)}, bf16[512,768]{1,0:T(8,128)(2,1)S(1)}, bf16[512,3072]{1,0:T(8,128)(2,1)S(1)}, bf16[512,3072]{1,0:T(8,128)(2,1)S(1)}) custom-call(bf16[768,768]{1,0:T(8,128)(2,1)S(1)} %get-tuple-element.227.w_out.refs_0_, bf16[768,3072]{1,0:T(8,128)(2,1)S(1)} %get-tuple-element.228.w_up.refs_1_, ...), custom_call_target="tpu_custom_call" | custom-call | flops 12000000000 | bytes 1000000 | tf_op jit(solution)/shard_map/middle/pallas_call | solution.py:147
  103.6 4.4 %collective-permute-done.20.refs_1_ = bf16[768,1536]{1,0:T(8,128)(2,1)S(1)} collective-permute-done((bf16[768,1536]{1,0:T(8,128)(2,1)S(1)}, bf16[768,1536]{1,0:T(8,128)(2,1)S(1)}, u32[]{:S(2)}, u32[]{:S(2)}) %collective-permute-start.20) | collective-permute-done | bytes 2359328 | tf_op jit(solution)/shard_map/ppermute | solution.py:39
  108.0 1.6 unpack.5.refs_0_.weight_ref
  109.6 9.1 %turn.1 = (bf16[4,128,768]{2,1,0:T(8,128)(2,1)S(1)}, f32[512,768]{1,0:T(8,128)S(1)}, bf16[512,768]{1,0:T(8,128)(2,1)S(1)}, f32[8,768]{1,0:T(8,128)S(1)}, bf16[76...) custom-call(bf16[768,3072]{1,0:T(8,128)(2,1)S(1)} %unpack.5.refs_0_.weight_ref, ...), custom_call_target="tpu_custom_call" | custom-call | flops 14000000000 | bytes 1000000 | tf_op jit(solution)/shard_map/turn/pallas_call | solution.py:147
  119.4 3.8 %hidden_back.1 = (bf16[512,3072]{1,0:T(8,128)(2,1)S(1)}, f32[1,3072]{1,0:T(1,128)S(1)}) custom-call(bf16[768,3072]{1,0:T(8,128)(2,1)S(1)} %unpack.5.refs_0_.weight_ref, bf16[512,768]{1,0:T(8,128)(2,1)S(1)} %get-tuple-element.241.gzb_ref, bf16[512,3072]{1,0:T(8,128)(2,1)S(1)} %get-tuple-element.242.slope_ref), custom_call_target="tpu_custom_call" | custom-call | flops 12000000000 | bytes 1000000 | tf_op jit(solution)/shard_map/hidden_back/pallas_call | solution.py:147
  124.3 1.9 collective-permute-start.24
  126.8 10.6 %first_back.1 = (f32[512,768]{1,0:T(8,128)S(1)}, bf16[512,768]{1,0:T(8,128)(2,1)S(1)}, f32[8,768]{1,0:T(8,128)S(1)}, bf16[768,1920]{1,0:T(8,128)(2,1)S(1)}, bf16[768,1920]{1,0:T(8,128)(2,1)S(1)}) custom-call(bf16[768,768]{1,0:T(8,128)(2,1)S(1)} %get-tuple-element.227.w_out.refs_0_, bf16[768,3072]{1,0:T(8,128)(2,1)S(1)} %get-tuple-element.228.w_up.refs_1_, ...), custom_call_target="tpu_custom_call" | custom-call | flops 20000000000 | bytes 1000000 | tf_op jit(solution)/shard_map/first_back/pallas_call | solution.py:147
  137.4 5.1 %collective-permute-done.23.refs_2_ = bf16[384,1536]{1,0:T(8,128)(2,1)S(1)} collective-permute-done((bf16[384,1536]{1,0:T(8,128)(2,1)S(1)}, bf16[384,1536]{1,0:T(8,128)(2,1)S(1)}, u32[]{:S(2)}, u32[]{:S(2)}) %collective-permute-start.23) | collective-permute-done | bytes 1179680 | tf_op jit(solution)/shard_map/ppermute | solution.py:39
  142.7 5.3 %attend_back.2 = (bf16[512,384]{1,0:T(8,128)(2,1)S(1)}, bf16[512,384]{1,0:T(8,128)(2,1)S(1)}, bf16[512,384]{1,0:T(8,128)(2,1)S(1)}) custom-call(bf16[512,2304]{1,0:T(8,128)(2,1)S(1)} %get-tuple-element.221.refs_0_, bf16[6,512,512]{2,1,0:T(8,128)(2,1)S(1)} %get-tuple-element.256.refs_1_, bf16[512,768]{1,0:T(8,128)(2,1)S(1)} %get-tuple-element.276.refs_2_), custom_call_target="tpu_custom_call" | custom-call | flops 2000000000 | bytes 1000000 | tf_op jit(solution)/shard_map/attend_back/pallas_call | solution.py:147
  149.1 1.9 collective-permute-start.26
  151.0 5.6 %attend_back.3 = (bf16[512,384]{1,0:T(8,128)(2,1)S(1)}, bf16[512,384]{1,0:T(8,128)(2,1)S(1)}, bf16[512,384]{1,0:T(8,128)(2,1)S(1)}) custom-call(bf16[512,2304]{1,0:T(8,128)(2,1)S(1)} %get-tuple-element.221.refs_0_, bf16[6,512,512]{2,1,0:T(8,128)(2,1)S(1)} %get-tuple-element.271.refs_1_, bf16[512,768]{1,0:T(8,128)(2,1)S(1)} %get-tuple-element.276.refs_2_), custom_call_target="tpu_custom_call" | custom-call | flops 2000000000 | bytes 1000000 | tf_op jit(solution)/shard_map/attend_back/pallas_call | solution.py:147
  156.6 2.7 %input_back.1.own_ref = bf16[4,128,768]{2,1,0:T(8,128)(2,1)S(1)} custom-call(bf16[768,2304]{1,0:T(8,128)(2,1)S(1)} %unpack.3.refs_0_, f32[512,768]{1,0:T(8,128)S(1)} %get-tuple-element.268.refs_1_, bf16[512,384]{1,0:T(8,128)(2,1)S(1)} %get-tuple-element.280.refs_2_.refs_4_, bf16[512,384]{1,0:T(8,128)(2,1)S(1)} %get-tuple-element.269.refs_3_.refs_5_, ...), custom_call_target="tpu_custom_call" | custom-call | flops 1000000000 | bytes 1000000 | tf_op jit(solution)/shard_map/input_back/pallas_call | solution.py:147
  159.4 2.9 %last.1 = (bf16[776,1152]{1,0:T(8,128)(2,1)S(1)}, bf16[776,1152]{1,0:T(8,128)(2,1)S(1)}) custom-call(bf16[512,768]{1,0:T(8,128)(2,1)S(1)} %get-tuple-element.209.x_ref.refs_0_, f32[8,768]{1,0:T(8,128)S(1)} %get-tuple-element.253.refs_1_, f32[8,768]{1,0:T(8,128)S(1)} %get-tuple-element.254.refs_2_, f32[1,3072]{1,0:T(1,128)S(1)} %get-tuple-element.255.refs_3_, ...), custom_call_target="tpu_custom_call" | custom-call | flops 1000000000 | bytes 1000000 | tf_op jit(solution)/shard_map/last/pallas_call | solution.py:147
  162.3 11.9 %collective-permute-done.26.refs_3_ = bf16[192,1536]{1,0:T(8,128)(2,1)S(1)} collective-permute-done((bf16[192,1536]{1,0:T(8,128)(2,1)S(1)}, bf16[192,1536]{1,0:T(8,128)(2,1)S(1)}, u32[]{:S(2)}, u32[]{:S(2)}) %collective-permute-start.26) | collective-permute-done | bytes 589856 | tf_op jit(solution)/shard_map/ppermute | solution.py:39
  175.3 3.7 %collective-permute-done.30.core_ref = bf16[2,128,768]{2,1,0:T(8,128)(2,1)S(1)} collective-permute-done((bf16[2,128,768]{2,1,0:T(8,128)(2,1)S(1)}, bf16[2,128,768]{2,1,0:T(8,128)(2,1)S(1)}, u32[]{:S(2)}, u32[]{:S(2)}) %collective-permute-start.30) | collective-permute-done | bytes 393248 | tf_op jit(solution)/shard_map/ppermute | solution.py:39
  179.9 1.3 collective-permute-start.33
  181.2 14.4 %collective-permute-done.31.refs_2_ = bf16[392,1152]{1,0:T(8,128)(2,1)S(1)} collective-permute-done((bf16[392,1152]{1,0:T(8,128)(2,1)S(1)}, bf16[392,1152]{1,0:T(8,128)(2,1)S(1)}, u32[]{:S(2)}, u32[]{:S(2)}) %collective-permute-start.31) | collective-permute-done | bytes 903200 | tf_op jit(solution)/shard_map/ppermute | solution.py:39
  196.6 2.2 collective-permute-done.34.refs_3_
  199.8 1.1 collective-permute-start.36
  200.9 4.8 %collective-permute-done.32.refs_3_ = bf16[200,1152]{1,0:T(8,128)(2,1)S(1)} collective-permute-done((bf16[200,1152]{1,0:T(8,128)(2,1)S(1)}, bf16[200,1152]{1,0:T(8,128)(2,1)S(1)}, u32[]{:S(2)}, u32[]{:S(2)}) %collective-permute-start.32) | collective-permute-done | bytes 460832 | tf_op jit(solution)/shard_map/ppermute | solution.py:39
  205.9 5.3 %collective-permute-done.36.refs_5_ = bf16[48,1536]{1,0:T(8,128)(2,1)S(1)} collective-permute-done((bf16[48,1536]{1,0:T(8,128)(2,1)S(1)}, bf16[48,1536]{1,0:T(8,128)(2,1)S(1)}, u32[]{:S(2)}, u32[]{:S(2)}) %collective-permute-start.36) | collective-permute-done | bytes 147488 | tf_op jit(solution)/shard_map/ppermute | solution.py:39
  212.3 2.7 %collective-permute-start.42 = (bf16[48,1920]{1,0:T(8,128)(2,1)S(1)}, bf16[48,1920]{1,0:T(8,128)(2,1)S(1)}, u32[]{:S(2)}, u32[]{:S(2)}) collective-permute-start(bf16[48,1920]{1,0:T(8,128)(2,1)S(1)} %add.64), channel_id=1, source_target_pairs={{0,16},{1,17},{2,6},{3,7},{4,20},{5,21},{6,2},{7,3},{8,24},{9,25},... | collective-permute-start | bytes 552968 | tf_op jit(solution)/shard_map/ppermute | solution.py:39
  214.9 1.3 deliver.2
  216.3 1.2 collective-permute-start.39
  217.6 8.9 %collective-permute-done.42.refs_5_ = bf16[48,1920]{1,0:T(8,128)(2,1)S(1)} collective-permute-done((bf16[48,1920]{1,0:T(8,128)(2,1)S(1)}, bf16[48,1920]{1,0:T(8,128)(2,1)S(1)}, u32[]{:S(2)}, u32[]{:S(2)}) %collective-permute-start.42) | collective-permute-done | bytes 184352 | tf_op jit(solution)/shard_map/ppermute | solution.py:39
  226.7 3.1 %collective-permute-start.44 = (bf16[96,1536]{1,0:T(8,128)(2,1)S(1)}, bf16[96,1536]{1,0:T(8,128)(2,1)S(1)}, u32[]{:S(2)}, u32[]{:S(2)}) collective-permute-start(bf16[96,1536]{1,0:T(8,128)(2,1)S(1)} %constant_dynamic-update-slice_fusion.7.refs_0_), channel_id=1, source_target_pairs={{0,2},{1,3},{2,0},{3,1},{4,6},{5,7},{6,4},{7,5},{8,10},{9,11},{10,... | collective-permute-start | bytes 884744 | tf_op jit(solution)/shard_map/ppermute | solution.py:39
  231.1 1.2 settle.3
  232.3 1.6 collective-permute-done.45
  233.9 2.9 %collective-permute-start.46 = (bf16[96,1920]{1,0:T(8,128)(2,1)S(1)}, bf16[96,1920]{1,0:T(8,128)(2,1)S(1)}, u32[]{:S(2)}, u32[]{:S(2)}) collective-permute-start(bf16[96,1920]{1,0:T(8,128)(2,1)S(1)} %constant_dynamic-update-slice_fusion.9.refs_0_), channel_id=1, source_target_pairs={{0,2},{1,3},{2,0},{3,1},{4,6},{5,7},{6,4},{7,5},{8,10},{9,11},{10,... | collective-permute-start | bytes 1105928 | tf_op jit(solution)/shard_map/ppermute | solution.py:39
  236.8 1.1 collective-permute-start.47
  238.1 1.2 settle.4
  239.3 1.3 deliver.3
  240.6 1.0 settle.5
  (150 shorter events, 17.1 us)
Async XLA Ops:
  0.6 6.8 %copy-start = (bf16[4,2,128,768]{3,2,1,0:T(8,128)(2,1)S(1)}, bf16[4,2,128,768]{3,2,1,0:T(8,128)(2,1)}, u32[]{:S(2)}) copy-start(bf16[4,2,128,768]{3,2,1,0:T(8,128)(2,1)} %param.15) | copy-start | bytes 4718596
  1.7 5.9 %copy-start.16 = (bf16[192,1536]{1,0:T(8,128)(2,1)S(1)}, bf16[192,1536]{1,0:T(8,128)(2,1)}, u32[]{:S(2)}) copy-start(bf16[192,1536]{1,0:T(8,128)(2,1)} %param.23) | copy-start | bytes 1769476
  1.7 5.9 %copy-start.17 = (bf16[384,192]{0,1:T(8,128)(2,1)S(1)}, bf16[384,192]{0,1:T(8,128)(2,1)}, u32[]{:S(2)}) copy-start(bf16[384,192]{0,1:T(8,128)(2,1)} %param.19) | copy-start | bytes 442372
  1.7 7.3 %collective-permute-start = (bf16[48,1152]{1,0:T(8,128)(2,1)S(1)}, bf16[48,1152]{1,0:T(8,128)(2,1)S(1)}, u32[]{:S(2)}, u32[]{:S(2)}) collective-permute-start(bf16[48,1152]{1,0:T(8,128)(2,1)S(1)} %bitcast.15), channel_id=1, source_target_pairs={{0,16},{1,17},{2,10},{3,11},{4,20},{5,21},{6,14},{7,15},{8,24},{9,... | collective-permute-start | bytes 331784 | tf_op jit(solution)/shard_map/ppermute | solution.py:39
  8.9 18.7 %copy-start.4 = (f32[1536]{0:T(1024)S(1)}, f32[1536]{0:T(1024)}, u32[]{:S(2)}) copy-start(f32[1536]{0:T(1024)} %up_ref) | copy-start | bytes 18436
  9.0 18.7 %copy-start.5 = (f32[768]{0:T(1024)S(1)}, f32[768]{0:T(1024)}, u32[]{:S(2)}) copy-start(f32[768]{0:T(1024)} %refs_0_.1) | copy-start | bytes 9220
  9.0 18.7 %copy-start.6 = (f32[768]{0:T(1024)S(1)}, f32[768]{0:T(1024)}, u32[]{:S(2)}) copy-start(f32[768]{0:T(1024)} %refs_1_.1) | copy-start | bytes 9220
  9.0 18.7 %copy-start.7 = (f32[768]{0:T(1024)S(1)}, f32[768]{0:T(1024)}, u32[]{:S(2)}) copy-start(f32[768]{0:T(1024)} %refs_2_.1) | copy-start | bytes 9220
  9.0 18.7 %copy-start.8 = (f32[768]{0:T(1024)S(1)}, f32[768]{0:T(1024)}, u32[]{:S(2)}) copy-start(f32[768]{0:T(1024)} %refs_3_.1) | copy-start | bytes 9220
  9.0 18.7 %copy-start.9 = (f32[768]{0:T(1024)S(1)}, f32[768]{0:T(1024)}, u32[]{:S(2)}) copy-start(f32[768]{0:T(1024)} %refs_4_.1) | copy-start | bytes 9220
  9.0 18.7 %copy-start.10 = (f32[768]{0:T(1024)S(1)}, f32[768]{0:T(1024)}, u32[]{:S(2)}) copy-start(f32[768]{0:T(1024)} %refs_5_.1) | copy-start | bytes 9220
  9.0 18.7 %copy-start.11 = (f32[2,384]{1,0:T(2,128)S(1)}, f32[2,384]{1,0:T(2,128)}, u32[]{:S(2)}) copy-start(f32[2,384]{1,0:T(2,128)} %qv_ref.1) | copy-start | bytes 9220
  9.1 13.4 %collective-permute-start.1 = (bf16[96,1152]{1,0:T(8,128)(2,1)S(1)}, bf16[96,1152]{1,0:T(8,128)(2,1)S(1)}, u32[]{:S(2)}, u32[]{:S(2)}) collective-permute-start(bf16[96,1152]{1,0:T(8,128)(2,1)S(1)} %pad_maximum_fusion.15), channel_id=1, source_target_pairs={{0,8},{1,9},{2,18},{3,19},{4,12},{5,13},{6,22},{7,23},{8,0},{9,1},... | collective-permute-start | bytes 663560 | tf_op jit(solution)/shard_map/ppermute | solution.py:39
  10.9 9.9 %collective-permute-start.3 = (bf16[1,136,768]{2,1,0:T(8,128)(2,1)S(1)}, bf16[1,136,768]{2,1,0:T(8,128)(2,1)S(1)}, u32[]{:S(2)}, u32[]{:S(2)}) collective-permute-start(bf16[1,136,768]{2,1,0:T(8,128)(2,1)S(1)} %get-tuple-element.180), channel_id=1, source_target_pairs={{0,2},{1,3},{2,0},{3,1},{4,6},{5,7},{6,4},{7,5},{8,10},{9,11},{10,... | collective-permute-start | bytes 626696 | tf_op jit(solution)/shard_map/ppermute | solution.py:39
  10.9 9.9 %collective-permute-start.4 = (bf16[1,136,768]{2,1,0:T(8,128)(2,1)S(1)}, bf16[1,136,768]{2,1,0:T(8,128)(2,1)S(1)}, u32[]{:S(2)}, u32[]{:S(2)}) collective-permute-start(bf16[1,136,768]{2,1,0:T(8,128)(2,1)S(1)} %get-tuple-element.181), channel_id=1, source_target_pairs={{0,4},{1,5},{2,6},{3,7},{4,0},{5,1},{6,2},{7,3},{8,12},{9,13},{10,... | collective-permute-start | bytes 626696 | tf_op jit(solution)/shard_map/ppermute | solution.py:39
  12.4 10.2 %collective-permute-start.5 = (bf16[1,136,768]{2,1,0:T(8,128)(2,1)S(1)}, bf16[1,136,768]{2,1,0:T(8,128)(2,1)S(1)}, u32[]{:S(2)}, u32[]{:S(2)}) collective-permute-start(bf16[1,136,768]{2,1,0:T(8,128)(2,1)S(1)} %get-tuple-element.182), channel_id=1, source_target_pairs={{0,6},{1,7},{2,4},{3,5},{4,2},{5,3},{6,0},{7,1},{8,14},{9,15},{10,... | collective-permute-start | bytes 626696 | tf_op jit(solution)/shard_map/ppermute | solution.py:39
  12.7 8.0 %collective-permute-start.2 = (bf16[48,1536]{1,0:T(8,128)(2,1)S(1)}, bf16[48,1536]{1,0:T(8,128)(2,1)S(1)}, u32[]{:S(2)}, u32[]{:S(2)}) collective-permute-start(bf16[48,1536]{1,0:T(8,128)(2,1)S(1)} %dynamic-slice_bitcast_fusion.2), channel_id=1, source_target_pairs={{0,16},{1,17},{2,3},{3,2},{4,20},{5,21},{6,7},{7,6},{8,24},{9,25},... | collective-permute-start | bytes 442376 | tf_op jit(solution)/shard_map/ppermute | solution.py:39
  22.6 12.8 %collective-permute-start.6 = (bf16[192,1152]{1,0:T(8,128)(2,1)S(1)}, bf16[192,1152]{1,0:T(8,128)(2,1)S(1)}, u32[]{:S(2)}, u32[]{:S(2)}) collective-permute-start(bf16[192,1152]{1,0:T(8,128)(2,1)S(1)} %pad_maximum_fusion.7), channel_id=1, source_target_pairs={{0,1},{1,0},{2,6},{3,7},{4,5},{5,4},{6,2},{7,3},{8,9},{9,8},{10,14... | collective-permute-start | bytes 1327112 | tf_op jit(solution)/shard_map/ppermute | solution.py:39
  24.2 8.4 %collective-permute-start.7 = (bf16[48,1920]{1,0:T(8,128)(2,1)S(1)}, bf16[48,1920]{1,0:T(8,128)(2,1)S(1)}, u32[]{:S(2)}, u32[]{:S(2)}) collective-permute-start(bf16[48,1920]{1,0:T(8,128)(2,1)S(1)} %fusion.2), channel_id=1, source_target_pairs={{0,16},{1,17},{2,10},{3,11},{4,20},{5,21},{6,14},{7,15},{8,24},{9,... | collective-permute-start | bytes 552968 | tf_op jit(solution)/shard_map/ppermute | solution.py:39
  27.6 7.9 %collective-permute-start.8 = (bf16[96,1536]{1,0:T(8,128)(2,1)S(1)}, bf16[96,1536]{1,0:T(8,128)(2,1)S(1)}, u32[]{:S(2)}, u32[]{:S(2)}) collective-permute-start(bf16[96,1536]{1,0:T(8,128)(2,1)S(1)} %pad_maximum_fusion.14), channel_id=1, source_target_pairs={{0,8},{1,9},{2,6},{3,7},{4,12},{5,13},{6,2},{7,3},{8,0},{9,1},{10,... | collective-permute-start | bytes 884744 | tf_op jit(solution)/shard_map/ppermute | solution.py:39
  35.6 13.1 %collective-permute-start.9 = (bf16[384,1152]{1,0:T(8,128)(2,1)S(1)}, bf16[384,1152]{1,0:T(8,128)(2,1)S(1)}, u32[]{:S(2)}, u32[]{:S(2)}) collective-permute-start(bf16[384,1152]{1,0:T(8,128)(2,1)S(1)} %pad_maximum_fusion.2), channel_id=1, source_target_pairs={{0,4},{1,5},{2,3},{3,2},{4,0},{5,1},{6,7},{7,6},{8,12},{9,13},{10,... | collective-permute-start | bytes 2654216 | tf_op jit(solution)/shard_map/ppermute | solution.py:39
  37.0 11.4 %collective-permute-start.11 = (bf16[2,128,768]{2,1,0:T(8,128)(2,1)S(1)}, bf16[2,128,768]{2,1,0:T(8,128)(2,1)S(1)}, u32[]{:S(2)}, u32[]{:S(2)}) collective-permute-start(bf16[2,128,768]{2,1,0:T(8,128)(2,1)S(1)} %pad_maximum_fusion.9), channel_id=1, source_target_pairs={{0,2},{1,3},{2,0},{3,1},{4,6},{5,7},{6,4},{7,5},{8,10},{9,11},{10,... | collective-permute-start | bytes 1179656 | tf_op jit(solution)/shard_map/ppermute | solution.py:39
  37.0 11.4 %collective-permute-start.10 = (bf16[96,1920]{1,0:T(8,128)(2,1)S(1)}, bf16[96,1920]{1,0:T(8,128)(2,1)S(1)}, u32[]{:S(2)}, u32[]{:S(2)}) collective-permute-start(bf16[96,1920]{1,0:T(8,128)(2,1)S(1)} %pad_maximum_fusion.13), channel_id=1, source_target_pairs={{0,8},{1,9},{2,18},{3,19},{4,12},{5,13},{6,22},{7,23},{8,0},{9,1},... | collective-permute-start | bytes 1105928 | tf_op jit(solution)/shard_map/ppermute | solution.py:39
  38.0 3.8 %collective-permute-start.12 = (f32[1,2304]{1,0:T(1,128)S(1)}, f32[1,2304]{1,0:T(1,128)S(1)}, u32[]{:S(2)}, u32[]{:S(2)}) collective-permute-start(f32[1,2304]{1,0:T(1,128)S(1)} %get-tuple-element.200), channel_id=1, source_target_pairs={{0,1},{1,0},{2,3},{3,2},{4,5},{5,4},{6,7},{7,6},{8,9},{9,8},{10,11... | collective-permute-start | bytes 27656 | tf_op jit(solution)/shard_map/ppermute | solution.py:39
  48.4 14.3 %copy-start.2 = (bf16[2,128,768]{2,1,0:T(8,128)(2,1)}, bf16[2,128,768]{2,1,0:T(8,128)(2,1)S(1)}, u32[]{:S(2)}) copy-start(bf16[2,128,768]{2,1,0:T(8,128)(2,1)S(1)} %collective-permute-done.11.refs_4_) | copy-start | bytes 1179652
  48.9 3.8 %collective-permute-start.13 = (bf16[768,1152]{1,0:T(8,128)(2,1)S(1)}, bf16[768,1152]{1,0:T(8,128)(2,1)S(1)}, u32[]{:S(2)}, u32[]{:S(2)}) collective-permute-start(bf16[768,1152]{1,0:T(8,128)(2,1)S(1)} %pad_maximum_fusion.1.refs_0_), channel_id=1, source_target_pairs={{0,2},{1,3},{2,0},{3,1},{4,6},{5,7},{6,4},{7,5},{8,10},{9,11},{10,... | collective-permute-start | bytes 5308424 | tf_op jit(solution)/shard_map/ppermute | solution.py:39
  49.0 20.4 %collective-permute-start.15 = (bf16[192,1536]{1,0:T(8,128)(2,1)S(1)}, bf16[192,1536]{1,0:T(8,128)(2,1)S(1)}, u32[]{:S(2)}, u32[]{:S(2)}) collective-permute-start(bf16[192,1536]{1,0:T(8,128)(2,1)S(1)} %pad_maximum_fusion.6), channel_id=1, source_target_pairs={{0,4},{1,5},{2,18},{3,19},{4,0},{5,1},{6,22},{7,23},{8,12},{9,13},... | collective-permute-start | bytes 1769480 | tf_op jit(solution)/shard_map/ppermute | solution.py:39
  50.4 11.5 %collective-permute-start.14 = (bf16[192,1920]{1,0:T(8,128)(2,1)S(1)}, bf16[192,1920]{1,0:T(8,128)(2,1)S(1)}, u32[]{:S(2)}, u32[]{:S(2)}) collective-permute-start(bf16[192,1920]{1,0:T(8,128)(2,1)S(1)} %pad_maximum_fusion.5), channel_id=1, source_target_pairs={{0,1},{1,0},{2,6},{3,7},{4,5},{5,4},{6,2},{7,3},{8,9},{9,8},{10,14... | collective-permute-start | bytes 2211848 | tf_op jit(solution)/shard_map/ppermute | solution.py:39
  62.0 20.7 %collective-permute-start.16 = (bf16[384,1920]{1,0:T(8,128)(2,1)S(1)}, bf16[384,1920]{1,0:T(8,128)(2,1)S(1)}, u32[]{:S(2)}, u32[]{:S(2)}) collective-permute-start(bf16[384,1920]{1,0:T(8,128)(2,1)S(1)} %constant_dynamic-update-slice_fusion), channel_id=1, source_target_pairs={{0,4},{1,5},{2,3},{3,2},{4,0},{5,1},{6,7},{7,6},{8,12},{9,13},{10,... | collective-permute-start | bytes 4423688 | tf_op jit(solution)/shard_map/ppermute | solution.py:39
  77.1 17.2 %copy-start.14 = (bf16[512,384]{1,0:T(8,128)(2,1)}, bf16[512,384]{1,0:T(8,128)(2,1)S(1)}, u32[]{:S(2)}) copy-start(bf16[512,384]{1,0:T(8,128)(2,1)S(1)} %get-tuple-element.229.mixed1_ref.refs_9_) | copy-start | bytes 1179652
  82.9 9.0 %collective-permute-start.17 = (bf16[768,1920]{1,0:T(8,128)(2,1)S(1)}, bf16[768,1920]{1,0:T(8,128)(2,1)S(1)}, u32[]{:S(2)}, u32[]{:S(2)}) collective-permute-start(bf16[768,1920]{1,0:T(8,128)(2,1)S(1)} %pad_maximum_fusion.refs_0_), channel_id=1, source_target_pairs={{0,2},{1,3},{2,0},{3,1},{4,6},{5,7},{6,4},{7,5},{8,10},{9,11},{10,... | collective-permute-start | bytes 8847368 | tf_op jit(solution)/shard_map/ppermute | solution.py:39
  86.9 16.4 %collective-permute-start.18 = (bf16[384,1536]{1,0:T(8,128)(2,1)}, bf16[384,1536]{1,0:T(8,128)(2,1)S(1)}, u32[]{:S(2)}, u32[]{:S(2)}) collective-permute-start(bf16[384,1536]{1,0:T(8,128)(2,1)} %get-tuple-element.353), channel_id=1, source_target_pairs={{0,1},{1,0},{2,10},{3,11},{4,5},{5,4},{6,14},{7,15},{8,9},{9,8},{1... | collective-permute-start | bytes 3538952 | tf_op jit(solution)/shard_map/ppermute | solution.py:39
  87.3 16.1 %collective-permute-start.19 = (bf16[2,128,768]{2,1,0:T(8,128)(2,1)S(1)}, bf16[2,128,768]{2,1,0:T(8,128)(2,1)S(1)}, u32[]{:S(2)}, u32[]{:S(2)}) collective-permute-start(bf16[2,128,768]{2,1,0:T(8,128)(2,1)S(1)} %pad_maximum_fusion.10), channel_id=1, source_target_pairs={{0,4},{1,5},{2,6},{3,7},{4,0},{5,1},{6,2},{7,3},{8,12},{9,13},{10,... | collective-permute-start | bytes 1179656 | tf_op jit(solution)/shard_map/ppermute | solution.py:39
  103.0 6.6 %copy-start.12 = (f32[512,768]{1,0:T(8,128)}, f32[512,768]{1,0:T(8,128)S(1)}, u32[]{:S(2)}) copy-start(f32[512,768]{1,0:T(8,128)S(1)} %get-tuple-element.235.refs_2_.refs_4_) | copy-start | bytes 4718596
  103.4 6.2 %copy-start.3 = (bf16[2,128,768]{2,1,0:T(8,128)(2,1)S(1)}, bf16[2,128,768]{2,1,0:T(8,128)(2,1)}, u32[]{:S(2)}) copy-start(bf16[2,128,768]{2,1,0:T(8,128)(2,1)} %copy-done.2) | copy-start | bytes 1179652
  103.4 4.6 %collective-permute-start.20 = (bf16[768,1536]{1,0:T(8,128)(2,1)S(1)}, bf16[768,1536]{1,0:T(8,128)(2,1)S(1)}, u32[]{:S(2)}, u32[]{:S(2)}) collective-permute-start(bf16[768,1536]{1,0:T(8,128)(2,1)S(1)} %constant_dynamic-update-slice_fusion.4.refs_0_), channel_id=1, source_target_pairs={{0,2},{1,3},{2,0},{3,1},{4,6},{5,7},{6,4},{7,5},{8,10},{9,11},{10,... | collective-permute-start | bytes 7077896 | tf_op jit(solution)/shard_map/ppermute | solution.py:39
  118.8 5.2 %collective-permute-start.21 = (bf16[768,1536]{1,0:T(8,128)(2,1)S(1)}, bf16[768,1536]{1,0:T(8,128)(2,1)S(1)}, u32[]{:S(2)}, u32[]{:S(2)}) collective-permute-start(bf16[768,1536]{1,0:T(8,128)(2,1)S(1)} %get-tuple-element.244), channel_id=1, source_target_pairs={{0,2},{1,3},{2,0},{3,1},{4,6},{5,7},{6,4},{7,5},{8,10},{9,11},{10,... | collective-permute-start | bytes 7077896 | tf_op jit(solution)/shard_map/ppermute | solution.py:39
  119.0 4.9 %collective-permute-start.22 = (bf16[2,128,768]{2,1,0:T(8,128)(2,1)S(1)}, bf16[2,128,768]{2,1,0:T(8,128)(2,1)S(1)}, u32[]{:S(2)}, u32[]{:S(2)}) collective-permute-start(bf16[2,128,768]{2,1,0:T(8,128)(2,1)S(1)} %slice.34), channel_id=1, source_target_pairs={{0,2},{1,3},{2,0},{3,1},{4,6},{5,7},{6,4},{7,5},{8,10},{9,11},{10,... | collective-permute-start | bytes 1179656 | tf_op jit(solution)/shard_map/ppermute | solution.py:39
  124.0 2.7 %copy-start.13 = (f32[512,768]{1,0:T(8,128)S(1)}, f32[512,768]{1,0:T(8,128)}, u32[]{:S(2)}) copy-start(f32[512,768]{1,0:T(8,128)} %copy-done.12) | copy-start | bytes 4718596
  124.3 13.0 %collective-permute-start.24 = (bf16[2,128,768]{2,1,0:T(8,128)(2,1)S(1)}, bf16[2,128,768]{2,1,0:T(8,128)(2,1)S(1)}, u32[]{:S(2)}, u32[]{:S(2)}) collective-permute-start(bf16[2,128,768]{2,1,0:T(8,128)(2,1)S(1)} %pad_maximum_fusion.11), channel_id=1, source_target_pairs={{0,4},{1,5},{2,6},{3,7},{4,0},{5,1},{6,2},{7,3},{8,12},{9,13},{10,... | collective-permute-start | bytes 1179656 | tf_op jit(solution)/shard_map/ppermute | solution.py:39
  126.2 16.2 %collective-permute-start.23 = (bf16[384,1536]{1,0:T(8,128)(2,1)S(1)}, bf16[384,1536]{1,0:T(8,128)(2,1)S(1)}, u32[]{:S(2)}, u32[]{:S(2)}) collective-permute-start(bf16[384,1536]{1,0:T(8,128)(2,1)S(1)} %add.53), channel_id=1, source_target_pairs={{0,1},{1,0},{2,10},{3,11},{4,5},{5,4},{6,14},{7,15},{8,9},{9,8},{1... | collective-permute-start | bytes 3538952 | tf_op jit(solution)/shard_map/ppermute | solution.py:39
  142.4 5.6 %collective-permute-start.25 = (bf16[768,1920]{1,0:T(8,128)(2,1)S(1)}, bf16[768,1920]{1,0:T(8,128)(2,1)S(1)}, u32[]{:S(2)}, u32[]{:S(2)}) collective-permute-start(bf16[768,1920]{1,0:T(8,128)(2,1)S(1)} %get-tuple-element.266), channel_id=1, source_target_pairs={{0,2},{1,3},{2,0},{3,1},{4,6},{5,7},{6,4},{7,5},{8,10},{9,11},{10,... | collective-permute-start | bytes 8847368 | tf_op jit(solution)/shard_map/ppermute | solution.py:39
  148.4 25.8 %collective-permute-start.27 = (bf16[384,1920]{1,0:T(8,128)(2,1)S(1)}, bf16[384,1920]{1,0:T(8,128)(2,1)S(1)}, u32[]{:S(2)}, u32[]{:S(2)}) collective-permute-start(bf16[384,1920]{1,0:T(8,128)(2,1)S(1)} %add.55), channel_id=1, source_target_pairs={{0,4},{1,5},{2,10},{3,11},{4,0},{5,1},{6,14},{7,15},{8,12},{9,13},... | collective-permute-start | bytes 4423688 | tf_op jit(solution)/shard_map/ppermute | solution.py:39
  148.7 25.5 %collective-permute-start.28 = (bf16[4,128,768]{2,1,0:T(8,128)(2,1)S(1)}, bf16[4,128,768]{2,1,0:T(8,128)(2,1)S(1)}, u32[]{:S(2)}, u32[]{:S(2)}) collective-permute-start(bf16[4,128,768]{2,1,0:T(8,128)(2,1)S(1)} %pad_maximum_fusion.3), channel_id=1, source_target_pairs={{0,1},{1,0},{2,3},{3,2},{4,5},{5,4},{6,7},{7,6},{8,9},{9,8},{10,11... | collective-permute-start | bytes 2359304 | tf_op jit(solution)/shard_map/ppermute | solution.py:39
  149.1 25.1 %collective-permute-start.26 = (bf16[192,1536]{1,0:T(8,128)(2,1)S(1)}, bf16[192,1536]{1,0:T(8,128)(2,1)S(1)}, u32[]{:S(2)}, u32[]{:S(2)}) collective-permute-start(bf16[192,1536]{1,0:T(8,128)(2,1)S(1)} %add.54), channel_id=1, source_target_pairs={{0,4},{1,5},{2,18},{3,19},{4,0},{5,1},{6,22},{7,23},{8,12},{9,13},... | collective-permute-start | bytes 1769480 | tf_op jit(solution)/shard_map/ppermute | solution.py:39
  174.6 4.3 %collective-permute-start.29 = (bf16[776,1152]{1,0:T(8,128)(2,1)S(1)}, bf16[776,1152]{1,0:T(8,128)(2,1)S(1)}, u32[]{:S(2)}, u32[]{:S(2)}) collective-permute-start(bf16[776,1152]{1,0:T(8,128)(2,1)S(1)} %get-tuple-element.290), channel_id=1, source_target_pairs={{0,2},{1,3},{2,0},{3,1},{4,6},{5,7},{6,4},{7,5},{8,10},{9,11},{10,... | collective-permute-start | bytes 5363720 | tf_op jit(solution)/shard_map/ppermute | solution.py:39
  174.7 4.2 %collective-permute-start.30 = (bf16[2,128,768]{2,1,0:T(8,128)(2,1)S(1)}, bf16[2,128,768]{2,1,0:T(8,128)(2,1)S(1)}, u32[]{:S(2)}, u32[]{:S(2)}) collective-permute-start(bf16[2,128,768]{2,1,0:T(8,128)(2,1)S(1)} %slice.39), channel_id=1, source_target_pairs={{0,2},{1,3},{2,0},{3,1},{4,6},{5,7},{6,4},{7,5},{8,10},{9,11},{10,... | collective-permute-start | bytes 1179656 | tf_op jit(solution)/shard_map/ppermute | solution.py:39
  179.2 16.5 %collective-permute-start.31 = (bf16[392,1152]{1,0:T(8,128)(2,1)S(1)}, bf16[392,1152]{1,0:T(8,128)(2,1)S(1)}, u32[]{:S(2)}, u32[]{:S(2)}) collective-permute-start(bf16[392,1152]{1,0:T(8,128)(2,1)S(1)} %add.58.refs_3_), channel_id=1, source_target_pairs={{0,4},{1,5},{2,3},{3,2},{4,0},{5,1},{6,7},{7,6},{8,12},{9,13},{10,... | collective-permute-start | bytes 2709512 | tf_op jit(solution)/shard_map/ppermute | solution.py:39
  179.4 19.4 %collective-permute-start.34 = (bf16[192,1920]{1,0:T(8,128)(2,1)S(1)}, bf16[192,1920]{1,0:T(8,128)(2,1)S(1)}, u32[]{:S(2)}, u32[]{:S(2)}) collective-permute-start(bf16[192,1920]{1,0:T(8,128)(2,1)S(1)} %add.57), channel_id=1, source_target_pairs={{0,1},{1,0},{2,18},{3,19},{4,5},{5,4},{6,22},{7,23},{8,9},{9,8},{1... | collective-permute-start | bytes 2211848 | tf_op jit(solution)/shard_map/ppermute | solution.py:39
  179.9 16.6 %collective-permute-start.33 = (bf16[96,1536]{1,0:T(8,128)(2,1)S(1)}, bf16[96,1536]{1,0:T(8,128)(2,1)S(1)}, u32[]{:S(2)}, u32[]{:S(2)}) collective-permute-start(bf16[96,1536]{1,0:T(8,128)(2,1)S(1)} %add.56), channel_id=1, source_target_pairs={{0,8},{1,9},{2,6},{3,7},{4,12},{5,13},{6,2},{7,3},{8,0},{9,1},{10,... | collective-permute-start | bytes 884744 | tf_op jit(solution)/shard_map/ppermute | solution.py:39
  195.9 9.8 %collective-permute-start.32 = (bf16[200,1152]{1,0:T(8,128)(2,1)S(1)}, bf16[200,1152]{1,0:T(8,128)(2,1)S(1)}, u32[]{:S(2)}, u32[]{:S(2)}) collective-permute-start(bf16[200,1152]{1,0:T(8,128)(2,1)S(1)} %add.59.refs_4_), channel_id=1, source_target_pairs={{0,1},{1,0},{2,10},{3,11},{4,5},{5,4},{6,14},{7,15},{8,9},{9,8},{1... | collective-permute-start | bytes 1382408 | tf_op jit(solution)/shard_map/ppermute | solution.py:39
  196.5 14.7 %collective-permute-start.37 = (bf16[2,128,768]{2,1,0:T(8,128)(2,1)S(1)}, bf16[2,128,768]{2,1,0:T(8,128)(2,1)S(1)}, u32[]{:S(2)}, u32[]{:S(2)}) collective-permute-start(bf16[2,128,768]{2,1,0:T(8,128)(2,1)S(1)} %pad_maximum_fusion.12), channel_id=1, source_target_pairs={{0,4},{1,5},{2,6},{3,7},{4,0},{5,1},{6,2},{7,3},{8,12},{9,13},{10,... | collective-permute-start | bytes 1179656 | tf_op jit(solution)/shard_map/ppermute | solution.py:39
  199.0 13.1 %collective-permute-start.38 = (bf16[96,1920]{1,0:T(8,128)(2,1)S(1)}, bf16[96,1920]{1,0:T(8,128)(2,1)S(1)}, u32[]{:S(2)}, u32[]{:S(2)}) collective-permute-start(bf16[96,1920]{1,0:T(8,128)(2,1)S(1)} %add.61), channel_id=1, source_target_pairs={{0,8},{1,9},{2,3},{3,2},{4,12},{5,13},{6,7},{7,6},{8,0},{9,1},{10,... | collective-permute-start | bytes 1105928 | tf_op jit(solution)/shard_map/ppermute | solution.py:39
  199.8 11.4 %collective-permute-start.36 = (bf16[48,1536]{1,0:T(8,128)(2,1)S(1)}, bf16[48,1536]{1,0:T(8,128)(2,1)S(1)}, u32[]{:S(2)}, u32[]{:S(2)}) collective-permute-start(bf16[48,1536]{1,0:T(8,128)(2,1)S(1)} %add.60), channel_id=1, source_target_pairs={{0,16},{1,17},{2,3},{3,2},{4,20},{5,21},{6,7},{7,6},{8,24},{9,25},... | collective-permute-start | bytes 442376 | tf_op jit(solution)/shard_map/ppermute | solution.py:39
  205.8 11.7 %collective-permute-start.35 = (bf16[104,1152]{1,0:T(8,128)(2,1)S(1)}, bf16[104,1152]{1,0:T(8,128)(2,1)S(1)}, u32[]{:S(2)}, u32[]{:S(2)}) collective-permute-start(bf16[104,1152]{1,0:T(8,128)(2,1)S(1)} %add.62.refs_5_), channel_id=1, source_target_pairs={{0,8},{1,9},{2,18},{3,19},{4,12},{5,13},{6,22},{7,23},{8,0},{9,1},... | collective-permute-start | bytes 718856 | tf_op jit(solution)/shard_map/ppermute | solution.py:39
  211.3 6.4 %collective-permute-start.41 = (bf16[48,1536]{1,0:T(8,128)(2,1)S(1)}, bf16[48,1536]{1,0:T(8,128)(2,1)S(1)}, u32[]{:S(2)}, u32[]{:S(2)}) collective-permute-start(bf16[48,1536]{1,0:T(8,128)(2,1)S(1)} %add.63), channel_id=1, source_target_pairs={{0,4},{1,5},{2,6},{3,7},{4,0},{5,1},{6,2},{7,3},{8,12},{9,13},{10,... | collective-permute-start | bytes 442376 | tf_op jit(solution)/shard_map/ppermute | solution.py:39
  212.3 14.2 %collective-permute-start.42 = (bf16[48,1920]{1,0:T(8,128)(2,1)S(1)}, bf16[48,1920]{1,0:T(8,128)(2,1)S(1)}, u32[]{:S(2)}, u32[]{:S(2)}) collective-permute-start(bf16[48,1920]{1,0:T(8,128)(2,1)S(1)} %add.64), channel_id=1, source_target_pairs={{0,16},{1,17},{2,6},{3,7},{4,20},{5,21},{6,2},{7,3},{8,24},{9,25},... | collective-permute-start | bytes 552968 | tf_op jit(solution)/shard_map/ppermute | solution.py:39
  216.3 23.0 %collective-permute-start.39 = (bf16[4,128,768]{2,1,0:T(8,128)(2,1)S(1)}, bf16[4,128,768]{2,1,0:T(8,128)(2,1)S(1)}, u32[]{:S(2)}, u32[]{:S(2)}) collective-permute-start(bf16[4,128,768]{2,1,0:T(8,128)(2,1)S(1)} %pad_maximum_fusion.4), channel_id=1, source_target_pairs={{0,1},{1,0},{2,3},{3,2},{4,5},{5,4},{6,7},{7,6},{8,9},{9,8},{10,11... | collective-permute-start | bytes 2359304 | tf_op jit(solution)/shard_map/ppermute | solution.py:39
  217.5 12.3 %collective-permute-start.40 = (bf16[56,1152]{1,0:T(8,128)(2,1)S(1)}, bf16[56,1152]{1,0:T(8,128)(2,1)S(1)}, u32[]{:S(2)}, u32[]{:S(2)}) collective-permute-start(bf16[56,1152]{1,0:T(8,128)(2,1)S(1)} %add.65.refs_0_), channel_id=1, source_target_pairs={{0,16},{1,17},{2,6},{3,7},{4,20},{5,21},{6,2},{7,3},{8,24},{9,25},... | collective-permute-start | bytes 387080 | tf_op jit(solution)/shard_map/ppermute | solution.py:39
  226.6 7.2 %collective-permute-start.45 = (bf16[48,1920]{1,0:T(8,128)(2,1)S(1)}, bf16[48,1920]{1,0:T(8,128)(2,1)S(1)}, u32[]{:S(2)}, u32[]{:S(2)}) collective-permute-start(bf16[48,1920]{1,0:T(8,128)(2,1)S(1)} %add.66), channel_id=1, source_target_pairs={{0,4},{1,5},{2,6},{3,7},{4,0},{5,1},{6,2},{7,3},{8,12},{9,13},{10,... | collective-permute-start | bytes 552968 | tf_op jit(solution)/shard_map/ppermute | solution.py:39
  226.7 4.4 %collective-permute-start.44 = (bf16[96,1536]{1,0:T(8,128)(2,1)S(1)}, bf16[96,1536]{1,0:T(8,128)(2,1)S(1)}, u32[]{:S(2)}, u32[]{:S(2)}) collective-permute-start(bf16[96,1536]{1,0:T(8,128)(2,1)S(1)} %constant_dynamic-update-slice_fusion.7.refs_0_), channel_id=1, source_target_pairs={{0,2},{1,3},{2,0},{3,1},{4,6},{5,7},{6,4},{7,5},{8,10},{9,11},{10,... | collective-permute-start | bytes 884744 | tf_op jit(solution)/shard_map/ppermute | solution.py:39
  230.0 6.8 %collective-permute-start.43 = (bf16[48,1152]{1,0:T(8,128)(2,1)S(1)}, bf16[48,1152]{1,0:T(8,128)(2,1)S(1)}, u32[]{:S(2)}, u32[]{:S(2)}) collective-permute-start(bf16[48,1152]{1,0:T(8,128)(2,1)S(1)} %add.67), channel_id=1, source_target_pairs={{0,4},{1,5},{2,6},{3,7},{4,0},{5,1},{6,2},{7,3},{8,12},{9,13},{10,... | collective-permute-start | bytes 331784 | tf_op jit(solution)/shard_map/ppermute | solution.py:39
  233.9 4.2 %collective-permute-start.46 = (bf16[96,1920]{1,0:T(8,128)(2,1)S(1)}, bf16[96,1920]{1,0:T(8,128)(2,1)S(1)}, u32[]{:S(2)}, u32[]{:S(2)}) collective-permute-start(bf16[96,1920]{1,0:T(8,128)(2,1)S(1)} %constant_dynamic-update-slice_fusion.9.refs_0_), channel_id=1, source_target_pairs={{0,2},{1,3},{2,0},{3,1},{4,6},{5,7},{6,4},{7,5},{8,10},{9,11},{10,... | collective-permute-start | bytes 1105928 | tf_op jit(solution)/shard_map/ppermute | solution.py:39
  236.8 3.8 %collective-permute-start.47 = (bf16[96,1152]{1,0:T(8,128)(2,1)S(1)}, bf16[96,1152]{1,0:T(8,128)(2,1)S(1)}, u32[]{:S(2)}, u32[]{:S(2)}) collective-permute-start(bf16[96,1152]{1,0:T(8,128)(2,1)S(1)} %constant_dynamic-update-slice_fusion.11.refs_0_), channel_id=1, source_target_pairs={{0,2},{1,3},{2,0},{3,1},{4,6},{5,7},{6,4},{7,5},{8,10},{9,11},{10,... | collective-permute-start | bytes 663560 | tf_op jit(solution)/shard_map/ppermute | solution.py:39
  (3 other events, 5.4 us)

commit v5 on v4

--- a/solution.py
+++ b/solution.py
@@ -45,7 +45,7 @@
     (("z2", "z1", "x", "y"), ("y", "x", "z2", "z1")),
 )
 SCATTER = (
-    (("x", "y", "z1", "z2"), ("y", "z1", "z2", "x")),
+    (("x", "y", "z1", "z2"), ("y", "x", "z2", "z1")),
     (("x", "y", "z1", "z2"), ("z1", "z2", "y", "x")),
     (("y", "x", "z1", "z2"), ("z1", "z2", "x", "y")),
 )
@@ -693,7 +693,7 @@
         out[high - low :, :] = total.astype(BF16)
 
 
-def add_up(terms, low, high, vec=(), lone=()):
+def add_up(terms, low, high, vec=(), lone=(), time=1):
     count, terms = len(terms), list(terms) + list(lone)
     cols = terms[0].shape[1]
     return call(
@@ -703,7 +703,7 @@
         [VMEM] * len(terms),
         VMEM,
         [],
-        1,
+        time,
         4,
         tuple(terms),
     )
@@ -764,13 +764,13 @@
     )
 
 
-def settle_kernel(pair_ref, got_ref, *refs, cuts):
-    outs, four = refs[: len(cuts)], refs[len(cuts)]
-    rows = pair_ref.shape[0] // 2
+def settle_kernel(*refs, cuts, count):
+    given, outs, four = refs[:count], refs[count:-1], refs[-1]
+    rows = four.shape[0] // 4
     for i in range(4):
-        ref = (pair_ref, got_ref)[i // 2]
+        ref = given[i * count // 4]
         owner = lax.axis_index("ctx") ^ ((i & 1) * 2 + (i >> 1))
-        low = i % 2 * rows
+        low = i % (4 // count) * rows
         four[pl.ds(pl.multiple_of(owner * rows, 16), rows), :] = ref[low : low + rows, :].astype(F32)
     for out, (low, high, form) in zip(outs, cuts):
         if form == "plain":
@@ -781,19 +781,19 @@
                 out[j] = four[:, low + j * step : low + (j + 1) * step]
 
 
-def settle(pair, got, cuts):
-    rows, cols = pair.shape[0] // 2, pair.shape[1]
+def settle(given, cuts):
+    rows, cols = given[0].shape[0] * len(given) // 4, given[0].shape[1]
     shapes = {"plain": lambda n: (4 * rows, n), "three": lambda n: (3, 4 * rows, n // 3)}
     return call(
-        lambda *refs: settle_kernel(*refs, cuts=cuts),
+        lambda *refs: settle_kernel(*refs, cuts=cuts, count=len(given)),
         "settle",
         tuple(struct(shapes[form](high - low), F32) for low, high, form in cuts),
-        [VMEM, VMEM],
+        [VMEM] * len(given),
         (VMEM,) * len(cuts),
         [pltpu.VMEM((4 * rows, cols), F32)],
         3,
         7,
-        (pair, got),
+        tuple(given),
     )
 
 
@@ -975,14 +975,13 @@
     parts[0] = after(parts[0], chunks2)
     qkv_own, qkv_sib = last(packs[0], rows_b, sums1, sums2, sum_up, parts)
     if fast:
-        chunks2, qkv_sib, got, got2, y_out = phase(chunks2, qkv_sib, got, got2, y_out)
+        got3, core_x = shed(qkv_sib, 0, 0), exchange(chunks2[2:], CORE, sizes)
+        chunks2, qkv_own, got2, y_out, got = phase(chunks2, qkv_own, got2, y_out, got)
         down, up = down + [got], up + [got2]
         send = add_up(down, 2 * rows, 4 * rows)
-        send2 = add_up(up, 4 * rows, 8 * rows)
-        qkv_sib, send, send2, chunks2 = phase(qkv_sib, send, send2, chunks2)
-        got3, got, got2, core_x = (
-            shed(qkv_sib, 0, 0), shed(send, 2, 3), shed(send2, 1, 2), exchange(chunks2[2:], CORE, sizes)
-        )
+        send2 = add_up(up, 4 * rows, 8 * rows, time=30)
+        send, send2, got3 = phase(send, send2, got3)
+        got, got2 = shed(send, 2, 3), shed(send2, 1, 2)
         got3, core_x = phase(got3, core_x)
         qkv = [qkv_own, got3]
         sent3 = add_up(qkv, 8 * rows, 16 * rows, (0, 1))
@@ -1024,24 +1023,24 @@
         got1, got2 = exchange(pair1, CORE, sizes), exchange(pair2, X, sizes)
         got3, pair1, pair2 = phase(got3, pair1, pair2)
         qkv = qkv + [got3]
-        pair3 = add_up(qkv, 0, rows)
-        got = exchange(pair3, X, sizes)
-        vec = vectors(after(send3, pair3), got3, local_width, local_units)
-        pair3, got1, bup = phase(pair3, got1, vec[1])
+        sent_last = got3
+        piece = add_up(qkv, 0, rows)
+        got3 = [exchange(piece, dims, sizes) for dims in (X, CORE, FAR)]
+        vec = vectors(after(send3, piece), sent_last, local_width, local_units)
+        piece, got1, bup = phase(piece, got1, vec[1])
         vec = (vec[0], bup) + tuple(vec[2:])
-        (grad_down,) = settle(pair1, got1, ((0, local_units, "plain"),))
+        (grad_down,) = settle((pair1, got1), ((0, local_units, "plain"),))
         grad_down, got2 = phase(grad_down, got2)
         pair2 = joined(pair2, got2)
         got2 = exchange(pair2, CORE, sizes)
-        got, pair2 = phase(got, pair2)
-        pair3 = joined(pair3, got)
-        got3 = exchange(pair3, CORE, sizes)
-        pair3, got2 = phase(pair3, got2)
+        pair2, y_x = phase(pair2, y_x)
+        grad_x = deliver(chunks2, core_x, x_x, y_x)
+        grad_x, *got3 = phase(grad_x, *got3)
+        (grad_qkv,) = settle([piece] + got3, ((0, 3 * local_width, "three"),))
         grad_wout, grad_up = settle(
-            pair2, got2, ((0, local_width, "plain"), (local_width, local_width + local_units, "plain"))
+            (pair2, after(got2, grad_qkv)),
+            ((0, local_width, "plain"), (local_width, local_width + local_units, "plain")),
         )
-        grad_x = deliver(chunks2, core_x, x_x, after(y_x, grad_up))
-        (grad_qkv,) = settle(pair3, after(got3, grad_x), ((0, 3 * local_width, "three"),))
         layer_output = layer_output.reshape(micro, seqs, local_len, width)
         grad_x = grad_x.reshape(micro, seqs, local_len, width)
     else:

time: 243 us -> 234 us (0.963)
  waiting for transfers between devices: 103 us -> 93.7 us
    ppermute x48 -> x49, waiting for transfers between devices: 103 us -> 93.7 us  [exchange(): return lax.ppermute(value, AXES, pairs)]
    ppermute x48 -> x49, starting transfers between devices: 50.9 us -> 51.4 us  [exchange(): return lax.ppermute(value, AXES, pairs)]
  transfers between devices with their start and end apart: 48 -> 49, of which waited for: 26 -> 25; matrix products, arithmetic and copies ran while one was open for 2% -> 2% of each run, Pallas kernels for 27% -> 28%
where the time goes in v5:
time: 234 us
  waiting for transfers between devices  93.7 us (40%)
  Pallas kernels  79.1 us (34%)
  starting transfers between devices  51.4 us (22%)
  local copies, waits for them, and re-layouts  6.37 us (3%)
    ppermute x49, waiting for transfers between devices, exchange(): return lax.ppermute(value, AXES, pairs)  93.7 us
    pallas_call x36, Pallas kernels, call(): pl.pallas_call(kernel, name=name, out_shape=outs, in_specs=specs, out_spe...  79.1 us
    ppermute x49, starting transfers between devices, exchange(): return lax.ppermute(value, AXES, pairs)  51.4 us
  transfers between devices with their start and end apart: 49, of which 25 were waited for; matrix products, arithmetic and copies ran while one was open for 2% of the time, Pallas kernels for 28%

profile of v5, /device:TPU:0, one launch (start us, length us, event | category | flops | bytes accessed | tf_op | source)
XLA Modules:
  0.0 233.9 jit_solution(812573599464798436)
XLA Ops:
  0.7 1.0 dynamic-slice_bitcast_fusion.3
  1.7 4.1 %collective-permute-start = (bf16[48,1152]{1,0:T(8,128)(2,1)S(1)}, bf16[48,1152]{1,0:T(8,128)(2,1)S(1)}, u32[]{:S(2)}, u32[]{:S(2)}) collective-permute-start(bf16[48,1152]{1,0:T(8,128)(2,1)S(1)} %bitcast.15), channel_id=1, source_target_pairs={{0,16},{1,17},{2,10},{3,11},{4,20},{5,21},{6,14},{7,15},{8,24},{9,... | collective-permute-start | bytes 331784 | tf_op jit(solution)/shard_map/ppermute | solution.py:39
  5.9 0.9 dynamic-slice_bitcast_fusion.2
  7.7 1.2 dynamic-slice_bitcast_fusion
  9.1 1.8 collective-permute-start.1
  10.9 1.5 collective-permute-start.4
  12.7 3.4 %collective-permute-start.2 = (bf16[48,1536]{1,0:T(8,128)(2,1)S(1)}, bf16[48,1536]{1,0:T(8,128)(2,1)S(1)}, u32[]{:S(2)}, u32[]{:S(2)}) collective-permute-start(bf16[48,1536]{1,0:T(8,128)(2,1)S(1)} %dynamic-slice_bitcast_fusion.2), channel_id=1, source_target_pairs={{0,16},{1,17},{2,3},{3,2},{4,20},{5,21},{6,7},{7,6},{8,24},{9,25},... | collective-permute-start | bytes 442376 | tf_op jit(solution)/shard_map/ppermute | solution.py:39
  16.1 4.6 %collective-permute-done.2 = bf16[48,1536]{1,0:T(8,128)(2,1)S(1)} collective-permute-done((bf16[48,1536]{1,0:T(8,128)(2,1)S(1)}, bf16[48,1536]{1,0:T(8,128)(2,1)S(1)}, u32[]{:S(2)}, u32[]{:S(2)}) %collective-permute-start.2) | collective-permute-done | bytes 147488 | tf_op jit(solution)/shard_map/ppermute | solution.py:39
  20.8 1.8 collective-permute-done.5
  22.6 1.6 collective-permute-start.6
  24.2 3.4 %collective-permute-start.7 = (bf16[48,1920]{1,0:T(8,128)(2,1)S(1)}, bf16[48,1920]{1,0:T(8,128)(2,1)S(1)}, u32[]{:S(2)}, u32[]{:S(2)}) collective-permute-start(bf16[48,1920]{1,0:T(8,128)(2,1)S(1)} %fusion.2), channel_id=1, source_target_pairs={{0,16},{1,17},{2,10},{3,11},{4,20},{5,21},{6,14},{7,15},{8,24},{9,... | collective-permute-start | bytes 552968 | tf_op jit(solution)/shard_map/ppermute | solution.py:39
  27.8 4.8 %collective-permute-done.7 = bf16[48,1920]{1,0:T(8,128)(2,1)S(1)} collective-permute-done((bf16[48,1920]{1,0:T(8,128)(2,1)S(1)}, bf16[48,1920]{1,0:T(8,128)(2,1)S(1)}, u32[]{:S(2)}, u32[]{:S(2)}) %collective-permute-start.7) | collective-permute-done | bytes 184352 | tf_op jit(solution)/shard_map/ppermute | solution.py:39
  32.6 2.8 %collective-permute-done.8 = bf16[96,1536]{1,0:T(8,128)(2,1)S(1)} collective-permute-done((bf16[96,1536]{1,0:T(8,128)(2,1)S(1)}, bf16[96,1536]{1,0:T(8,128)(2,1)S(1)}, u32[]{:S(2)}, u32[]{:S(2)}) %collective-permute-start.8) | collective-permute-done | bytes 294944 | tf_op jit(solution)/shard_map/ppermute | solution.py:39
  35.6 1.4 collective-permute-start.9
  37.0 1.1 collective-permute-start.10
  38.5 3.3 %collective-permute-done.12 = f32[1,2304]{1,0:T(1,128)S(1)} collective-permute-done((f32[1,2304]{1,0:T(1,128)S(1)}, f32[1,2304]{1,0:T(1,128)S(1)}, u32[]{:S(2)}, u32[]{:S(2)}) %collective-permute-start.12) | collective-permute-done | bytes 9248 | tf_op jit(solution)/shard_map/ppermute | solution.py:39
  41.9 6.6 %collective-permute-done.10 = bf16[96,1920]{1,0:T(8,128)(2,1)S(1)} collective-permute-done((bf16[96,1920]{1,0:T(8,128)(2,1)S(1)}, bf16[96,1920]{1,0:T(8,128)(2,1)S(1)}, u32[]{:S(2)}, u32[]{:S(2)}) %collective-permute-start.10) | collective-permute-done | bytes 368672 | tf_op jit(solution)/shard_map/ppermute | solution.py:39
  49.0 1.4 collective-permute-start.15
  52.7 1.3 unpack.3.refs_0_
  54.0 2.6 %project.1 = (bf16[512,2304]{1,0:T(8,128)(2,1)S(1)}, bf16[512,768]{1,0:T(8,128)(2,1)S(1)}, f32[512,512]{1,0:T(8,128)S(1)}) custom-call(bf16[768,2304]{1,0:T(8,128)(2,1)S(1)} %unpack.3.refs_0_, bf16[1,136,768]{2,1,0:T(8,128)(2,1)S(1)} %get-tuple-element.340.refs_1_, bf16[1,136,768]{2,1,0:T(8,128)(2,1)S(1)} %collective-permute-done.3.refs_2_, ...), custom_call_target="tpu_custom_call" | custom-call | flops 5000000000 | bytes 1000000 | tf_op jit(solution)/shard_map/project/pallas_call | solution.py:147
  56.7 5.2 %collective-permute-done.14 = bf16[192,1920]{1,0:T(8,128)(2,1)S(1)} collective-permute-done((bf16[192,1920]{1,0:T(8,128)(2,1)S(1)}, bf16[192,1920]{1,0:T(8,128)(2,1)S(1)}, u32[]{:S(2)}, u32[]{:S(2)}) %collective-permute-start.14) | collective-permute-done | bytes 737312 | tf_op jit(solution)/shard_map/ppermute | solution.py:39
  62.8 6.7 %attend.2 = (bf16[512,384]{1,0:T(8,128)(2,1)S(1)}, bf16[6,512,512]{2,1,0:T(8,128)(2,1)S(1)}) custom-call(bf16[512,2304]{1,0:T(8,128)(2,1)S(1)} %get-tuple-element.220.refs_0_, f32[512,512]{1,0:T(8,128)S(1)} %get-tuple-element.216.refs_1_), custom_call_target="tpu_custom_call" | custom-call | flops 12000000000 | bytes 1000000 | tf_op jit(solution)/shard_map/attend/pallas_call | solution.py:147
  70.4 6.7 %attend.3 = (bf16[512,384]{1,0:T(8,128)(2,1)S(1)}, bf16[6,512,512]{2,1,0:T(8,128)(2,1)S(1)}) custom-call(bf16[512,2304]{1,0:T(8,128)(2,1)S(1)} %get-tuple-element.220.refs_0_, f32[512,512]{1,0:T(8,128)S(1)} %get-tuple-element.216.refs_1_), custom_call_target="tpu_custom_call" | custom-call | flops 12000000000 | bytes 1000000 | tf_op jit(solution)/shard_map/attend/pallas_call | solution.py:147
  77.1 5.6 %collective-permute-done.16 = bf16[384,1920]{1,0:T(8,128)(2,1)S(1)} collective-permute-done((bf16[384,1920]{1,0:T(8,128)(2,1)S(1)}, bf16[384,1920]{1,0:T(8,128)(2,1)S(1)}, u32[]{:S(2)}, u32[]{:S(2)}) %collective-permute-start.16) | collective-permute-done | bytes 1474592 | tf_op jit(solution)/shard_map/ppermute | solution.py:39
  82.9 4.0 %collective-permute-start.17 = (bf16[768,1920]{1,0:T(8,128)(2,1)S(1)}, bf16[768,1920]{1,0:T(8,128)(2,1)S(1)}, u32[]{:S(2)}, u32[]{:S(2)}) collective-permute-start(bf16[768,1920]{1,0:T(8,128)(2,1)S(1)} %pad_maximum_fusion.refs_0_), channel_id=1, source_target_pairs={{0,2},{1,3},{2,0},{3,1},{4,6},{5,7},{6,4},{7,5},{8,10},{9,11},{10,... | collective-permute-start | bytes 8847368 | tf_op jit(solution)/shard_map/ppermute | solution.py:39
  87.3 2.0 collective-permute-start.19
  89.3 2.6 %collective-permute-done.17.refs_1_ = bf16[768,1920]{1,0:T(8,128)(2,1)S(1)} collective-permute-done((bf16[768,1920]{1,0:T(8,128)(2,1)S(1)}, bf16[768,1920]{1,0:T(8,128)(2,1)S(1)}, u32[]{:S(2)}, u32[]{:S(2)}) %collective-permute-start.17) | collective-permute-done | bytes 2949152 | tf_op jit(solution)/shard_map/ppermute | solution.py:39
  91.9 2.3 %unpack.4 = (bf16[768,768]{1,0:T(8,128)(2,1)S(1)}, bf16[768,3072]{1,0:T(8,128)(2,1)S(1)}) custom-call(bf16[768,1920]{1,0:T(8,128)(2,1)S(1)} %pad_maximum_fusion.refs_0_, bf16[768,1920]{1,0:T(8,128)(2,1)S(1)} %collective-permute-done.17.refs_1_), custom_call_target="tpu_custom_call" | custom-call | flops 5000000000 | bytes 1000000 | tf_op jit(solution)/shard_map/unpack/pallas_call | solution.py:147
  94.2 8.7 %middle.1 = (f32[512,768]{1,0:T(8,128)S(1)}, f32[512,1]{1,0:T(8,128)S(1)}, bf16[512,768]{1,0:T(8,128)(2,1)S(1)}, bf16[512,3072]{1,0:T(8,128)(2,1)S(1)}, bf16[512,3072]{1,0:T(8,128)(2,1)S(1)}) custom-call(bf16[768,768]{1,0:T(8,128)(2,1)S(1)} %get-tuple-element.226.w_out.refs_0_, bf16[768,3072]{1,0:T(8,128)(2,1)S(1)} %get-tuple-element.227.w_up.refs_1_, ...), custom_call_target="tpu_custom_call" | custom-call | flops 12000000000 | bytes 1000000 | tf_op jit(solution)/shard_map/middle/pallas_call | solution.py:147
  103.5 4.5 %collective-permute-done.20.refs_1_ = bf16[768,1536]{1,0:T(8,128)(2,1)S(1)} collective-permute-done((bf16[768,1536]{1,0:T(8,128)(2,1)S(1)}, bf16[768,1536]{1,0:T(8,128)(2,1)S(1)}, u32[]{:S(2)}, u32[]{:S(2)}) %collective-permute-start.20) | collective-permute-done | bytes 2359328 | tf_op jit(solution)/shard_map/ppermute | solution.py:39
  108.0 1.6 unpack.5.refs_0_.weight_ref
  109.6 9.1 %turn.1 = (bf16[4,128,768]{2,1,0:T(8,128)(2,1)S(1)}, f32[512,768]{1,0:T(8,128)S(1)}, bf16[512,768]{1,0:T(8,128)(2,1)S(1)}, f32[8,768]{1,0:T(8,128)S(1)}, bf16[76...) custom-call(bf16[768,3072]{1,0:T(8,128)(2,1)S(1)} %unpack.5.refs_0_.weight_ref, ...), custom_call_target="tpu_custom_call" | custom-call | flops 14000000000 | bytes 1000000 | tf_op jit(solution)/shard_map/turn/pallas_call | solution.py:147
  119.4 3.8 %hidden_back.1 = (bf16[512,3072]{1,0:T(8,128)(2,1)S(1)}, f32[1,3072]{1,0:T(1,128)S(1)}) custom-call(bf16[768,3072]{1,0:T(8,128)(2,1)S(1)} %unpack.5.refs_0_.weight_ref, bf16[512,768]{1,0:T(8,128)(2,1)S(1)} %get-tuple-element.241.gzb_ref, bf16[512,3072]{1,0:T(8,128)(2,1)S(1)} %get-tuple-element.242.slope_ref), custom_call_target="tpu_custom_call" | custom-call | flops 12000000000 | bytes 1000000 | tf_op jit(solution)/shard_map/hidden_back/pallas_call | solution.py:147
  124.3 1.9 collective-permute-start.24
  126.7 10.6 %first_back.1 = (f32[512,768]{1,0:T(8,128)S(1)}, bf16[512,768]{1,0:T(8,128)(2,1)S(1)}, f32[8,768]{1,0:T(8,128)S(1)}, bf16[768,1920]{1,0:T(8,128)(2,1)S(1)}, bf16[768,1920]{1,0:T(8,128)(2,1)S(1)}) custom-call(bf16[768,768]{1,0:T(8,128)(2,1)S(1)} %get-tuple-element.226.w_out.refs_0_, bf16[768,3072]{1,0:T(8,128)(2,1)S(1)} %get-tuple-element.227.w_up.refs_1_, ...), custom_call_target="tpu_custom_call" | custom-call | flops 20000000000 | bytes 1000000 | tf_op jit(solution)/shard_map/first_back/pallas_call | solution.py:147
  137.3 5.1 %collective-permute-done.23.refs_2_ = bf16[384,1536]{1,0:T(8,128)(2,1)S(1)} collective-permute-done((bf16[384,1536]{1,0:T(8,128)(2,1)S(1)}, bf16[384,1536]{1,0:T(8,128)(2,1)S(1)}, u32[]{:S(2)}, u32[]{:S(2)}) %collective-permute-start.23) | collective-permute-done | bytes 1179680 | tf_op jit(solution)/shard_map/ppermute | solution.py:39
  142.7 5.3 %attend_back.2 = (bf16[512,384]{1,0:T(8,128)(2,1)S(1)}, bf16[512,384]{1,0:T(8,128)(2,1)S(1)}, bf16[512,384]{1,0:T(8,128)(2,1)S(1)}) custom-call(bf16[512,2304]{1,0:T(8,128)(2,1)S(1)} %get-tuple-element.220.refs_0_, bf16[6,512,512]{2,1,0:T(8,128)(2,1)S(1)} %get-tuple-element.254.refs_1_, bf16[512,768]{1,0:T(8,128)(2,1)S(1)} %get-tuple-element.273.refs_2_), custom_call_target="tpu_custom_call" | custom-call | flops 2000000000 | bytes 1000000 | tf_op jit(solution)/shard_map/attend_back/pallas_call | solution.py:147
  149.1 1.9 collective-permute-start.28
  151.0 5.6 %attend_back.3 = (bf16[512,384]{1,0:T(8,128)(2,1)S(1)}, bf16[512,384]{1,0:T(8,128)(2,1)S(1)}, bf16[512,384]{1,0:T(8,128)(2,1)S(1)}) custom-call(bf16[512,2304]{1,0:T(8,128)(2,1)S(1)} %get-tuple-element.220.refs_0_, bf16[6,512,512]{2,1,0:T(8,128)(2,1)S(1)} %get-tuple-element.268.refs_1_, bf16[512,768]{1,0:T(8,128)(2,1)S(1)} %get-tuple-element.273.refs_2_), custom_call_target="tpu_custom_call" | custom-call | flops 2000000000 | bytes 1000000 | tf_op jit(solution)/shard_map/attend_back/pallas_call | solution.py:147
  156.6 2.7 %input_back.1.own_ref = bf16[4,128,768]{2,1,0:T(8,128)(2,1)S(1)} custom-call(bf16[768,2304]{1,0:T(8,128)(2,1)S(1)} %unpack.3.refs_0_, f32[512,768]{1,0:T(8,128)S(1)} %get-tuple-element.253.refs_1_, bf16[512,384]{1,0:T(8,128)(2,1)S(1)} %get-tuple-element.280.refs_2_.refs_4_, bf16[512,384]{1,0:T(8,128)(2,1)S(1)} %get-tuple-element.266.refs_3_.refs_5_, ...), custom_call_target="tpu_custom_call" | custom-call | flops 1000000000 | bytes 1000000 | tf_op jit(solution)/shard_map/input_back/pallas_call | solution.py:147
  159.5 2.9 %last.1 = (bf16[776,1152]{1,0:T(8,128)(2,1)S(1)}, bf16[776,1152]{1,0:T(8,128)(2,1)S(1)}) custom-call(bf16[512,768]{1,0:T(8,128)(2,1)S(1)} %get-tuple-element.229.x_ref.refs_0_, f32[8,768]{1,0:T(8,128)S(1)} %get-tuple-element.277.refs_1_, f32[8,768]{1,0:T(8,128)S(1)} %get-tuple-element.278.refs_2_, f32[1,3072]{1,0:T(1,128)S(1)} %get-tuple-element.279.refs_3_, ...), custom_call_target="tpu_custom_call" | custom-call | flops 1000000000 | bytes 1000000 | tf_op jit(solution)/shard_map/last/pallas_call | solution.py:147
  162.9 11.2 %collective-permute-done.28.refs_3_ = bf16[192,1536]{1,0:T(8,128)(2,1)S(1)} collective-permute-done((bf16[192,1536]{1,0:T(8,128)(2,1)S(1)}, bf16[192,1536]{1,0:T(8,128)(2,1)S(1)}, u32[]{:S(2)}, u32[]{:S(2)}) %collective-permute-start.28) | collective-permute-done | bytes 589856 | tf_op jit(solution)/shard_map/ppermute | solution.py:39
  175.5 1.2 collective-permute-start.33
  176.8 14.5 %collective-permute-done.31.refs_2_ = bf16[392,1152]{1,0:T(8,128)(2,1)S(1)} collective-permute-done((bf16[392,1152]{1,0:T(8,128)(2,1)S(1)}, bf16[392,1152]{1,0:T(8,128)(2,1)S(1)}, u32[]{:S(2)}, u32[]{:S(2)}) %collective-permute-start.31) | collective-permute-done | bytes 903200 | tf_op jit(solution)/shard_map/ppermute | solution.py:39
  192.3 2.3 collective-permute-done.34.refs_3_
  195.4 1.0 collective-permute-start.36
  196.4 4.3 %collective-permute-done.32.refs_3_ = bf16[200,1152]{1,0:T(8,128)(2,1)S(1)} collective-permute-done((bf16[200,1152]{1,0:T(8,128)(2,1)S(1)}, bf16[200,1152]{1,0:T(8,128)(2,1)S(1)}, u32[]{:S(2)}, u32[]{:S(2)}) %collective-permute-start.32) | collective-permute-done | bytes 460832 | tf_op jit(solution)/shard_map/ppermute | solution.py:39
  201.0 1.1 collective-permute-done.36.refs_5_
  202.7 1.1 collective-permute-done.38.refs_4_
  204.0 2.3 collective-permute-start.41
  206.3 1.3 deliver.2
  207.7 1.2 collective-permute-start.44
  208.9 0.9 collective-permute-start.39
  209.8 8.5 %collective-permute-done.41.refs_5_ = bf16[48,1920]{1,0:T(8,128)(2,1)S(1)} collective-permute-done((bf16[48,1920]{1,0:T(8,128)(2,1)S(1)}, bf16[48,1920]{1,0:T(8,128)(2,1)S(1)}, u32[]{:S(2)}, u32[]{:S(2)}) %collective-permute-start.41) | collective-permute-done | bytes 184352 | tf_op jit(solution)/shard_map/ppermute | solution.py:39
  218.5 0.9 collective-permute-start.43
  219.4 0.9 collective-permute-start.42
  220.5 2.8 %collective-permute-start.47 = (bf16[48,1152]{1,0:T(8,128)(2,1)S(1)}, bf16[48,1152]{1,0:T(8,128)(2,1)S(1)}, u32[]{:S(2)}, u32[]{:S(2)}) collective-permute-start(bf16[48,1152]{1,0:T(8,128)(2,1)S(1)} %add.67.refs_0_), channel_id=1, source_target_pairs={{0,6},{1,7},{2,4},{3,5},{4,2},{5,3},{6,0},{7,1},{8,14},{9,15},{10,... | collective-permute-start | bytes 331784 | tf_op jit(solution)/shard_map/ppermute | solution.py:39
  223.2 1.0 collective-permute-start.46
  224.9 1.6 collective-permute-start.45
  226.5 1.2 settle.3
  228.0 1.3 deliver.3
  229.3 1.6 collective-permute-done.45.refs_1_
  230.9 1.0 settle.4
  231.9 1.2 settle.5
  (145 shorter events, 18.7 us)
Async XLA Ops:
  0.6 6.8 %copy-start = (bf16[4,2,128,768]{3,2,1,0:T(8,128)(2,1)S(1)}, bf16[4,2,128,768]{3,2,1,0:T(8,128)(2,1)}, u32[]{:S(2)}) copy-start(bf16[4,2,128,768]{3,2,1,0:T(8,128)(2,1)} %param.15) | copy-start | bytes 4718596
  1.7 5.9 %copy-start.14 = (bf16[192,1536]{1,0:T(8,128)(2,1)S(1)}, bf16[192,1536]{1,0:T(8,128)(2,1)}, u32[]{:S(2)}) copy-start(bf16[192,1536]{1,0:T(8,128)(2,1)} %param.23) | copy-start | bytes 1769476
  1.7 5.9 %copy-start.15 = (bf16[384,192]{0,1:T(8,128)(2,1)S(1)}, bf16[384,192]{0,1:T(8,128)(2,1)}, u32[]{:S(2)}) copy-start(bf16[384,192]{0,1:T(8,128)(2,1)} %param.19) | copy-start | bytes 442372
  1.7 7.3 %collective-permute-start = (bf16[48,1152]{1,0:T(8,128)(2,1)S(1)}, bf16[48,1152]{1,0:T(8,128)(2,1)S(1)}, u32[]{:S(2)}, u32[]{:S(2)}) collective-permute-start(bf16[48,1152]{1,0:T(8,128)(2,1)S(1)} %bitcast.15), channel_id=1, source_target_pairs={{0,16},{1,17},{2,10},{3,11},{4,20},{5,21},{6,14},{7,15},{8,24},{9,... | collective-permute-start | bytes 331784 | tf_op jit(solution)/shard_map/ppermute | solution.py:39
  8.9 18.7 %copy-start.4 = (f32[1536]{0:T(1024)S(1)}, f32[1536]{0:T(1024)}, u32[]{:S(2)}) copy-start(f32[1536]{0:T(1024)} %up_ref) | copy-start | bytes 18436
  9.0 18.7 %copy-start.5 = (f32[768]{0:T(1024)S(1)}, f32[768]{0:T(1024)}, u32[]{:S(2)}) copy-start(f32[768]{0:T(1024)} %refs_0_.1) | copy-start | bytes 9220
  9.0 18.7 %copy-start.6 = (f32[768]{0:T(1024)S(1)}, f32[768]{0:T(1024)}, u32[]{:S(2)}) copy-start(f32[768]{0:T(1024)} %refs_1_.1) | copy-start | bytes 9220
  9.0 18.7 %copy-start.7 = (f32[768]{0:T(1024)S(1)}, f32[768]{0:T(1024)}, u32[]{:S(2)}) copy-start(f32[768]{0:T(1024)} %refs_2_.1) | copy-start | bytes 9220
  9.0 18.7 %copy-start.8 = (f32[768]{0:T(1024)S(1)}, f32[768]{0:T(1024)}, u32[]{:S(2)}) copy-start(f32[768]{0:T(1024)} %refs_3_.1) | copy-start | bytes 9220
  9.0 18.7 %copy-start.9 = (f32[768]{0:T(1024)S(1)}, f32[768]{0:T(1024)}, u32[]{:S(2)}) copy-start(f32[768]{0:T(1024)} %refs_4_.1) | copy-start | bytes 9220
  9.0 18.7 %copy-start.10 = (f32[768]{0:T(1024)S(1)}, f32[768]{0:T(1024)}, u32[]{:S(2)}) copy-start(f32[768]{0:T(1024)} %refs_5_.1) | copy-start | bytes 9220
  9.0 18.7 %copy-start.11 = (f32[2,384]{1,0:T(2,128)S(1)}, f32[2,384]{1,0:T(2,128)}, u32[]{:S(2)}) copy-start(f32[2,384]{1,0:T(2,128)} %qv_ref.1) | copy-start | bytes 9220
  9.1 13.4 %collective-permute-start.1 = (bf16[96,1152]{1,0:T(8,128)(2,1)S(1)}, bf16[96,1152]{1,0:T(8,128)(2,1)S(1)}, u32[]{:S(2)}, u32[]{:S(2)}) collective-permute-start(bf16[96,1152]{1,0:T(8,128)(2,1)S(1)} %pad_maximum_fusion.15), channel_id=1, source_target_pairs={{0,8},{1,9},{2,18},{3,19},{4,12},{5,13},{6,22},{7,23},{8,0},{9,1},... | collective-permute-start | bytes 663560 | tf_op jit(solution)/shard_map/ppermute | solution.py:39
  10.9 9.9 %collective-permute-start.3 = (bf16[1,136,768]{2,1,0:T(8,128)(2,1)S(1)}, bf16[1,136,768]{2,1,0:T(8,128)(2,1)S(1)}, u32[]{:S(2)}, u32[]{:S(2)}) collective-permute-start(bf16[1,136,768]{2,1,0:T(8,128)(2,1)S(1)} %get-tuple-element.180), channel_id=1, source_target_pairs={{0,2},{1,3},{2,0},{3,1},{4,6},{5,7},{6,4},{7,5},{8,10},{9,11},{10,... | collective-permute-start | bytes 626696 | tf_op jit(solution)/shard_map/ppermute | solution.py:39
  10.9 9.9 %collective-permute-start.4 = (bf16[1,136,768]{2,1,0:T(8,128)(2,1)S(1)}, bf16[1,136,768]{2,1,0:T(8,128)(2,1)S(1)}, u32[]{:S(2)}, u32[]{:S(2)}) collective-permute-start(bf16[1,136,768]{2,1,0:T(8,128)(2,1)S(1)} %get-tuple-element.181), channel_id=1, source_target_pairs={{0,4},{1,5},{2,6},{3,7},{4,0},{5,1},{6,2},{7,3},{8,12},{9,13},{10,... | collective-permute-start | bytes 626696 | tf_op jit(solution)/shard_map/ppermute | solution.py:39
  12.4 10.2 %collective-permute-start.5 = (bf16[1,136,768]{2,1,0:T(8,128)(2,1)S(1)}, bf16[1,136,768]{2,1,0:T(8,128)(2,1)S(1)}, u32[]{:S(2)}, u32[]{:S(2)}) collective-permute-start(bf16[1,136,768]{2,1,0:T(8,128)(2,1)S(1)} %get-tuple-element.182), channel_id=1, source_target_pairs={{0,6},{1,7},{2,4},{3,5},{4,2},{5,3},{6,0},{7,1},{8,14},{9,15},{10,... | collective-permute-start | bytes 626696 | tf_op jit(solution)/shard_map/ppermute | solution.py:39
  12.7 8.0 %collective-permute-start.2 = (bf16[48,1536]{1,0:T(8,128)(2,1)S(1)}, bf16[48,1536]{1,0:T(8,128)(2,1)S(1)}, u32[]{:S(2)}, u32[]{:S(2)}) collective-permute-start(bf16[48,1536]{1,0:T(8,128)(2,1)S(1)} %dynamic-slice_bitcast_fusion.2), channel_id=1, source_target_pairs={{0,16},{1,17},{2,3},{3,2},{4,20},{5,21},{6,7},{7,6},{8,24},{9,25},... | collective-permute-start | bytes 442376 | tf_op jit(solution)/shard_map/ppermute | solution.py:39
  22.6 12.8 %collective-permute-start.6 = (bf16[192,1152]{1,0:T(8,128)(2,1)S(1)}, bf16[192,1152]{1,0:T(8,128)(2,1)S(1)}, u32[]{:S(2)}, u32[]{:S(2)}) collective-permute-start(bf16[192,1152]{1,0:T(8,128)(2,1)S(1)} %pad_maximum_fusion.7), channel_id=1, source_target_pairs={{0,1},{1,0},{2,6},{3,7},{4,5},{5,4},{6,2},{7,3},{8,9},{9,8},{10,14... | collective-permute-start | bytes 1327112 | tf_op jit(solution)/shard_map/ppermute | solution.py:39
  24.2 8.4 %collective-permute-start.7 = (bf16[48,1920]{1,0:T(8,128)(2,1)S(1)}, bf16[48,1920]{1,0:T(8,128)(2,1)S(1)}, u32[]{:S(2)}, u32[]{:S(2)}) collective-permute-start(bf16[48,1920]{1,0:T(8,128)(2,1)S(1)} %fusion.2), channel_id=1, source_target_pairs={{0,16},{1,17},{2,10},{3,11},{4,20},{5,21},{6,14},{7,15},{8,24},{9,... | collective-permute-start | bytes 552968 | tf_op jit(solution)/shard_map/ppermute | solution.py:39
  27.6 7.9 %collective-permute-start.8 = (bf16[96,1536]{1,0:T(8,128)(2,1)S(1)}, bf16[96,1536]{1,0:T(8,128)(2,1)S(1)}, u32[]{:S(2)}, u32[]{:S(2)}) collective-permute-start(bf16[96,1536]{1,0:T(8,128)(2,1)S(1)} %pad_maximum_fusion.14), channel_id=1, source_target_pairs={{0,8},{1,9},{2,6},{3,7},{4,12},{5,13},{6,2},{7,3},{8,0},{9,1},{10,... | collective-permute-start | bytes 884744 | tf_op jit(solution)/shard_map/ppermute | solution.py:39
  35.6 13.1 %collective-permute-start.9 = (bf16[384,1152]{1,0:T(8,128)(2,1)S(1)}, bf16[384,1152]{1,0:T(8,128)(2,1)S(1)}, u32[]{:S(2)}, u32[]{:S(2)}) collective-permute-start(bf16[384,1152]{1,0:T(8,128)(2,1)S(1)} %pad_maximum_fusion.2), channel_id=1, source_target_pairs={{0,4},{1,5},{2,3},{3,2},{4,0},{5,1},{6,7},{7,6},{8,12},{9,13},{10,... | collective-permute-start | bytes 2654216 | tf_op jit(solution)/shard_map/ppermute | solution.py:39
  37.0 11.4 %collective-permute-start.11 = (bf16[2,128,768]{2,1,0:T(8,128)(2,1)S(1)}, bf16[2,128,768]{2,1,0:T(8,128)(2,1)S(1)}, u32[]{:S(2)}, u32[]{:S(2)}) collective-permute-start(bf16[2,128,768]{2,1,0:T(8,128)(2,1)S(1)} %pad_maximum_fusion.9), channel_id=1, source_target_pairs={{0,2},{1,3},{2,0},{3,1},{4,6},{5,7},{6,4},{7,5},{8,10},{9,11},{10,... | collective-permute-start | bytes 1179656 | tf_op jit(solution)/shard_map/ppermute | solution.py:39
  37.0 11.4 %collective-permute-start.10 = (bf16[96,1920]{1,0:T(8,128)(2,1)S(1)}, bf16[96,1920]{1,0:T(8,128)(2,1)S(1)}, u32[]{:S(2)}, u32[]{:S(2)}) collective-permute-start(bf16[96,1920]{1,0:T(8,128)(2,1)S(1)} %pad_maximum_fusion.13), channel_id=1, source_target_pairs={{0,8},{1,9},{2,18},{3,19},{4,12},{5,13},{6,22},{7,23},{8,0},{9,1},... | collective-permute-start | bytes 1105928 | tf_op jit(solution)/shard_map/ppermute | solution.py:39
  38.0 3.8 %collective-permute-start.12 = (f32[1,2304]{1,0:T(1,128)S(1)}, f32[1,2304]{1,0:T(1,128)S(1)}, u32[]{:S(2)}, u32[]{:S(2)}) collective-permute-start(f32[1,2304]{1,0:T(1,128)S(1)} %get-tuple-element.200), channel_id=1, source_target_pairs={{0,1},{1,0},{2,3},{3,2},{4,5},{5,4},{6,7},{7,6},{8,9},{9,8},{10,11... | collective-permute-start | bytes 27656 | tf_op jit(solution)/shard_map/ppermute | solution.py:39
  48.4 14.3 %copy-start.2 = (bf16[2,128,768]{2,1,0:T(8,128)(2,1)}, bf16[2,128,768]{2,1,0:T(8,128)(2,1)S(1)}, u32[]{:S(2)}) copy-start(bf16[2,128,768]{2,1,0:T(8,128)(2,1)S(1)} %collective-permute-done.11.refs_4_) | copy-start | bytes 1179652
  48.9 3.8 %collective-permute-start.13 = (bf16[768,1152]{1,0:T(8,128)(2,1)S(1)}, bf16[768,1152]{1,0:T(8,128)(2,1)S(1)}, u32[]{:S(2)}, u32[]{:S(2)}) collective-permute-start(bf16[768,1152]{1,0:T(8,128)(2,1)S(1)} %pad_maximum_fusion.1.refs_0_), channel_id=1, source_target_pairs={{0,2},{1,3},{2,0},{3,1},{4,6},{5,7},{6,4},{7,5},{8,10},{9,11},{10,... | collective-permute-start | bytes 5308424 | tf_op jit(solution)/shard_map/ppermute | solution.py:39
  49.0 20.4 %collective-permute-start.15 = (bf16[192,1536]{1,0:T(8,128)(2,1)S(1)}, bf16[192,1536]{1,0:T(8,128)(2,1)S(1)}, u32[]{:S(2)}, u32[]{:S(2)}) collective-permute-start(bf16[192,1536]{1,0:T(8,128)(2,1)S(1)} %pad_maximum_fusion.6), channel_id=1, source_target_pairs={{0,4},{1,5},{2,18},{3,19},{4,0},{5,1},{6,22},{7,23},{8,12},{9,13},... | collective-permute-start | bytes 1769480 | tf_op jit(solution)/shard_map/ppermute | solution.py:39
  50.4 11.5 %collective-permute-start.14 = (bf16[192,1920]{1,0:T(8,128)(2,1)S(1)}, bf16[192,1920]{1,0:T(8,128)(2,1)S(1)}, u32[]{:S(2)}, u32[]{:S(2)}) collective-permute-start(bf16[192,1920]{1,0:T(8,128)(2,1)S(1)} %pad_maximum_fusion.5), channel_id=1, source_target_pairs={{0,1},{1,0},{2,6},{3,7},{4,5},{5,4},{6,2},{7,3},{8,9},{9,8},{10,14... | collective-permute-start | bytes 2211848 | tf_op jit(solution)/shard_map/ppermute | solution.py:39
  62.0 20.7 %collective-permute-start.16 = (bf16[384,1920]{1,0:T(8,128)(2,1)S(1)}, bf16[384,1920]{1,0:T(8,128)(2,1)S(1)}, u32[]{:S(2)}, u32[]{:S(2)}) collective-permute-start(bf16[384,1920]{1,0:T(8,128)(2,1)S(1)} %constant_dynamic-update-slice_fusion), channel_id=1, source_target_pairs={{0,4},{1,5},{2,3},{3,2},{4,0},{5,1},{6,7},{7,6},{8,12},{9,13},{10,... | collective-permute-start | bytes 4423688 | tf_op jit(solution)/shard_map/ppermute | solution.py:39
  82.9 9.0 %collective-permute-start.17 = (bf16[768,1920]{1,0:T(8,128)(2,1)S(1)}, bf16[768,1920]{1,0:T(8,128)(2,1)S(1)}, u32[]{:S(2)}, u32[]{:S(2)}) collective-permute-start(bf16[768,1920]{1,0:T(8,128)(2,1)S(1)} %pad_maximum_fusion.refs_0_), channel_id=1, source_target_pairs={{0,2},{1,3},{2,0},{3,1},{4,6},{5,7},{6,4},{7,5},{8,10},{9,11},{10,... | collective-permute-start | bytes 8847368 | tf_op jit(solution)/shard_map/ppermute | solution.py:39
  86.9 16.4 %collective-permute-start.18 = (bf16[384,1536]{1,0:T(8,128)(2,1)}, bf16[384,1536]{1,0:T(8,128)(2,1)S(1)}, u32[]{:S(2)}, u32[]{:S(2)}) collective-permute-start(bf16[384,1536]{1,0:T(8,128)(2,1)} %get-tuple-element.353), channel_id=1, source_target_pairs={{0,1},{1,0},{2,10},{3,11},{4,5},{5,4},{6,14},{7,15},{8,9},{9,8},{1... | collective-permute-start | bytes 3538952 | tf_op jit(solution)/shard_map/ppermute | solution.py:39
  87.3 16.1 %collective-permute-start.19 = (bf16[2,128,768]{2,1,0:T(8,128)(2,1)S(1)}, bf16[2,128,768]{2,1,0:T(8,128)(2,1)S(1)}, u32[]{:S(2)}, u32[]{:S(2)}) collective-permute-start(bf16[2,128,768]{2,1,0:T(8,128)(2,1)S(1)} %pad_maximum_fusion.10), channel_id=1, source_target_pairs={{0,4},{1,5},{2,6},{3,7},{4,0},{5,1},{6,2},{7,3},{8,12},{9,13},{10,... | collective-permute-start | bytes 1179656 | tf_op jit(solution)/shard_map/ppermute | solution.py:39
  103.0 6.7 %copy-start.12 = (f32[512,768]{1,0:T(8,128)}, f32[512,768]{1,0:T(8,128)S(1)}, u32[]{:S(2)}) copy-start(f32[512,768]{1,0:T(8,128)S(1)} %get-tuple-element.235.refs_2_.refs_4_) | copy-start | bytes 4718596
  103.4 6.2 %copy-start.3 = (bf16[2,128,768]{2,1,0:T(8,128)(2,1)S(1)}, bf16[2,128,768]{2,1,0:T(8,128)(2,1)}, u32[]{:S(2)}) copy-start(bf16[2,128,768]{2,1,0:T(8,128)(2,1)} %copy-done.2) | copy-start | bytes 1179652
  103.4 4.6 %collective-permute-start.20 = (bf16[768,1536]{1,0:T(8,128)(2,1)S(1)}, bf16[768,1536]{1,0:T(8,128)(2,1)S(1)}, u32[]{:S(2)}, u32[]{:S(2)}) collective-permute-start(bf16[768,1536]{1,0:T(8,128)(2,1)S(1)} %constant_dynamic-update-slice_fusion.4.refs_0_), channel_id=1, source_target_pairs={{0,2},{1,3},{2,0},{3,1},{4,6},{5,7},{6,4},{7,5},{8,10},{9,11},{10,... | collective-permute-start | bytes 7077896 | tf_op jit(solution)/shard_map/ppermute | solution.py:39
  118.8 5.2 %collective-permute-start.21 = (bf16[768,1536]{1,0:T(8,128)(2,1)S(1)}, bf16[768,1536]{1,0:T(8,128)(2,1)S(1)}, u32[]{:S(2)}, u32[]{:S(2)}) collective-permute-start(bf16[768,1536]{1,0:T(8,128)(2,1)S(1)} %get-tuple-element.244), channel_id=1, source_target_pairs={{0,2},{1,3},{2,0},{3,1},{4,6},{5,7},{6,4},{7,5},{8,10},{9,11},{10,... | collective-permute-start | bytes 7077896 | tf_op jit(solution)/shard_map/ppermute | solution.py:39
  119.0 4.9 %collective-permute-start.22 = (bf16[2,128,768]{2,1,0:T(8,128)(2,1)S(1)}, bf16[2,128,768]{2,1,0:T(8,128)(2,1)S(1)}, u32[]{:S(2)}, u32[]{:S(2)}) collective-permute-start(bf16[2,128,768]{2,1,0:T(8,128)(2,1)S(1)} %slice.34), channel_id=1, source_target_pairs={{0,2},{1,3},{2,0},{3,1},{4,6},{5,7},{6,4},{7,5},{8,10},{9,11},{10,... | collective-permute-start | bytes 1179656 | tf_op jit(solution)/shard_map/ppermute | solution.py:39
  124.0 2.7 %copy-start.13 = (f32[512,768]{1,0:T(8,128)S(1)}, f32[512,768]{1,0:T(8,128)}, u32[]{:S(2)}) copy-start(f32[512,768]{1,0:T(8,128)} %copy-done.12) | copy-start | bytes 4718596
  124.3 13.0 %collective-permute-start.24 = (bf16[2,128,768]{2,1,0:T(8,128)(2,1)S(1)}, bf16[2,128,768]{2,1,0:T(8,128)(2,1)S(1)}, u32[]{:S(2)}, u32[]{:S(2)}) collective-permute-start(bf16[2,128,768]{2,1,0:T(8,128)(2,1)S(1)} %pad_maximum_fusion.11), channel_id=1, source_target_pairs={{0,4},{1,5},{2,6},{3,7},{4,0},{5,1},{6,2},{7,3},{8,12},{9,13},{10,... | collective-permute-start | bytes 1179656 | tf_op jit(solution)/shard_map/ppermute | solution.py:39
  126.2 16.2 %collective-permute-start.23 = (bf16[384,1536]{1,0:T(8,128)(2,1)S(1)}, bf16[384,1536]{1,0:T(8,128)(2,1)S(1)}, u32[]{:S(2)}, u32[]{:S(2)}) collective-permute-start(bf16[384,1536]{1,0:T(8,128)(2,1)S(1)} %add.53), channel_id=1, source_target_pairs={{0,1},{1,0},{2,10},{3,11},{4,5},{5,4},{6,14},{7,15},{8,9},{9,8},{1... | collective-permute-start | bytes 3538952 | tf_op jit(solution)/shard_map/ppermute | solution.py:39
  142.4 5.6 %collective-permute-start.25 = (bf16[768,1920]{1,0:T(8,128)(2,1)S(1)}, bf16[768,1920]{1,0:T(8,128)(2,1)S(1)}, u32[]{:S(2)}, u32[]{:S(2)}) collective-permute-start(bf16[768,1920]{1,0:T(8,128)(2,1)S(1)} %get-tuple-element.264), channel_id=1, source_target_pairs={{0,2},{1,3},{2,0},{3,1},{4,6},{5,7},{6,4},{7,5},{8,10},{9,11},{10,... | collective-permute-start | bytes 8847368 | tf_op jit(solution)/shard_map/ppermute | solution.py:39
  148.4 25.8 %collective-permute-start.26 = (bf16[384,1920]{1,0:T(8,128)(2,1)S(1)}, bf16[384,1920]{1,0:T(8,128)(2,1)S(1)}, u32[]{:S(2)}, u32[]{:S(2)}) collective-permute-start(bf16[384,1920]{1,0:T(8,128)(2,1)S(1)} %add.55), channel_id=1, source_target_pairs={{0,4},{1,5},{2,10},{3,11},{4,0},{5,1},{6,14},{7,15},{8,12},{9,13},... | collective-permute-start | bytes 4423688 | tf_op jit(solution)/shard_map/ppermute | solution.py:39
  148.7 25.5 %collective-permute-start.27 = (bf16[4,128,768]{2,1,0:T(8,128)(2,1)S(1)}, bf16[4,128,768]{2,1,0:T(8,128)(2,1)S(1)}, u32[]{:S(2)}, u32[]{:S(2)}) collective-permute-start(bf16[4,128,768]{2,1,0:T(8,128)(2,1)S(1)} %pad_maximum_fusion.3), channel_id=1, source_target_pairs={{0,1},{1,0},{2,3},{3,2},{4,5},{5,4},{6,7},{7,6},{8,9},{9,8},{10,11... | collective-permute-start | bytes 2359304 | tf_op jit(solution)/shard_map/ppermute | solution.py:39
  149.1 25.1 %collective-permute-start.28 = (bf16[192,1536]{1,0:T(8,128)(2,1)S(1)}, bf16[192,1536]{1,0:T(8,128)(2,1)S(1)}, u32[]{:S(2)}, u32[]{:S(2)}) collective-permute-start(bf16[192,1536]{1,0:T(8,128)(2,1)S(1)} %add.54), channel_id=1, source_target_pairs={{0,4},{1,5},{2,18},{3,19},{4,0},{5,1},{6,22},{7,23},{8,12},{9,13},... | collective-permute-start | bytes 1769480 | tf_op jit(solution)/shard_map/ppermute | solution.py:39
  159.4 15.2 %collective-permute-start.30 = (bf16[2,128,768]{2,1,0:T(8,128)(2,1)S(1)}, bf16[2,128,768]{2,1,0:T(8,128)(2,1)S(1)}, u32[]{:S(2)}, u32[]{:S(2)}) collective-permute-start(bf16[2,128,768]{2,1,0:T(8,128)(2,1)S(1)} %slice.44), channel_id=1, source_target_pairs={{0,2},{1,3},{2,0},{3,1},{4,6},{5,7},{6,4},{7,5},{8,10},{9,11},{10,... | collective-permute-start | bytes 1179656 | tf_op jit(solution)/shard_map/ppermute | solution.py:39
  162.4 12.2 %collective-permute-start.29 = (bf16[776,1152]{1,0:T(8,128)(2,1)S(1)}, bf16[776,1152]{1,0:T(8,128)(2,1)S(1)}, u32[]{:S(2)}, u32[]{:S(2)}) collective-permute-start(bf16[776,1152]{1,0:T(8,128)(2,1)S(1)} %get-tuple-element.288), channel_id=1, source_target_pairs={{0,2},{1,3},{2,0},{3,1},{4,6},{5,7},{6,4},{7,5},{8,10},{9,11},{10,... | collective-permute-start | bytes 5363720 | tf_op jit(solution)/shard_map/ppermute | solution.py:39
  174.9 16.5 %collective-permute-start.31 = (bf16[392,1152]{1,0:T(8,128)(2,1)S(1)}, bf16[392,1152]{1,0:T(8,128)(2,1)S(1)}, u32[]{:S(2)}, u32[]{:S(2)}) collective-permute-start(bf16[392,1152]{1,0:T(8,128)(2,1)S(1)} %add.58.refs_3_), channel_id=1, source_target_pairs={{0,4},{1,5},{2,3},{3,2},{4,0},{5,1},{6,7},{7,6},{8,12},{9,13},{10,... | collective-permute-start | bytes 2709512 | tf_op jit(solution)/shard_map/ppermute | solution.py:39
  175.1 19.4 %collective-permute-start.34 = (bf16[192,1920]{1,0:T(8,128)(2,1)S(1)}, bf16[192,1920]{1,0:T(8,128)(2,1)S(1)}, u32[]{:S(2)}, u32[]{:S(2)}) collective-permute-start(bf16[192,1920]{1,0:T(8,128)(2,1)S(1)} %add.57), channel_id=1, source_target_pairs={{0,1},{1,0},{2,18},{3,19},{4,5},{5,4},{6,22},{7,23},{8,9},{9,8},{1... | collective-permute-start | bytes 2211848 | tf_op jit(solution)/shard_map/ppermute | solution.py:39
  175.5 16.6 %collective-permute-start.33 = (bf16[96,1536]{1,0:T(8,128)(2,1)S(1)}, bf16[96,1536]{1,0:T(8,128)(2,1)S(1)}, u32[]{:S(2)}, u32[]{:S(2)}) collective-permute-start(bf16[96,1536]{1,0:T(8,128)(2,1)S(1)} %add.56), channel_id=1, source_target_pairs={{0,8},{1,9},{2,6},{3,7},{4,12},{5,13},{6,2},{7,3},{8,0},{9,1},{10,... | collective-permute-start | bytes 884744 | tf_op jit(solution)/shard_map/ppermute | solution.py:39
  191.5 9.3 %collective-permute-start.32 = (bf16[200,1152]{1,0:T(8,128)(2,1)S(1)}, bf16[200,1152]{1,0:T(8,128)(2,1)S(1)}, u32[]{:S(2)}, u32[]{:S(2)}) collective-permute-start(bf16[200,1152]{1,0:T(8,128)(2,1)S(1)} %add.59.refs_4_), channel_id=1, source_target_pairs={{0,1},{1,0},{2,6},{3,7},{4,5},{5,4},{6,2},{7,3},{8,9},{9,8},{10,14... | collective-permute-start | bytes 1382408 | tf_op jit(solution)/shard_map/ppermute | solution.py:39
  192.1 10.1 %collective-permute-start.37 = (bf16[2,128,768]{2,1,0:T(8,128)(2,1)S(1)}, bf16[2,128,768]{2,1,0:T(8,128)(2,1)S(1)}, u32[]{:S(2)}, u32[]{:S(2)}) collective-permute-start(bf16[2,128,768]{2,1,0:T(8,128)(2,1)S(1)} %pad_maximum_fusion.12), channel_id=1, source_target_pairs={{0,4},{1,5},{2,6},{3,7},{4,0},{5,1},{6,2},{7,3},{8,12},{9,13},{10,... | collective-permute-start | bytes 1179656 | tf_op jit(solution)/shard_map/ppermute | solution.py:39
  194.7 9.2 %collective-permute-start.38 = (bf16[96,1920]{1,0:T(8,128)(2,1)S(1)}, bf16[96,1920]{1,0:T(8,128)(2,1)S(1)}, u32[]{:S(2)}, u32[]{:S(2)}) collective-permute-start(bf16[96,1920]{1,0:T(8,128)(2,1)S(1)} %add.61), channel_id=1, source_target_pairs={{0,8},{1,9},{2,3},{3,2},{4,12},{5,13},{6,7},{7,6},{8,0},{9,1},{10,... | collective-permute-start | bytes 1105928 | tf_op jit(solution)/shard_map/ppermute | solution.py:39
  195.4 6.6 %collective-permute-start.36 = (bf16[48,1536]{1,0:T(8,128)(2,1)S(1)}, bf16[48,1536]{1,0:T(8,128)(2,1)S(1)}, u32[]{:S(2)}, u32[]{:S(2)}) collective-permute-start(bf16[48,1536]{1,0:T(8,128)(2,1)S(1)} %add.60), channel_id=1, source_target_pairs={{0,16},{1,17},{2,3},{3,2},{4,20},{5,21},{6,7},{7,6},{8,24},{9,25},... | collective-permute-start | bytes 442376 | tf_op jit(solution)/shard_map/ppermute | solution.py:39
  200.9 8.0 %collective-permute-start.35 = (bf16[104,1152]{1,0:T(8,128)(2,1)S(1)}, bf16[104,1152]{1,0:T(8,128)(2,1)S(1)}, u32[]{:S(2)}, u32[]{:S(2)}) collective-permute-start(bf16[104,1152]{1,0:T(8,128)(2,1)S(1)} %add.62.refs_5_), channel_id=1, source_target_pairs={{0,8},{1,9},{2,18},{3,19},{4,12},{5,13},{6,22},{7,23},{8,0},{9,1},... | collective-permute-start | bytes 718856 | tf_op jit(solution)/shard_map/ppermute | solution.py:39
  202.3 7.5 %collective-permute-start.40 = (bf16[48,1536]{1,0:T(8,128)(2,1)S(1)}, bf16[48,1536]{1,0:T(8,128)(2,1)S(1)}, u32[]{:S(2)}, u32[]{:S(2)}) collective-permute-start(bf16[48,1536]{1,0:T(8,128)(2,1)S(1)} %add.63), channel_id=1, source_target_pairs={{0,4},{1,5},{2,6},{3,7},{4,0},{5,1},{6,2},{7,3},{8,12},{9,13},{10,... | collective-permute-start | bytes 442376 | tf_op jit(solution)/shard_map/ppermute | solution.py:39
  204.0 14.3 %collective-permute-start.41 = (bf16[48,1920]{1,0:T(8,128)(2,1)S(1)}, bf16[48,1920]{1,0:T(8,128)(2,1)S(1)}, u32[]{:S(2)}, u32[]{:S(2)}) collective-permute-start(bf16[48,1920]{1,0:T(8,128)(2,1)S(1)} %add.64), channel_id=1, source_target_pairs={{0,16},{1,17},{2,6},{3,7},{4,20},{5,21},{6,2},{7,3},{8,24},{9,25},... | collective-permute-start | bytes 552968 | tf_op jit(solution)/shard_map/ppermute | solution.py:39
  207.7 20.4 %collective-permute-start.44 = (bf16[4,128,768]{2,1,0:T(8,128)(2,1)S(1)}, bf16[4,128,768]{2,1,0:T(8,128)(2,1)S(1)}, u32[]{:S(2)}, u32[]{:S(2)}) collective-permute-start(bf16[4,128,768]{2,1,0:T(8,128)(2,1)S(1)} %pad_maximum_fusion.4), channel_id=1, source_target_pairs={{0,1},{1,0},{2,3},{3,2},{4,5},{5,4},{6,7},{7,6},{8,9},{9,8},{10,11... | collective-permute-start | bytes 2359304 | tf_op jit(solution)/shard_map/ppermute | solution.py:39
  208.9 11.5 %collective-permute-start.39 = (bf16[56,1152]{1,0:T(8,128)(2,1)S(1)}, bf16[56,1152]{1,0:T(8,128)(2,1)S(1)}, u32[]{:S(2)}, u32[]{:S(2)}) collective-permute-start(bf16[56,1152]{1,0:T(8,128)(2,1)S(1)} %add.65.refs_0_), channel_id=1, source_target_pairs={{0,16},{1,17},{2,10},{3,11},{4,20},{5,21},{6,14},{7,15},{8,24},{9,... | collective-permute-start | bytes 387080 | tf_op jit(solution)/shard_map/ppermute | solution.py:39
  218.5 9.3 %collective-permute-start.43 = (bf16[48,1920]{1,0:T(8,128)(2,1)S(1)}, bf16[48,1920]{1,0:T(8,128)(2,1)S(1)}, u32[]{:S(2)}, u32[]{:S(2)}) collective-permute-start(bf16[48,1920]{1,0:T(8,128)(2,1)S(1)} %add.66), channel_id=1, source_target_pairs={{0,4},{1,5},{2,6},{3,7},{4,0},{5,1},{6,2},{7,3},{8,12},{9,13},{10,... | collective-permute-start | bytes 552968 | tf_op jit(solution)/shard_map/ppermute | solution.py:39
  219.4 5.5 %collective-permute-start.42 = (bf16[96,1536]{1,0:T(8,128)(2,1)S(1)}, bf16[96,1536]{1,0:T(8,128)(2,1)S(1)}, u32[]{:S(2)}, u32[]{:S(2)}) collective-permute-start(bf16[96,1536]{1,0:T(8,128)(2,1)S(1)} %constant_dynamic-update-slice_fusion.7.refs_0_), channel_id=1, source_target_pairs={{0,2},{1,3},{2,0},{3,1},{4,6},{5,7},{6,4},{7,5},{8,10},{9,11},{10,... | collective-permute-start | bytes 884744 | tf_op jit(solution)/shard_map/ppermute | solution.py:39
  220.5 8.8 %collective-permute-start.47 = (bf16[48,1152]{1,0:T(8,128)(2,1)S(1)}, bf16[48,1152]{1,0:T(8,128)(2,1)S(1)}, u32[]{:S(2)}, u32[]{:S(2)}) collective-permute-start(bf16[48,1152]{1,0:T(8,128)(2,1)S(1)} %add.67.refs_0_), channel_id=1, source_target_pairs={{0,6},{1,7},{2,4},{3,5},{4,2},{5,3},{6,0},{7,1},{8,14},{9,15},{10,... | collective-permute-start | bytes 331784 | tf_op jit(solution)/shard_map/ppermute | solution.py:39
  223.2 6.1 %collective-permute-start.46 = (bf16[48,1152]{1,0:T(8,128)(2,1)S(1)}, bf16[48,1152]{1,0:T(8,128)(2,1)S(1)}, u32[]{:S(2)}, u32[]{:S(2)}) collective-permute-start(bf16[48,1152]{1,0:T(8,128)(2,1)S(1)} %add.67.refs_0_), channel_id=1, source_target_pairs={{0,2},{1,3},{2,0},{3,1},{4,6},{5,7},{6,4},{7,5},{8,10},{9,11},{10,... | collective-permute-start | bytes 331784 | tf_op jit(solution)/shard_map/ppermute | solution.py:39
  224.9 6.0 %collective-permute-start.45 = (bf16[48,1152]{1,0:T(8,128)(2,1)S(1)}, bf16[48,1152]{1,0:T(8,128)(2,1)S(1)}, u32[]{:S(2)}, u32[]{:S(2)}) collective-permute-start(bf16[48,1152]{1,0:T(8,128)(2,1)S(1)} %add.67.refs_0_), channel_id=1, source_target_pairs={{0,4},{1,5},{2,6},{3,7},{4,0},{5,1},{6,2},{7,3},{8,12},{9,13},{10,... | collective-permute-start | bytes 331784 | tf_op jit(solution)/shard_map/ppermute | solution.py:39
  227.7 4.2 %collective-permute-start.48 = (bf16[96,1920]{1,0:T(8,128)(2,1)S(1)}, bf16[96,1920]{1,0:T(8,128)(2,1)S(1)}, u32[]{:S(2)}, u32[]{:S(2)}) collective-permute-start(bf16[96,1920]{1,0:T(8,128)(2,1)S(1)} %constant_dynamic-update-slice_fusion.9.refs_0_), channel_id=1, source_target_pairs={{0,2},{1,3},{2,0},{3,1},{4,6},{5,7},{6,4},{7,5},{8,10},{9,11},{10,... | collective-permute-start | bytes 1105928 | tf_op jit(solution)/shard_map/ppermute | solution.py:39
  (2 other events, 2.9 us)

commit v6 on v5

--- a/solution.py
+++ b/solution.py
@@ -99,14 +99,15 @@
     return pl.ds(start if isinstance(start, int) else pl.multiple_of(start, unit or count), count)
 
 
-def piece_copies(spots, own_ref, sib_ref, sem, whole, low, cols, base=0):
+def piece_copies(spots, near, far, sem, whole, low, cols, base=0):
     rows = whole.shape[0] // 16
     copies = []
-    for half, ref in ((0, own_ref), (1, sib_ref)):
+    each = 16 // len(near)
+    for half, refs in ((0, near), (1, far)):
         for i in range(16):
             row, col = spots[half * 16 + i]
             copy = pltpu.make_async_copy(
-                ref.at[pl.ds(i * rows, rows), pl.ds(low, cols)],
+                refs[i // each].at[pl.ds(i % each * rows, rows), pl.ds(low, cols)],
                 whole.at[at_rows(row, rows), at_rows(col, cols, 128)],
                 sem.at[base + half * 16 + i],
             )
@@ -159,30 +160,31 @@
 B_OUT, GAIN1, SHIFT1, B_DOWN, GAIN2, SHIFT2 = range(6)
 
 
-def unpack_kernel(own_ref, sib_ref, *refs, orders):
-    outs, sem = refs[:-1], refs[-1]
+def unpack_kernel(*refs, orders, count):
+    near, far, outs, sem = refs[:count], refs[count : 2 * count], refs[2 * count : -1], refs[-1]
     copies = []
     spots = places(orders)
     low = 0
     for i, out in enumerate(outs):
         cols = out.shape[1] // 2
-        copies += piece_copies(spots, own_ref, sib_ref, sem, out, low, cols, 32 * i)
+        copies += piece_copies(spots, near, far, sem, out, low, cols, 32 * i)
         low += cols
     finish(copies)
 
 
-def unpack(orders, own, sib, widths):
-    rows = own.shape[0]
-    return call(
-        lambda *refs: unpack_kernel(*refs, orders=orders),
+def unpack(orders, near, far, widths):
+    count = len(near)
+    rows = near[0].shape[0] * count
+    return call(
+        lambda *refs: unpack_kernel(*refs, orders=orders, count=count),
         "unpack",
         tuple(struct((rows, width), BF16) for width in widths),
-        [ANY, ANY],
+        [ANY] * (2 * count),
         (VMEM,) * len(widths),
         [pltpu.SemaphoreType.DMA((32 * len(widths),))],
         5,
         2,
-        (own, sib),
+        tuple(near) + tuple(far),
     )
 
 
@@ -575,7 +577,7 @@
         [VMEM] * 3,
         (VMEM,) * 3,
         [pltpu.VMEM((length, length), BF16), pltpu.VMEM((128, length), BF16)],
-        2,
+        1,
         4,
         (proj, probs, grad_mixed),
     )
@@ -621,7 +623,7 @@
             pltpu.VMEM((width, 3 * width), BF16),
             pltpu.VMEM((8, 3 * width // 2), F32),
         ],
-        1,
+        10,
         7,
         (x, sums1, sums2, sum_up) + tuple(parts),
     )
@@ -758,7 +760,7 @@
         [VMEM] * 8,
         VMEM,
         [],
-        1,
+        2,
         3,
         (weight, gz1) + tuple(parts),
     )
@@ -897,33 +899,38 @@
         table, small = tables(b_qv, b_up, (b_out, ln1_gain, ln1_bias, b_down, ln2_gain, ln2_bias))
         g1, g2, g3, c_send, small = phase(g1, g2, g3, c_send, small)
         h1, h2, h3 = phase(joined(h1, g1), joined(h2, g2), joined(h3, g3))
-        g1, g2, ck, got = phase(
-            swap(h1, 0, 3), swap(h2, 1, 1), exchange(c_send, CORE, sizes), exchange(small, Y, sizes)
+        g1, g2, ck, got, f1 = phase(
+            swap(h1, 0, 3),
+            swap(h2, 1, 1),
+            exchange(c_send, CORE, sizes),
+            exchange(small, Y, sizes),
+            exchange(h1, CORE, sizes),
         )
         small = joined(small, got)
-        h1, h2, h3 = phase(joined(h1, g1), joined(h2, g2), h3)
-        g1, g2, g3 = swap(h1, 0, 4), swap(h2, 1, 2), swap(h3, 2, 2)
-        (wq,) = unpack(gathers[0], h1, g1, (3 * width,))
+        g1, h2, h3 = phase(g1, joined(h2, g2), h3)
+        k1, g2, g3 = exchange(g1, CORE, sizes), swap(h2, 1, 2), swap(h3, 2, 2)
+        (wq,) = unpack(gathers[0], (h1, g1), (f1, k1), (3 * width,))
         proj, rows_b, mask = project(wq, given, small, fast)
         proj, g2, c2, ck = phase(proj, g2, c2, ck)
         h2 = joined(h2, g2)
         g2 = swap(h2, 1, 3)
         mixed0, probs0 = attend(after(proj, h2), mask, 0)
-        mixed0, g3 = phase(mixed0, g3)
+        mixed0, g3, h2 = phase(mixed0, g3, h2)
         h3 = joined(h3, g3)
-        g3 = swap(h3, 2, 3)
+        f2, g3, f3 = exchange(h2, CORE, sizes), swap(h3, 2, 3), exchange(h3, CORE, sizes)
         mixed1, probs1 = attend(after(proj, h3, mixed0), mask, 1)
-        mixed1, g2 = phase(mixed1, g2)
-        h2, c_send = phase(joined(h2, g2), joined(c2, ck[1:]))
-        g2, cx = swap(h2, 1, 4), exchange(c_send, X, sizes)
-        wo, wu = unpack(gathers[1], h2, g2, (width, 2 * local_units))
+        mixed1, g2, f2 = phase(mixed1, g2, f2)
+        g2, c_send = phase(g2, joined(c2, ck[1:]))
+        k2, cx = exchange(g2, CORE, sizes), exchange(c_send, X, sizes)
+        wo, wu = unpack(gathers[1], (h2, g2), (f2, k2), (width, 2 * local_units))
     else:
         parts = (shards[0], w_out.T, w_up, w_down.T)
         pieces = [cut(gather_plain(s)) for s in parts]
-        (wq,) = unpack(None, *pieces[0], (3 * width,))
-        (wo,) = unpack(None, *pieces[1], (width,))
-        (wu,) = unpack(None, *pieces[2], (2 * local_units,))
-        (wd,) = unpack(None, *pieces[3], (2 * local_units,))
+        split = lambda pair: ((pair[0],), (pair[1],))
+        (wq,) = unpack(None, *split(pieces[0]), (3 * width,))
+        (wo,) = unpack(None, *split(pieces[1]), (width,))
+        (wu,) = unpack(None, *split(pieces[2]), (2 * local_units,))
+        (wd,) = unpack(None, *split(pieces[3]), (2 * local_units,))
         order = lambda value: (value[:1], value[1:3], value[2:])
         given, cot = order(to_owners(rows_in)), order(to_owners(cot_in))
         table, small = tables(b_qv, b_up, (b_out, ln1_gain, ln1_bias, b_down, ln2_gain, ln2_bias))
@@ -934,10 +941,9 @@
 
     normed1, scale1, first_b, act, slope = middle(wo, wu, mixed0, mixed1, rows_b, table, small)
     if fast:
-        act, g3, cx = phase(act, g3, cx)
+        act, g3, f3, cx = phase(act, g3, f3, cx)
         cot = (c0, ck, cx)
-        h3 = joined(h3, g3)
-        (wd,) = unpack(gathers[2], h3, swap(h3, 2, 4), (2 * local_units,))
+        (wd,) = unpack(gathers[2], (h3, g3), (f3, exchange(g3, CORE, sizes)), (2 * local_units,))
     chunks, gz, gzb, sums2, down_own, down_sib = turn(packs[2], wd, act, normed1, cot, table, local_len)
 
     rows = shard_rows // 4
@@ -961,27 +967,34 @@
         send, y_send, grad_mixed = phase(
             add_up(down, 4 * rows, 8 * rows), joined(chunks[:1], core_out[:1], x_out), grad_mixed
         )
-        got, got2 = shed(send, 2, 2), shed(up_sib, 1, 0)
+        got, got2, y_out = shed(send, 2, 2), shed(up_sib, 1, 0), exchange(y_send, Y, sizes)
     parts0 = attend_back(proj, probs0, grad_mixed, 0)
     if fast:
         head, got2, grad_mixed = phase(parts0[0], got2, grad_mixed)
         parts0 = (head,) + tuple(parts0[1:])
         up = [up_own, got2]
-        send2, grad_mixed, y_send = phase(add_up(up, 8 * rows, 16 * rows), grad_mixed, y_send)
-        got2, y_out = shed(send2, 1, 1), exchange(y_send, Y, sizes)
+        send2, grad_mixed = phase(add_up(up, 8 * rows, 16 * rows), grad_mixed)
+        got2 = shed(send2, 1, 1)
     parts1 = attend_back(proj, probs1, grad_mixed, 1)
     parts = list(parts0) + list(parts1)
+    if fast:
+        parts[3], got = phase(parts[3], got)
+        down = down + [got]
+        send = add_up(down, 2 * rows, 4 * rows)
+        got = shed(send, 2, 3)
+        parts[3], send = phase(parts[3], send)
     chunks2 = input_back(wq, gz1, parts, local_len, fast)
+    if fast:
+        chunks2, y_out = phase(chunks2, y_out)
     parts[0] = after(parts[0], chunks2)
     qkv_own, qkv_sib = last(packs[0], rows_b, sums1, sums2, sum_up, parts)
     if fast:
         got3, core_x = shed(qkv_sib, 0, 0), exchange(chunks2[2:], CORE, sizes)
-        chunks2, qkv_own, got2, y_out, got = phase(chunks2, qkv_own, got2, y_out, got)
-        down, up = down + [got], up + [got2]
-        send = add_up(down, 2 * rows, 4 * rows)
+        chunks2, qkv_own, got2 = phase(chunks2, qkv_own, got2)
+        up = up + [got2]
         send2 = add_up(up, 4 * rows, 8 * rows, time=30)
-        send, send2, got3 = phase(send, send2, got3)
-        got, got2 = shed(send, 2, 3), shed(send2, 1, 2)
+        send2, got3 = phase(send2, got3)
+        got2 = shed(send2, 1, 2)
         got3, core_x = phase(got3, core_x)
         qkv = [qkv_own, got3]
         sent3 = add_up(qkv, 8 * rows, 16 * rows, (0, 1))

time: 234 us -> 229 us (0.979)
  waiting for transfers between devices: 93.7 us -> 78 us
  starting transfers between devices: 51.4 us -> 62.7 us
    ppermute x49 -> x52, waiting for transfers between devices: 93.7 us -> 78 us  [exchange(): return lax.ppermute(value, AXES, pairs)]
    ppermute x49 -> x52, starting transfers between devices: 51.4 us -> 62.7 us  [exchange(): return lax.ppermute(value, AXES, pairs)]
  transfers between devices with their start and end apart: 49 -> 52, of which waited for: 25 -> 22; matrix products, arithmetic and copies ran while one was open for 2% -> 2% of each run, Pallas kernels for 28% -> 29%
where the time goes in v6:
time: 229 us; the launch traced here: 228 us
  Pallas kernels  79.3 us (35%)
  waiting for transfers between devices  78 us (34%)
  starting transfers between devices  62.7 us (27%)
  local copies, waits for them, and re-layouts  5.48 us (2%)
    pallas_call x36, Pallas kernels, call(): pl.pallas_call(kernel, name=name, out_shape=outs, in_specs=specs, out_spe...  79.3 us
    ppermute x52, waiting for transfers between devices, exchange(): return lax.ppermute(value, AXES, pairs)  78 us
    ppermute x52, starting transfers between devices, exchange(): return lax.ppermute(value, AXES, pairs)  62.7 us
  transfers between devices with their start and end apart: 52, of which 22 were waited for; matrix products, arithmetic and copies ran while one was open for 2% of the time, Pallas kernels for 29%

profile of v6, /device:TPU:0, one launch (start us, length us, event | category | flops | bytes accessed | tf_op | source)
XLA Modules:
  0.0 228.3 jit_solution(7821878364300153806)
XLA Ops:
  0.7 1.0 dynamic-slice_bitcast_fusion.3
  1.7 4.1 %collective-permute-start = (bf16[48,1152]{1,0:T(8,128)(2,1)S(1)}, bf16[48,1152]{1,0:T(8,128)(2,1)S(1)}, u32[]{:S(2)}, u32[]{:S(2)}) collective-permute-start(bf16[48,1152]{1,0:T(8,128)(2,1)S(1)} %bitcast.15), channel_id=1, source_target_pairs={{0,16},{1,17},{2,10},{3,11},{4,20},{5,21},{6,14},{7,15},{8,24},{9,... | collective-permute-start | bytes 331784 | tf_op jit(solution)/shard_map/ppermute | solution.py:39
  8.6 1.2 dynamic-slice_bitcast_fusion
  10.0 1.6 collective-permute-start.1
  11.6 1.5 collective-permute-start.4
  13.5 2.7 %collective-permute-start.2 = (bf16[48,1536]{1,0:T(8,128)(2,1)S(1)}, bf16[48,1536]{1,0:T(8,128)(2,1)S(1)}, u32[]{:S(2)}, u32[]{:S(2)}) collective-permute-start(bf16[48,1536]{1,0:T(8,128)(2,1)S(1)} %dynamic-slice_bitcast_fusion.2), channel_id=1, source_target_pairs={{0,16},{1,17},{2,3},{3,2},{4,20},{5,21},{6,7},{7,6},{8,24},{9,25},... | collective-permute-start | bytes 442376 | tf_op jit(solution)/shard_map/ppermute | solution.py:39
  16.2 4.8 %collective-permute-done.2 = bf16[48,1536]{1,0:T(8,128)(2,1)S(1)} collective-permute-done((bf16[48,1536]{1,0:T(8,128)(2,1)S(1)}, bf16[48,1536]{1,0:T(8,128)(2,1)S(1)}, u32[]{:S(2)}, u32[]{:S(2)}) %collective-permute-start.2) | collective-permute-done | bytes 147488 | tf_op jit(solution)/shard_map/ppermute | solution.py:39
  21.0 2.3 %collective-permute-done.5 = bf16[1,136,768]{2,1,0:T(8,128)(2,1)S(1)} collective-permute-done((bf16[1,136,768]{2,1,0:T(8,128)(2,1)S(1)}, bf16[1,136,768]{2,1,0:T(8,128)(2,1)S(1)}, u32[]{:S(2)}, u32[]{:S(2)}) %collective-permute-start.5) | collective-permute-done | bytes 208928 | tf_op jit(solution)/shard_map/ppermute | solution.py:39
  23.4 1.6 collective-permute-start.6
  24.9 2.7 %collective-permute-start.7 = (bf16[48,1920]{1,0:T(8,128)(2,1)S(1)}, bf16[48,1920]{1,0:T(8,128)(2,1)S(1)}, u32[]{:S(2)}, u32[]{:S(2)}) collective-permute-start(bf16[48,1920]{1,0:T(8,128)(2,1)S(1)} %fusion.2), channel_id=1, source_target_pairs={{0,16},{1,17},{2,10},{3,11},{4,20},{5,21},{6,14},{7,15},{8,24},{9,... | collective-permute-start | bytes 552968 | tf_op jit(solution)/shard_map/ppermute | solution.py:39
  27.9 5.5 %collective-permute-done.7 = bf16[48,1920]{1,0:T(8,128)(2,1)S(1)} collective-permute-done((bf16[48,1920]{1,0:T(8,128)(2,1)S(1)}, bf16[48,1920]{1,0:T(8,128)(2,1)S(1)}, u32[]{:S(2)}, u32[]{:S(2)}) %collective-permute-start.7) | collective-permute-done | bytes 184352 | tf_op jit(solution)/shard_map/ppermute | solution.py:39
  33.3 2.2 collective-permute-done.8
  35.8 1.5 collective-permute-start.9
  37.2 0.9 collective-permute-start.10
  38.9 3.1 %collective-permute-done.12 = f32[1,2304]{1,0:T(1,128)S(1)} collective-permute-done((f32[1,2304]{1,0:T(1,128)S(1)}, f32[1,2304]{1,0:T(1,128)S(1)}, u32[]{:S(2)}, u32[]{:S(2)}) %collective-permute-start.12) | collective-permute-done | bytes 9248 | tf_op jit(solution)/shard_map/ppermute | solution.py:39
  42.0 6.6 %collective-permute-done.10 = bf16[96,1920]{1,0:T(8,128)(2,1)S(1)} collective-permute-done((bf16[96,1920]{1,0:T(8,128)(2,1)S(1)}, bf16[96,1920]{1,0:T(8,128)(2,1)S(1)}, u32[]{:S(2)}, u32[]{:S(2)}) %collective-permute-start.10) | collective-permute-done | bytes 368672 | tf_op jit(solution)/shard_map/ppermute | solution.py:39
  49.1 1.5 collective-permute-start.16
  51.4 1.5 unpack.3.refs_0_
  52.9 2.6 %project.1 = (bf16[512,2304]{1,0:T(8,128)(2,1)S(1)}, bf16[512,768]{1,0:T(8,128)(2,1)S(1)}, f32[512,512]{1,0:T(8,128)S(1)}) custom-call(bf16[768,2304]{1,0:T(8,128)(2,1)S(1)} %unpack.3.refs_0_, bf16[1,136,768]{2,1,0:T(8,128)(2,1)S(1)} %get-tuple-element.350.refs_1_, bf16[1,136,768]{2,1,0:T(8,128)(2,1)S(1)} %collective-permute-done.3.refs_2_, ...), custom_call_target="tpu_custom_call" | custom-call | flops 5000000000 | bytes 1000000 | tf_op jit(solution)/shard_map/project/pallas_call | solution.py:148
  55.6 6.4 %collective-permute-done.15 = bf16[192,1920]{1,0:T(8,128)(2,1)S(1)} collective-permute-done((bf16[192,1920]{1,0:T(8,128)(2,1)S(1)}, bf16[192,1920]{1,0:T(8,128)(2,1)S(1)}, u32[]{:S(2)}, u32[]{:S(2)}) %collective-permute-start.15) | collective-permute-done | bytes 737312 | tf_op jit(solution)/shard_map/ppermute | solution.py:39
  62.8 6.7 %attend.2 = (bf16[512,384]{1,0:T(8,128)(2,1)S(1)}, bf16[6,512,512]{2,1,0:T(8,128)(2,1)S(1)}) custom-call(bf16[512,2304]{1,0:T(8,128)(2,1)S(1)} %get-tuple-element.227.refs_0_, f32[512,512]{1,0:T(8,128)S(1)} %get-tuple-element.221.refs_1_), custom_call_target="tpu_custom_call" | custom-call | flops 12000000000 | bytes 1000000 | tf_op jit(solution)/shard_map/attend/pallas_call | solution.py:148
  69.4 6.8 %collective-permute-start.18 = (bf16[384,1920]{1,0:T(8,128)(2,1)S(1)}, bf16[384,1920]{1,0:T(8,128)(2,1)S(1)}, u32[]{:S(2)}, u32[]{:S(2)}) collective-permute-start(bf16[384,1920]{1,0:T(8,128)(2,1)S(1)} %constant_dynamic-update-slice_fusion.refs_0_), channel_id=1, source_target_pairs={{0,2},{1,3},{2,0},{3,1},{4,6},{5,7},{6,4},{7,5},{8,10},{9,11},{10,... | collective-permute-start | bytes 4423688 | tf_op jit(solution)/shard_map/ppermute | solution.py:39
  76.3 6.7 %attend.3 = (bf16[512,384]{1,0:T(8,128)(2,1)S(1)}, bf16[6,512,512]{2,1,0:T(8,128)(2,1)S(1)}) custom-call(bf16[512,2304]{1,0:T(8,128)(2,1)S(1)} %get-tuple-element.227.refs_0_, f32[512,512]{1,0:T(8,128)S(1)} %get-tuple-element.221.refs_1_), custom_call_target="tpu_custom_call" | custom-call | flops 12000000000 | bytes 1000000 | tf_op jit(solution)/shard_map/attend/pallas_call | solution.py:148
  83.0 3.5 %collective-permute-start.19 = (bf16[384,1920]{1,0:T(8,128)(2,1)S(1)}, bf16[384,1920]{1,0:T(8,128)(2,1)S(1)}, u32[]{:S(2)}, u32[]{:S(2)}) collective-permute-start(bf16[384,1920]{1,0:T(8,128)(2,1)S(1)} %collective-permute-done.17.refs_1_), channel_id=1, source_target_pairs={{0,2},{1,3},{2,0},{3,1},{4,6},{5,7},{6,4},{7,5},{8,10},{9,11},{10,... | collective-permute-start | bytes 4423688 | tf_op jit(solution)/shard_map/ppermute | solution.py:39
  86.5 1.4 collective-permute-start.20
  88.0 1.0 collective-permute-start.22
  89.4 2.4 %unpack.4 = (bf16[768,768]{1,0:T(8,128)(2,1)S(1)}, bf16[768,3072]{1,0:T(8,128)(2,1)S(1)}) custom-call(bf16[384,1920]{1,0:T(8,128)(2,1)S(1)} %constant_dynamic-update-slice_fusion.refs_0_, bf16[384,1920]{1,0:T(8,128)(2,1)S(1)} %collective-permute-done.17.refs_1_, bf16[384,1920]{1,0:T(8,128)(2,1)S(1)} %collective-permute-done.18.refs_2_, ...), custom_call_target="tpu_custom_call" | custom-call | flops 5000000000 | bytes 1000000 | tf_op jit(solution)/shard_map/unpack/pallas_call | solution.py:148
  91.8 8.7 %middle.1 = (f32[512,768]{1,0:T(8,128)S(1)}, f32[512,1]{1,0:T(8,128)S(1)}, bf16[512,768]{1,0:T(8,128)(2,1)S(1)}, bf16[512,3072]{1,0:T(8,128)(2,1)S(1)}, bf16[512,3072]{1,0:T(8,128)(2,1)S(1)}) custom-call(bf16[768,768]{1,0:T(8,128)(2,1)S(1)} %get-tuple-element.234.w_out.refs_0_, bf16[768,3072]{1,0:T(8,128)(2,1)S(1)} %get-tuple-element.235.w_up.refs_1_, ...), custom_call_target="tpu_custom_call" | custom-call | flops 12000000000 | bytes 1000000 | tf_op jit(solution)/shard_map/middle/pallas_call | solution.py:148
  100.6 2.2 collective-permute-done.20.refs_1_
  102.7 2.8 %collective-permute-done.23.refs_3_ = bf16[384,1536]{1,0:T(8,128)(2,1)S(1)} collective-permute-done((bf16[384,1536]{1,0:T(8,128)(2,1)S(1)}, bf16[384,1536]{1,0:T(8,128)(2,1)S(1)}, u32[]{:S(2)}, u32[]{:S(2)}) %collective-permute-start.23) | collective-permute-done | bytes 1179680 | tf_op jit(solution)/shard_map/ppermute | solution.py:39
  105.6 1.7 unpack.5.refs_0_.weight_ref
  107.3 9.1 %turn.1 = (bf16[4,128,768]{2,1,0:T(8,128)(2,1)S(1)}, f32[512,768]{1,0:T(8,128)S(1)}, bf16[512,768]{1,0:T(8,128)(2,1)S(1)}, f32[8,768]{1,0:T(8,128)S(1)}, bf16[76...) custom-call(bf16[768,3072]{1,0:T(8,128)(2,1)S(1)} %unpack.5.refs_0_.weight_ref, ...), custom_call_target="tpu_custom_call" | custom-call | flops 14000000000 | bytes 1000000 | tf_op jit(solution)/shard_map/turn/pallas_call | solution.py:148
  117.0 3.8 %hidden_back.1 = (bf16[512,3072]{1,0:T(8,128)(2,1)S(1)}, f32[1,3072]{1,0:T(1,128)S(1)}) custom-call(bf16[768,3072]{1,0:T(8,128)(2,1)S(1)} %unpack.5.refs_0_.weight_ref, bf16[512,768]{1,0:T(8,128)(2,1)S(1)} %get-tuple-element.250.gzb_ref, bf16[512,3072]{1,0:T(8,128)(2,1)S(1)} %get-tuple-element.251.slope_ref), custom_call_target="tpu_custom_call" | custom-call | flops 12000000000 | bytes 1000000 | tf_op jit(solution)/shard_map/hidden_back/pallas_call | solution.py:148
  121.9 2.2 collective-permute-start.27
  124.4 10.5 %first_back.1 = (f32[512,768]{1,0:T(8,128)S(1)}, bf16[512,768]{1,0:T(8,128)(2,1)S(1)}, f32[8,768]{1,0:T(8,128)S(1)}, bf16[768,1920]{1,0:T(8,128)(2,1)S(1)}, bf16[768,1920]{1,0:T(8,128)(2,1)S(1)}) custom-call(bf16[768,768]{1,0:T(8,128)(2,1)S(1)} %get-tuple-element.234.w_out.refs_0_, bf16[768,3072]{1,0:T(8,128)(2,1)S(1)} %get-tuple-element.235.w_up.refs_1_, ...), custom_call_target="tpu_custom_call" | custom-call | flops 20000000000 | bytes 1000000 | tf_op jit(solution)/shard_map/first_back/pallas_call | solution.py:148
  134.9 5.4 %collective-permute-done.26.refs_2_ = bf16[384,1536]{1,0:T(8,128)(2,1)S(1)} collective-permute-done((bf16[384,1536]{1,0:T(8,128)(2,1)S(1)}, bf16[384,1536]{1,0:T(8,128)(2,1)S(1)}, u32[]{:S(2)}, u32[]{:S(2)}) %collective-permute-start.26) | collective-permute-done | bytes 1179680 | tf_op jit(solution)/shard_map/ppermute | solution.py:39
  140.7 1.3 collective-permute-start.30
  142.0 5.3 %attend_back.2 = (bf16[512,384]{1,0:T(8,128)(2,1)S(1)}, bf16[512,384]{1,0:T(8,128)(2,1)S(1)}, bf16[512,384]{1,0:T(8,128)(2,1)S(1)}) custom-call(bf16[512,2304]{1,0:T(8,128)(2,1)S(1)} %get-tuple-element.227.refs_0_, bf16[6,512,512]{2,1,0:T(8,128)(2,1)S(1)} %get-tuple-element.263.refs_1_, bf16[512,768]{1,0:T(8,128)(2,1)S(1)} %get-tuple-element.281.refs_2_), custom_call_target="tpu_custom_call" | custom-call | flops 1000000000 | bytes 1000000 | tf_op jit(solution)/shard_map/attend_back/pallas_call | solution.py:148
  147.7 1.0 collective-permute-start.31
  148.7 5.6 %attend_back.3 = (bf16[512,384]{1,0:T(8,128)(2,1)S(1)}, bf16[512,384]{1,0:T(8,128)(2,1)S(1)}, bf16[512,384]{1,0:T(8,128)(2,1)S(1)}) custom-call(bf16[512,2304]{1,0:T(8,128)(2,1)S(1)} %get-tuple-element.227.refs_0_, bf16[6,512,512]{2,1,0:T(8,128)(2,1)S(1)} %get-tuple-element.277.refs_1_, bf16[512,768]{1,0:T(8,128)(2,1)S(1)} %get-tuple-element.281.refs_2_), custom_call_target="tpu_custom_call" | custom-call | flops 1000000000 | bytes 1000000 | tf_op jit(solution)/shard_map/attend_back/pallas_call | solution.py:148
  154.5 2.7 %input_back.1.own_ref = bf16[4,128,768]{2,1,0:T(8,128)(2,1)S(1)} custom-call(bf16[768,2304]{1,0:T(8,128)(2,1)S(1)} %unpack.3.refs_0_, f32[512,768]{1,0:T(8,128)S(1)} %get-tuple-element.262.refs_1_, bf16[512,384]{1,0:T(8,128)(2,1)S(1)} %get-tuple-element.294.refs_2_.refs_4_, bf16[512,384]{1,0:T(8,128)(2,1)S(1)} %get-tuple-element.275.refs_3_.refs_5_, ...), custom_call_target="tpu_custom_call" | custom-call | flops 2000000000 | bytes 1000000 | tf_op jit(solution)/shard_map/input_back/pallas_call | solution.py:148
  157.2 3.9 %collective-permute-done.30.y_ref = bf16[4,128,768]{2,1,0:T(8,128)(2,1)S(1)} collective-permute-done((bf16[4,128,768]{2,1,0:T(8,128)(2,1)S(1)}, bf16[4,128,768]{2,1,0:T(8,128)(2,1)S(1)}, u32[]{:S(2)}, u32[]{:S(2)}) %collective-permute-start.30) | collective-permute-done | bytes 786464 | tf_op jit(solution)/shard_map/ppermute | solution.py:39
  161.4 2.9 %last.1 = (bf16[776,1152]{1,0:T(8,128)(2,1)S(1)}, bf16[776,1152]{1,0:T(8,128)(2,1)S(1)}) custom-call(bf16[512,768]{1,0:T(8,128)(2,1)S(1)} %get-tuple-element.237.x_ref.refs_0_, f32[8,768]{1,0:T(8,128)S(1)} %get-tuple-element.291.refs_1_, f32[8,768]{1,0:T(8,128)S(1)} %get-tuple-element.292.refs_2_, f32[1,3072]{1,0:T(1,128)S(1)} %get-tuple-element.293.refs_3_, ...), custom_call_target="tpu_custom_call" | custom-call | flops 10000000000 | bytes 1000000 | tf_op jit(solution)/shard_map/last/pallas_call | solution.py:148
  164.7 2.4 %collective-permute-done.31.refs_2_ = bf16[384,1920]{1,0:T(8,128)(2,1)S(1)} collective-permute-done((bf16[384,1920]{1,0:T(8,128)(2,1)S(1)}, bf16[384,1920]{1,0:T(8,128)(2,1)S(1)}, u32[]{:S(2)}, u32[]{:S(2)}) %collective-permute-start.31) | collective-permute-done | bytes 1474592 | tf_op jit(solution)/shard_map/ppermute | solution.py:39
  169.2 1.2 collective-permute-start.37
  170.4 1.0 collective-permute-start.36
  171.5 13.2 %collective-permute-done.34.refs_2_ = bf16[392,1152]{1,0:T(8,128)(2,1)S(1)} collective-permute-done((bf16[392,1152]{1,0:T(8,128)(2,1)S(1)}, bf16[392,1152]{1,0:T(8,128)(2,1)S(1)}, u32[]{:S(2)}, u32[]{:S(2)}) %collective-permute-start.34) | collective-permute-done | bytes 903200 | tf_op jit(solution)/shard_map/ppermute | solution.py:39
  184.9 1.3 collective-permute-start.35
  187.4 1.1 collective-permute-start.41
  188.5 1.6 collective-permute-start.39
  190.0 5.2 %collective-permute-done.35.refs_3_ = bf16[200,1152]{1,0:T(8,128)(2,1)S(1)} collective-permute-done((bf16[200,1152]{1,0:T(8,128)(2,1)S(1)}, bf16[200,1152]{1,0:T(8,128)(2,1)S(1)}, u32[]{:S(2)}, u32[]{:S(2)}) %collective-permute-start.35) | collective-permute-done | bytes 460832 | tf_op jit(solution)/shard_map/ppermute | solution.py:39
  198.2 1.2 collective-permute-start.44
  199.4 1.3 deliver.2
  200.7 1.5 collective-permute-start.47
  202.3 2.1 collective-permute-start.42
  204.4 7.2 %collective-permute-done.44.refs_5_ = bf16[48,1920]{1,0:T(8,128)(2,1)S(1)} collective-permute-done((bf16[48,1920]{1,0:T(8,128)(2,1)S(1)}, bf16[48,1920]{1,0:T(8,128)(2,1)S(1)}, u32[]{:S(2)}, u32[]{:S(2)}) %collective-permute-start.44) | collective-permute-done | bytes 184352 | tf_op jit(solution)/shard_map/ppermute | solution.py:39
  212.5 3.1 %collective-permute-start.45 = (bf16[96,1536]{1,0:T(8,128)(2,1)S(1)}, bf16[96,1536]{1,0:T(8,128)(2,1)S(1)}, u32[]{:S(2)}, u32[]{:S(2)}) collective-permute-start(bf16[96,1536]{1,0:T(8,128)(2,1)S(1)} %constant_dynamic-update-slice_fusion.4.refs_0_), channel_id=1, source_target_pairs={{0,2},{1,3},{2,0},{3,1},{4,6},{5,7},{6,4},{7,5},{8,10},{9,11},{10,... | collective-permute-start | bytes 884744 | tf_op jit(solution)/shard_map/ppermute | solution.py:39
  215.6 3.4 %collective-permute-start.50 = (bf16[48,1152]{1,0:T(8,128)(2,1)S(1)}, bf16[48,1152]{1,0:T(8,128)(2,1)S(1)}, u32[]{:S(2)}, u32[]{:S(2)}) collective-permute-start(bf16[48,1152]{1,0:T(8,128)(2,1)S(1)} %add.67.refs_0_), channel_id=1, source_target_pairs={{0,6},{1,7},{2,4},{3,5},{4,2},{5,3},{6,0},{7,1},{8,14},{9,15},{10,... | collective-permute-start | bytes 331784 | tf_op jit(solution)/shard_map/ppermute | solution.py:39
  219.7 1.2 collective-permute-start.48
  220.9 1.2 settle.3
  222.4 1.3 deliver.3
  223.7 1.6 collective-permute-done.48.refs_1_
  225.3 1.0 settle.4
  226.3 1.2 settle.5
  (144 shorter events, 19.7 us)
Async XLA Ops:
  0.6 6.8 %copy-start = (bf16[4,2,128,768]{3,2,1,0:T(8,128)(2,1)S(1)}, bf16[4,2,128,768]{3,2,1,0:T(8,128)(2,1)}, u32[]{:S(2)}) copy-start(bf16[4,2,128,768]{3,2,1,0:T(8,128)(2,1)} %param.15) | copy-start | bytes 4718596
  1.7 8.1 %collective-permute-start = (bf16[48,1152]{1,0:T(8,128)(2,1)S(1)}, bf16[48,1152]{1,0:T(8,128)(2,1)S(1)}, u32[]{:S(2)}, u32[]{:S(2)}) collective-permute-start(bf16[48,1152]{1,0:T(8,128)(2,1)S(1)} %bitcast.15), channel_id=1, source_target_pairs={{0,16},{1,17},{2,10},{3,11},{4,20},{5,21},{6,14},{7,15},{8,24},{9,... | collective-permute-start | bytes 331784 | tf_op jit(solution)/shard_map/ppermute | solution.py:39
  9.9 17.9 %copy-start.4 = (f32[1536]{0:T(1024)S(1)}, f32[1536]{0:T(1024)}, u32[]{:S(2)}) copy-start(f32[1536]{0:T(1024)} %up_ref) | copy-start | bytes 18436
  9.9 17.9 %copy-start.5 = (f32[768]{0:T(1024)S(1)}, f32[768]{0:T(1024)}, u32[]{:S(2)}) copy-start(f32[768]{0:T(1024)} %refs_0_.1) | copy-start | bytes 9220
  9.9 17.8 %copy-start.6 = (f32[768]{0:T(1024)S(1)}, f32[768]{0:T(1024)}, u32[]{:S(2)}) copy-start(f32[768]{0:T(1024)} %refs_1_.1) | copy-start | bytes 9220
  9.9 17.8 %copy-start.7 = (f32[768]{0:T(1024)S(1)}, f32[768]{0:T(1024)}, u32[]{:S(2)}) copy-start(f32[768]{0:T(1024)} %refs_2_.1) | copy-start | bytes 9220
  9.9 17.8 %copy-start.8 = (f32[768]{0:T(1024)S(1)}, f32[768]{0:T(1024)}, u32[]{:S(2)}) copy-start(f32[768]{0:T(1024)} %refs_3_.1) | copy-start | bytes 9220
  9.9 17.8 %copy-start.9 = (f32[768]{0:T(1024)S(1)}, f32[768]{0:T(1024)}, u32[]{:S(2)}) copy-start(f32[768]{0:T(1024)} %refs_4_.1) | copy-start | bytes 9220
  9.9 17.8 %copy-start.10 = (f32[768]{0:T(1024)S(1)}, f32[768]{0:T(1024)}, u32[]{:S(2)}) copy-start(f32[768]{0:T(1024)} %refs_5_.1) | copy-start | bytes 9220
  10.0 17.8 %copy-start.11 = (f32[2,384]{1,0:T(2,128)S(1)}, f32[2,384]{1,0:T(2,128)}, u32[]{:S(2)}) copy-start(f32[2,384]{1,0:T(2,128)} %qv_ref.1) | copy-start | bytes 9220
  10.0 13.3 %collective-permute-start.1 = (bf16[96,1152]{1,0:T(8,128)(2,1)S(1)}, bf16[96,1152]{1,0:T(8,128)(2,1)S(1)}, u32[]{:S(2)}, u32[]{:S(2)}) collective-permute-start(bf16[96,1152]{1,0:T(8,128)(2,1)S(1)} %pad_maximum_fusion.13), channel_id=1, source_target_pairs={{0,8},{1,9},{2,18},{3,19},{4,12},{5,13},{6,22},{7,23},{8,0},{9,1},... | collective-permute-start | bytes 663560 | tf_op jit(solution)/shard_map/ppermute | solution.py:39
  11.6 9.4 %collective-permute-start.3 = (bf16[1,136,768]{2,1,0:T(8,128)(2,1)S(1)}, bf16[1,136,768]{2,1,0:T(8,128)(2,1)S(1)}, u32[]{:S(2)}, u32[]{:S(2)}) collective-permute-start(bf16[1,136,768]{2,1,0:T(8,128)(2,1)S(1)} %get-tuple-element.185), channel_id=1, source_target_pairs={{0,2},{1,3},{2,0},{3,1},{4,6},{5,7},{6,4},{7,5},{8,10},{9,11},{10,... | collective-permute-start | bytes 626696 | tf_op jit(solution)/shard_map/ppermute | solution.py:39
  11.6 9.4 %collective-permute-start.4 = (bf16[1,136,768]{2,1,0:T(8,128)(2,1)S(1)}, bf16[1,136,768]{2,1,0:T(8,128)(2,1)S(1)}, u32[]{:S(2)}, u32[]{:S(2)}) collective-permute-start(bf16[1,136,768]{2,1,0:T(8,128)(2,1)S(1)} %get-tuple-element.186), channel_id=1, source_target_pairs={{0,4},{1,5},{2,6},{3,7},{4,0},{5,1},{6,2},{7,3},{8,12},{9,13},{10,... | collective-permute-start | bytes 626696 | tf_op jit(solution)/shard_map/ppermute | solution.py:39
  13.1 10.2 %collective-permute-start.5 = (bf16[1,136,768]{2,1,0:T(8,128)(2,1)S(1)}, bf16[1,136,768]{2,1,0:T(8,128)(2,1)S(1)}, u32[]{:S(2)}, u32[]{:S(2)}) collective-permute-start(bf16[1,136,768]{2,1,0:T(8,128)(2,1)S(1)} %get-tuple-element.187), channel_id=1, source_target_pairs={{0,6},{1,7},{2,4},{3,5},{4,2},{5,3},{6,0},{7,1},{8,14},{9,15},{10,... | collective-permute-start | bytes 626696 | tf_op jit(solution)/shard_map/ppermute | solution.py:39
  13.5 7.5 %collective-permute-start.2 = (bf16[48,1536]{1,0:T(8,128)(2,1)S(1)}, bf16[48,1536]{1,0:T(8,128)(2,1)S(1)}, u32[]{:S(2)}, u32[]{:S(2)}) collective-permute-start(bf16[48,1536]{1,0:T(8,128)(2,1)S(1)} %dynamic-slice_bitcast_fusion.2), channel_id=1, source_target_pairs={{0,16},{1,17},{2,3},{3,2},{4,20},{5,21},{6,7},{7,6},{8,24},{9,25},... | collective-permute-start | bytes 442376 | tf_op jit(solution)/shard_map/ppermute | solution.py:39
  23.4 12.2 %collective-permute-start.6 = (bf16[192,1152]{1,0:T(8,128)(2,1)S(1)}, bf16[192,1152]{1,0:T(8,128)(2,1)S(1)}, u32[]{:S(2)}, u32[]{:S(2)}) collective-permute-start(bf16[192,1152]{1,0:T(8,128)(2,1)S(1)} %pad_maximum_fusion.5), channel_id=1, source_target_pairs={{0,1},{1,0},{2,6},{3,7},{4,5},{5,4},{6,2},{7,3},{8,9},{9,8},{10,14... | collective-permute-start | bytes 1327112 | tf_op jit(solution)/shard_map/ppermute | solution.py:39
  24.9 8.4 %collective-permute-start.7 = (bf16[48,1920]{1,0:T(8,128)(2,1)S(1)}, bf16[48,1920]{1,0:T(8,128)(2,1)S(1)}, u32[]{:S(2)}, u32[]{:S(2)}) collective-permute-start(bf16[48,1920]{1,0:T(8,128)(2,1)S(1)} %fusion.2), channel_id=1, source_target_pairs={{0,16},{1,17},{2,10},{3,11},{4,20},{5,21},{6,14},{7,15},{8,24},{9,... | collective-permute-start | bytes 552968 | tf_op jit(solution)/shard_map/ppermute | solution.py:39
  27.6 7.9 %collective-permute-start.8 = (bf16[96,1536]{1,0:T(8,128)(2,1)S(1)}, bf16[96,1536]{1,0:T(8,128)(2,1)S(1)}, u32[]{:S(2)}, u32[]{:S(2)}) collective-permute-start(bf16[96,1536]{1,0:T(8,128)(2,1)S(1)} %pad_maximum_fusion.12), channel_id=1, source_target_pairs={{0,8},{1,9},{2,6},{3,7},{4,12},{5,13},{6,2},{7,3},{8,0},{9,1},{10,... | collective-permute-start | bytes 884744 | tf_op jit(solution)/shard_map/ppermute | solution.py:39
  35.7 13.0 %collective-permute-start.13 = (bf16[384,1152]{1,0:T(8,128)(2,1)S(1)}, bf16[384,1152]{1,0:T(8,128)(2,1)S(1)}, u32[]{:S(2)}, u32[]{:S(2)}) collective-permute-start(bf16[384,1152]{1,0:T(8,128)(2,1)S(1)} %pad_maximum_fusion.refs_0_), channel_id=1, source_target_pairs={{0,2},{1,3},{2,0},{3,1},{4,6},{5,7},{6,4},{7,5},{8,10},{9,11},{10,... | collective-permute-start | bytes 2654216 | tf_op jit(solution)/shard_map/ppermute | solution.py:39
  35.8 13.1 %collective-permute-start.9 = (bf16[384,1152]{1,0:T(8,128)(2,1)S(1)}, bf16[384,1152]{1,0:T(8,128)(2,1)S(1)}, u32[]{:S(2)}, u32[]{:S(2)}) collective-permute-start(bf16[384,1152]{1,0:T(8,128)(2,1)S(1)} %pad_maximum_fusion.refs_0_), channel_id=1, source_target_pairs={{0,4},{1,5},{2,3},{3,2},{4,0},{5,1},{6,7},{7,6},{8,12},{9,13},{10,... | collective-permute-start | bytes 2654216 | tf_op jit(solution)/shard_map/ppermute | solution.py:39
  37.2 11.4 %collective-permute-start.11 = (bf16[2,128,768]{2,1,0:T(8,128)(2,1)S(1)}, bf16[2,128,768]{2,1,0:T(8,128)(2,1)S(1)}, u32[]{:S(2)}, u32[]{:S(2)}) collective-permute-start(bf16[2,128,768]{2,1,0:T(8,128)(2,1)S(1)} %pad_maximum_fusion.7), channel_id=1, source_target_pairs={{0,2},{1,3},{2,0},{3,1},{4,6},{5,7},{6,4},{7,5},{8,10},{9,11},{10,... | collective-permute-start | bytes 1179656 | tf_op jit(solution)/shard_map/ppermute | solution.py:39
  37.2 11.4 %collective-permute-start.10 = (bf16[96,1920]{1,0:T(8,128)(2,1)S(1)}, bf16[96,1920]{1,0:T(8,128)(2,1)S(1)}, u32[]{:S(2)}, u32[]{:S(2)}) collective-permute-start(bf16[96,1920]{1,0:T(8,128)(2,1)S(1)} %pad_maximum_fusion.11), channel_id=1, source_target_pairs={{0,8},{1,9},{2,18},{3,19},{4,12},{5,13},{6,22},{7,23},{8,0},{9,1},... | collective-permute-start | bytes 1105928 | tf_op jit(solution)/shard_map/ppermute | solution.py:39
  38.2 3.8 %collective-permute-start.12 = (f32[1,2304]{1,0:T(1,128)S(1)}, f32[1,2304]{1,0:T(1,128)S(1)}, u32[]{:S(2)}, u32[]{:S(2)}) collective-permute-start(f32[1,2304]{1,0:T(1,128)S(1)} %get-tuple-element.205), channel_id=1, source_target_pairs={{0,1},{1,0},{2,3},{3,2},{4,5},{5,4},{6,7},{7,6},{8,9},{9,8},{10,11... | collective-permute-start | bytes 27656 | tf_op jit(solution)/shard_map/ppermute | solution.py:39
  48.7 14.1 %copy-start.2 = (bf16[2,128,768]{2,1,0:T(8,128)(2,1)}, bf16[2,128,768]{2,1,0:T(8,128)(2,1)S(1)}, u32[]{:S(2)}) copy-start(bf16[2,128,768]{2,1,0:T(8,128)(2,1)S(1)} %collective-permute-done.11.refs_4_) | copy-start | bytes 1179652
  48.9 2.5 %collective-permute-start.14 = (bf16[384,1152]{1,0:T(8,128)(2,1)S(1)}, bf16[384,1152]{1,0:T(8,128)(2,1)S(1)}, u32[]{:S(2)}, u32[]{:S(2)}) collective-permute-start(bf16[384,1152]{1,0:T(8,128)(2,1)S(1)} %collective-permute-done.9.refs_1_), channel_id=1, source_target_pairs={{0,2},{1,3},{2,0},{3,1},{4,6},{5,7},{6,4},{7,5},{8,10},{9,11},{10,... | collective-permute-start | bytes 2654216 | tf_op jit(solution)/shard_map/ppermute | solution.py:39
  49.1 20.4 %collective-permute-start.16 = (bf16[192,1536]{1,0:T(8,128)(2,1)S(1)}, bf16[192,1536]{1,0:T(8,128)(2,1)S(1)}, u32[]{:S(2)}, u32[]{:S(2)}) collective-permute-start(bf16[192,1536]{1,0:T(8,128)(2,1)S(1)} %pad_maximum_fusion.4), channel_id=1, source_target_pairs={{0,4},{1,5},{2,18},{3,19},{4,0},{5,1},{6,22},{7,23},{8,12},{9,13},... | collective-permute-start | bytes 1769480 | tf_op jit(solution)/shard_map/ppermute | solution.py:39
  50.5 11.5 %collective-permute-start.15 = (bf16[192,1920]{1,0:T(8,128)(2,1)S(1)}, bf16[192,1920]{1,0:T(8,128)(2,1)S(1)}, u32[]{:S(2)}, u32[]{:S(2)}) collective-permute-start(bf16[192,1920]{1,0:T(8,128)(2,1)S(1)} %pad_maximum_fusion.3), channel_id=1, source_target_pairs={{0,1},{1,0},{2,6},{3,7},{4,5},{5,4},{6,2},{7,3},{8,9},{9,8},{10,14... | collective-permute-start | bytes 2211848 | tf_op jit(solution)/shard_map/ppermute | solution.py:39
  62.1 20.9 %collective-permute-start.17 = (bf16[384,1920]{1,0:T(8,128)(2,1)S(1)}, bf16[384,1920]{1,0:T(8,128)(2,1)S(1)}, u32[]{:S(2)}, u32[]{:S(2)}) collective-permute-start(bf16[384,1920]{1,0:T(8,128)(2,1)S(1)} %constant_dynamic-update-slice_fusion.refs_0_), channel_id=1, source_target_pairs={{0,4},{1,5},{2,3},{3,2},{4,0},{5,1},{6,7},{7,6},{8,12},{9,13},{10,... | collective-permute-start | bytes 4423688 | tf_op jit(solution)/shard_map/ppermute | solution.py:39
  62.8 13.5 %slice-start = ((bf16[2,128,768]{2,1,0:T(8,128)(2,1)}), bf16[1,128,768]{2,1,0:T(8,128)(2,1)S(1)}, s32[]{:S(2)}) async-start(bf16[2,128,768]{2,1,0:T(8,128)(2,1)} %copy-done.2), calls=%async_computation | async-start | bytes 393216 | tf_op jit(solution)/shard_map/slice | solution.py:923
  69.4 13.6 %collective-permute-start.18 = (bf16[384,1920]{1,0:T(8,128)(2,1)S(1)}, bf16[384,1920]{1,0:T(8,128)(2,1)S(1)}, u32[]{:S(2)}, u32[]{:S(2)}) collective-permute-start(bf16[384,1920]{1,0:T(8,128)(2,1)S(1)} %constant_dynamic-update-slice_fusion.refs_0_), channel_id=1, source_target_pairs={{0,2},{1,3},{2,0},{3,1},{4,6},{5,7},{6,4},{7,5},{8,10},{9,11},{10,... | collective-permute-start | bytes 4423688 | tf_op jit(solution)/shard_map/ppermute | solution.py:39
  83.0 6.4 %collective-permute-start.19 = (bf16[384,1920]{1,0:T(8,128)(2,1)S(1)}, bf16[384,1920]{1,0:T(8,128)(2,1)S(1)}, u32[]{:S(2)}, u32[]{:S(2)}) collective-permute-start(bf16[384,1920]{1,0:T(8,128)(2,1)S(1)} %collective-permute-done.17.refs_1_), channel_id=1, source_target_pairs={{0,2},{1,3},{2,0},{3,1},{4,6},{5,7},{6,4},{7,5},{8,10},{9,11},{10,... | collective-permute-start | bytes 4423688 | tf_op jit(solution)/shard_map/ppermute | solution.py:39
  86.5 14.0 %collective-permute-start.21 = (bf16[384,1536]{1,0:T(8,128)(2,1)S(1)}, bf16[384,1536]{1,0:T(8,128)(2,1)S(1)}, u32[]{:S(2)}, u32[]{:S(2)}) collective-permute-start(bf16[384,1536]{1,0:T(8,128)(2,1)S(1)} %constant_dynamic-update-slice_fusion.2.refs_0_), channel_id=1, source_target_pairs={{0,2},{1,3},{2,0},{3,1},{4,6},{5,7},{6,4},{7,5},{8,10},{9,11},{10,... | collective-permute-start | bytes 3538952 | tf_op jit(solution)/shard_map/ppermute | solution.py:39
  86.5 16.2 %collective-permute-start.20 = (bf16[384,1536]{1,0:T(8,128)(2,1)S(1)}, bf16[384,1536]{1,0:T(8,128)(2,1)S(1)}, u32[]{:S(2)}, u32[]{:S(2)}) collective-permute-start(bf16[384,1536]{1,0:T(8,128)(2,1)S(1)} %constant_dynamic-update-slice_fusion.2.refs_0_), channel_id=1, source_target_pairs={{0,1},{1,0},{2,10},{3,11},{4,5},{5,4},{6,14},{7,15},{8,9},{9,8},{1... | collective-permute-start | bytes 3538952 | tf_op jit(solution)/shard_map/ppermute | solution.py:39
  88.0 14.8 %collective-permute-start.22 = (bf16[2,128,768]{2,1,0:T(8,128)(2,1)S(1)}, bf16[2,128,768]{2,1,0:T(8,128)(2,1)S(1)}, u32[]{:S(2)}, u32[]{:S(2)}) collective-permute-start(bf16[2,128,768]{2,1,0:T(8,128)(2,1)S(1)} %pad_maximum_fusion.8), channel_id=1, source_target_pairs={{0,4},{1,5},{2,6},{3,7},{4,0},{5,1},{6,2},{7,3},{8,12},{9,13},{10,... | collective-permute-start | bytes 1179656 | tf_op jit(solution)/shard_map/ppermute | solution.py:39
  102.7 4.5 %copy-start.3 = (bf16[2,128,768]{2,1,0:T(8,128)(2,1)S(1)}, bf16[2,128,768]{2,1,0:T(8,128)(2,1)}, u32[]{:S(2)}) copy-start(bf16[2,128,768]{2,1,0:T(8,128)(2,1)} %copy-done.2) | copy-start | bytes 1179652
  102.7 2.8 %collective-permute-start.23 = (bf16[384,1536]{1,0:T(8,128)(2,1)S(1)}, bf16[384,1536]{1,0:T(8,128)(2,1)S(1)}, u32[]{:S(2)}, u32[]{:S(2)}) collective-permute-start(bf16[384,1536]{1,0:T(8,128)(2,1)S(1)} %collective-permute-done.20.refs_1_), channel_id=1, source_target_pairs={{0,2},{1,3},{2,0},{3,1},{4,6},{5,7},{6,4},{7,5},{8,10},{9,11},{10,... | collective-permute-start | bytes 3538952 | tf_op jit(solution)/shard_map/ppermute | solution.py:39
  116.4 5.2 %collective-permute-start.24 = (bf16[768,1536]{1,0:T(8,128)(2,1)S(1)}, bf16[768,1536]{1,0:T(8,128)(2,1)S(1)}, u32[]{:S(2)}, u32[]{:S(2)}) collective-permute-start(bf16[768,1536]{1,0:T(8,128)(2,1)S(1)} %get-tuple-element.253), channel_id=1, source_target_pairs={{0,2},{1,3},{2,0},{3,1},{4,6},{5,7},{6,4},{7,5},{8,10},{9,11},{10,... | collective-permute-start | bytes 7077896 | tf_op jit(solution)/shard_map/ppermute | solution.py:39
  116.6 4.9 %collective-permute-start.25 = (bf16[2,128,768]{2,1,0:T(8,128)(2,1)S(1)}, bf16[2,128,768]{2,1,0:T(8,128)(2,1)S(1)}, u32[]{:S(2)}, u32[]{:S(2)}) collective-permute-start(bf16[2,128,768]{2,1,0:T(8,128)(2,1)S(1)} %slice.34), channel_id=1, source_target_pairs={{0,2},{1,3},{2,0},{3,1},{4,6},{5,7},{6,4},{7,5},{8,10},{9,11},{10,... | collective-permute-start | bytes 1179656 | tf_op jit(solution)/shard_map/ppermute | solution.py:39
  121.9 13.0 %collective-permute-start.27 = (bf16[2,128,768]{2,1,0:T(8,128)(2,1)S(1)}, bf16[2,128,768]{2,1,0:T(8,128)(2,1)S(1)}, u32[]{:S(2)}, u32[]{:S(2)}) collective-permute-start(bf16[2,128,768]{2,1,0:T(8,128)(2,1)S(1)} %pad_maximum_fusion.9), channel_id=1, source_target_pairs={{0,4},{1,5},{2,6},{3,7},{4,0},{5,1},{6,2},{7,3},{8,12},{9,13},{10,... | collective-permute-start | bytes 1179656 | tf_op jit(solution)/shard_map/ppermute | solution.py:39
  124.1 16.2 %collective-permute-start.26 = (bf16[384,1536]{1,0:T(8,128)(2,1)S(1)}, bf16[384,1536]{1,0:T(8,128)(2,1)S(1)}, u32[]{:S(2)}, u32[]{:S(2)}) collective-permute-start(bf16[384,1536]{1,0:T(8,128)(2,1)S(1)} %add.53), channel_id=1, source_target_pairs={{0,1},{1,0},{2,10},{3,11},{4,5},{5,4},{6,14},{7,15},{8,9},{9,8},{1... | collective-permute-start | bytes 3538952 | tf_op jit(solution)/shard_map/ppermute | solution.py:39
  140.3 7.0 %collective-permute-start.28 = (bf16[768,1920]{1,0:T(8,128)(2,1)S(1)}, bf16[768,1920]{1,0:T(8,128)(2,1)S(1)}, u32[]{:S(2)}, u32[]{:S(2)}) collective-permute-start(bf16[768,1920]{1,0:T(8,128)(2,1)S(1)} %get-tuple-element.273), channel_id=1, source_target_pairs={{0,2},{1,3},{2,0},{3,1},{4,6},{5,7},{6,4},{7,5},{8,10},{9,11},{10,... | collective-permute-start | bytes 8847368 | tf_op jit(solution)/shard_map/ppermute | solution.py:39
  140.6 13.7 %collective-permute-start.29 = (bf16[192,1536]{1,0:T(8,128)(2,1)S(1)}, bf16[192,1536]{1,0:T(8,128)(2,1)S(1)}, u32[]{:S(2)}, u32[]{:S(2)}) collective-permute-start(bf16[192,1536]{1,0:T(8,128)(2,1)S(1)} %add.54), channel_id=1, source_target_pairs={{0,4},{1,5},{2,18},{3,19},{4,0},{5,1},{6,22},{7,23},{8,12},{9,13},... | collective-permute-start | bytes 1769480 | tf_op jit(solution)/shard_map/ppermute | solution.py:39
  140.7 20.4 %collective-permute-start.30 = (bf16[4,128,768]{2,1,0:T(8,128)(2,1)S(1)}, bf16[4,128,768]{2,1,0:T(8,128)(2,1)S(1)}, u32[]{:S(2)}, u32[]{:S(2)}) collective-permute-start(bf16[4,128,768]{2,1,0:T(8,128)(2,1)S(1)} %pad_maximum_fusion.1), channel_id=1, source_target_pairs={{0,1},{1,0},{2,3},{3,2},{4,5},{5,4},{6,7},{7,6},{8,9},{9,8},{10,11... | collective-permute-start | bytes 2359304 | tf_op jit(solution)/shard_map/ppermute | solution.py:39
  147.7 19.4 %collective-permute-start.31 = (bf16[384,1920]{1,0:T(8,128)(2,1)S(1)}, bf16[384,1920]{1,0:T(8,128)(2,1)S(1)}, u32[]{:S(2)}, u32[]{:S(2)}) collective-permute-start(bf16[384,1920]{1,0:T(8,128)(2,1)S(1)} %add.55), channel_id=1, source_target_pairs={{0,4},{1,5},{2,10},{3,11},{4,0},{5,1},{6,14},{7,15},{8,12},{9,13},... | collective-permute-start | bytes 4423688 | tf_op jit(solution)/shard_map/ppermute | solution.py:39
  161.1 6.9 %collective-permute-start.33 = (bf16[2,128,768]{2,1,0:T(8,128)(2,1)S(1)}, bf16[2,128,768]{2,1,0:T(8,128)(2,1)S(1)}, u32[]{:S(2)}, u32[]{:S(2)}) collective-permute-start(bf16[2,128,768]{2,1,0:T(8,128)(2,1)S(1)} %slice.39), channel_id=1, source_target_pairs={{0,2},{1,3},{2,0},{3,1},{4,6},{5,7},{6,4},{7,5},{8,10},{9,11},{10,... | collective-permute-start | bytes 1179656 | tf_op jit(solution)/shard_map/ppermute | solution.py:39
  164.3 3.8 %collective-permute-start.32 = (bf16[776,1152]{1,0:T(8,128)(2,1)S(1)}, bf16[776,1152]{1,0:T(8,128)(2,1)S(1)}, u32[]{:S(2)}, u32[]{:S(2)}) collective-permute-start(bf16[776,1152]{1,0:T(8,128)(2,1)S(1)} %get-tuple-element.299), channel_id=1, source_target_pairs={{0,2},{1,3},{2,0},{3,1},{4,6},{5,7},{6,4},{7,5},{8,10},{9,11},{10,... | collective-permute-start | bytes 5363720 | tf_op jit(solution)/shard_map/ppermute | solution.py:39
  168.3 16.5 %collective-permute-start.34 = (bf16[392,1152]{1,0:T(8,128)(2,1)S(1)}, bf16[392,1152]{1,0:T(8,128)(2,1)S(1)}, u32[]{:S(2)}, u32[]{:S(2)}) collective-permute-start(bf16[392,1152]{1,0:T(8,128)(2,1)S(1)} %add.58.refs_3_), channel_id=1, source_target_pairs={{0,4},{1,5},{2,3},{3,2},{4,0},{5,1},{6,7},{7,6},{8,12},{9,13},{10,... | collective-permute-start | bytes 2709512 | tf_op jit(solution)/shard_map/ppermute | solution.py:39
  169.2 18.0 %collective-permute-start.37 = (bf16[192,1920]{1,0:T(8,128)(2,1)S(1)}, bf16[192,1920]{1,0:T(8,128)(2,1)S(1)}, u32[]{:S(2)}, u32[]{:S(2)}) collective-permute-start(bf16[192,1920]{1,0:T(8,128)(2,1)S(1)} %add.57), channel_id=1, source_target_pairs={{0,1},{1,0},{2,18},{3,19},{4,5},{5,4},{6,22},{7,23},{8,9},{9,8},{1... | collective-permute-start | bytes 2211848 | tf_op jit(solution)/shard_map/ppermute | solution.py:39
  170.4 15.9 %collective-permute-start.36 = (bf16[96,1536]{1,0:T(8,128)(2,1)S(1)}, bf16[96,1536]{1,0:T(8,128)(2,1)S(1)}, u32[]{:S(2)}, u32[]{:S(2)}) collective-permute-start(bf16[96,1536]{1,0:T(8,128)(2,1)S(1)} %add.56), channel_id=1, source_target_pairs={{0,8},{1,9},{2,6},{3,7},{4,12},{5,13},{6,2},{7,3},{8,0},{9,1},{10,... | collective-permute-start | bytes 884744 | tf_op jit(solution)/shard_map/ppermute | solution.py:39
  184.9 10.3 %collective-permute-start.35 = (bf16[200,1152]{1,0:T(8,128)(2,1)S(1)}, bf16[200,1152]{1,0:T(8,128)(2,1)S(1)}, u32[]{:S(2)}, u32[]{:S(2)}) collective-permute-start(bf16[200,1152]{1,0:T(8,128)(2,1)S(1)} %add.59.refs_4_), channel_id=1, source_target_pairs={{0,1},{1,0},{2,6},{3,7},{4,5},{5,4},{6,2},{7,3},{8,9},{9,8},{10,14... | collective-permute-start | bytes 1382408 | tf_op jit(solution)/shard_map/ppermute | solution.py:39
  186.3 10.0 %collective-permute-start.40 = (bf16[2,128,768]{2,1,0:T(8,128)(2,1)S(1)}, bf16[2,128,768]{2,1,0:T(8,128)(2,1)S(1)}, u32[]{:S(2)}, u32[]{:S(2)}) collective-permute-start(bf16[2,128,768]{2,1,0:T(8,128)(2,1)S(1)} %pad_maximum_fusion.10), channel_id=1, source_target_pairs={{0,4},{1,5},{2,6},{3,7},{4,0},{5,1},{6,2},{7,3},{8,12},{9,13},{10,... | collective-permute-start | bytes 1179656 | tf_op jit(solution)/shard_map/ppermute | solution.py:39
  187.4 10.7 %collective-permute-start.41 = (bf16[96,1920]{1,0:T(8,128)(2,1)S(1)}, bf16[96,1920]{1,0:T(8,128)(2,1)S(1)}, u32[]{:S(2)}, u32[]{:S(2)}) collective-permute-start(bf16[96,1920]{1,0:T(8,128)(2,1)S(1)} %add.61), channel_id=1, source_target_pairs={{0,8},{1,9},{2,3},{3,2},{4,12},{5,13},{6,7},{7,6},{8,0},{9,1},{10,... | collective-permute-start | bytes 1105928 | tf_op jit(solution)/shard_map/ppermute | solution.py:39
  188.5 7.8 %collective-permute-start.39 = (bf16[48,1536]{1,0:T(8,128)(2,1)S(1)}, bf16[48,1536]{1,0:T(8,128)(2,1)S(1)}, u32[]{:S(2)}, u32[]{:S(2)}) collective-permute-start(bf16[48,1536]{1,0:T(8,128)(2,1)S(1)} %add.60), channel_id=1, source_target_pairs={{0,16},{1,17},{2,3},{3,2},{4,20},{5,21},{6,7},{7,6},{8,24},{9,25},... | collective-permute-start | bytes 442376 | tf_op jit(solution)/shard_map/ppermute | solution.py:39
  195.4 6.8 %collective-permute-start.38 = (bf16[104,1152]{1,0:T(8,128)(2,1)S(1)}, bf16[104,1152]{1,0:T(8,128)(2,1)S(1)}, u32[]{:S(2)}, u32[]{:S(2)}) collective-permute-start(bf16[104,1152]{1,0:T(8,128)(2,1)S(1)} %add.62.refs_5_), channel_id=1, source_target_pairs={{0,8},{1,9},{2,18},{3,19},{4,12},{5,13},{6,22},{7,23},{8,0},{9,1},... | collective-permute-start | bytes 718856 | tf_op jit(solution)/shard_map/ppermute | solution.py:39
  196.4 8.0 %collective-permute-start.43 = (bf16[48,1536]{1,0:T(8,128)(2,1)S(1)}, bf16[48,1536]{1,0:T(8,128)(2,1)S(1)}, u32[]{:S(2)}, u32[]{:S(2)}) collective-permute-start(bf16[48,1536]{1,0:T(8,128)(2,1)S(1)} %add.63), channel_id=1, source_target_pairs={{0,4},{1,5},{2,6},{3,7},{4,0},{5,1},{6,2},{7,3},{8,12},{9,13},{10,... | collective-permute-start | bytes 442376 | tf_op jit(solution)/shard_map/ppermute | solution.py:39
  198.2 13.4 %collective-permute-start.44 = (bf16[48,1920]{1,0:T(8,128)(2,1)S(1)}, bf16[48,1920]{1,0:T(8,128)(2,1)S(1)}, u32[]{:S(2)}, u32[]{:S(2)}) collective-permute-start(bf16[48,1920]{1,0:T(8,128)(2,1)S(1)} %add.64), channel_id=1, source_target_pairs={{0,16},{1,17},{2,6},{3,7},{4,20},{5,21},{6,2},{7,3},{8,24},{9,25},... | collective-permute-start | bytes 552968 | tf_op jit(solution)/shard_map/ppermute | solution.py:39
  200.7 21.7 %collective-permute-start.47 = (bf16[4,128,768]{2,1,0:T(8,128)(2,1)S(1)}, bf16[4,128,768]{2,1,0:T(8,128)(2,1)S(1)}, u32[]{:S(2)}, u32[]{:S(2)}) collective-permute-start(bf16[4,128,768]{2,1,0:T(8,128)(2,1)S(1)} %pad_maximum_fusion.2), channel_id=1, source_target_pairs={{0,1},{1,0},{2,3},{3,2},{4,5},{5,4},{6,7},{7,6},{8,9},{9,8},{10,11... | collective-permute-start | bytes 2359304 | tf_op jit(solution)/shard_map/ppermute | solution.py:39
  202.3 13.2 %collective-permute-start.42 = (bf16[56,1152]{1,0:T(8,128)(2,1)S(1)}, bf16[56,1152]{1,0:T(8,128)(2,1)S(1)}, u32[]{:S(2)}, u32[]{:S(2)}) collective-permute-start(bf16[56,1152]{1,0:T(8,128)(2,1)S(1)} %add.65.refs_0_), channel_id=1, source_target_pairs={{0,16},{1,17},{2,10},{3,11},{4,20},{5,21},{6,14},{7,15},{8,24},{9,... | collective-permute-start | bytes 387080 | tf_op jit(solution)/shard_map/ppermute | solution.py:39
  211.8 10.4 %collective-permute-start.46 = (bf16[48,1920]{1,0:T(8,128)(2,1)S(1)}, bf16[48,1920]{1,0:T(8,128)(2,1)S(1)}, u32[]{:S(2)}, u32[]{:S(2)}) collective-permute-start(bf16[48,1920]{1,0:T(8,128)(2,1)S(1)} %add.66), channel_id=1, source_target_pairs={{0,4},{1,5},{2,6},{3,7},{4,0},{5,1},{6,2},{7,3},{8,12},{9,13},{10,... | collective-permute-start | bytes 552968 | tf_op jit(solution)/shard_map/ppermute | solution.py:39
  212.5 7.2 %collective-permute-start.45 = (bf16[96,1536]{1,0:T(8,128)(2,1)S(1)}, bf16[96,1536]{1,0:T(8,128)(2,1)S(1)}, u32[]{:S(2)}, u32[]{:S(2)}) collective-permute-start(bf16[96,1536]{1,0:T(8,128)(2,1)S(1)} %constant_dynamic-update-slice_fusion.4.refs_0_), channel_id=1, source_target_pairs={{0,2},{1,3},{2,0},{3,1},{4,6},{5,7},{6,4},{7,5},{8,10},{9,11},{10,... | collective-permute-start | bytes 884744 | tf_op jit(solution)/shard_map/ppermute | solution.py:39
  215.6 8.1 %collective-permute-start.50 = (bf16[48,1152]{1,0:T(8,128)(2,1)S(1)}, bf16[48,1152]{1,0:T(8,128)(2,1)S(1)}, u32[]{:S(2)}, u32[]{:S(2)}) collective-permute-start(bf16[48,1152]{1,0:T(8,128)(2,1)S(1)} %add.67.refs_0_), channel_id=1, source_target_pairs={{0,6},{1,7},{2,4},{3,5},{4,2},{5,3},{6,0},{7,1},{8,14},{9,15},{10,... | collective-permute-start | bytes 331784 | tf_op jit(solution)/shard_map/ppermute | solution.py:39
  219.1 4.6 %collective-permute-start.49 = (bf16[48,1152]{1,0:T(8,128)(2,1)S(1)}, bf16[48,1152]{1,0:T(8,128)(2,1)S(1)}, u32[]{:S(2)}, u32[]{:S(2)}) collective-permute-start(bf16[48,1152]{1,0:T(8,128)(2,1)S(1)} %add.67.refs_0_), channel_id=1, source_target_pairs={{0,2},{1,3},{2,0},{3,1},{4,6},{5,7},{6,4},{7,5},{8,10},{9,11},{10,... | collective-permute-start | bytes 331784 | tf_op jit(solution)/shard_map/ppermute | solution.py:39
  219.7 5.6 %collective-permute-start.48 = (bf16[48,1152]{1,0:T(8,128)(2,1)S(1)}, bf16[48,1152]{1,0:T(8,128)(2,1)S(1)}, u32[]{:S(2)}, u32[]{:S(2)}) collective-permute-start(bf16[48,1152]{1,0:T(8,128)(2,1)S(1)} %add.67.refs_0_), channel_id=1, source_target_pairs={{0,4},{1,5},{2,6},{3,7},{4,0},{5,1},{6,2},{7,3},{8,12},{9,13},{10,... | collective-permute-start | bytes 331784 | tf_op jit(solution)/shard_map/ppermute | solution.py:39
  222.1 4.2 %collective-permute-start.51 = (bf16[96,1920]{1,0:T(8,128)(2,1)S(1)}, bf16[96,1920]{1,0:T(8,128)(2,1)S(1)}, u32[]{:S(2)}, u32[]{:S(2)}) collective-permute-start(bf16[96,1920]{1,0:T(8,128)(2,1)S(1)} %constant_dynamic-update-slice_fusion.6.refs_0_), channel_id=1, source_target_pairs={{0,2},{1,3},{2,0},{3,1},{4,6},{5,7},{6,4},{7,5},{8,10},{9,11},{10,... | collective-permute-start | bytes 1105928 | tf_op jit(solution)/shard_map/ppermute | solution.py:39
  (3 other events, 4.1 us)

commit v7 on v6

--- a/solution.py
+++ b/solution.py
@@ -42,7 +42,7 @@
 GATHER = (
     (("z2", "z1", "y", "x"), ("z1", "z2", "x", "y")),
     (("z2", "z1", "y", "x"), ("z1", "z2", "x", "y")),
-    (("z2", "z1", "x", "y"), ("y", "x", "z2", "z1")),
+    (("x", "z2", "z1", "y"), ("y", "x", "z2", "z1")),
 )
 SCATTER = (
     (("x", "y", "z1", "z2"), ("y", "x", "z2", "z1")),
@@ -885,20 +885,21 @@
         h1 = jnp.swapaxes(h1, 0, 1).reshape(part, 3 * local_width)
         h2, h3 = [lax.dynamic_slice_in_dim(s, c * part, part, 0) for s in shards[1:]]
         g1 = swap(h1, 0, 0)
+        h3 = after(h3, h1)
         x0, x1, x2, x3 = seen(after(rows_in, h1))
-        g1, x1, x2, x3, h2, h3, cot_in, b_up = phase(g1, x1, x2, x3, h2, h3, cot_in, b_up)
-        h1 = joined(h1, g1)
+        g1, g3, x1, x2, x3, h2, cot_in, b_up = phase(g1, swap(h3, 2, 0), x1, x2, x3, h2, cot_in, b_up)
+        h1, h3 = joined(h1, g1), joined(h3, g3)
         g1, g3, xk, xx, xd = phase(
-            swap(h1, 0, 1), swap(h3, 2, 0), exchange(x1, CORE, sizes), exchange(x2, X, sizes), exchange(x3, FAR, sizes)
+            swap(h1, 0, 1), swap(h3, 2, 1), exchange(x1, CORE, sizes), exchange(x2, X, sizes), exchange(x3, FAR, sizes)
         )
         given = (x0, xk, joined(xx, xd))
         h1, h2, h3, cot_in, b_up = phase(joined(h1, g1), h2, joined(h3, g3), cot_in, b_up)
-        g1, g2, g3 = swap(h1, 0, 2), swap(h2, 1, 0), swap(h3, 2, 1)
+        g1, g2 = swap(h1, 0, 2), swap(h2, 1, 0)
         c0, c1, c2, c3 = seen(cot_in)
         c_send = joined(c1, c3)
         table, small = tables(b_qv, b_up, (b_out, ln1_gain, ln1_bias, b_down, ln2_gain, ln2_bias))
-        g1, g2, g3, c_send, small = phase(g1, g2, g3, c_send, small)
-        h1, h2, h3 = phase(joined(h1, g1), joined(h2, g2), joined(h3, g3))
+        g1, g2, c_send, small = phase(g1, g2, c_send, small)
+        h1, h2, h3 = phase(joined(h1, g1), joined(h2, g2), h3)
         g1, g2, ck, got, f1 = phase(
             swap(h1, 0, 3),
             swap(h2, 1, 1),

time: 229 us -> 224 us (0.978)
  starting transfers between devices: 62.7 us -> 54.7 us
  waiting for transfers between devices: 78 us -> 81.5 us
    ppermute x52, starting transfers between devices: 62.7 us -> 54.7 us  [exchange(): return lax.ppermute(value, AXES, pairs)]
    ppermute x52, waiting for transfers between devices: 78 us -> 81.5 us  [exchange(): return lax.ppermute(value, AXES, pairs)]
  transfers between devices with their start and end apart: 52 -> 52, of which waited for: 22 -> 22; matrix products, arithmetic and copies ran while one was open for 2% -> 2% of each run, Pallas kernels for 29% -> 30%
where the time goes in v7:
time: 224 us
  waiting for transfers between devices  81.5 us (36%)
  Pallas kernels  79.2 us (35%)
  starting transfers between devices  54.7 us (24%)
  local copies, waits for them, and re-layouts  5.48 us (2%)
    ppermute x52, waiting for transfers between devices, exchange(): return lax.ppermute(value, AXES, pairs)  81.5 us
    pallas_call x36, Pallas kernels, call(): pl.pallas_call(kernel, name=name, out_shape=outs, in_specs=specs, out_spe...  79.2 us
    ppermute x52, starting transfers between devices, exchange(): return lax.ppermute(value, AXES, pairs)  54.7 us
  transfers between devices with their start and end apart: 52, of which 22 were waited for; matrix products, arithmetic and copies ran while one was open for 2% of the time, Pallas kernels for 30%

profile of v7, /device:TPU:0, one launch (start us, length us, event | category | flops | bytes accessed | tf_op | source)
XLA Modules:
  0.0 223.6 jit_solution(10696121634679613334)
XLA Ops:
  0.7 1.0 dynamic-slice_bitcast_fusion.3
  1.7 4.1 %collective-permute-start = (bf16[48,1152]{1,0:T(8,128)(2,1)S(1)}, bf16[48,1152]{1,0:T(8,128)(2,1)S(1)}, u32[]{:S(2)}, u32[]{:S(2)}) collective-permute-start(bf16[48,1152]{1,0:T(8,128)(2,1)S(1)} %bitcast.15), channel_id=1, source_target_pairs={{0,16},{1,17},{2,10},{3,11},{4,20},{5,21},{6,14},{7,15},{8,24},{9,... | collective-permute-start | bytes 331784 | tf_op jit(solution)/shard_map/ppermute | solution.py:39
  6.8 1.6 collective-permute-start.1
  10.2 1.2 dynamic-slice_bitcast_fusion
  12.1 2.4 %collective-permute-start.2 = (bf16[96,1152]{1,0:T(8,128)(2,1)S(1)}, bf16[96,1152]{1,0:T(8,128)(2,1)S(1)}, u32[]{:S(2)}, u32[]{:S(2)}) collective-permute-start(bf16[96,1152]{1,0:T(8,128)(2,1)S(1)} %pad_maximum_fusion.13), channel_id=1, source_target_pairs={{0,8},{1,9},{2,18},{3,19},{4,12},{5,13},{6,22},{7,23},{8,0},{9,1},... | collective-permute-start | bytes 663560 | tf_op jit(solution)/shard_map/ppermute | solution.py:39
  14.5 1.5 collective-permute-start.5
  16.3 6.1 %collective-permute-done.5 = bf16[1,136,768]{2,1,0:T(8,128)(2,1)S(1)} collective-permute-done((bf16[1,136,768]{2,1,0:T(8,128)(2,1)S(1)}, bf16[1,136,768]{2,1,0:T(8,128)(2,1)S(1)}, u32[]{:S(2)}, u32[]{:S(2)}) %collective-permute-start.5) | collective-permute-done | bytes 208928 | tf_op jit(solution)/shard_map/ppermute | solution.py:39
  22.4 3.7 %collective-permute-done.6 = bf16[1,136,768]{2,1,0:T(8,128)(2,1)S(1)} collective-permute-done((bf16[1,136,768]{2,1,0:T(8,128)(2,1)S(1)}, bf16[1,136,768]{2,1,0:T(8,128)(2,1)S(1)}, u32[]{:S(2)}, u32[]{:S(2)}) %collective-permute-start.6) | collective-permute-done | bytes 208928 | tf_op jit(solution)/shard_map/ppermute | solution.py:39
  26.3 1.6 collective-permute-start.7
  28.0 2.9 %collective-permute-start.8 = (bf16[48,1920]{1,0:T(8,128)(2,1)S(1)}, bf16[48,1920]{1,0:T(8,128)(2,1)S(1)}, u32[]{:S(2)}, u32[]{:S(2)}) collective-permute-start(bf16[48,1920]{1,0:T(8,128)(2,1)S(1)} %fusion.2), channel_id=1, source_target_pairs={{0,16},{1,17},{2,10},{3,11},{4,20},{5,21},{6,14},{7,15},{8,24},{9,... | collective-permute-start | bytes 552968 | tf_op jit(solution)/shard_map/ppermute | solution.py:39
  31.1 4.8 %collective-permute-done.8 = bf16[48,1920]{1,0:T(8,128)(2,1)S(1)} collective-permute-done((bf16[48,1920]{1,0:T(8,128)(2,1)S(1)}, bf16[48,1920]{1,0:T(8,128)(2,1)S(1)}, u32[]{:S(2)}, u32[]{:S(2)}) %collective-permute-start.8) | collective-permute-done | bytes 184352 | tf_op jit(solution)/shard_map/ppermute | solution.py:39
  36.0 1.8 collective-permute-start.9
  38.4 3.5 %collective-permute-done.12 = f32[1,2304]{1,0:T(1,128)S(1)} collective-permute-done((f32[1,2304]{1,0:T(1,128)S(1)}, f32[1,2304]{1,0:T(1,128)S(1)}, u32[]{:S(2)}, u32[]{:S(2)}) %collective-permute-start.12) | collective-permute-done | bytes 9248 | tf_op jit(solution)/shard_map/ppermute | solution.py:39
  42.0 6.2 %collective-permute-done.10 = bf16[96,1920]{1,0:T(8,128)(2,1)S(1)} collective-permute-done((bf16[96,1920]{1,0:T(8,128)(2,1)S(1)}, bf16[96,1920]{1,0:T(8,128)(2,1)S(1)}, u32[]{:S(2)}, u32[]{:S(2)}) %collective-permute-start.10) | collective-permute-done | bytes 368672 | tf_op jit(solution)/shard_map/ppermute | solution.py:39
  48.2 0.9 collective-permute-done.9.refs_1_
  50.6 1.2 collective-permute-done.14.refs_3_
  51.8 1.4 unpack.3.refs_0_
  53.2 2.6 %project.1 = (bf16[512,2304]{1,0:T(8,128)(2,1)S(1)}, bf16[512,768]{1,0:T(8,128)(2,1)S(1)}, f32[512,512]{1,0:T(8,128)S(1)}) custom-call(bf16[768,2304]{1,0:T(8,128)(2,1)S(1)} %unpack.3.refs_0_, bf16[1,136,768]{2,1,0:T(8,128)(2,1)S(1)} %get-tuple-element.350.refs_1_, bf16[1,136,768]{2,1,0:T(8,128)(2,1)S(1)} %collective-permute-done.4.refs_2_, ...), custom_call_target="tpu_custom_call" | custom-call | flops 5000000000 | bytes 1000000 | tf_op jit(solution)/shard_map/project/pallas_call | solution.py:148
  55.8 5.6 %collective-permute-done.15 = bf16[192,1920]{1,0:T(8,128)(2,1)S(1)} collective-permute-done((bf16[192,1920]{1,0:T(8,128)(2,1)S(1)}, bf16[192,1920]{1,0:T(8,128)(2,1)S(1)}, u32[]{:S(2)}, u32[]{:S(2)}) %collective-permute-start.15) | collective-permute-done | bytes 737312 | tf_op jit(solution)/shard_map/ppermute | solution.py:39
  61.5 1.6 collective-permute-start.17
  63.1 6.7 %attend.2 = (bf16[512,384]{1,0:T(8,128)(2,1)S(1)}, bf16[6,512,512]{2,1,0:T(8,128)(2,1)S(1)}) custom-call(bf16[512,2304]{1,0:T(8,128)(2,1)S(1)} %get-tuple-element.227.refs_0_, f32[512,512]{1,0:T(8,128)S(1)} %get-tuple-element.221.refs_1_), custom_call_target="tpu_custom_call" | custom-call | flops 12000000000 | bytes 1000000 | tf_op jit(solution)/shard_map/attend/pallas_call | solution.py:148
  70.3 6.7 %attend.3 = (bf16[512,384]{1,0:T(8,128)(2,1)S(1)}, bf16[6,512,512]{2,1,0:T(8,128)(2,1)S(1)}) custom-call(bf16[512,2304]{1,0:T(8,128)(2,1)S(1)} %get-tuple-element.227.refs_0_, f32[512,512]{1,0:T(8,128)S(1)} %get-tuple-element.221.refs_1_), custom_call_target="tpu_custom_call" | custom-call | flops 12000000000 | bytes 1000000 | tf_op jit(solution)/shard_map/attend/pallas_call | solution.py:148
  76.9 4.0 %collective-permute-done.17.refs_1_ = bf16[384,1920]{1,0:T(8,128)(2,1)S(1)} collective-permute-done((bf16[384,1920]{1,0:T(8,128)(2,1)S(1)}, bf16[384,1920]{1,0:T(8,128)(2,1)S(1)}, u32[]{:S(2)}, u32[]{:S(2)}) %collective-permute-start.17) | collective-permute-done | bytes 1474592 | tf_op jit(solution)/shard_map/ppermute | solution.py:39
  81.9 1.5 collective-permute-start.22
  84.2 2.4 %unpack.4 = (bf16[768,768]{1,0:T(8,128)(2,1)S(1)}, bf16[768,3072]{1,0:T(8,128)(2,1)S(1)}) custom-call(bf16[384,1920]{1,0:T(8,128)(2,1)S(1)} %constant_dynamic-update-slice_fusion.refs_0_, bf16[384,1920]{1,0:T(8,128)(2,1)S(1)} %collective-permute-done.17.refs_1_, bf16[384,1920]{1,0:T(8,128)(2,1)S(1)} %collective-permute-done.18.refs_2_, ...), custom_call_target="tpu_custom_call" | custom-call | flops 5000000000 | bytes 1000000 | tf_op jit(solution)/shard_map/unpack/pallas_call | solution.py:148
  86.6 8.7 %middle.1 = (f32[512,768]{1,0:T(8,128)S(1)}, f32[512,1]{1,0:T(8,128)S(1)}, bf16[512,768]{1,0:T(8,128)(2,1)S(1)}, bf16[512,3072]{1,0:T(8,128)(2,1)S(1)}, bf16[512,3072]{1,0:T(8,128)(2,1)S(1)}) custom-call(bf16[768,768]{1,0:T(8,128)(2,1)S(1)} %get-tuple-element.234.w_out.refs_0_, bf16[768,3072]{1,0:T(8,128)(2,1)S(1)} %get-tuple-element.235.w_up.refs_1_, ...), custom_call_target="tpu_custom_call" | custom-call | flops 12000000000 | bytes 1000000 | tf_op jit(solution)/shard_map/middle/pallas_call | solution.py:148
  95.3 2.3 %collective-permute-done.20.refs_1_ = bf16[384,1536]{1,0:T(8,128)(2,1)S(1)} collective-permute-done((bf16[384,1536]{1,0:T(8,128)(2,1)S(1)}, bf16[384,1536]{1,0:T(8,128)(2,1)S(1)}, u32[]{:S(2)}, u32[]{:S(2)}) %collective-permute-start.20) | collective-permute-done | bytes 1179680 | tf_op jit(solution)/shard_map/ppermute | solution.py:39
  97.6 2.8 %collective-permute-done.23.refs_3_ = bf16[384,1536]{1,0:T(8,128)(2,1)S(1)} collective-permute-done((bf16[384,1536]{1,0:T(8,128)(2,1)S(1)}, bf16[384,1536]{1,0:T(8,128)(2,1)S(1)}, u32[]{:S(2)}, u32[]{:S(2)}) %collective-permute-start.23) | collective-permute-done | bytes 1179680 | tf_op jit(solution)/shard_map/ppermute | solution.py:39
  100.5 1.7 unpack.5.refs_0_.weight_ref
  102.1 9.1 %turn.1 = (bf16[4,128,768]{2,1,0:T(8,128)(2,1)S(1)}, f32[512,768]{1,0:T(8,128)S(1)}, bf16[512,768]{1,0:T(8,128)(2,1)S(1)}, f32[8,768]{1,0:T(8,128)S(1)}, bf16[76...) custom-call(bf16[768,3072]{1,0:T(8,128)(2,1)S(1)} %unpack.5.refs_0_.weight_ref, ...), custom_call_target="tpu_custom_call" | custom-call | flops 14000000000 | bytes 1000000 | tf_op jit(solution)/shard_map/turn/pallas_call | solution.py:148
  111.9 3.8 %hidden_back.1 = (bf16[512,3072]{1,0:T(8,128)(2,1)S(1)}, f32[1,3072]{1,0:T(1,128)S(1)}) custom-call(bf16[768,3072]{1,0:T(8,128)(2,1)S(1)} %unpack.5.refs_0_.weight_ref, bf16[512,768]{1,0:T(8,128)(2,1)S(1)} %get-tuple-element.250.gzb_ref, bf16[512,3072]{1,0:T(8,128)(2,1)S(1)} %get-tuple-element.251.slope_ref), custom_call_target="tpu_custom_call" | custom-call | flops 12000000000 | bytes 1000000 | tf_op jit(solution)/shard_map/hidden_back/pallas_call | solution.py:148
  116.8 1.6 collective-permute-start.27
  118.8 10.5 %first_back.1 = (f32[512,768]{1,0:T(8,128)S(1)}, bf16[512,768]{1,0:T(8,128)(2,1)S(1)}, f32[8,768]{1,0:T(8,128)S(1)}, bf16[768,1920]{1,0:T(8,128)(2,1)S(1)}, bf16[768,1920]{1,0:T(8,128)(2,1)S(1)}) custom-call(bf16[768,768]{1,0:T(8,128)(2,1)S(1)} %get-tuple-element.234.w_out.refs_0_, bf16[768,3072]{1,0:T(8,128)(2,1)S(1)} %get-tuple-element.235.w_up.refs_1_, ...), custom_call_target="tpu_custom_call" | custom-call | flops 20000000000 | bytes 1000000 | tf_op jit(solution)/shard_map/first_back/pallas_call | solution.py:148
  129.4 5.2 %collective-permute-done.26.refs_2_ = bf16[384,1536]{1,0:T(8,128)(2,1)S(1)} collective-permute-done((bf16[384,1536]{1,0:T(8,128)(2,1)S(1)}, bf16[384,1536]{1,0:T(8,128)(2,1)S(1)}, u32[]{:S(2)}, u32[]{:S(2)}) %collective-permute-start.26) | collective-permute-done | bytes 1179680 | tf_op jit(solution)/shard_map/ppermute | solution.py:39
  136.0 5.3 %attend_back.2 = (bf16[512,384]{1,0:T(8,128)(2,1)S(1)}, bf16[512,384]{1,0:T(8,128)(2,1)S(1)}, bf16[512,384]{1,0:T(8,128)(2,1)S(1)}) custom-call(bf16[512,2304]{1,0:T(8,128)(2,1)S(1)} %get-tuple-element.227.refs_0_, bf16[6,512,512]{2,1,0:T(8,128)(2,1)S(1)} %get-tuple-element.263.refs_1_, bf16[512,768]{1,0:T(8,128)(2,1)S(1)} %get-tuple-element.281.refs_2_), custom_call_target="tpu_custom_call" | custom-call | flops 1000000000 | bytes 1000000 | tf_op jit(solution)/shard_map/attend_back/pallas_call | solution.py:148
  141.7 1.5 collective-permute-start.31
  143.2 5.6 %attend_back.3 = (bf16[512,384]{1,0:T(8,128)(2,1)S(1)}, bf16[512,384]{1,0:T(8,128)(2,1)S(1)}, bf16[512,384]{1,0:T(8,128)(2,1)S(1)}) custom-call(bf16[512,2304]{1,0:T(8,128)(2,1)S(1)} %get-tuple-element.227.refs_0_, bf16[6,512,512]{2,1,0:T(8,128)(2,1)S(1)} %get-tuple-element.277.refs_1_, bf16[512,768]{1,0:T(8,128)(2,1)S(1)} %get-tuple-element.281.refs_2_), custom_call_target="tpu_custom_call" | custom-call | flops 1000000000 | bytes 1000000 | tf_op jit(solution)/shard_map/attend_back/pallas_call | solution.py:148
  148.9 2.7 %input_back.1.own_ref = bf16[4,128,768]{2,1,0:T(8,128)(2,1)S(1)} custom-call(bf16[768,2304]{1,0:T(8,128)(2,1)S(1)} %unpack.3.refs_0_, f32[512,768]{1,0:T(8,128)S(1)} %get-tuple-element.262.refs_1_, bf16[512,384]{1,0:T(8,128)(2,1)S(1)} %get-tuple-element.294.refs_2_.refs_4_, bf16[512,384]{1,0:T(8,128)(2,1)S(1)} %get-tuple-element.275.refs_3_.refs_5_, ...), custom_call_target="tpu_custom_call" | custom-call | flops 2000000000 | bytes 1000000 | tf_op jit(solution)/shard_map/input_back/pallas_call | solution.py:148
  151.6 2.5 %collective-permute-done.30.y_ref = bf16[4,128,768]{2,1,0:T(8,128)(2,1)S(1)} collective-permute-done((bf16[4,128,768]{2,1,0:T(8,128)(2,1)S(1)}, bf16[4,128,768]{2,1,0:T(8,128)(2,1)S(1)}, u32[]{:S(2)}, u32[]{:S(2)}) %collective-permute-start.30) | collective-permute-done | bytes 786464 | tf_op jit(solution)/shard_map/ppermute | solution.py:39
  154.1 1.9 collective-permute-start.33
  156.1 2.9 %last.1 = (bf16[776,1152]{1,0:T(8,128)(2,1)S(1)}, bf16[776,1152]{1,0:T(8,128)(2,1)S(1)}) custom-call(bf16[512,768]{1,0:T(8,128)(2,1)S(1)} %get-tuple-element.237.x_ref.refs_0_, f32[8,768]{1,0:T(8,128)S(1)} %get-tuple-element.291.refs_1_, f32[8,768]{1,0:T(8,128)S(1)} %get-tuple-element.292.refs_2_, f32[1,3072]{1,0:T(1,128)S(1)} %get-tuple-element.293.refs_3_, ...), custom_call_target="tpu_custom_call" | custom-call | flops 10000000000 | bytes 1000000 | tf_op jit(solution)/shard_map/last/pallas_call | solution.py:148
  159.1 2.0 collective-permute-done.31.refs_2_
  161.4 1.4 collective-permute-done.32.refs_1_
  163.0 1.6 collective-permute-start.34
  165.1 1.7 collective-permute-start.36
  166.8 12.6 %collective-permute-done.34.refs_2_ = bf16[392,1152]{1,0:T(8,128)(2,1)S(1)} collective-permute-done((bf16[392,1152]{1,0:T(8,128)(2,1)S(1)}, bf16[392,1152]{1,0:T(8,128)(2,1)S(1)}, u32[]{:S(2)}, u32[]{:S(2)}) %collective-permute-start.34) | collective-permute-done | bytes 903200 | tf_op jit(solution)/shard_map/ppermute | solution.py:39
  180.2 1.5 collective-permute-start.40
  182.0 1.8 collective-permute-start.41
  183.8 1.1 collective-permute-start.39
  185.0 5.7 %collective-permute-done.35.refs_3_ = bf16[200,1152]{1,0:T(8,128)(2,1)S(1)} collective-permute-done((bf16[200,1152]{1,0:T(8,128)(2,1)S(1)}, bf16[200,1152]{1,0:T(8,128)(2,1)S(1)}, u32[]{:S(2)}, u32[]{:S(2)}) %collective-permute-start.35) | collective-permute-done | bytes 460832 | tf_op jit(solution)/shard_map/ppermute | solution.py:39
  190.8 1.1 collective-permute-start.38
  192.0 1.5 collective-permute-start.43
  193.6 3.0 %collective-permute-start.44 = (bf16[48,1920]{1,0:T(8,128)(2,1)S(1)}, bf16[48,1920]{1,0:T(8,128)(2,1)S(1)}, u32[]{:S(2)}, u32[]{:S(2)}) collective-permute-start(bf16[48,1920]{1,0:T(8,128)(2,1)S(1)} %add.64), channel_id=1, source_target_pairs={{0,16},{1,17},{2,6},{3,7},{4,20},{5,21},{6,2},{7,3},{8,24},{9,25},... | collective-permute-start | bytes 552968 | tf_op jit(solution)/shard_map/ppermute | solution.py:39
  196.6 1.3 deliver.2
  198.3 1.0 collective-permute-start.42
  199.3 7.3 %collective-permute-done.44.refs_5_ = bf16[48,1920]{1,0:T(8,128)(2,1)S(1)} collective-permute-done((bf16[48,1920]{1,0:T(8,128)(2,1)S(1)}, bf16[48,1920]{1,0:T(8,128)(2,1)S(1)}, u32[]{:S(2)}, u32[]{:S(2)}) %collective-permute-start.44) | collective-permute-done | bytes 184352 | tf_op jit(solution)/shard_map/ppermute | solution.py:39
  207.5 3.1 %collective-permute-start.45 = (bf16[96,1536]{1,0:T(8,128)(2,1)S(1)}, bf16[96,1536]{1,0:T(8,128)(2,1)S(1)}, u32[]{:S(2)}, u32[]{:S(2)}) collective-permute-start(bf16[96,1536]{1,0:T(8,128)(2,1)S(1)} %constant_dynamic-update-slice_fusion.4.refs_0_), channel_id=1, source_target_pairs={{0,2},{1,3},{2,0},{3,1},{4,6},{5,7},{6,4},{7,5},{8,10},{9,11},{10,... | collective-permute-start | bytes 884744 | tf_op jit(solution)/shard_map/ppermute | solution.py:39
  210.7 3.4 %collective-permute-start.50 = (bf16[48,1152]{1,0:T(8,128)(2,1)S(1)}, bf16[48,1152]{1,0:T(8,128)(2,1)S(1)}, u32[]{:S(2)}, u32[]{:S(2)}) collective-permute-start(bf16[48,1152]{1,0:T(8,128)(2,1)S(1)} %add.67.refs_0_), channel_id=1, source_target_pairs={{0,6},{1,7},{2,4},{3,5},{4,2},{5,3},{6,0},{7,1},{8,14},{9,15},{10,... | collective-permute-start | bytes 331784 | tf_op jit(solution)/shard_map/ppermute | solution.py:39
  214.8 1.5 collective-permute-start.48
  216.3 1.2 settle.3
  217.8 1.3 deliver.3
  219.0 1.6 collective-permute-done.48.refs_1_
  220.6 1.0 settle.4
  221.7 1.2 settle.5
  (144 shorter events, 18.4 us)
Async XLA Ops:
  0.6 8.4 %copy-start = (bf16[4,2,128,768]{3,2,1,0:T(8,128)(2,1)S(1)}, bf16[4,2,128,768]{3,2,1,0:T(8,128)(2,1)}, u32[]{:S(2)}) copy-start(bf16[4,2,128,768]{3,2,1,0:T(8,128)(2,1)} %param.15) | copy-start | bytes 4718596
  1.7 9.7 %collective-permute-start = (bf16[48,1152]{1,0:T(8,128)(2,1)S(1)}, bf16[48,1152]{1,0:T(8,128)(2,1)S(1)}, u32[]{:S(2)}, u32[]{:S(2)}) collective-permute-start(bf16[48,1152]{1,0:T(8,128)(2,1)S(1)} %bitcast.15), channel_id=1, source_target_pairs={{0,16},{1,17},{2,10},{3,11},{4,20},{5,21},{6,14},{7,15},{8,24},{9,... | collective-permute-start | bytes 331784 | tf_op jit(solution)/shard_map/ppermute | solution.py:39
  6.8 5.2 %collective-permute-start.1 = (bf16[48,1536]{1,0:T(8,128)(2,1)S(1)}, bf16[48,1536]{1,0:T(8,128)(2,1)S(1)}, u32[]{:S(2)}, u32[]{:S(2)}) collective-permute-start(bf16[48,1536]{1,0:T(8,128)(2,1)S(1)} %dynamic-slice_bitcast_fusion.2), channel_id=1, source_target_pairs={{0,4},{1,5},{2,3},{3,2},{4,0},{5,1},{6,7},{7,6},{8,12},{9,13},{10,... | collective-permute-start | bytes 442376 | tf_op jit(solution)/shard_map/ppermute | solution.py:39
  12.0 14.1 %collective-permute-start.3 = (bf16[96,1536]{1,0:T(8,128)(2,1)S(1)}, bf16[96,1536]{1,0:T(8,128)(2,1)S(1)}, u32[]{:S(2)}, u32[]{:S(2)}) collective-permute-start(bf16[96,1536]{1,0:T(8,128)(2,1)S(1)} %pad_maximum_fusion.12), channel_id=1, source_target_pairs={{0,16},{1,17},{2,6},{3,7},{4,20},{5,21},{6,2},{7,3},{8,24},{9,25},... | collective-permute-start | bytes 884744 | tf_op jit(solution)/shard_map/ppermute | solution.py:39
  12.1 14.0 %collective-permute-start.2 = (bf16[96,1152]{1,0:T(8,128)(2,1)S(1)}, bf16[96,1152]{1,0:T(8,128)(2,1)S(1)}, u32[]{:S(2)}, u32[]{:S(2)}) collective-permute-start(bf16[96,1152]{1,0:T(8,128)(2,1)S(1)} %pad_maximum_fusion.13), channel_id=1, source_target_pairs={{0,8},{1,9},{2,18},{3,19},{4,12},{5,13},{6,22},{7,23},{8,0},{9,1},... | collective-permute-start | bytes 663560 | tf_op jit(solution)/shard_map/ppermute | solution.py:39
  14.5 1.9 collective-permute-start.4
  14.5 8.0 %collective-permute-start.5 = (bf16[1,136,768]{2,1,0:T(8,128)(2,1)S(1)}, bf16[1,136,768]{2,1,0:T(8,128)(2,1)S(1)}, u32[]{:S(2)}, u32[]{:S(2)}) collective-permute-start(bf16[1,136,768]{2,1,0:T(8,128)(2,1)S(1)} %get-tuple-element.187), channel_id=1, source_target_pairs={{0,4},{1,5},{2,6},{3,7},{4,0},{5,1},{6,2},{7,3},{8,12},{9,13},{10,... | collective-permute-start | bytes 626696 | tf_op jit(solution)/shard_map/ppermute | solution.py:39
  15.9 10.2 %collective-permute-start.6 = (bf16[1,136,768]{2,1,0:T(8,128)(2,1)S(1)}, bf16[1,136,768]{2,1,0:T(8,128)(2,1)S(1)}, u32[]{:S(2)}, u32[]{:S(2)}) collective-permute-start(bf16[1,136,768]{2,1,0:T(8,128)(2,1)S(1)} %get-tuple-element.188), channel_id=1, source_target_pairs={{0,6},{1,7},{2,4},{3,5},{4,2},{5,3},{6,0},{7,1},{8,14},{9,15},{10,... | collective-permute-start | bytes 626696 | tf_op jit(solution)/shard_map/ppermute | solution.py:39
  26.2 4.8 %copy-start.4 = (f32[1536]{0:T(1024)S(1)}, f32[1536]{0:T(1024)}, u32[]{:S(2)}) copy-start(f32[1536]{0:T(1024)} %up_ref) | copy-start | bytes 18436
  26.2 4.8 %copy-start.5 = (f32[768]{0:T(1024)S(1)}, f32[768]{0:T(1024)}, u32[]{:S(2)}) copy-start(f32[768]{0:T(1024)} %refs_0_.1) | copy-start | bytes 9220
  26.2 4.8 %copy-start.6 = (f32[768]{0:T(1024)S(1)}, f32[768]{0:T(1024)}, u32[]{:S(2)}) copy-start(f32[768]{0:T(1024)} %refs_1_.1) | copy-start | bytes 9220
  26.2 4.8 %copy-start.7 = (f32[768]{0:T(1024)S(1)}, f32[768]{0:T(1024)}, u32[]{:S(2)}) copy-start(f32[768]{0:T(1024)} %refs_2_.1) | copy-start | bytes 9220
  26.2 4.8 %copy-start.8 = (f32[768]{0:T(1024)S(1)}, f32[768]{0:T(1024)}, u32[]{:S(2)}) copy-start(f32[768]{0:T(1024)} %refs_3_.1) | copy-start | bytes 9220
  26.2 4.8 %copy-start.9 = (f32[768]{0:T(1024)S(1)}, f32[768]{0:T(1024)}, u32[]{:S(2)}) copy-start(f32[768]{0:T(1024)} %refs_4_.1) | copy-start | bytes 9220
  26.2 4.7 %copy-start.10 = (f32[768]{0:T(1024)S(1)}, f32[768]{0:T(1024)}, u32[]{:S(2)}) copy-start(f32[768]{0:T(1024)} %refs_5_.1) | copy-start | bytes 9220
  26.3 4.7 %copy-start.11 = (f32[2,384]{1,0:T(2,128)S(1)}, f32[2,384]{1,0:T(2,128)}, u32[]{:S(2)}) copy-start(f32[2,384]{1,0:T(2,128)} %qv_ref.1) | copy-start | bytes 9220
  26.3 9.5 %collective-permute-start.7 = (bf16[192,1152]{1,0:T(8,128)(2,1)S(1)}, bf16[192,1152]{1,0:T(8,128)(2,1)S(1)}, u32[]{:S(2)}, u32[]{:S(2)}) collective-permute-start(bf16[192,1152]{1,0:T(8,128)(2,1)S(1)} %pad_maximum_fusion.5), channel_id=1, source_target_pairs={{0,1},{1,0},{2,6},{3,7},{4,5},{5,4},{6,2},{7,3},{8,9},{9,8},{10,14... | collective-permute-start | bytes 1327112 | tf_op jit(solution)/shard_map/ppermute | solution.py:39
  28.0 7.9 %collective-permute-start.8 = (bf16[48,1920]{1,0:T(8,128)(2,1)S(1)}, bf16[48,1920]{1,0:T(8,128)(2,1)S(1)}, u32[]{:S(2)}, u32[]{:S(2)}) collective-permute-start(bf16[48,1920]{1,0:T(8,128)(2,1)S(1)} %fusion.2), channel_id=1, source_target_pairs={{0,16},{1,17},{2,10},{3,11},{4,20},{5,21},{6,14},{7,15},{8,24},{9,... | collective-permute-start | bytes 552968 | tf_op jit(solution)/shard_map/ppermute | solution.py:39
  36.0 12.3 %collective-permute-start.13 = (bf16[384,1152]{1,0:T(8,128)(2,1)S(1)}, bf16[384,1152]{1,0:T(8,128)(2,1)S(1)}, u32[]{:S(2)}, u32[]{:S(2)}) collective-permute-start(bf16[384,1152]{1,0:T(8,128)(2,1)S(1)} %pad_maximum_fusion.refs_0_), channel_id=1, source_target_pairs={{0,2},{1,3},{2,0},{3,1},{4,6},{5,7},{6,4},{7,5},{8,10},{9,11},{10,... | collective-permute-start | bytes 2654216 | tf_op jit(solution)/shard_map/ppermute | solution.py:39
  36.0 13.1 %collective-permute-start.9 = (bf16[384,1152]{1,0:T(8,128)(2,1)S(1)}, bf16[384,1152]{1,0:T(8,128)(2,1)S(1)}, u32[]{:S(2)}, u32[]{:S(2)}) collective-permute-start(bf16[384,1152]{1,0:T(8,128)(2,1)S(1)} %pad_maximum_fusion.refs_0_), channel_id=1, source_target_pairs={{0,4},{1,5},{2,3},{3,2},{4,0},{5,1},{6,7},{7,6},{8,12},{9,13},{10,... | collective-permute-start | bytes 2654216 | tf_op jit(solution)/shard_map/ppermute | solution.py:39
  37.9 10.4 %collective-permute-start.11 = (bf16[2,128,768]{2,1,0:T(8,128)(2,1)S(1)}, bf16[2,128,768]{2,1,0:T(8,128)(2,1)S(1)}, u32[]{:S(2)}, u32[]{:S(2)}) collective-permute-start(bf16[2,128,768]{2,1,0:T(8,128)(2,1)S(1)} %pad_maximum_fusion.7), channel_id=1, source_target_pairs={{0,2},{1,3},{2,0},{3,1},{4,6},{5,7},{6,4},{7,5},{8,10},{9,11},{10,... | collective-permute-start | bytes 1179656 | tf_op jit(solution)/shard_map/ppermute | solution.py:39
  37.9 10.3 %collective-permute-start.10 = (bf16[96,1920]{1,0:T(8,128)(2,1)S(1)}, bf16[96,1920]{1,0:T(8,128)(2,1)S(1)}, u32[]{:S(2)}, u32[]{:S(2)}) collective-permute-start(bf16[96,1920]{1,0:T(8,128)(2,1)S(1)} %pad_maximum_fusion.11), channel_id=1, source_target_pairs={{0,8},{1,9},{2,18},{3,19},{4,12},{5,13},{6,22},{7,23},{8,0},{9,1},... | collective-permute-start | bytes 1105928 | tf_op jit(solution)/shard_map/ppermute | solution.py:39
  38.2 3.8 %collective-permute-start.12 = (f32[1,2304]{1,0:T(1,128)S(1)}, f32[1,2304]{1,0:T(1,128)S(1)}, u32[]{:S(2)}, u32[]{:S(2)}) collective-permute-start(f32[1,2304]{1,0:T(1,128)S(1)} %get-tuple-element.205), channel_id=1, source_target_pairs={{0,1},{1,0},{2,3},{3,2},{4,5},{5,4},{6,7},{7,6},{8,9},{9,8},{10,11... | collective-permute-start | bytes 27656 | tf_op jit(solution)/shard_map/ppermute | solution.py:39
  48.2 14.9 %copy-start.2 = (bf16[2,128,768]{2,1,0:T(8,128)(2,1)}, bf16[2,128,768]{2,1,0:T(8,128)(2,1)S(1)}, u32[]{:S(2)}) copy-start(bf16[2,128,768]{2,1,0:T(8,128)(2,1)S(1)} %collective-permute-done.11.refs_4_) | copy-start | bytes 1179652
  49.2 2.6 %collective-permute-start.14 = (bf16[384,1152]{1,0:T(8,128)(2,1)S(1)}, bf16[384,1152]{1,0:T(8,128)(2,1)S(1)}, u32[]{:S(2)}, u32[]{:S(2)}) collective-permute-start(bf16[384,1152]{1,0:T(8,128)(2,1)S(1)} %collective-permute-done.9.refs_1_), channel_id=1, source_target_pairs={{0,2},{1,3},{2,0},{3,1},{4,6},{5,7},{6,4},{7,5},{8,10},{9,11},{10,... | collective-permute-start | bytes 2654216 | tf_op jit(solution)/shard_map/ppermute | solution.py:39
  49.8 20.0 %collective-permute-start.16 = (bf16[192,1536]{1,0:T(8,128)(2,1)S(1)}, bf16[192,1536]{1,0:T(8,128)(2,1)S(1)}, u32[]{:S(2)}, u32[]{:S(2)}) collective-permute-start(bf16[192,1536]{1,0:T(8,128)(2,1)S(1)} %pad_maximum_fusion.4), channel_id=1, source_target_pairs={{0,8},{1,9},{2,18},{3,19},{4,12},{5,13},{6,22},{7,23},{8,0},{9,1},... | collective-permute-start | bytes 1769480 | tf_op jit(solution)/shard_map/ppermute | solution.py:39
  49.8 11.5 %collective-permute-start.15 = (bf16[192,1920]{1,0:T(8,128)(2,1)S(1)}, bf16[192,1920]{1,0:T(8,128)(2,1)S(1)}, u32[]{:S(2)}, u32[]{:S(2)}) collective-permute-start(bf16[192,1920]{1,0:T(8,128)(2,1)S(1)} %pad_maximum_fusion.3), channel_id=1, source_target_pairs={{0,1},{1,0},{2,6},{3,7},{4,5},{5,4},{6,2},{7,3},{8,9},{9,8},{10,14... | collective-permute-start | bytes 2211848 | tf_op jit(solution)/shard_map/ppermute | solution.py:39
  61.5 19.4 %collective-permute-start.17 = (bf16[384,1920]{1,0:T(8,128)(2,1)S(1)}, bf16[384,1920]{1,0:T(8,128)(2,1)S(1)}, u32[]{:S(2)}, u32[]{:S(2)}) collective-permute-start(bf16[384,1920]{1,0:T(8,128)(2,1)S(1)} %constant_dynamic-update-slice_fusion.refs_0_), channel_id=1, source_target_pairs={{0,4},{1,5},{2,3},{3,2},{4,0},{5,1},{6,7},{7,6},{8,12},{9,13},{10,... | collective-permute-start | bytes 4423688 | tf_op jit(solution)/shard_map/ppermute | solution.py:39
  63.1 7.1 %slice-start = ((bf16[2,128,768]{2,1,0:T(8,128)(2,1)}), bf16[1,128,768]{2,1,0:T(8,128)(2,1)S(1)}, s32[]{:S(2)}) async-start(bf16[2,128,768]{2,1,0:T(8,128)(2,1)} %copy-done.2), calls=%async_computation | async-start | bytes 393216 | tf_op jit(solution)/shard_map/slice | solution.py:924
  69.7 11.2 %collective-permute-start.18 = (bf16[384,1920]{1,0:T(8,128)(2,1)S(1)}, bf16[384,1920]{1,0:T(8,128)(2,1)S(1)}, u32[]{:S(2)}, u32[]{:S(2)}) collective-permute-start(bf16[384,1920]{1,0:T(8,128)(2,1)S(1)} %constant_dynamic-update-slice_fusion.refs_0_), channel_id=1, source_target_pairs={{0,2},{1,3},{2,0},{3,1},{4,6},{5,7},{6,4},{7,5},{8,10},{9,11},{10,... | collective-permute-start | bytes 4423688 | tf_op jit(solution)/shard_map/ppermute | solution.py:39
  80.9 3.3 %collective-permute-start.19 = (bf16[384,1920]{1,0:T(8,128)(2,1)S(1)}, bf16[384,1920]{1,0:T(8,128)(2,1)S(1)}, u32[]{:S(2)}, u32[]{:S(2)}) collective-permute-start(bf16[384,1920]{1,0:T(8,128)(2,1)S(1)} %collective-permute-done.17.refs_1_), channel_id=1, source_target_pairs={{0,2},{1,3},{2,0},{3,1},{4,6},{5,7},{6,4},{7,5},{8,10},{9,11},{10,... | collective-permute-start | bytes 4423688 | tf_op jit(solution)/shard_map/ppermute | solution.py:39
  80.9 14.4 %collective-permute-start.21 = (bf16[384,1536]{1,0:T(8,128)(2,1)S(1)}, bf16[384,1536]{1,0:T(8,128)(2,1)S(1)}, u32[]{:S(2)}, u32[]{:S(2)}) collective-permute-start(bf16[384,1536]{1,0:T(8,128)(2,1)S(1)} %constant_dynamic-update-slice_fusion.2.refs_0_), channel_id=1, source_target_pairs={{0,2},{1,3},{2,0},{3,1},{4,6},{5,7},{6,4},{7,5},{8,10},{9,11},{10,... | collective-permute-start | bytes 3538952 | tf_op jit(solution)/shard_map/ppermute | solution.py:39
  81.4 16.2 %collective-permute-start.20 = (bf16[384,1536]{1,0:T(8,128)(2,1)S(1)}, bf16[384,1536]{1,0:T(8,128)(2,1)S(1)}, u32[]{:S(2)}, u32[]{:S(2)}) collective-permute-start(bf16[384,1536]{1,0:T(8,128)(2,1)S(1)} %constant_dynamic-update-slice_fusion.2.refs_0_), channel_id=1, source_target_pairs={{0,1},{1,0},{2,10},{3,11},{4,5},{5,4},{6,14},{7,15},{8,9},{9,8},{1... | collective-permute-start | bytes 3538952 | tf_op jit(solution)/shard_map/ppermute | solution.py:39
  81.9 15.7 %collective-permute-start.22 = (bf16[2,128,768]{2,1,0:T(8,128)(2,1)S(1)}, bf16[2,128,768]{2,1,0:T(8,128)(2,1)S(1)}, u32[]{:S(2)}, u32[]{:S(2)}) collective-permute-start(bf16[2,128,768]{2,1,0:T(8,128)(2,1)S(1)} %pad_maximum_fusion.8), channel_id=1, source_target_pairs={{0,4},{1,5},{2,6},{3,7},{4,0},{5,1},{6,2},{7,3},{8,12},{9,13},{10,... | collective-permute-start | bytes 1179656 | tf_op jit(solution)/shard_map/ppermute | solution.py:39
  97.6 4.5 %copy-start.3 = (bf16[2,128,768]{2,1,0:T(8,128)(2,1)S(1)}, bf16[2,128,768]{2,1,0:T(8,128)(2,1)}, u32[]{:S(2)}) copy-start(bf16[2,128,768]{2,1,0:T(8,128)(2,1)} %copy-done.2) | copy-start | bytes 1179652
  97.6 2.8 %collective-permute-start.23 = (bf16[384,1536]{1,0:T(8,128)(2,1)S(1)}, bf16[384,1536]{1,0:T(8,128)(2,1)S(1)}, u32[]{:S(2)}, u32[]{:S(2)}) collective-permute-start(bf16[384,1536]{1,0:T(8,128)(2,1)S(1)} %collective-permute-done.20.refs_1_), channel_id=1, source_target_pairs={{0,2},{1,3},{2,0},{3,1},{4,6},{5,7},{6,4},{7,5},{8,10},{9,11},{10,... | collective-permute-start | bytes 3538952 | tf_op jit(solution)/shard_map/ppermute | solution.py:39
  111.2 5.2 %collective-permute-start.24 = (bf16[768,1536]{1,0:T(8,128)(2,1)S(1)}, bf16[768,1536]{1,0:T(8,128)(2,1)S(1)}, u32[]{:S(2)}, u32[]{:S(2)}) collective-permute-start(bf16[768,1536]{1,0:T(8,128)(2,1)S(1)} %get-tuple-element.253), channel_id=1, source_target_pairs={{0,2},{1,3},{2,0},{3,1},{4,6},{5,7},{6,4},{7,5},{8,10},{9,11},{10,... | collective-permute-start | bytes 7077896 | tf_op jit(solution)/shard_map/ppermute | solution.py:39
  111.5 4.9 %collective-permute-start.25 = (bf16[2,128,768]{2,1,0:T(8,128)(2,1)S(1)}, bf16[2,128,768]{2,1,0:T(8,128)(2,1)S(1)}, u32[]{:S(2)}, u32[]{:S(2)}) collective-permute-start(bf16[2,128,768]{2,1,0:T(8,128)(2,1)S(1)} %slice.34), channel_id=1, source_target_pairs={{0,2},{1,3},{2,0},{3,1},{4,6},{5,7},{6,4},{7,5},{8,10},{9,11},{10,... | collective-permute-start | bytes 1179656 | tf_op jit(solution)/shard_map/ppermute | solution.py:39
  116.8 12.6 %collective-permute-start.27 = (bf16[2,128,768]{2,1,0:T(8,128)(2,1)S(1)}, bf16[2,128,768]{2,1,0:T(8,128)(2,1)S(1)}, u32[]{:S(2)}, u32[]{:S(2)}) collective-permute-start(bf16[2,128,768]{2,1,0:T(8,128)(2,1)S(1)} %pad_maximum_fusion.9), channel_id=1, source_target_pairs={{0,4},{1,5},{2,6},{3,7},{4,0},{5,1},{6,2},{7,3},{8,12},{9,13},{10,... | collective-permute-start | bytes 1179656 | tf_op jit(solution)/shard_map/ppermute | solution.py:39
  118.4 16.2 %collective-permute-start.26 = (bf16[384,1536]{1,0:T(8,128)(2,1)S(1)}, bf16[384,1536]{1,0:T(8,128)(2,1)S(1)}, u32[]{:S(2)}, u32[]{:S(2)}) collective-permute-start(bf16[384,1536]{1,0:T(8,128)(2,1)S(1)} %add.53), channel_id=1, source_target_pairs={{0,1},{1,0},{2,10},{3,11},{4,5},{5,4},{6,14},{7,15},{8,9},{9,8},{1... | collective-permute-start | bytes 3538952 | tf_op jit(solution)/shard_map/ppermute | solution.py:39
  134.6 6.7 %collective-permute-start.28 = (bf16[768,1920]{1,0:T(8,128)(2,1)S(1)}, bf16[768,1920]{1,0:T(8,128)(2,1)S(1)}, u32[]{:S(2)}, u32[]{:S(2)}) collective-permute-start(bf16[768,1920]{1,0:T(8,128)(2,1)S(1)} %get-tuple-element.273), channel_id=1, source_target_pairs={{0,2},{1,3},{2,0},{3,1},{4,6},{5,7},{6,4},{7,5},{8,10},{9,11},{10,... | collective-permute-start | bytes 8847368 | tf_op jit(solution)/shard_map/ppermute | solution.py:39
  134.9 13.9 %collective-permute-start.29 = (bf16[192,1536]{1,0:T(8,128)(2,1)S(1)}, bf16[192,1536]{1,0:T(8,128)(2,1)S(1)}, u32[]{:S(2)}, u32[]{:S(2)}) collective-permute-start(bf16[192,1536]{1,0:T(8,128)(2,1)S(1)} %add.54), channel_id=1, source_target_pairs={{0,4},{1,5},{2,18},{3,19},{4,0},{5,1},{6,22},{7,23},{8,12},{9,13},... | collective-permute-start | bytes 1769480 | tf_op jit(solution)/shard_map/ppermute | solution.py:39
  135.4 18.7 %collective-permute-start.30 = (bf16[4,128,768]{2,1,0:T(8,128)(2,1)S(1)}, bf16[4,128,768]{2,1,0:T(8,128)(2,1)S(1)}, u32[]{:S(2)}, u32[]{:S(2)}) collective-permute-start(bf16[4,128,768]{2,1,0:T(8,128)(2,1)S(1)} %pad_maximum_fusion.1), channel_id=1, source_target_pairs={{0,1},{1,0},{2,3},{3,2},{4,5},{5,4},{6,7},{7,6},{8,9},{9,8},{10,11... | collective-permute-start | bytes 2359304 | tf_op jit(solution)/shard_map/ppermute | solution.py:39
  141.7 19.4 %collective-permute-start.31 = (bf16[384,1920]{1,0:T(8,128)(2,1)S(1)}, bf16[384,1920]{1,0:T(8,128)(2,1)S(1)}, u32[]{:S(2)}, u32[]{:S(2)}) collective-permute-start(bf16[384,1920]{1,0:T(8,128)(2,1)S(1)} %add.55), channel_id=1, source_target_pairs={{0,4},{1,5},{2,10},{3,11},{4,0},{5,1},{6,14},{7,15},{8,12},{9,13},... | collective-permute-start | bytes 4423688 | tf_op jit(solution)/shard_map/ppermute | solution.py:39
  154.1 8.6 %collective-permute-start.33 = (bf16[2,128,768]{2,1,0:T(8,128)(2,1)S(1)}, bf16[2,128,768]{2,1,0:T(8,128)(2,1)S(1)}, u32[]{:S(2)}, u32[]{:S(2)}) collective-permute-start(bf16[2,128,768]{2,1,0:T(8,128)(2,1)S(1)} %slice.39), channel_id=1, source_target_pairs={{0,2},{1,3},{2,0},{3,1},{4,6},{5,7},{6,4},{7,5},{8,10},{9,11},{10,... | collective-permute-start | bytes 1179656 | tf_op jit(solution)/shard_map/ppermute | solution.py:39
  159.0 3.8 %collective-permute-start.32 = (bf16[776,1152]{1,0:T(8,128)(2,1)S(1)}, bf16[776,1152]{1,0:T(8,128)(2,1)S(1)}, u32[]{:S(2)}, u32[]{:S(2)}) collective-permute-start(bf16[776,1152]{1,0:T(8,128)(2,1)S(1)} %get-tuple-element.299), channel_id=1, source_target_pairs={{0,2},{1,3},{2,0},{3,1},{4,6},{5,7},{6,4},{7,5},{8,10},{9,11},{10,... | collective-permute-start | bytes 5363720 | tf_op jit(solution)/shard_map/ppermute | solution.py:39
  163.0 16.5 %collective-permute-start.34 = (bf16[392,1152]{1,0:T(8,128)(2,1)S(1)}, bf16[392,1152]{1,0:T(8,128)(2,1)S(1)}, u32[]{:S(2)}, u32[]{:S(2)}) collective-permute-start(bf16[392,1152]{1,0:T(8,128)(2,1)S(1)} %add.58.refs_3_), channel_id=1, source_target_pairs={{0,4},{1,5},{2,3},{3,2},{4,0},{5,1},{6,7},{7,6},{8,12},{9,13},{10,... | collective-permute-start | bytes 2709512 | tf_op jit(solution)/shard_map/ppermute | solution.py:39
  164.6 17.2 %collective-permute-start.37 = (bf16[192,1920]{1,0:T(8,128)(2,1)S(1)}, bf16[192,1920]{1,0:T(8,128)(2,1)S(1)}, u32[]{:S(2)}, u32[]{:S(2)}) collective-permute-start(bf16[192,1920]{1,0:T(8,128)(2,1)S(1)} %add.57), channel_id=1, source_target_pairs={{0,1},{1,0},{2,18},{3,19},{4,5},{5,4},{6,22},{7,23},{8,9},{9,8},{1... | collective-permute-start | bytes 2211848 | tf_op jit(solution)/shard_map/ppermute | solution.py:39
  165.1 15.2 %collective-permute-start.36 = (bf16[96,1536]{1,0:T(8,128)(2,1)S(1)}, bf16[96,1536]{1,0:T(8,128)(2,1)S(1)}, u32[]{:S(2)}, u32[]{:S(2)}) collective-permute-start(bf16[96,1536]{1,0:T(8,128)(2,1)S(1)} %add.56), channel_id=1, source_target_pairs={{0,8},{1,9},{2,6},{3,7},{4,12},{5,13},{6,2},{7,3},{8,0},{9,1},{10,... | collective-permute-start | bytes 884744 | tf_op jit(solution)/shard_map/ppermute | solution.py:39
  179.6 11.0 %collective-permute-start.35 = (bf16[200,1152]{1,0:T(8,128)(2,1)S(1)}, bf16[200,1152]{1,0:T(8,128)(2,1)S(1)}, u32[]{:S(2)}, u32[]{:S(2)}) collective-permute-start(bf16[200,1152]{1,0:T(8,128)(2,1)S(1)} %add.59.refs_4_), channel_id=1, source_target_pairs={{0,1},{1,0},{2,6},{3,7},{4,5},{5,4},{6,2},{7,3},{8,9},{9,8},{10,14... | collective-permute-start | bytes 1382408 | tf_op jit(solution)/shard_map/ppermute | solution.py:39
  180.2 11.6 %collective-permute-start.40 = (bf16[2,128,768]{2,1,0:T(8,128)(2,1)S(1)}, bf16[2,128,768]{2,1,0:T(8,128)(2,1)S(1)}, u32[]{:S(2)}, u32[]{:S(2)}) collective-permute-start(bf16[2,128,768]{2,1,0:T(8,128)(2,1)S(1)} %pad_maximum_fusion.10), channel_id=1, source_target_pairs={{0,4},{1,5},{2,6},{3,7},{4,0},{5,1},{6,2},{7,3},{8,12},{9,13},{10,... | collective-permute-start | bytes 1179656 | tf_op jit(solution)/shard_map/ppermute | solution.py:39
  182.0 11.5 %collective-permute-start.41 = (bf16[96,1920]{1,0:T(8,128)(2,1)S(1)}, bf16[96,1920]{1,0:T(8,128)(2,1)S(1)}, u32[]{:S(2)}, u32[]{:S(2)}) collective-permute-start(bf16[96,1920]{1,0:T(8,128)(2,1)S(1)} %add.61), channel_id=1, source_target_pairs={{0,8},{1,9},{2,3},{3,2},{4,12},{5,13},{6,7},{7,6},{8,0},{9,1},{10,... | collective-permute-start | bytes 1105928 | tf_op jit(solution)/shard_map/ppermute | solution.py:39
  183.8 8.1 %collective-permute-start.39 = (bf16[48,1536]{1,0:T(8,128)(2,1)S(1)}, bf16[48,1536]{1,0:T(8,128)(2,1)S(1)}, u32[]{:S(2)}, u32[]{:S(2)}) collective-permute-start(bf16[48,1536]{1,0:T(8,128)(2,1)S(1)} %add.60), channel_id=1, source_target_pairs={{0,16},{1,17},{2,3},{3,2},{4,20},{5,21},{6,7},{7,6},{8,24},{9,25},... | collective-permute-start | bytes 442376 | tf_op jit(solution)/shard_map/ppermute | solution.py:39
  190.8 7.4 %collective-permute-start.38 = (bf16[104,1152]{1,0:T(8,128)(2,1)S(1)}, bf16[104,1152]{1,0:T(8,128)(2,1)S(1)}, u32[]{:S(2)}, u32[]{:S(2)}) collective-permute-start(bf16[104,1152]{1,0:T(8,128)(2,1)S(1)} %add.62.refs_5_), channel_id=1, source_target_pairs={{0,8},{1,9},{2,18},{3,19},{4,12},{5,13},{6,22},{7,23},{8,0},{9,1},... | collective-permute-start | bytes 718856 | tf_op jit(solution)/shard_map/ppermute | solution.py:39
  192.0 7.3 %collective-permute-start.43 = (bf16[48,1536]{1,0:T(8,128)(2,1)S(1)}, bf16[48,1536]{1,0:T(8,128)(2,1)S(1)}, u32[]{:S(2)}, u32[]{:S(2)}) collective-permute-start(bf16[48,1536]{1,0:T(8,128)(2,1)S(1)} %add.63), channel_id=1, source_target_pairs={{0,4},{1,5},{2,6},{3,7},{4,0},{5,1},{6,2},{7,3},{8,12},{9,13},{10,... | collective-permute-start | bytes 442376 | tf_op jit(solution)/shard_map/ppermute | solution.py:39
  193.6 13.0 %collective-permute-start.44 = (bf16[48,1920]{1,0:T(8,128)(2,1)S(1)}, bf16[48,1920]{1,0:T(8,128)(2,1)S(1)}, u32[]{:S(2)}, u32[]{:S(2)}) collective-permute-start(bf16[48,1920]{1,0:T(8,128)(2,1)S(1)} %add.64), channel_id=1, source_target_pairs={{0,16},{1,17},{2,6},{3,7},{4,20},{5,21},{6,2},{7,3},{8,24},{9,25},... | collective-permute-start | bytes 552968 | tf_op jit(solution)/shard_map/ppermute | solution.py:39
  198.0 19.8 %collective-permute-start.47 = (bf16[4,128,768]{2,1,0:T(8,128)(2,1)S(1)}, bf16[4,128,768]{2,1,0:T(8,128)(2,1)S(1)}, u32[]{:S(2)}, u32[]{:S(2)}) collective-permute-start(bf16[4,128,768]{2,1,0:T(8,128)(2,1)S(1)} %pad_maximum_fusion.2), channel_id=1, source_target_pairs={{0,1},{1,0},{2,3},{3,2},{4,5},{5,4},{6,7},{7,6},{8,9},{9,8},{10,11... | collective-permute-start | bytes 2359304 | tf_op jit(solution)/shard_map/ppermute | solution.py:39
  198.3 12.3 %collective-permute-start.42 = (bf16[56,1152]{1,0:T(8,128)(2,1)S(1)}, bf16[56,1152]{1,0:T(8,128)(2,1)S(1)}, u32[]{:S(2)}, u32[]{:S(2)}) collective-permute-start(bf16[56,1152]{1,0:T(8,128)(2,1)S(1)} %add.65.refs_0_), channel_id=1, source_target_pairs={{0,16},{1,17},{2,10},{3,11},{4,20},{5,21},{6,14},{7,15},{8,24},{9,... | collective-permute-start | bytes 387080 | tf_op jit(solution)/shard_map/ppermute | solution.py:39
  206.8 10.7 %collective-permute-start.46 = (bf16[48,1920]{1,0:T(8,128)(2,1)S(1)}, bf16[48,1920]{1,0:T(8,128)(2,1)S(1)}, u32[]{:S(2)}, u32[]{:S(2)}) collective-permute-start(bf16[48,1920]{1,0:T(8,128)(2,1)S(1)} %add.66), channel_id=1, source_target_pairs={{0,4},{1,5},{2,6},{3,7},{4,0},{5,1},{6,2},{7,3},{8,12},{9,13},{10,... | collective-permute-start | bytes 552968 | tf_op jit(solution)/shard_map/ppermute | solution.py:39
  207.5 7.3 %collective-permute-start.45 = (bf16[96,1536]{1,0:T(8,128)(2,1)S(1)}, bf16[96,1536]{1,0:T(8,128)(2,1)S(1)}, u32[]{:S(2)}, u32[]{:S(2)}) collective-permute-start(bf16[96,1536]{1,0:T(8,128)(2,1)S(1)} %constant_dynamic-update-slice_fusion.4.refs_0_), channel_id=1, source_target_pairs={{0,2},{1,3},{2,0},{3,1},{4,6},{5,7},{6,4},{7,5},{8,10},{9,11},{10,... | collective-permute-start | bytes 884744 | tf_op jit(solution)/shard_map/ppermute | solution.py:39
  210.7 8.3 %collective-permute-start.50 = (bf16[48,1152]{1,0:T(8,128)(2,1)S(1)}, bf16[48,1152]{1,0:T(8,128)(2,1)S(1)}, u32[]{:S(2)}, u32[]{:S(2)}) collective-permute-start(bf16[48,1152]{1,0:T(8,128)(2,1)S(1)} %add.67.refs_0_), channel_id=1, source_target_pairs={{0,6},{1,7},{2,4},{3,5},{4,2},{5,3},{6,0},{7,1},{8,14},{9,15},{10,... | collective-permute-start | bytes 331784 | tf_op jit(solution)/shard_map/ppermute | solution.py:39
  214.1 4.9 %collective-permute-start.49 = (bf16[48,1152]{1,0:T(8,128)(2,1)S(1)}, bf16[48,1152]{1,0:T(8,128)(2,1)S(1)}, u32[]{:S(2)}, u32[]{:S(2)}) collective-permute-start(bf16[48,1152]{1,0:T(8,128)(2,1)S(1)} %add.67.refs_0_), channel_id=1, source_target_pairs={{0,2},{1,3},{2,0},{3,1},{4,6},{5,7},{6,4},{7,5},{8,10},{9,11},{10,... | collective-permute-start | bytes 331784 | tf_op jit(solution)/shard_map/ppermute | solution.py:39
  214.8 5.8 %collective-permute-start.48 = (bf16[48,1152]{1,0:T(8,128)(2,1)S(1)}, bf16[48,1152]{1,0:T(8,128)(2,1)S(1)}, u32[]{:S(2)}, u32[]{:S(2)}) collective-permute-start(bf16[48,1152]{1,0:T(8,128)(2,1)S(1)} %add.67.refs_0_), channel_id=1, source_target_pairs={{0,4},{1,5},{2,6},{3,7},{4,0},{5,1},{6,2},{7,3},{8,12},{9,13},{10,... | collective-permute-start | bytes 331784 | tf_op jit(solution)/shard_map/ppermute | solution.py:39
  217.5 4.2 %collective-permute-start.51 = (bf16[96,1920]{1,0:T(8,128)(2,1)S(1)}, bf16[96,1920]{1,0:T(8,128)(2,1)S(1)}, u32[]{:S(2)}, u32[]{:S(2)}) collective-permute-start(bf16[96,1920]{1,0:T(8,128)(2,1)S(1)} %constant_dynamic-update-slice_fusion.6.refs_0_), channel_id=1, source_target_pairs={{0,2},{1,3},{2,0},{3,1},{4,6},{5,7},{6,4},{7,5},{8,10},{9,11},{10,... | collective-permute-start | bytes 1105928 | tf_op jit(solution)/shard_map/ppermute | solution.py:39
  (3 other events, 4.1 us)

commit v8 on v7

--- a/solution.py
+++ b/solution.py
@@ -324,9 +324,9 @@
         mixed0_ref[...], w_out[:, :narrow], NT, preferred_element_type=F32
     ) + lax.dot_general(mixed1_ref[...], w_out[:, narrow:], NT, preferred_element_type=F32)
 
-    @tiles(length, 64)
+    @tiles(length, 128)
     def _(at):
-        here = pl.ds(at, 64)
+        here = pl.ds(at, 128)
         value = x_ref[here, :].astype(F32) + normed_ref[here, :] + table_ref[B_OUT : B_OUT + 1, :]
         centred = value - row_mean(value)
         scale = lax.rsqrt(row_mean(centred * centred) + 1e-12)
@@ -385,9 +385,9 @@
     sums_ref[...] = jnp.zeros_like(sums_ref)
     row = lambda which: table_ref[which : which + 1, :]
 
-    @tiles(length, 64)
+    @tiles(length, 128)
     def _(at):
-        here = pl.ds(at, 64)
+        here = pl.ds(at, 128)
         value = normed_ref[here, :] * row(GAIN1) + row(SHIFT1) + gz_ref[here, :] + row(B_DOWN)
         centred = value - row_mean(value)
         scale = lax.rsqrt(row_mean(centred * centred) + 1e-12)
@@ -397,7 +397,7 @@
         if orders is not None:
             c = lax.axis_index("ctx") ^ chunk
             chunk = (c & 1) * 2 + (c >> 1)
-        chunks_ref[chunk, pl.ds(pl.multiple_of(lax.rem(at, block), 64), 64), :] = result
+        chunks_ref[chunk, pl.ds(pl.multiple_of(lax.rem(at, block), 128), 128), :] = result
         coming = cot_ref[here, :].astype(F32)
         raised = coming * row(GAIN2)
         back = scale * (raised - row_mean(raised) - unit * row_mean(raised * unit))
@@ -485,9 +485,9 @@
     gz1_ref[...] = lax.dot_general(gh_ref[...], w_up[...], NT, preferred_element_type=F32)
     sums_ref[...] = jnp.zeros_like(sums_ref)
 
-    @tiles(length, 64)
+    @tiles(length, 128)
     def _(at):
-        here = pl.ds(at, 64)
+        here = pl.ds(at, 128)
         coming = gz_ref[here, :] + gz1_ref[here, :]
         unit = normed_ref[here, :]
         raised = coming * table_ref[GAIN1 : GAIN1 + 1, :]

time: 224 us -> 223 us (level)
  transfers between devices with their start and end apart: 52 -> 52, of which waited for: 22 -> 22; matrix products, arithmetic and copies ran while one was open for 2% -> 2% of each run, Pallas kernels for 30% -> 29%
where the time goes in v8:
time: 223 us
  waiting for transfers between devices  82.6 us (37%)
  Pallas kernels  77.1 us (35%)
  starting transfers between devices  54.7 us (25%)
  local copies, waits for them, and re-layouts  5.48 us (2%)
    ppermute x52, waiting for transfers between devices, exchange(): return lax.ppermute(value, AXES, pairs)  82.6 us
    pallas_call x36, Pallas kernels, call(): pl.pallas_call(kernel, name=name, out_shape=outs, in_specs=specs, out_spe...  77.1 us
    ppermute x52, starting transfers between devices, exchange(): return lax.ppermute(value, AXES, pairs)  54.7 us
  transfers between devices with their start and end apart: 52, of which 22 were waited for; matrix products, arithmetic and copies ran while one was open for 2% of the time, Pallas kernels for 29%

profile of v8, /device:TPU:0, one launch (start us, length us, event | category | flops | bytes accessed | tf_op | source)
XLA Modules:
  0.0 222.6 jit_solution(149078063871959167)
XLA Ops:
  0.7 1.0 dynamic-slice_bitcast_fusion.3
  1.7 4.1 %collective-permute-start = (bf16[48,1152]{1,0:T(8,128)(2,1)S(1)}, bf16[48,1152]{1,0:T(8,128)(2,1)S(1)}, u32[]{:S(2)}, u32[]{:S(2)}) collective-permute-start(bf16[48,1152]{1,0:T(8,128)(2,1)S(1)} %bitcast.15), channel_id=1, source_target_pairs={{0,16},{1,17},{2,10},{3,11},{4,20},{5,21},{6,14},{7,15},{8,24},{9,... | collective-permute-start | bytes 331784 | tf_op jit(solution)/shard_map/ppermute | solution.py:39
  6.8 1.6 collective-permute-start.1
  10.2 1.2 dynamic-slice_bitcast_fusion
  12.1 2.4 %collective-permute-start.2 = (bf16[96,1152]{1,0:T(8,128)(2,1)S(1)}, bf16[96,1152]{1,0:T(8,128)(2,1)S(1)}, u32[]{:S(2)}, u32[]{:S(2)}) collective-permute-start(bf16[96,1152]{1,0:T(8,128)(2,1)S(1)} %pad_maximum_fusion.13), channel_id=1, source_target_pairs={{0,8},{1,9},{2,18},{3,19},{4,12},{5,13},{6,22},{7,23},{8,0},{9,1},... | collective-permute-start | bytes 663560 | tf_op jit(solution)/shard_map/ppermute | solution.py:39
  14.5 1.5 collective-permute-start.5
  16.3 6.1 %collective-permute-done.5 = bf16[1,136,768]{2,1,0:T(8,128)(2,1)S(1)} collective-permute-done((bf16[1,136,768]{2,1,0:T(8,128)(2,1)S(1)}, bf16[1,136,768]{2,1,0:T(8,128)(2,1)S(1)}, u32[]{:S(2)}, u32[]{:S(2)}) %collective-permute-start.5) | collective-permute-done | bytes 208928 | tf_op jit(solution)/shard_map/ppermute | solution.py:39
  22.4 3.7 %collective-permute-done.6 = bf16[1,136,768]{2,1,0:T(8,128)(2,1)S(1)} collective-permute-done((bf16[1,136,768]{2,1,0:T(8,128)(2,1)S(1)}, bf16[1,136,768]{2,1,0:T(8,128)(2,1)S(1)}, u32[]{:S(2)}, u32[]{:S(2)}) %collective-permute-start.6) | collective-permute-done | bytes 208928 | tf_op jit(solution)/shard_map/ppermute | solution.py:39
  26.3 1.6 collective-permute-start.7
  28.0 2.9 %collective-permute-start.8 = (bf16[48,1920]{1,0:T(8,128)(2,1)S(1)}, bf16[48,1920]{1,0:T(8,128)(2,1)S(1)}, u32[]{:S(2)}, u32[]{:S(2)}) collective-permute-start(bf16[48,1920]{1,0:T(8,128)(2,1)S(1)} %fusion.2), channel_id=1, source_target_pairs={{0,16},{1,17},{2,10},{3,11},{4,20},{5,21},{6,14},{7,15},{8,24},{9,... | collective-permute-start | bytes 552968 | tf_op jit(solution)/shard_map/ppermute | solution.py:39
  31.1 4.8 %collective-permute-done.8 = bf16[48,1920]{1,0:T(8,128)(2,1)S(1)} collective-permute-done((bf16[48,1920]{1,0:T(8,128)(2,1)S(1)}, bf16[48,1920]{1,0:T(8,128)(2,1)S(1)}, u32[]{:S(2)}, u32[]{:S(2)}) %collective-permute-start.8) | collective-permute-done | bytes 184352 | tf_op jit(solution)/shard_map/ppermute | solution.py:39
  36.0 1.8 collective-permute-start.9
  38.4 3.5 %collective-permute-done.12 = f32[1,2304]{1,0:T(1,128)S(1)} collective-permute-done((f32[1,2304]{1,0:T(1,128)S(1)}, f32[1,2304]{1,0:T(1,128)S(1)}, u32[]{:S(2)}, u32[]{:S(2)}) %collective-permute-start.12) | collective-permute-done | bytes 9248 | tf_op jit(solution)/shard_map/ppermute | solution.py:39
  42.0 6.2 %collective-permute-done.10 = bf16[96,1920]{1,0:T(8,128)(2,1)S(1)} collective-permute-done((bf16[96,1920]{1,0:T(8,128)(2,1)S(1)}, bf16[96,1920]{1,0:T(8,128)(2,1)S(1)}, u32[]{:S(2)}, u32[]{:S(2)}) %collective-permute-start.10) | collective-permute-done | bytes 368672 | tf_op jit(solution)/shard_map/ppermute | solution.py:39
  48.2 0.9 collective-permute-done.9.refs_1_
  50.6 1.2 collective-permute-done.14.refs_3_
  51.8 1.4 unpack.3.refs_0_
  53.2 2.6 %project.1 = (bf16[512,2304]{1,0:T(8,128)(2,1)S(1)}, bf16[512,768]{1,0:T(8,128)(2,1)S(1)}, f32[512,512]{1,0:T(8,128)S(1)}) custom-call(bf16[768,2304]{1,0:T(8,128)(2,1)S(1)} %unpack.3.refs_0_, bf16[1,136,768]{2,1,0:T(8,128)(2,1)S(1)} %get-tuple-element.350.refs_1_, bf16[1,136,768]{2,1,0:T(8,128)(2,1)S(1)} %collective-permute-done.4.refs_2_, ...), custom_call_target="tpu_custom_call" | custom-call | flops 5000000000 | bytes 1000000 | tf_op jit(solution)/shard_map/project/pallas_call | solution.py:148
  55.8 5.6 %collective-permute-done.15 = bf16[192,1920]{1,0:T(8,128)(2,1)S(1)} collective-permute-done((bf16[192,1920]{1,0:T(8,128)(2,1)S(1)}, bf16[192,1920]{1,0:T(8,128)(2,1)S(1)}, u32[]{:S(2)}, u32[]{:S(2)}) %collective-permute-start.15) | collective-permute-done | bytes 737312 | tf_op jit(solution)/shard_map/ppermute | solution.py:39
  61.5 1.6 collective-permute-start.17
  63.1 6.7 %attend.2 = (bf16[512,384]{1,0:T(8,128)(2,1)S(1)}, bf16[6,512,512]{2,1,0:T(8,128)(2,1)S(1)}) custom-call(bf16[512,2304]{1,0:T(8,128)(2,1)S(1)} %get-tuple-element.227.refs_0_, f32[512,512]{1,0:T(8,128)S(1)} %get-tuple-element.221.refs_1_), custom_call_target="tpu_custom_call" | custom-call | flops 12000000000 | bytes 1000000 | tf_op jit(solution)/shard_map/attend/pallas_call | solution.py:148
  70.3 6.7 %attend.3 = (bf16[512,384]{1,0:T(8,128)(2,1)S(1)}, bf16[6,512,512]{2,1,0:T(8,128)(2,1)S(1)}) custom-call(bf16[512,2304]{1,0:T(8,128)(2,1)S(1)} %get-tuple-element.227.refs_0_, f32[512,512]{1,0:T(8,128)S(1)} %get-tuple-element.221.refs_1_), custom_call_target="tpu_custom_call" | custom-call | flops 12000000000 | bytes 1000000 | tf_op jit(solution)/shard_map/attend/pallas_call | solution.py:148
  76.9 4.0 %collective-permute-done.17.refs_1_ = bf16[384,1920]{1,0:T(8,128)(2,1)S(1)} collective-permute-done((bf16[384,1920]{1,0:T(8,128)(2,1)S(1)}, bf16[384,1920]{1,0:T(8,128)(2,1)S(1)}, u32[]{:S(2)}, u32[]{:S(2)}) %collective-permute-start.17) | collective-permute-done | bytes 1474592 | tf_op jit(solution)/shard_map/ppermute | solution.py:39
  81.9 1.5 collective-permute-start.22
  84.2 2.4 %unpack.4 = (bf16[768,768]{1,0:T(8,128)(2,1)S(1)}, bf16[768,3072]{1,0:T(8,128)(2,1)S(1)}) custom-call(bf16[384,1920]{1,0:T(8,128)(2,1)S(1)} %constant_dynamic-update-slice_fusion.refs_0_, bf16[384,1920]{1,0:T(8,128)(2,1)S(1)} %collective-permute-done.17.refs_1_, bf16[384,1920]{1,0:T(8,128)(2,1)S(1)} %collective-permute-done.18.refs_2_, ...), custom_call_target="tpu_custom_call" | custom-call | flops 5000000000 | bytes 1000000 | tf_op jit(solution)/shard_map/unpack/pallas_call | solution.py:148
  86.6 8.0 %middle.1 = (f32[512,768]{1,0:T(8,128)S(1)}, f32[512,1]{1,0:T(8,128)S(1)}, bf16[512,768]{1,0:T(8,128)(2,1)S(1)}, bf16[512,3072]{1,0:T(8,128)(2,1)S(1)}, bf16[512,3072]{1,0:T(8,128)(2,1)S(1)}) custom-call(bf16[768,768]{1,0:T(8,128)(2,1)S(1)} %get-tuple-element.234.w_out.refs_0_, bf16[768,3072]{1,0:T(8,128)(2,1)S(1)} %get-tuple-element.235.w_up.refs_1_, ...), custom_call_target="tpu_custom_call" | custom-call | flops 12000000000 | bytes 1000000 | tf_op jit(solution)/shard_map/middle/pallas_call | solution.py:148
  94.6 3.0 %collective-permute-done.20.refs_1_ = bf16[384,1536]{1,0:T(8,128)(2,1)S(1)} collective-permute-done((bf16[384,1536]{1,0:T(8,128)(2,1)S(1)}, bf16[384,1536]{1,0:T(8,128)(2,1)S(1)}, u32[]{:S(2)}, u32[]{:S(2)}) %collective-permute-start.20) | collective-permute-done | bytes 1179680 | tf_op jit(solution)/shard_map/ppermute | solution.py:39
  97.6 2.8 %collective-permute-done.23.refs_3_ = bf16[384,1536]{1,0:T(8,128)(2,1)S(1)} collective-permute-done((bf16[384,1536]{1,0:T(8,128)(2,1)S(1)}, bf16[384,1536]{1,0:T(8,128)(2,1)S(1)}, u32[]{:S(2)}, u32[]{:S(2)}) %collective-permute-start.23) | collective-permute-done | bytes 1179680 | tf_op jit(solution)/shard_map/ppermute | solution.py:39
  100.5 1.7 unpack.5.refs_0_.weight_ref
  102.1 8.1 %turn.1 = (bf16[4,128,768]{2,1,0:T(8,128)(2,1)S(1)}, f32[512,768]{1,0:T(8,128)S(1)}, bf16[512,768]{1,0:T(8,128)(2,1)S(1)}, f32[8,768]{1,0:T(8,128)S(1)}, bf16[76...) custom-call(bf16[768,3072]{1,0:T(8,128)(2,1)S(1)} %unpack.5.refs_0_.weight_ref, ...), custom_call_target="tpu_custom_call" | custom-call | flops 14000000000 | bytes 1000000 | tf_op jit(solution)/shard_map/turn/pallas_call | solution.py:148
  110.9 3.8 %hidden_back.1 = (bf16[512,3072]{1,0:T(8,128)(2,1)S(1)}, f32[1,3072]{1,0:T(1,128)S(1)}) custom-call(bf16[768,3072]{1,0:T(8,128)(2,1)S(1)} %unpack.5.refs_0_.weight_ref, bf16[512,768]{1,0:T(8,128)(2,1)S(1)} %get-tuple-element.250.gzb_ref, bf16[512,3072]{1,0:T(8,128)(2,1)S(1)} %get-tuple-element.251.slope_ref), custom_call_target="tpu_custom_call" | custom-call | flops 12000000000 | bytes 1000000 | tf_op jit(solution)/shard_map/hidden_back/pallas_call | solution.py:148
  115.8 1.6 collective-permute-start.27
  117.8 10.2 %first_back.1 = (f32[512,768]{1,0:T(8,128)S(1)}, bf16[512,768]{1,0:T(8,128)(2,1)S(1)}, f32[8,768]{1,0:T(8,128)S(1)}, bf16[768,1920]{1,0:T(8,128)(2,1)S(1)}, bf16[768,1920]{1,0:T(8,128)(2,1)S(1)}) custom-call(bf16[768,768]{1,0:T(8,128)(2,1)S(1)} %get-tuple-element.234.w_out.refs_0_, bf16[768,3072]{1,0:T(8,128)(2,1)S(1)} %get-tuple-element.235.w_up.refs_1_, ...), custom_call_target="tpu_custom_call" | custom-call | flops 20000000000 | bytes 1000000 | tf_op jit(solution)/shard_map/first_back/pallas_call | solution.py:148
  128.0 5.6 %collective-permute-done.26.refs_2_ = bf16[384,1536]{1,0:T(8,128)(2,1)S(1)} collective-permute-done((bf16[384,1536]{1,0:T(8,128)(2,1)S(1)}, bf16[384,1536]{1,0:T(8,128)(2,1)S(1)}, u32[]{:S(2)}, u32[]{:S(2)}) %collective-permute-start.26) | collective-permute-done | bytes 1179680 | tf_op jit(solution)/shard_map/ppermute | solution.py:39
  135.0 5.3 %attend_back.2 = (bf16[512,384]{1,0:T(8,128)(2,1)S(1)}, bf16[512,384]{1,0:T(8,128)(2,1)S(1)}, bf16[512,384]{1,0:T(8,128)(2,1)S(1)}) custom-call(bf16[512,2304]{1,0:T(8,128)(2,1)S(1)} %get-tuple-element.227.refs_0_, bf16[6,512,512]{2,1,0:T(8,128)(2,1)S(1)} %get-tuple-element.263.refs_1_, bf16[512,768]{1,0:T(8,128)(2,1)S(1)} %get-tuple-element.281.refs_2_), custom_call_target="tpu_custom_call" | custom-call | flops 1000000000 | bytes 1000000 | tf_op jit(solution)/shard_map/attend_back/pallas_call | solution.py:148
  140.6 1.5 collective-permute-start.31
  142.2 5.6 %attend_back.3 = (bf16[512,384]{1,0:T(8,128)(2,1)S(1)}, bf16[512,384]{1,0:T(8,128)(2,1)S(1)}, bf16[512,384]{1,0:T(8,128)(2,1)S(1)}) custom-call(bf16[512,2304]{1,0:T(8,128)(2,1)S(1)} %get-tuple-element.227.refs_0_, bf16[6,512,512]{2,1,0:T(8,128)(2,1)S(1)} %get-tuple-element.277.refs_1_, bf16[512,768]{1,0:T(8,128)(2,1)S(1)} %get-tuple-element.281.refs_2_), custom_call_target="tpu_custom_call" | custom-call | flops 1000000000 | bytes 1000000 | tf_op jit(solution)/shard_map/attend_back/pallas_call | solution.py:148
  147.9 2.7 %input_back.1.own_ref = bf16[4,128,768]{2,1,0:T(8,128)(2,1)S(1)} custom-call(bf16[768,2304]{1,0:T(8,128)(2,1)S(1)} %unpack.3.refs_0_, f32[512,768]{1,0:T(8,128)S(1)} %get-tuple-element.262.refs_1_, bf16[512,384]{1,0:T(8,128)(2,1)S(1)} %get-tuple-element.294.refs_2_.refs_4_, bf16[512,384]{1,0:T(8,128)(2,1)S(1)} %get-tuple-element.275.refs_3_.refs_5_, ...), custom_call_target="tpu_custom_call" | custom-call | flops 2000000000 | bytes 1000000 | tf_op jit(solution)/shard_map/input_back/pallas_call | solution.py:148
  150.6 2.5 %collective-permute-done.30.y_ref = bf16[4,128,768]{2,1,0:T(8,128)(2,1)S(1)} collective-permute-done((bf16[4,128,768]{2,1,0:T(8,128)(2,1)S(1)}, bf16[4,128,768]{2,1,0:T(8,128)(2,1)S(1)}, u32[]{:S(2)}, u32[]{:S(2)}) %collective-permute-start.30) | collective-permute-done | bytes 786464 | tf_op jit(solution)/shard_map/ppermute | solution.py:39
  153.1 1.9 collective-permute-start.33
  155.1 2.9 %last.1 = (bf16[776,1152]{1,0:T(8,128)(2,1)S(1)}, bf16[776,1152]{1,0:T(8,128)(2,1)S(1)}) custom-call(bf16[512,768]{1,0:T(8,128)(2,1)S(1)} %get-tuple-element.237.x_ref.refs_0_, f32[8,768]{1,0:T(8,128)S(1)} %get-tuple-element.291.refs_1_, f32[8,768]{1,0:T(8,128)S(1)} %get-tuple-element.292.refs_2_, f32[1,3072]{1,0:T(1,128)S(1)} %get-tuple-element.293.refs_3_, ...), custom_call_target="tpu_custom_call" | custom-call | flops 10000000000 | bytes 1000000 | tf_op jit(solution)/shard_map/last/pallas_call | solution.py:148
  158.0 2.0 collective-permute-done.31.refs_2_
  160.3 1.4 collective-permute-done.32.refs_1_
  162.0 1.6 collective-permute-start.34
  164.0 1.7 collective-permute-start.36
  165.8 12.6 %collective-permute-done.34.refs_2_ = bf16[392,1152]{1,0:T(8,128)(2,1)S(1)} collective-permute-done((bf16[392,1152]{1,0:T(8,128)(2,1)S(1)}, bf16[392,1152]{1,0:T(8,128)(2,1)S(1)}, u32[]{:S(2)}, u32[]{:S(2)}) %collective-permute-start.34) | collective-permute-done | bytes 903200 | tf_op jit(solution)/shard_map/ppermute | solution.py:39
  179.2 1.5 collective-permute-start.40
  181.0 1.8 collective-permute-start.41
  182.8 1.1 collective-permute-start.39
  183.9 5.7 %collective-permute-done.35.refs_3_ = bf16[200,1152]{1,0:T(8,128)(2,1)S(1)} collective-permute-done((bf16[200,1152]{1,0:T(8,128)(2,1)S(1)}, bf16[200,1152]{1,0:T(8,128)(2,1)S(1)}, u32[]{:S(2)}, u32[]{:S(2)}) %collective-permute-start.35) | collective-permute-done | bytes 460832 | tf_op jit(solution)/shard_map/ppermute | solution.py:39
  189.8 1.1 collective-permute-start.38
  191.0 1.5 collective-permute-start.43
  192.6 3.0 %collective-permute-start.44 = (bf16[48,1920]{1,0:T(8,128)(2,1)S(1)}, bf16[48,1920]{1,0:T(8,128)(2,1)S(1)}, u32[]{:S(2)}, u32[]{:S(2)}) collective-permute-start(bf16[48,1920]{1,0:T(8,128)(2,1)S(1)} %add.64), channel_id=1, source_target_pairs={{0,16},{1,17},{2,6},{3,7},{4,20},{5,21},{6,2},{7,3},{8,24},{9,25},... | collective-permute-start | bytes 552968 | tf_op jit(solution)/shard_map/ppermute | solution.py:39
  195.6 1.3 deliver.2
  197.3 1.0 collective-permute-start.42
  198.3 7.3 %collective-permute-done.44.refs_5_ = bf16[48,1920]{1,0:T(8,128)(2,1)S(1)} collective-permute-done((bf16[48,1920]{1,0:T(8,128)(2,1)S(1)}, bf16[48,1920]{1,0:T(8,128)(2,1)S(1)}, u32[]{:S(2)}, u32[]{:S(2)}) %collective-permute-start.44) | collective-permute-done | bytes 184352 | tf_op jit(solution)/shard_map/ppermute | solution.py:39
  206.5 3.1 %collective-permute-start.45 = (bf16[96,1536]{1,0:T(8,128)(2,1)S(1)}, bf16[96,1536]{1,0:T(8,128)(2,1)S(1)}, u32[]{:S(2)}, u32[]{:S(2)}) collective-permute-start(bf16[96,1536]{1,0:T(8,128)(2,1)S(1)} %constant_dynamic-update-slice_fusion.4.refs_0_), channel_id=1, source_target_pairs={{0,2},{1,3},{2,0},{3,1},{4,6},{5,7},{6,4},{7,5},{8,10},{9,11},{10,... | collective-permute-start | bytes 884744 | tf_op jit(solution)/shard_map/ppermute | solution.py:39
  209.7 3.4 %collective-permute-start.50 = (bf16[48,1152]{1,0:T(8,128)(2,1)S(1)}, bf16[48,1152]{1,0:T(8,128)(2,1)S(1)}, u32[]{:S(2)}, u32[]{:S(2)}) collective-permute-start(bf16[48,1152]{1,0:T(8,128)(2,1)S(1)} %add.67.refs_0_), channel_id=1, source_target_pairs={{0,6},{1,7},{2,4},{3,5},{4,2},{5,3},{6,0},{7,1},{8,14},{9,15},{10,... | collective-permute-start | bytes 331784 | tf_op jit(solution)/shard_map/ppermute | solution.py:39
  213.8 1.5 collective-permute-start.48
  215.3 1.2 settle.3
  216.8 1.3 deliver.3
  218.0 1.6 collective-permute-done.48.refs_1_
  219.6 1.0 settle.4
  220.7 1.2 settle.5
  (144 shorter events, 18.4 us)
Async XLA Ops:
  0.6 8.4 %copy-start = (bf16[4,2,128,768]{3,2,1,0:T(8,128)(2,1)S(1)}, bf16[4,2,128,768]{3,2,1,0:T(8,128)(2,1)}, u32[]{:S(2)}) copy-start(bf16[4,2,128,768]{3,2,1,0:T(8,128)(2,1)} %param.15) | copy-start | bytes 4718596
  1.7 9.7 %collective-permute-start = (bf16[48,1152]{1,0:T(8,128)(2,1)S(1)}, bf16[48,1152]{1,0:T(8,128)(2,1)S(1)}, u32[]{:S(2)}, u32[]{:S(2)}) collective-permute-start(bf16[48,1152]{1,0:T(8,128)(2,1)S(1)} %bitcast.15), channel_id=1, source_target_pairs={{0,16},{1,17},{2,10},{3,11},{4,20},{5,21},{6,14},{7,15},{8,24},{9,... | collective-permute-start | bytes 331784 | tf_op jit(solution)/shard_map/ppermute | solution.py:39
  6.8 5.2 %collective-permute-start.1 = (bf16[48,1536]{1,0:T(8,128)(2,1)S(1)}, bf16[48,1536]{1,0:T(8,128)(2,1)S(1)}, u32[]{:S(2)}, u32[]{:S(2)}) collective-permute-start(bf16[48,1536]{1,0:T(8,128)(2,1)S(1)} %dynamic-slice_bitcast_fusion.2), channel_id=1, source_target_pairs={{0,4},{1,5},{2,3},{3,2},{4,0},{5,1},{6,7},{7,6},{8,12},{9,13},{10,... | collective-permute-start | bytes 442376 | tf_op jit(solution)/shard_map/ppermute | solution.py:39
  12.0 14.1 %collective-permute-start.3 = (bf16[96,1536]{1,0:T(8,128)(2,1)S(1)}, bf16[96,1536]{1,0:T(8,128)(2,1)S(1)}, u32[]{:S(2)}, u32[]{:S(2)}) collective-permute-start(bf16[96,1536]{1,0:T(8,128)(2,1)S(1)} %pad_maximum_fusion.12), channel_id=1, source_target_pairs={{0,16},{1,17},{2,6},{3,7},{4,20},{5,21},{6,2},{7,3},{8,24},{9,25},... | collective-permute-start | bytes 884744 | tf_op jit(solution)/shard_map/ppermute | solution.py:39
  12.1 14.0 %collective-permute-start.2 = (bf16[96,1152]{1,0:T(8,128)(2,1)S(1)}, bf16[96,1152]{1,0:T(8,128)(2,1)S(1)}, u32[]{:S(2)}, u32[]{:S(2)}) collective-permute-start(bf16[96,1152]{1,0:T(8,128)(2,1)S(1)} %pad_maximum_fusion.13), channel_id=1, source_target_pairs={{0,8},{1,9},{2,18},{3,19},{4,12},{5,13},{6,22},{7,23},{8,0},{9,1},... | collective-permute-start | bytes 663560 | tf_op jit(solution)/shard_map/ppermute | solution.py:39
  14.5 1.9 collective-permute-start.4
  14.5 8.0 %collective-permute-start.5 = (bf16[1,136,768]{2,1,0:T(8,128)(2,1)S(1)}, bf16[1,136,768]{2,1,0:T(8,128)(2,1)S(1)}, u32[]{:S(2)}, u32[]{:S(2)}) collective-permute-start(bf16[1,136,768]{2,1,0:T(8,128)(2,1)S(1)} %get-tuple-element.187), channel_id=1, source_target_pairs={{0,4},{1,5},{2,6},{3,7},{4,0},{5,1},{6,2},{7,3},{8,12},{9,13},{10,... | collective-permute-start | bytes 626696 | tf_op jit(solution)/shard_map/ppermute | solution.py:39
  15.9 10.2 %collective-permute-start.6 = (bf16[1,136,768]{2,1,0:T(8,128)(2,1)S(1)}, bf16[1,136,768]{2,1,0:T(8,128)(2,1)S(1)}, u32[]{:S(2)}, u32[]{:S(2)}) collective-permute-start(bf16[1,136,768]{2,1,0:T(8,128)(2,1)S(1)} %get-tuple-element.188), channel_id=1, source_target_pairs={{0,6},{1,7},{2,4},{3,5},{4,2},{5,3},{6,0},{7,1},{8,14},{9,15},{10,... | collective-permute-start | bytes 626696 | tf_op jit(solution)/shard_map/ppermute | solution.py:39
  26.2 4.8 %copy-start.4 = (f32[1536]{0:T(1024)S(1)}, f32[1536]{0:T(1024)}, u32[]{:S(2)}) copy-start(f32[1536]{0:T(1024)} %up_ref) | copy-start | bytes 18436
  26.2 4.8 %copy-start.5 = (f32[768]{0:T(1024)S(1)}, f32[768]{0:T(1024)}, u32[]{:S(2)}) copy-start(f32[768]{0:T(1024)} %refs_0_.1) | copy-start | bytes 9220
  26.2 4.8 %copy-start.6 = (f32[768]{0:T(1024)S(1)}, f32[768]{0:T(1024)}, u32[]{:S(2)}) copy-start(f32[768]{0:T(1024)} %refs_1_.1) | copy-start | bytes 9220
  26.2 4.8 %copy-start.7 = (f32[768]{0:T(1024)S(1)}, f32[768]{0:T(1024)}, u32[]{:S(2)}) copy-start(f32[768]{0:T(1024)} %refs_2_.1) | copy-start | bytes 9220
  26.2 4.8 %copy-start.8 = (f32[768]{0:T(1024)S(1)}, f32[768]{0:T(1024)}, u32[]{:S(2)}) copy-start(f32[768]{0:T(1024)} %refs_3_.1) | copy-start | bytes 9220
  26.2 4.8 %copy-start.9 = (f32[768]{0:T(1024)S(1)}, f32[768]{0:T(1024)}, u32[]{:S(2)}) copy-start(f32[768]{0:T(1024)} %refs_4_.1) | copy-start | bytes 9220
  26.2 4.7 %copy-start.10 = (f32[768]{0:T(1024)S(1)}, f32[768]{0:T(1024)}, u32[]{:S(2)}) copy-start(f32[768]{0:T(1024)} %refs_5_.1) | copy-start | bytes 9220
  26.3 4.7 %copy-start.11 = (f32[2,384]{1,0:T(2,128)S(1)}, f32[2,384]{1,0:T(2,128)}, u32[]{:S(2)}) copy-start(f32[2,384]{1,0:T(2,128)} %qv_ref.1) | copy-start | bytes 9220
  26.3 9.5 %collective-permute-start.7 = (bf16[192,1152]{1,0:T(8,128)(2,1)S(1)}, bf16[192,1152]{1,0:T(8,128)(2,1)S(1)}, u32[]{:S(2)}, u32[]{:S(2)}) collective-permute-start(bf16[192,1152]{1,0:T(8,128)(2,1)S(1)} %pad_maximum_fusion.5), channel_id=1, source_target_pairs={{0,1},{1,0},{2,6},{3,7},{4,5},{5,4},{6,2},{7,3},{8,9},{9,8},{10,14... | collective-permute-start | bytes 1327112 | tf_op jit(solution)/shard_map/ppermute | solution.py:39
  28.0 7.9 %collective-permute-start.8 = (bf16[48,1920]{1,0:T(8,128)(2,1)S(1)}, bf16[48,1920]{1,0:T(8,128)(2,1)S(1)}, u32[]{:S(2)}, u32[]{:S(2)}) collective-permute-start(bf16[48,1920]{1,0:T(8,128)(2,1)S(1)} %fusion.2), channel_id=1, source_target_pairs={{0,16},{1,17},{2,10},{3,11},{4,20},{5,21},{6,14},{7,15},{8,24},{9,... | collective-permute-start | bytes 552968 | tf_op jit(solution)/shard_map/ppermute | solution.py:39
  36.0 12.3 %collective-permute-start.13 = (bf16[384,1152]{1,0:T(8,128)(2,1)S(1)}, bf16[384,1152]{1,0:T(8,128)(2,1)S(1)}, u32[]{:S(2)}, u32[]{:S(2)}) collective-permute-start(bf16[384,1152]{1,0:T(8,128)(2,1)S(1)} %pad_maximum_fusion.refs_0_), channel_id=1, source_target_pairs={{0,2},{1,3},{2,0},{3,1},{4,6},{5,7},{6,4},{7,5},{8,10},{9,11},{10,... | collective-permute-start | bytes 2654216 | tf_op jit(solution)/shard_map/ppermute | solution.py:39
  36.0 13.1 %collective-permute-start.9 = (bf16[384,1152]{1,0:T(8,128)(2,1)S(1)}, bf16[384,1152]{1,0:T(8,128)(2,1)S(1)}, u32[]{:S(2)}, u32[]{:S(2)}) collective-permute-start(bf16[384,1152]{1,0:T(8,128)(2,1)S(1)} %pad_maximum_fusion.refs_0_), channel_id=1, source_target_pairs={{0,4},{1,5},{2,3},{3,2},{4,0},{5,1},{6,7},{7,6},{8,12},{9,13},{10,... | collective-permute-start | bytes 2654216 | tf_op jit(solution)/shard_map/ppermute | solution.py:39
  37.9 10.4 %collective-permute-start.11 = (bf16[2,128,768]{2,1,0:T(8,128)(2,1)S(1)}, bf16[2,128,768]{2,1,0:T(8,128)(2,1)S(1)}, u32[]{:S(2)}, u32[]{:S(2)}) collective-permute-start(bf16[2,128,768]{2,1,0:T(8,128)(2,1)S(1)} %pad_maximum_fusion.7), channel_id=1, source_target_pairs={{0,2},{1,3},{2,0},{3,1},{4,6},{5,7},{6,4},{7,5},{8,10},{9,11},{10,... | collective-permute-start | bytes 1179656 | tf_op jit(solution)/shard_map/ppermute | solution.py:39
  37.9 10.3 %collective-permute-start.10 = (bf16[96,1920]{1,0:T(8,128)(2,1)S(1)}, bf16[96,1920]{1,0:T(8,128)(2,1)S(1)}, u32[]{:S(2)}, u32[]{:S(2)}) collective-permute-start(bf16[96,1920]{1,0:T(8,128)(2,1)S(1)} %pad_maximum_fusion.11), channel_id=1, source_target_pairs={{0,8},{1,9},{2,18},{3,19},{4,12},{5,13},{6,22},{7,23},{8,0},{9,1},... | collective-permute-start | bytes 1105928 | tf_op jit(solution)/shard_map/ppermute | solution.py:39
  38.2 3.8 %collective-permute-start.12 = (f32[1,2304]{1,0:T(1,128)S(1)}, f32[1,2304]{1,0:T(1,128)S(1)}, u32[]{:S(2)}, u32[]{:S(2)}) collective-permute-start(f32[1,2304]{1,0:T(1,128)S(1)} %get-tuple-element.205), channel_id=1, source_target_pairs={{0,1},{1,0},{2,3},{3,2},{4,5},{5,4},{6,7},{7,6},{8,9},{9,8},{10,11... | collective-permute-start | bytes 27656 | tf_op jit(solution)/shard_map/ppermute | solution.py:39
  48.2 14.9 %copy-start.2 = (bf16[2,128,768]{2,1,0:T(8,128)(2,1)}, bf16[2,128,768]{2,1,0:T(8,128)(2,1)S(1)}, u32[]{:S(2)}) copy-start(bf16[2,128,768]{2,1,0:T(8,128)(2,1)S(1)} %collective-permute-done.11.refs_4_) | copy-start | bytes 1179652
  49.2 2.6 %collective-permute-start.14 = (bf16[384,1152]{1,0:T(8,128)(2,1)S(1)}, bf16[384,1152]{1,0:T(8,128)(2,1)S(1)}, u32[]{:S(2)}, u32[]{:S(2)}) collective-permute-start(bf16[384,1152]{1,0:T(8,128)(2,1)S(1)} %collective-permute-done.9.refs_1_), channel_id=1, source_target_pairs={{0,2},{1,3},{2,0},{3,1},{4,6},{5,7},{6,4},{7,5},{8,10},{9,11},{10,... | collective-permute-start | bytes 2654216 | tf_op jit(solution)/shard_map/ppermute | solution.py:39
  49.8 20.0 %collective-permute-start.16 = (bf16[192,1536]{1,0:T(8,128)(2,1)S(1)}, bf16[192,1536]{1,0:T(8,128)(2,1)S(1)}, u32[]{:S(2)}, u32[]{:S(2)}) collective-permute-start(bf16[192,1536]{1,0:T(8,128)(2,1)S(1)} %pad_maximum_fusion.4), channel_id=1, source_target_pairs={{0,8},{1,9},{2,18},{3,19},{4,12},{5,13},{6,22},{7,23},{8,0},{9,1},... | collective-permute-start | bytes 1769480 | tf_op jit(solution)/shard_map/ppermute | solution.py:39
  49.8 11.5 %collective-permute-start.15 = (bf16[192,1920]{1,0:T(8,128)(2,1)S(1)}, bf16[192,1920]{1,0:T(8,128)(2,1)S(1)}, u32[]{:S(2)}, u32[]{:S(2)}) collective-permute-start(bf16[192,1920]{1,0:T(8,128)(2,1)S(1)} %pad_maximum_fusion.3), channel_id=1, source_target_pairs={{0,1},{1,0},{2,6},{3,7},{4,5},{5,4},{6,2},{7,3},{8,9},{9,8},{10,14... | collective-permute-start | bytes 2211848 | tf_op jit(solution)/shard_map/ppermute | solution.py:39
  61.5 19.4 %collective-permute-start.17 = (bf16[384,1920]{1,0:T(8,128)(2,1)S(1)}, bf16[384,1920]{1,0:T(8,128)(2,1)S(1)}, u32[]{:S(2)}, u32[]{:S(2)}) collective-permute-start(bf16[384,1920]{1,0:T(8,128)(2,1)S(1)} %constant_dynamic-update-slice_fusion.refs_0_), channel_id=1, source_target_pairs={{0,4},{1,5},{2,3},{3,2},{4,0},{5,1},{6,7},{7,6},{8,12},{9,13},{10,... | collective-permute-start | bytes 4423688 | tf_op jit(solution)/shard_map/ppermute | solution.py:39
  63.1 7.1 %slice-start = ((bf16[2,128,768]{2,1,0:T(8,128)(2,1)}), bf16[1,128,768]{2,1,0:T(8,128)(2,1)S(1)}, s32[]{:S(2)}) async-start(bf16[2,128,768]{2,1,0:T(8,128)(2,1)} %copy-done.2), calls=%async_computation | async-start | bytes 393216 | tf_op jit(solution)/shard_map/slice | solution.py:924
  69.7 11.2 %collective-permute-start.18 = (bf16[384,1920]{1,0:T(8,128)(2,1)S(1)}, bf16[384,1920]{1,0:T(8,128)(2,1)S(1)}, u32[]{:S(2)}, u32[]{:S(2)}) collective-permute-start(bf16[384,1920]{1,0:T(8,128)(2,1)S(1)} %constant_dynamic-update-slice_fusion.refs_0_), channel_id=1, source_target_pairs={{0,2},{1,3},{2,0},{3,1},{4,6},{5,7},{6,4},{7,5},{8,10},{9,11},{10,... | collective-permute-start | bytes 4423688 | tf_op jit(solution)/shard_map/ppermute | solution.py:39
  80.9 3.3 %collective-permute-start.19 = (bf16[384,1920]{1,0:T(8,128)(2,1)S(1)}, bf16[384,1920]{1,0:T(8,128)(2,1)S(1)}, u32[]{:S(2)}, u32[]{:S(2)}) collective-permute-start(bf16[384,1920]{1,0:T(8,128)(2,1)S(1)} %collective-permute-done.17.refs_1_), channel_id=1, source_target_pairs={{0,2},{1,3},{2,0},{3,1},{4,6},{5,7},{6,4},{7,5},{8,10},{9,11},{10,... | collective-permute-start | bytes 4423688 | tf_op jit(solution)/shard_map/ppermute | solution.py:39
  80.9 13.7 %collective-permute-start.21 = (bf16[384,1536]{1,0:T(8,128)(2,1)S(1)}, bf16[384,1536]{1,0:T(8,128)(2,1)S(1)}, u32[]{:S(2)}, u32[]{:S(2)}) collective-permute-start(bf16[384,1536]{1,0:T(8,128)(2,1)S(1)} %constant_dynamic-update-slice_fusion.2.refs_0_), channel_id=1, source_target_pairs={{0,2},{1,3},{2,0},{3,1},{4,6},{5,7},{6,4},{7,5},{8,10},{9,11},{10,... | collective-permute-start | bytes 3538952 | tf_op jit(solution)/shard_map/ppermute | solution.py:39
  81.4 16.2 %collective-permute-start.20 = (bf16[384,1536]{1,0:T(8,128)(2,1)S(1)}, bf16[384,1536]{1,0:T(8,128)(2,1)S(1)}, u32[]{:S(2)}, u32[]{:S(2)}) collective-permute-start(bf16[384,1536]{1,0:T(8,128)(2,1)S(1)} %constant_dynamic-update-slice_fusion.2.refs_0_), channel_id=1, source_target_pairs={{0,1},{1,0},{2,10},{3,11},{4,5},{5,4},{6,14},{7,15},{8,9},{9,8},{1... | collective-permute-start | bytes 3538952 | tf_op jit(solution)/shard_map/ppermute | solution.py:39
  81.9 15.7 %collective-permute-start.22 = (bf16[2,128,768]{2,1,0:T(8,128)(2,1)S(1)}, bf16[2,128,768]{2,1,0:T(8,128)(2,1)S(1)}, u32[]{:S(2)}, u32[]{:S(2)}) collective-permute-start(bf16[2,128,768]{2,1,0:T(8,128)(2,1)S(1)} %pad_maximum_fusion.8), channel_id=1, source_target_pairs={{0,4},{1,5},{2,6},{3,7},{4,0},{5,1},{6,2},{7,3},{8,12},{9,13},{10,... | collective-permute-start | bytes 1179656 | tf_op jit(solution)/shard_map/ppermute | solution.py:39
  97.6 4.5 %copy-start.3 = (bf16[2,128,768]{2,1,0:T(8,128)(2,1)S(1)}, bf16[2,128,768]{2,1,0:T(8,128)(2,1)}, u32[]{:S(2)}) copy-start(bf16[2,128,768]{2,1,0:T(8,128)(2,1)} %copy-done.2) | copy-start | bytes 1179652
  97.6 2.8 %collective-permute-start.23 = (bf16[384,1536]{1,0:T(8,128)(2,1)S(1)}, bf16[384,1536]{1,0:T(8,128)(2,1)S(1)}, u32[]{:S(2)}, u32[]{:S(2)}) collective-permute-start(bf16[384,1536]{1,0:T(8,128)(2,1)S(1)} %collective-permute-done.20.refs_1_), channel_id=1, source_target_pairs={{0,2},{1,3},{2,0},{3,1},{4,6},{5,7},{6,4},{7,5},{8,10},{9,11},{10,... | collective-permute-start | bytes 3538952 | tf_op jit(solution)/shard_map/ppermute | solution.py:39
  110.2 5.2 %collective-permute-start.24 = (bf16[768,1536]{1,0:T(8,128)(2,1)S(1)}, bf16[768,1536]{1,0:T(8,128)(2,1)S(1)}, u32[]{:S(2)}, u32[]{:S(2)}) collective-permute-start(bf16[768,1536]{1,0:T(8,128)(2,1)S(1)} %get-tuple-element.253), channel_id=1, source_target_pairs={{0,2},{1,3},{2,0},{3,1},{4,6},{5,7},{6,4},{7,5},{8,10},{9,11},{10,... | collective-permute-start | bytes 7077896 | tf_op jit(solution)/shard_map/ppermute | solution.py:39
  110.5 4.9 %collective-permute-start.25 = (bf16[2,128,768]{2,1,0:T(8,128)(2,1)S(1)}, bf16[2,128,768]{2,1,0:T(8,128)(2,1)S(1)}, u32[]{:S(2)}, u32[]{:S(2)}) collective-permute-start(bf16[2,128,768]{2,1,0:T(8,128)(2,1)S(1)} %slice.34), channel_id=1, source_target_pairs={{0,2},{1,3},{2,0},{3,1},{4,6},{5,7},{6,4},{7,5},{8,10},{9,11},{10,... | collective-permute-start | bytes 1179656 | tf_op jit(solution)/shard_map/ppermute | solution.py:39
  115.8 12.2 %collective-permute-start.27 = (bf16[2,128,768]{2,1,0:T(8,128)(2,1)S(1)}, bf16[2,128,768]{2,1,0:T(8,128)(2,1)S(1)}, u32[]{:S(2)}, u32[]{:S(2)}) collective-permute-start(bf16[2,128,768]{2,1,0:T(8,128)(2,1)S(1)} %pad_maximum_fusion.9), channel_id=1, source_target_pairs={{0,4},{1,5},{2,6},{3,7},{4,0},{5,1},{6,2},{7,3},{8,12},{9,13},{10,... | collective-permute-start | bytes 1179656 | tf_op jit(solution)/shard_map/ppermute | solution.py:39
  117.4 16.2 %collective-permute-start.26 = (bf16[384,1536]{1,0:T(8,128)(2,1)S(1)}, bf16[384,1536]{1,0:T(8,128)(2,1)S(1)}, u32[]{:S(2)}, u32[]{:S(2)}) collective-permute-start(bf16[384,1536]{1,0:T(8,128)(2,1)S(1)} %add.53), channel_id=1, source_target_pairs={{0,1},{1,0},{2,10},{3,11},{4,5},{5,4},{6,14},{7,15},{8,9},{9,8},{1... | collective-permute-start | bytes 3538952 | tf_op jit(solution)/shard_map/ppermute | solution.py:39
  133.6 6.7 %collective-permute-start.28 = (bf16[768,1920]{1,0:T(8,128)(2,1)S(1)}, bf16[768,1920]{1,0:T(8,128)(2,1)S(1)}, u32[]{:S(2)}, u32[]{:S(2)}) collective-permute-start(bf16[768,1920]{1,0:T(8,128)(2,1)S(1)} %get-tuple-element.273), channel_id=1, source_target_pairs={{0,2},{1,3},{2,0},{3,1},{4,6},{5,7},{6,4},{7,5},{8,10},{9,11},{10,... | collective-permute-start | bytes 8847368 | tf_op jit(solution)/shard_map/ppermute | solution.py:39
  133.9 13.9 %collective-permute-start.29 = (bf16[192,1536]{1,0:T(8,128)(2,1)S(1)}, bf16[192,1536]{1,0:T(8,128)(2,1)S(1)}, u32[]{:S(2)}, u32[]{:S(2)}) collective-permute-start(bf16[192,1536]{1,0:T(8,128)(2,1)S(1)} %add.54), channel_id=1, source_target_pairs={{0,4},{1,5},{2,18},{3,19},{4,0},{5,1},{6,22},{7,23},{8,12},{9,13},... | collective-permute-start | bytes 1769480 | tf_op jit(solution)/shard_map/ppermute | solution.py:39
  134.4 18.7 %collective-permute-start.30 = (bf16[4,128,768]{2,1,0:T(8,128)(2,1)S(1)}, bf16[4,128,768]{2,1,0:T(8,128)(2,1)S(1)}, u32[]{:S(2)}, u32[]{:S(2)}) collective-permute-start(bf16[4,128,768]{2,1,0:T(8,128)(2,1)S(1)} %pad_maximum_fusion.1), channel_id=1, source_target_pairs={{0,1},{1,0},{2,3},{3,2},{4,5},{5,4},{6,7},{7,6},{8,9},{9,8},{10,11... | collective-permute-start | bytes 2359304 | tf_op jit(solution)/shard_map/ppermute | solution.py:39
  140.6 19.4 %collective-permute-start.31 = (bf16[384,1920]{1,0:T(8,128)(2,1)S(1)}, bf16[384,1920]{1,0:T(8,128)(2,1)S(1)}, u32[]{:S(2)}, u32[]{:S(2)}) collective-permute-start(bf16[384,1920]{1,0:T(8,128)(2,1)S(1)} %add.55), channel_id=1, source_target_pairs={{0,4},{1,5},{2,10},{3,11},{4,0},{5,1},{6,14},{7,15},{8,12},{9,13},... | collective-permute-start | bytes 4423688 | tf_op jit(solution)/shard_map/ppermute | solution.py:39
  153.1 8.6 %collective-permute-start.33 = (bf16[2,128,768]{2,1,0:T(8,128)(2,1)S(1)}, bf16[2,128,768]{2,1,0:T(8,128)(2,1)S(1)}, u32[]{:S(2)}, u32[]{:S(2)}) collective-permute-start(bf16[2,128,768]{2,1,0:T(8,128)(2,1)S(1)} %slice.39), channel_id=1, source_target_pairs={{0,2},{1,3},{2,0},{3,1},{4,6},{5,7},{6,4},{7,5},{8,10},{9,11},{10,... | collective-permute-start | bytes 1179656 | tf_op jit(solution)/shard_map/ppermute | solution.py:39
  158.0 3.8 %collective-permute-start.32 = (bf16[776,1152]{1,0:T(8,128)(2,1)S(1)}, bf16[776,1152]{1,0:T(8,128)(2,1)S(1)}, u32[]{:S(2)}, u32[]{:S(2)}) collective-permute-start(bf16[776,1152]{1,0:T(8,128)(2,1)S(1)} %get-tuple-element.299), channel_id=1, source_target_pairs={{0,2},{1,3},{2,0},{3,1},{4,6},{5,7},{6,4},{7,5},{8,10},{9,11},{10,... | collective-permute-start | bytes 5363720 | tf_op jit(solution)/shard_map/ppermute | solution.py:39
  162.0 16.5 %collective-permute-start.34 = (bf16[392,1152]{1,0:T(8,128)(2,1)S(1)}, bf16[392,1152]{1,0:T(8,128)(2,1)S(1)}, u32[]{:S(2)}, u32[]{:S(2)}) collective-permute-start(bf16[392,1152]{1,0:T(8,128)(2,1)S(1)} %add.58.refs_3_), channel_id=1, source_target_pairs={{0,4},{1,5},{2,3},{3,2},{4,0},{5,1},{6,7},{7,6},{8,12},{9,13},{10,... | collective-permute-start | bytes 2709512 | tf_op jit(solution)/shard_map/ppermute | solution.py:39
  163.6 17.2 %collective-permute-start.37 = (bf16[192,1920]{1,0:T(8,128)(2,1)S(1)}, bf16[192,1920]{1,0:T(8,128)(2,1)S(1)}, u32[]{:S(2)}, u32[]{:S(2)}) collective-permute-start(bf16[192,1920]{1,0:T(8,128)(2,1)S(1)} %add.57), channel_id=1, source_target_pairs={{0,1},{1,0},{2,18},{3,19},{4,5},{5,4},{6,22},{7,23},{8,9},{9,8},{1... | collective-permute-start | bytes 2211848 | tf_op jit(solution)/shard_map/ppermute | solution.py:39
  164.0 15.2 %collective-permute-start.36 = (bf16[96,1536]{1,0:T(8,128)(2,1)S(1)}, bf16[96,1536]{1,0:T(8,128)(2,1)S(1)}, u32[]{:S(2)}, u32[]{:S(2)}) collective-permute-start(bf16[96,1536]{1,0:T(8,128)(2,1)S(1)} %add.56), channel_id=1, source_target_pairs={{0,8},{1,9},{2,6},{3,7},{4,12},{5,13},{6,2},{7,3},{8,0},{9,1},{10,... | collective-permute-start | bytes 884744 | tf_op jit(solution)/shard_map/ppermute | solution.py:39
  178.6 11.0 %collective-permute-start.35 = (bf16[200,1152]{1,0:T(8,128)(2,1)S(1)}, bf16[200,1152]{1,0:T(8,128)(2,1)S(1)}, u32[]{:S(2)}, u32[]{:S(2)}) collective-permute-start(bf16[200,1152]{1,0:T(8,128)(2,1)S(1)} %add.59.refs_4_), channel_id=1, source_target_pairs={{0,1},{1,0},{2,6},{3,7},{4,5},{5,4},{6,2},{7,3},{8,9},{9,8},{10,14... | collective-permute-start | bytes 1382408 | tf_op jit(solution)/shard_map/ppermute | solution.py:39
  179.2 11.6 %collective-permute-start.40 = (bf16[2,128,768]{2,1,0:T(8,128)(2,1)S(1)}, bf16[2,128,768]{2,1,0:T(8,128)(2,1)S(1)}, u32[]{:S(2)}, u32[]{:S(2)}) collective-permute-start(bf16[2,128,768]{2,1,0:T(8,128)(2,1)S(1)} %pad_maximum_fusion.10), channel_id=1, source_target_pairs={{0,4},{1,5},{2,6},{3,7},{4,0},{5,1},{6,2},{7,3},{8,12},{9,13},{10,... | collective-permute-start | bytes 1179656 | tf_op jit(solution)/shard_map/ppermute | solution.py:39
  181.0 11.5 %collective-permute-start.41 = (bf16[96,1920]{1,0:T(8,128)(2,1)S(1)}, bf16[96,1920]{1,0:T(8,128)(2,1)S(1)}, u32[]{:S(2)}, u32[]{:S(2)}) collective-permute-start(bf16[96,1920]{1,0:T(8,128)(2,1)S(1)} %add.61), channel_id=1, source_target_pairs={{0,8},{1,9},{2,3},{3,2},{4,12},{5,13},{6,7},{7,6},{8,0},{9,1},{10,... | collective-permute-start | bytes 1105928 | tf_op jit(solution)/shard_map/ppermute | solution.py:39
  182.8 8.1 %collective-permute-start.39 = (bf16[48,1536]{1,0:T(8,128)(2,1)S(1)}, bf16[48,1536]{1,0:T(8,128)(2,1)S(1)}, u32[]{:S(2)}, u32[]{:S(2)}) collective-permute-start(bf16[48,1536]{1,0:T(8,128)(2,1)S(1)} %add.60), channel_id=1, source_target_pairs={{0,16},{1,17},{2,3},{3,2},{4,20},{5,21},{6,7},{7,6},{8,24},{9,25},... | collective-permute-start | bytes 442376 | tf_op jit(solution)/shard_map/ppermute | solution.py:39
  189.8 7.4 %collective-permute-start.38 = (bf16[104,1152]{1,0:T(8,128)(2,1)S(1)}, bf16[104,1152]{1,0:T(8,128)(2,1)S(1)}, u32[]{:S(2)}, u32[]{:S(2)}) collective-permute-start(bf16[104,1152]{1,0:T(8,128)(2,1)S(1)} %add.62.refs_5_), channel_id=1, source_target_pairs={{0,8},{1,9},{2,18},{3,19},{4,12},{5,13},{6,22},{7,23},{8,0},{9,1},... | collective-permute-start | bytes 718856 | tf_op jit(solution)/shard_map/ppermute | solution.py:39
  191.0 7.3 %collective-permute-start.43 = (bf16[48,1536]{1,0:T(8,128)(2,1)S(1)}, bf16[48,1536]{1,0:T(8,128)(2,1)S(1)}, u32[]{:S(2)}, u32[]{:S(2)}) collective-permute-start(bf16[48,1536]{1,0:T(8,128)(2,1)S(1)} %add.63), channel_id=1, source_target_pairs={{0,4},{1,5},{2,6},{3,7},{4,0},{5,1},{6,2},{7,3},{8,12},{9,13},{10,... | collective-permute-start | bytes 442376 | tf_op jit(solution)/shard_map/ppermute | solution.py:39
  192.6 13.0 %collective-permute-start.44 = (bf16[48,1920]{1,0:T(8,128)(2,1)S(1)}, bf16[48,1920]{1,0:T(8,128)(2,1)S(1)}, u32[]{:S(2)}, u32[]{:S(2)}) collective-permute-start(bf16[48,1920]{1,0:T(8,128)(2,1)S(1)} %add.64), channel_id=1, source_target_pairs={{0,16},{1,17},{2,6},{3,7},{4,20},{5,21},{6,2},{7,3},{8,24},{9,25},... | collective-permute-start | bytes 552968 | tf_op jit(solution)/shard_map/ppermute | solution.py:39
  197.0 19.8 %collective-permute-start.47 = (bf16[4,128,768]{2,1,0:T(8,128)(2,1)S(1)}, bf16[4,128,768]{2,1,0:T(8,128)(2,1)S(1)}, u32[]{:S(2)}, u32[]{:S(2)}) collective-permute-start(bf16[4,128,768]{2,1,0:T(8,128)(2,1)S(1)} %pad_maximum_fusion.2), channel_id=1, source_target_pairs={{0,1},{1,0},{2,3},{3,2},{4,5},{5,4},{6,7},{7,6},{8,9},{9,8},{10,11... | collective-permute-start | bytes 2359304 | tf_op jit(solution)/shard_map/ppermute | solution.py:39
  197.3 12.3 %collective-permute-start.42 = (bf16[56,1152]{1,0:T(8,128)(2,1)S(1)}, bf16[56,1152]{1,0:T(8,128)(2,1)S(1)}, u32[]{:S(2)}, u32[]{:S(2)}) collective-permute-start(bf16[56,1152]{1,0:T(8,128)(2,1)S(1)} %add.65.refs_0_), channel_id=1, source_target_pairs={{0,16},{1,17},{2,10},{3,11},{4,20},{5,21},{6,14},{7,15},{8,24},{9,... | collective-permute-start | bytes 387080 | tf_op jit(solution)/shard_map/ppermute | solution.py:39
  205.8 10.7 %collective-permute-start.46 = (bf16[48,1920]{1,0:T(8,128)(2,1)S(1)}, bf16[48,1920]{1,0:T(8,128)(2,1)S(1)}, u32[]{:S(2)}, u32[]{:S(2)}) collective-permute-start(bf16[48,1920]{1,0:T(8,128)(2,1)S(1)} %add.66), channel_id=1, source_target_pairs={{0,4},{1,5},{2,6},{3,7},{4,0},{5,1},{6,2},{7,3},{8,12},{9,13},{10,... | collective-permute-start | bytes 552968 | tf_op jit(solution)/shard_map/ppermute | solution.py:39
  206.5 7.3 %collective-permute-start.45 = (bf16[96,1536]{1,0:T(8,128)(2,1)S(1)}, bf16[96,1536]{1,0:T(8,128)(2,1)S(1)}, u32[]{:S(2)}, u32[]{:S(2)}) collective-permute-start(bf16[96,1536]{1,0:T(8,128)(2,1)S(1)} %constant_dynamic-update-slice_fusion.4.refs_0_), channel_id=1, source_target_pairs={{0,2},{1,3},{2,0},{3,1},{4,6},{5,7},{6,4},{7,5},{8,10},{9,11},{10,... | collective-permute-start | bytes 884744 | tf_op jit(solution)/shard_map/ppermute | solution.py:39
  209.7 8.3 %collective-permute-start.50 = (bf16[48,1152]{1,0:T(8,128)(2,1)S(1)}, bf16[48,1152]{1,0:T(8,128)(2,1)S(1)}, u32[]{:S(2)}, u32[]{:S(2)}) collective-permute-start(bf16[48,1152]{1,0:T(8,128)(2,1)S(1)} %add.67.refs_0_), channel_id=1, source_target_pairs={{0,6},{1,7},{2,4},{3,5},{4,2},{5,3},{6,0},{7,1},{8,14},{9,15},{10,... | collective-permute-start | bytes 331784 | tf_op jit(solution)/shard_map/ppermute | solution.py:39
  213.1 4.9 %collective-permute-start.49 = (bf16[48,1152]{1,0:T(8,128)(2,1)S(1)}, bf16[48,1152]{1,0:T(8,128)(2,1)S(1)}, u32[]{:S(2)}, u32[]{:S(2)}) collective-permute-start(bf16[48,1152]{1,0:T(8,128)(2,1)S(1)} %add.67.refs_0_), channel_id=1, source_target_pairs={{0,2},{1,3},{2,0},{3,1},{4,6},{5,7},{6,4},{7,5},{8,10},{9,11},{10,... | collective-permute-start | bytes 331784 | tf_op jit(solution)/shard_map/ppermute | solution.py:39
  213.8 5.8 %collective-permute-start.48 = (bf16[48,1152]{1,0:T(8,128)(2,1)S(1)}, bf16[48,1152]{1,0:T(8,128)(2,1)S(1)}, u32[]{:S(2)}, u32[]{:S(2)}) collective-permute-start(bf16[48,1152]{1,0:T(8,128)(2,1)S(1)} %add.67.refs_0_), channel_id=1, source_target_pairs={{0,4},{1,5},{2,6},{3,7},{4,0},{5,1},{6,2},{7,3},{8,12},{9,13},{10,... | collective-permute-start | bytes 331784 | tf_op jit(solution)/shard_map/ppermute | solution.py:39
  216.5 4.2 %collective-permute-start.51 = (bf16[96,1920]{1,0:T(8,128)(2,1)S(1)}, bf16[96,1920]{1,0:T(8,128)(2,1)S(1)}, u32[]{:S(2)}, u32[]{:S(2)}) collective-permute-start(bf16[96,1920]{1,0:T(8,128)(2,1)S(1)} %constant_dynamic-update-slice_fusion.6.refs_0_), channel_id=1, source_target_pairs={{0,2},{1,3},{2,0},{3,1},{4,6},{5,7},{6,4},{7,5},{8,10},{9,11},{10,... | collective-permute-start | bytes 1105928 | tf_op jit(solution)/shard_map/ppermute | solution.py:39
  (3 other events, 4.1 us)

commit v9 on v8

--- a/solution.py
+++ b/solution.py
@@ -340,10 +340,10 @@
     for y in range(2):
         row = pl.ds(lax.axis_index("tp") ^ y, 1)
 
-        @tiles(half, 256)
+        @tiles(half, 512)
         def _(at):
-            here = pl.ds(pl.multiple_of(y * half + at, 256), 256)
-            bias = small_ref[row, pl.ds(pl.multiple_of(2 * narrow + at, 256), 256)]
+            here = pl.ds(pl.multiple_of(y * half + at, 512), 512)
+            bias = small_ref[row, pl.ds(pl.multiple_of(2 * narrow + at, 512), 512)]
             hidden = jnp.dot(first_ref[...], w_up[:, here], preferred_element_type=F32) + bias
             phi = 0.5 + 0.5 * lax.erf(hidden * 0.7071067811865476)
             act_ref[:, here] = (hidden * phi).astype(BF16)
@@ -368,7 +368,7 @@
         (VMEM,) * 5,
         [],
         12,
-        3,
+        6,
         (w_out, w_up, mixed0, mixed1, x, table, small),
     )
 

time: 223 us -> 223 us (level)
  no operation moved by 1% of the time
where the time goes in v9:
time: 223 us
  waiting for transfers between devices  83 us (37%)
  Pallas kernels  76.7 us (34%)
  starting transfers between devices  54.7 us (25%)
  local copies, waits for them, and re-layouts  5.48 us (2%)
    ppermute x52, waiting for transfers between devices, exchange(): return lax.ppermute(value, AXES, pairs)  83 us
    pallas_call x36, Pallas kernels, call(): pl.pallas_call(kernel, name=name, out_shape=outs, in_specs=specs, out_spe...  76.7 us
    ppermute x52, starting transfers between devices, exchange(): return lax.ppermute(value, AXES, pairs)  54.7 us
  transfers between devices with their start and end apart: 52, of which 22 were waited for; matrix products, arithmetic and copies ran while one was open for 2% of the time, Pallas kernels for 29%

profile of v9, /device:TPU:0, one launch (start us, length us, event | category | flops | bytes accessed | tf_op | source)
XLA Modules:
  0.0 222.6 jit_solution(5997242861371785627)
XLA Ops:
  0.7 1.0 dynamic-slice_bitcast_fusion.3
  1.7 4.1 %collective-permute-start = (bf16[48,1152]{1,0:T(8,128)(2,1)S(1)}, bf16[48,1152]{1,0:T(8,128)(2,1)S(1)}, u32[]{:S(2)}, u32[]{:S(2)}) collective-permute-start(bf16[48,1152]{1,0:T(8,128)(2,1)S(1)} %bitcast.15), channel_id=1, source_target_pairs={{0,16},{1,17},{2,10},{3,11},{4,20},{5,21},{6,14},{7,15},{8,24},{9,... | collective-permute-start | bytes 331784 | tf_op jit(solution)/shard_map/ppermute | solution.py:39
  6.8 1.6 collective-permute-start.1
  10.2 1.2 dynamic-slice_bitcast_fusion
  12.1 2.4 %collective-permute-start.2 = (bf16[96,1152]{1,0:T(8,128)(2,1)S(1)}, bf16[96,1152]{1,0:T(8,128)(2,1)S(1)}, u32[]{:S(2)}, u32[]{:S(2)}) collective-permute-start(bf16[96,1152]{1,0:T(8,128)(2,1)S(1)} %pad_maximum_fusion.13), channel_id=1, source_target_pairs={{0,8},{1,9},{2,18},{3,19},{4,12},{5,13},{6,22},{7,23},{8,0},{9,1},... | collective-permute-start | bytes 663560 | tf_op jit(solution)/shard_map/ppermute | solution.py:39
  14.5 1.5 collective-permute-start.5
  16.3 6.1 %collective-permute-done.5 = bf16[1,136,768]{2,1,0:T(8,128)(2,1)S(1)} collective-permute-done((bf16[1,136,768]{2,1,0:T(8,128)(2,1)S(1)}, bf16[1,136,768]{2,1,0:T(8,128)(2,1)S(1)}, u32[]{:S(2)}, u32[]{:S(2)}) %collective-permute-start.5) | collective-permute-done | bytes 208928 | tf_op jit(solution)/shard_map/ppermute | solution.py:39
  22.4 3.7 %collective-permute-done.6 = bf16[1,136,768]{2,1,0:T(8,128)(2,1)S(1)} collective-permute-done((bf16[1,136,768]{2,1,0:T(8,128)(2,1)S(1)}, bf16[1,136,768]{2,1,0:T(8,128)(2,1)S(1)}, u32[]{:S(2)}, u32[]{:S(2)}) %collective-permute-start.6) | collective-permute-done | bytes 208928 | tf_op jit(solution)/shard_map/ppermute | solution.py:39
  26.3 1.6 collective-permute-start.7
  28.0 2.9 %collective-permute-start.8 = (bf16[48,1920]{1,0:T(8,128)(2,1)S(1)}, bf16[48,1920]{1,0:T(8,128)(2,1)S(1)}, u32[]{:S(2)}, u32[]{:S(2)}) collective-permute-start(bf16[48,1920]{1,0:T(8,128)(2,1)S(1)} %fusion.2), channel_id=1, source_target_pairs={{0,16},{1,17},{2,10},{3,11},{4,20},{5,21},{6,14},{7,15},{8,24},{9,... | collective-permute-start | bytes 552968 | tf_op jit(solution)/shard_map/ppermute | solution.py:39
  31.1 4.8 %collective-permute-done.8 = bf16[48,1920]{1,0:T(8,128)(2,1)S(1)} collective-permute-done((bf16[48,1920]{1,0:T(8,128)(2,1)S(1)}, bf16[48,1920]{1,0:T(8,128)(2,1)S(1)}, u32[]{:S(2)}, u32[]{:S(2)}) %collective-permute-start.8) | collective-permute-done | bytes 184352 | tf_op jit(solution)/shard_map/ppermute | solution.py:39
  36.0 1.8 collective-permute-start.9
  38.4 3.5 %collective-permute-done.12 = f32[1,2304]{1,0:T(1,128)S(1)} collective-permute-done((f32[1,2304]{1,0:T(1,128)S(1)}, f32[1,2304]{1,0:T(1,128)S(1)}, u32[]{:S(2)}, u32[]{:S(2)}) %collective-permute-start.12) | collective-permute-done | bytes 9248 | tf_op jit(solution)/shard_map/ppermute | solution.py:39
  42.0 6.2 %collective-permute-done.10 = bf16[96,1920]{1,0:T(8,128)(2,1)S(1)} collective-permute-done((bf16[96,1920]{1,0:T(8,128)(2,1)S(1)}, bf16[96,1920]{1,0:T(8,128)(2,1)S(1)}, u32[]{:S(2)}, u32[]{:S(2)}) %collective-permute-start.10) | collective-permute-done | bytes 368672 | tf_op jit(solution)/shard_map/ppermute | solution.py:39
  48.2 0.9 collective-permute-done.9.refs_1_
  50.6 1.2 collective-permute-done.14.refs_3_
  51.8 1.4 unpack.3.refs_0_
  53.2 2.6 %project.1 = (bf16[512,2304]{1,0:T(8,128)(2,1)S(1)}, bf16[512,768]{1,0:T(8,128)(2,1)S(1)}, f32[512,512]{1,0:T(8,128)S(1)}) custom-call(bf16[768,2304]{1,0:T(8,128)(2,1)S(1)} %unpack.3.refs_0_, bf16[1,136,768]{2,1,0:T(8,128)(2,1)S(1)} %get-tuple-element.350.refs_1_, bf16[1,136,768]{2,1,0:T(8,128)(2,1)S(1)} %collective-permute-done.4.refs_2_, ...), custom_call_target="tpu_custom_call" | custom-call | flops 5000000000 | bytes 1000000 | tf_op jit(solution)/shard_map/project/pallas_call | solution.py:148
  55.8 5.6 %collective-permute-done.15 = bf16[192,1920]{1,0:T(8,128)(2,1)S(1)} collective-permute-done((bf16[192,1920]{1,0:T(8,128)(2,1)S(1)}, bf16[192,1920]{1,0:T(8,128)(2,1)S(1)}, u32[]{:S(2)}, u32[]{:S(2)}) %collective-permute-start.15) | collective-permute-done | bytes 737312 | tf_op jit(solution)/shard_map/ppermute | solution.py:39
  61.5 1.6 collective-permute-start.17
  63.1 6.7 %attend.2 = (bf16[512,384]{1,0:T(8,128)(2,1)S(1)}, bf16[6,512,512]{2,1,0:T(8,128)(2,1)S(1)}) custom-call(bf16[512,2304]{1,0:T(8,128)(2,1)S(1)} %get-tuple-element.227.refs_0_, f32[512,512]{1,0:T(8,128)S(1)} %get-tuple-element.221.refs_1_), custom_call_target="tpu_custom_call" | custom-call | flops 12000000000 | bytes 1000000 | tf_op jit(solution)/shard_map/attend/pallas_call | solution.py:148
  70.3 6.6 %attend.3 = (bf16[512,384]{1,0:T(8,128)(2,1)S(1)}, bf16[6,512,512]{2,1,0:T(8,128)(2,1)S(1)}) custom-call(bf16[512,2304]{1,0:T(8,128)(2,1)S(1)} %get-tuple-element.227.refs_0_, f32[512,512]{1,0:T(8,128)S(1)} %get-tuple-element.221.refs_1_), custom_call_target="tpu_custom_call" | custom-call | flops 12000000000 | bytes 1000000 | tf_op jit(solution)/shard_map/attend/pallas_call | solution.py:148
  76.9 4.0 %collective-permute-done.17.refs_1_ = bf16[384,1920]{1,0:T(8,128)(2,1)S(1)} collective-permute-done((bf16[384,1920]{1,0:T(8,128)(2,1)S(1)}, bf16[384,1920]{1,0:T(8,128)(2,1)S(1)}, u32[]{:S(2)}, u32[]{:S(2)}) %collective-permute-start.17) | collective-permute-done | bytes 1474592 | tf_op jit(solution)/shard_map/ppermute | solution.py:39
  81.9 1.5 collective-permute-start.22
  84.2 2.4 %unpack.4 = (bf16[768,768]{1,0:T(8,128)(2,1)S(1)}, bf16[768,3072]{1,0:T(8,128)(2,1)S(1)}) custom-call(bf16[384,1920]{1,0:T(8,128)(2,1)S(1)} %constant_dynamic-update-slice_fusion.refs_0_, bf16[384,1920]{1,0:T(8,128)(2,1)S(1)} %collective-permute-done.17.refs_1_, bf16[384,1920]{1,0:T(8,128)(2,1)S(1)} %collective-permute-done.18.refs_2_, ...), custom_call_target="tpu_custom_call" | custom-call | flops 5000000000 | bytes 1000000 | tf_op jit(solution)/shard_map/unpack/pallas_call | solution.py:148
  86.6 7.5 %middle.1 = (f32[512,768]{1,0:T(8,128)S(1)}, f32[512,1]{1,0:T(8,128)S(1)}, bf16[512,768]{1,0:T(8,128)(2,1)S(1)}, bf16[512,3072]{1,0:T(8,128)(2,1)S(1)}, bf16[512,3072]{1,0:T(8,128)(2,1)S(1)}) custom-call(bf16[768,768]{1,0:T(8,128)(2,1)S(1)} %get-tuple-element.234.w_out.refs_0_, bf16[768,3072]{1,0:T(8,128)(2,1)S(1)} %get-tuple-element.235.w_up.refs_1_, ...), custom_call_target="tpu_custom_call" | custom-call | flops 12000000000 | bytes 1000000 | tf_op jit(solution)/shard_map/middle/pallas_call | solution.py:148
  94.1 3.5 %collective-permute-done.20.refs_1_ = bf16[384,1536]{1,0:T(8,128)(2,1)S(1)} collective-permute-done((bf16[384,1536]{1,0:T(8,128)(2,1)S(1)}, bf16[384,1536]{1,0:T(8,128)(2,1)S(1)}, u32[]{:S(2)}, u32[]{:S(2)}) %collective-permute-start.20) | collective-permute-done | bytes 1179680 | tf_op jit(solution)/shard_map/ppermute | solution.py:39
  97.6 2.8 %collective-permute-done.23.refs_3_ = bf16[384,1536]{1,0:T(8,128)(2,1)S(1)} collective-permute-done((bf16[384,1536]{1,0:T(8,128)(2,1)S(1)}, bf16[384,1536]{1,0:T(8,128)(2,1)S(1)}, u32[]{:S(2)}, u32[]{:S(2)}) %collective-permute-start.23) | collective-permute-done | bytes 1179680 | tf_op jit(solution)/shard_map/ppermute | solution.py:39
  100.5 1.7 unpack.5.refs_0_.weight_ref
  102.1 8.1 %turn.1 = (bf16[4,128,768]{2,1,0:T(8,128)(2,1)S(1)}, f32[512,768]{1,0:T(8,128)S(1)}, bf16[512,768]{1,0:T(8,128)(2,1)S(1)}, f32[8,768]{1,0:T(8,128)S(1)}, bf16[76...) custom-call(bf16[768,3072]{1,0:T(8,128)(2,1)S(1)} %unpack.5.refs_0_.weight_ref, ...), custom_call_target="tpu_custom_call" | custom-call | flops 14000000000 | bytes 1000000 | tf_op jit(solution)/shard_map/turn/pallas_call | solution.py:148
  110.9 3.8 %hidden_back.1 = (bf16[512,3072]{1,0:T(8,128)(2,1)S(1)}, f32[1,3072]{1,0:T(1,128)S(1)}) custom-call(bf16[768,3072]{1,0:T(8,128)(2,1)S(1)} %unpack.5.refs_0_.weight_ref, bf16[512,768]{1,0:T(8,128)(2,1)S(1)} %get-tuple-element.250.gzb_ref, bf16[512,3072]{1,0:T(8,128)(2,1)S(1)} %get-tuple-element.251.slope_ref), custom_call_target="tpu_custom_call" | custom-call | flops 12000000000 | bytes 1000000 | tf_op jit(solution)/shard_map/hidden_back/pallas_call | solution.py:148
  115.8 1.6 collective-permute-start.27
  117.8 10.2 %first_back.1 = (f32[512,768]{1,0:T(8,128)S(1)}, bf16[512,768]{1,0:T(8,128)(2,1)S(1)}, f32[8,768]{1,0:T(8,128)S(1)}, bf16[768,1920]{1,0:T(8,128)(2,1)S(1)}, bf16[768,1920]{1,0:T(8,128)(2,1)S(1)}) custom-call(bf16[768,768]{1,0:T(8,128)(2,1)S(1)} %get-tuple-element.234.w_out.refs_0_, bf16[768,3072]{1,0:T(8,128)(2,1)S(1)} %get-tuple-element.235.w_up.refs_1_, ...), custom_call_target="tpu_custom_call" | custom-call | flops 20000000000 | bytes 1000000 | tf_op jit(solution)/shard_map/first_back/pallas_call | solution.py:148
  128.1 5.5 %collective-permute-done.26.refs_2_ = bf16[384,1536]{1,0:T(8,128)(2,1)S(1)} collective-permute-done((bf16[384,1536]{1,0:T(8,128)(2,1)S(1)}, bf16[384,1536]{1,0:T(8,128)(2,1)S(1)}, u32[]{:S(2)}, u32[]{:S(2)}) %collective-permute-start.26) | collective-permute-done | bytes 1179680 | tf_op jit(solution)/shard_map/ppermute | solution.py:39
  135.0 5.3 %attend_back.2 = (bf16[512,384]{1,0:T(8,128)(2,1)S(1)}, bf16[512,384]{1,0:T(8,128)(2,1)S(1)}, bf16[512,384]{1,0:T(8,128)(2,1)S(1)}) custom-call(bf16[512,2304]{1,0:T(8,128)(2,1)S(1)} %get-tuple-element.227.refs_0_, bf16[6,512,512]{2,1,0:T(8,128)(2,1)S(1)} %get-tuple-element.263.refs_1_, bf16[512,768]{1,0:T(8,128)(2,1)S(1)} %get-tuple-element.281.refs_2_), custom_call_target="tpu_custom_call" | custom-call | flops 1000000000 | bytes 1000000 | tf_op jit(solution)/shard_map/attend_back/pallas_call | solution.py:148
  140.7 1.5 collective-permute-start.31
  142.2 5.6 %attend_back.3 = (bf16[512,384]{1,0:T(8,128)(2,1)S(1)}, bf16[512,384]{1,0:T(8,128)(2,1)S(1)}, bf16[512,384]{1,0:T(8,128)(2,1)S(1)}) custom-call(bf16[512,2304]{1,0:T(8,128)(2,1)S(1)} %get-tuple-element.227.refs_0_, bf16[6,512,512]{2,1,0:T(8,128)(2,1)S(1)} %get-tuple-element.277.refs_1_, bf16[512,768]{1,0:T(8,128)(2,1)S(1)} %get-tuple-element.281.refs_2_), custom_call_target="tpu_custom_call" | custom-call | flops 1000000000 | bytes 1000000 | tf_op jit(solution)/shard_map/attend_back/pallas_call | solution.py:148
  148.0 2.7 %input_back.1.own_ref = bf16[4,128,768]{2,1,0:T(8,128)(2,1)S(1)} custom-call(bf16[768,2304]{1,0:T(8,128)(2,1)S(1)} %unpack.3.refs_0_, f32[512,768]{1,0:T(8,128)S(1)} %get-tuple-element.262.refs_1_, bf16[512,384]{1,0:T(8,128)(2,1)S(1)} %get-tuple-element.294.refs_2_.refs_4_, bf16[512,384]{1,0:T(8,128)(2,1)S(1)} %get-tuple-element.275.refs_3_.refs_5_, ...), custom_call_target="tpu_custom_call" | custom-call | flops 2000000000 | bytes 1000000 | tf_op jit(solution)/shard_map/input_back/pallas_call | solution.py:148
  150.7 2.5 %collective-permute-done.30.y_ref = bf16[4,128,768]{2,1,0:T(8,128)(2,1)S(1)} collective-permute-done((bf16[4,128,768]{2,1,0:T(8,128)(2,1)S(1)}, bf16[4,128,768]{2,1,0:T(8,128)(2,1)S(1)}, u32[]{:S(2)}, u32[]{:S(2)}) %collective-permute-start.30) | collective-permute-done | bytes 786464 | tf_op jit(solution)/shard_map/ppermute | solution.py:39
  153.2 1.9 collective-permute-start.33
  155.1 2.9 %last.1 = (bf16[776,1152]{1,0:T(8,128)(2,1)S(1)}, bf16[776,1152]{1,0:T(8,128)(2,1)S(1)}) custom-call(bf16[512,768]{1,0:T(8,128)(2,1)S(1)} %get-tuple-element.237.x_ref.refs_0_, f32[8,768]{1,0:T(8,128)S(1)} %get-tuple-element.291.refs_1_, f32[8,768]{1,0:T(8,128)S(1)} %get-tuple-element.292.refs_2_, f32[1,3072]{1,0:T(1,128)S(1)} %get-tuple-element.293.refs_3_, ...), custom_call_target="tpu_custom_call" | custom-call | flops 10000000000 | bytes 1000000 | tf_op jit(solution)/shard_map/last/pallas_call | solution.py:148
  158.1 2.0 collective-permute-done.31.refs_2_
  160.4 1.4 collective-permute-done.32.refs_1_
  162.0 1.6 collective-permute-start.34
  164.1 1.7 collective-permute-start.36
  165.9 12.6 %collective-permute-done.34.refs_2_ = bf16[392,1152]{1,0:T(8,128)(2,1)S(1)} collective-permute-done((bf16[392,1152]{1,0:T(8,128)(2,1)S(1)}, bf16[392,1152]{1,0:T(8,128)(2,1)S(1)}, u32[]{:S(2)}, u32[]{:S(2)}) %collective-permute-start.34) | collective-permute-done | bytes 903200 | tf_op jit(solution)/shard_map/ppermute | solution.py:39
  179.2 1.5 collective-permute-start.40
  181.0 1.8 collective-permute-start.41
  182.8 1.1 collective-permute-start.39
  184.0 5.7 %collective-permute-done.35.refs_3_ = bf16[200,1152]{1,0:T(8,128)(2,1)S(1)} collective-permute-done((bf16[200,1152]{1,0:T(8,128)(2,1)S(1)}, bf16[200,1152]{1,0:T(8,128)(2,1)S(1)}, u32[]{:S(2)}, u32[]{:S(2)}) %collective-permute-start.35) | collective-permute-done | bytes 460832 | tf_op jit(solution)/shard_map/ppermute | solution.py:39
  189.8 1.1 collective-permute-start.38
  191.0 1.5 collective-permute-start.43
  192.6 3.0 %collective-permute-start.44 = (bf16[48,1920]{1,0:T(8,128)(2,1)S(1)}, bf16[48,1920]{1,0:T(8,128)(2,1)S(1)}, u32[]{:S(2)}, u32[]{:S(2)}) collective-permute-start(bf16[48,1920]{1,0:T(8,128)(2,1)S(1)} %add.64), channel_id=1, source_target_pairs={{0,16},{1,17},{2,6},{3,7},{4,20},{5,21},{6,2},{7,3},{8,24},{9,25},... | collective-permute-start | bytes 552968 | tf_op jit(solution)/shard_map/ppermute | solution.py:39
  195.6 1.3 deliver.2
  197.3 1.0 collective-permute-start.42
  198.3 7.3 %collective-permute-done.44.refs_5_ = bf16[48,1920]{1,0:T(8,128)(2,1)S(1)} collective-permute-done((bf16[48,1920]{1,0:T(8,128)(2,1)S(1)}, bf16[48,1920]{1,0:T(8,128)(2,1)S(1)}, u32[]{:S(2)}, u32[]{:S(2)}) %collective-permute-start.44) | collective-permute-done | bytes 184352 | tf_op jit(solution)/shard_map/ppermute | solution.py:39
  206.5 3.2 %collective-permute-start.45 = (bf16[96,1536]{1,0:T(8,128)(2,1)S(1)}, bf16[96,1536]{1,0:T(8,128)(2,1)S(1)}, u32[]{:S(2)}, u32[]{:S(2)}) collective-permute-start(bf16[96,1536]{1,0:T(8,128)(2,1)S(1)} %constant_dynamic-update-slice_fusion.4.refs_0_), channel_id=1, source_target_pairs={{0,2},{1,3},{2,0},{3,1},{4,6},{5,7},{6,4},{7,5},{8,10},{9,11},{10,... | collective-permute-start | bytes 884744 | tf_op jit(solution)/shard_map/ppermute | solution.py:39
  209.7 3.4 %collective-permute-start.50 = (bf16[48,1152]{1,0:T(8,128)(2,1)S(1)}, bf16[48,1152]{1,0:T(8,128)(2,1)S(1)}, u32[]{:S(2)}, u32[]{:S(2)}) collective-permute-start(bf16[48,1152]{1,0:T(8,128)(2,1)S(1)} %add.67.refs_0_), channel_id=1, source_target_pairs={{0,6},{1,7},{2,4},{3,5},{4,2},{5,3},{6,0},{7,1},{8,14},{9,15},{10,... | collective-permute-start | bytes 331784 | tf_op jit(solution)/shard_map/ppermute | solution.py:39
  213.8 1.5 collective-permute-start.48
  215.3 1.2 settle.3
  216.8 1.3 deliver.3
  218.0 1.6 collective-permute-done.48.refs_1_
  219.6 1.0 settle.4
  220.7 1.2 settle.5
  (144 shorter events, 18.4 us)
Async XLA Ops:
  0.6 8.4 %copy-start = (bf16[4,2,128,768]{3,2,1,0:T(8,128)(2,1)S(1)}, bf16[4,2,128,768]{3,2,1,0:T(8,128)(2,1)}, u32[]{:S(2)}) copy-start(bf16[4,2,128,768]{3,2,1,0:T(8,128)(2,1)} %param.15) | copy-start | bytes 4718596
  1.7 9.7 %collective-permute-start = (bf16[48,1152]{1,0:T(8,128)(2,1)S(1)}, bf16[48,1152]{1,0:T(8,128)(2,1)S(1)}, u32[]{:S(2)}, u32[]{:S(2)}) collective-permute-start(bf16[48,1152]{1,0:T(8,128)(2,1)S(1)} %bitcast.15), channel_id=1, source_target_pairs={{0,16},{1,17},{2,10},{3,11},{4,20},{5,21},{6,14},{7,15},{8,24},{9,... | collective-permute-start | bytes 331784 | tf_op jit(solution)/shard_map/ppermute | solution.py:39
  6.8 5.2 %collective-permute-start.1 = (bf16[48,1536]{1,0:T(8,128)(2,1)S(1)}, bf16[48,1536]{1,0:T(8,128)(2,1)S(1)}, u32[]{:S(2)}, u32[]{:S(2)}) collective-permute-start(bf16[48,1536]{1,0:T(8,128)(2,1)S(1)} %dynamic-slice_bitcast_fusion.2), channel_id=1, source_target_pairs={{0,4},{1,5},{2,3},{3,2},{4,0},{5,1},{6,7},{7,6},{8,12},{9,13},{10,... | collective-permute-start | bytes 442376 | tf_op jit(solution)/shard_map/ppermute | solution.py:39
  12.0 14.1 %collective-permute-start.3 = (bf16[96,1536]{1,0:T(8,128)(2,1)S(1)}, bf16[96,1536]{1,0:T(8,128)(2,1)S(1)}, u32[]{:S(2)}, u32[]{:S(2)}) collective-permute-start(bf16[96,1536]{1,0:T(8,128)(2,1)S(1)} %pad_maximum_fusion.12), channel_id=1, source_target_pairs={{0,16},{1,17},{2,6},{3,7},{4,20},{5,21},{6,2},{7,3},{8,24},{9,25},... | collective-permute-start | bytes 884744 | tf_op jit(solution)/shard_map/ppermute | solution.py:39
  12.1 14.0 %collective-permute-start.2 = (bf16[96,1152]{1,0:T(8,128)(2,1)S(1)}, bf16[96,1152]{1,0:T(8,128)(2,1)S(1)}, u32[]{:S(2)}, u32[]{:S(2)}) collective-permute-start(bf16[96,1152]{1,0:T(8,128)(2,1)S(1)} %pad_maximum_fusion.13), channel_id=1, source_target_pairs={{0,8},{1,9},{2,18},{3,19},{4,12},{5,13},{6,22},{7,23},{8,0},{9,1},... | collective-permute-start | bytes 663560 | tf_op jit(solution)/shard_map/ppermute | solution.py:39
  14.5 1.9 collective-permute-start.4
  14.5 8.0 %collective-permute-start.5 = (bf16[1,136,768]{2,1,0:T(8,128)(2,1)S(1)}, bf16[1,136,768]{2,1,0:T(8,128)(2,1)S(1)}, u32[]{:S(2)}, u32[]{:S(2)}) collective-permute-start(bf16[1,136,768]{2,1,0:T(8,128)(2,1)S(1)} %get-tuple-element.187), channel_id=1, source_target_pairs={{0,4},{1,5},{2,6},{3,7},{4,0},{5,1},{6,2},{7,3},{8,12},{9,13},{10,... | collective-permute-start | bytes 626696 | tf_op jit(solution)/shard_map/ppermute | solution.py:39
  15.9 10.2 %collective-permute-start.6 = (bf16[1,136,768]{2,1,0:T(8,128)(2,1)S(1)}, bf16[1,136,768]{2,1,0:T(8,128)(2,1)S(1)}, u32[]{:S(2)}, u32[]{:S(2)}) collective-permute-start(bf16[1,136,768]{2,1,0:T(8,128)(2,1)S(1)} %get-tuple-element.188), channel_id=1, source_target_pairs={{0,6},{1,7},{2,4},{3,5},{4,2},{5,3},{6,0},{7,1},{8,14},{9,15},{10,... | collective-permute-start | bytes 626696 | tf_op jit(solution)/shard_map/ppermute | solution.py:39
  26.2 4.8 %copy-start.4 = (f32[1536]{0:T(1024)S(1)}, f32[1536]{0:T(1024)}, u32[]{:S(2)}) copy-start(f32[1536]{0:T(1024)} %up_ref) | copy-start | bytes 18436
  26.2 4.8 %copy-start.5 = (f32[768]{0:T(1024)S(1)}, f32[768]{0:T(1024)}, u32[]{:S(2)}) copy-start(f32[768]{0:T(1024)} %refs_0_.1) | copy-start | bytes 9220
  26.2 4.8 %copy-start.6 = (f32[768]{0:T(1024)S(1)}, f32[768]{0:T(1024)}, u32[]{:S(2)}) copy-start(f32[768]{0:T(1024)} %refs_1_.1) | copy-start | bytes 9220
  26.2 4.8 %copy-start.7 = (f32[768]{0:T(1024)S(1)}, f32[768]{0:T(1024)}, u32[]{:S(2)}) copy-start(f32[768]{0:T(1024)} %refs_2_.1) | copy-start | bytes 9220
  26.2 4.7 %copy-start.8 = (f32[768]{0:T(1024)S(1)}, f32[768]{0:T(1024)}, u32[]{:S(2)}) copy-start(f32[768]{0:T(1024)} %refs_3_.1) | copy-start | bytes 9220
  26.2 4.7 %copy-start.9 = (f32[768]{0:T(1024)S(1)}, f32[768]{0:T(1024)}, u32[]{:S(2)}) copy-start(f32[768]{0:T(1024)} %refs_4_.1) | copy-start | bytes 9220
  26.2 4.7 %copy-start.10 = (f32[768]{0:T(1024)S(1)}, f32[768]{0:T(1024)}, u32[]{:S(2)}) copy-start(f32[768]{0:T(1024)} %refs_5_.1) | copy-start | bytes 9220
  26.3 4.7 %copy-start.11 = (f32[2,384]{1,0:T(2,128)S(1)}, f32[2,384]{1,0:T(2,128)}, u32[]{:S(2)}) copy-start(f32[2,384]{1,0:T(2,128)} %qv_ref.1) | copy-start | bytes 9220
  26.3 9.5 %collective-permute-start.7 = (bf16[192,1152]{1,0:T(8,128)(2,1)S(1)}, bf16[192,1152]{1,0:T(8,128)(2,1)S(1)}, u32[]{:S(2)}, u32[]{:S(2)}) collective-permute-start(bf16[192,1152]{1,0:T(8,128)(2,1)S(1)} %pad_maximum_fusion.5), channel_id=1, source_target_pairs={{0,1},{1,0},{2,6},{3,7},{4,5},{5,4},{6,2},{7,3},{8,9},{9,8},{10,14... | collective-permute-start | bytes 1327112 | tf_op jit(solution)/shard_map/ppermute | solution.py:39
  28.0 7.9 %collective-permute-start.8 = (bf16[48,1920]{1,0:T(8,128)(2,1)S(1)}, bf16[48,1920]{1,0:T(8,128)(2,1)S(1)}, u32[]{:S(2)}, u32[]{:S(2)}) collective-permute-start(bf16[48,1920]{1,0:T(8,128)(2,1)S(1)} %fusion.2), channel_id=1, source_target_pairs={{0,16},{1,17},{2,10},{3,11},{4,20},{5,21},{6,14},{7,15},{8,24},{9,... | collective-permute-start | bytes 552968 | tf_op jit(solution)/shard_map/ppermute | solution.py:39
  36.0 12.3 %collective-permute-start.13 = (bf16[384,1152]{1,0:T(8,128)(2,1)S(1)}, bf16[384,1152]{1,0:T(8,128)(2,1)S(1)}, u32[]{:S(2)}, u32[]{:S(2)}) collective-permute-start(bf16[384,1152]{1,0:T(8,128)(2,1)S(1)} %pad_maximum_fusion.refs_0_), channel_id=1, source_target_pairs={{0,2},{1,3},{2,0},{3,1},{4,6},{5,7},{6,4},{7,5},{8,10},{9,11},{10,... | collective-permute-start | bytes 2654216 | tf_op jit(solution)/shard_map/ppermute | solution.py:39
  36.0 13.1 %collective-permute-start.9 = (bf16[384,1152]{1,0:T(8,128)(2,1)S(1)}, bf16[384,1152]{1,0:T(8,128)(2,1)S(1)}, u32[]{:S(2)}, u32[]{:S(2)}) collective-permute-start(bf16[384,1152]{1,0:T(8,128)(2,1)S(1)} %pad_maximum_fusion.refs_0_), channel_id=1, source_target_pairs={{0,4},{1,5},{2,3},{3,2},{4,0},{5,1},{6,7},{7,6},{8,12},{9,13},{10,... | collective-permute-start | bytes 2654216 | tf_op jit(solution)/shard_map/ppermute | solution.py:39
  37.9 10.4 %collective-permute-start.11 = (bf16[2,128,768]{2,1,0:T(8,128)(2,1)S(1)}, bf16[2,128,768]{2,1,0:T(8,128)(2,1)S(1)}, u32[]{:S(2)}, u32[]{:S(2)}) collective-permute-start(bf16[2,128,768]{2,1,0:T(8,128)(2,1)S(1)} %pad_maximum_fusion.7), channel_id=1, source_target_pairs={{0,2},{1,3},{2,0},{3,1},{4,6},{5,7},{6,4},{7,5},{8,10},{9,11},{10,... | collective-permute-start | bytes 1179656 | tf_op jit(solution)/shard_map/ppermute | solution.py:39
  37.9 10.3 %collective-permute-start.10 = (bf16[96,1920]{1,0:T(8,128)(2,1)S(1)}, bf16[96,1920]{1,0:T(8,128)(2,1)S(1)}, u32[]{:S(2)}, u32[]{:S(2)}) collective-permute-start(bf16[96,1920]{1,0:T(8,128)(2,1)S(1)} %pad_maximum_fusion.11), channel_id=1, source_target_pairs={{0,8},{1,9},{2,18},{3,19},{4,12},{5,13},{6,22},{7,23},{8,0},{9,1},... | collective-permute-start | bytes 1105928 | tf_op jit(solution)/shard_map/ppermute | solution.py:39
  38.2 3.8 %collective-permute-start.12 = (f32[1,2304]{1,0:T(1,128)S(1)}, f32[1,2304]{1,0:T(1,128)S(1)}, u32[]{:S(2)}, u32[]{:S(2)}) collective-permute-start(f32[1,2304]{1,0:T(1,128)S(1)} %get-tuple-element.205), channel_id=1, source_target_pairs={{0,1},{1,0},{2,3},{3,2},{4,5},{5,4},{6,7},{7,6},{8,9},{9,8},{10,11... | collective-permute-start | bytes 27656 | tf_op jit(solution)/shard_map/ppermute | solution.py:39
  48.2 14.9 %copy-start.2 = (bf16[2,128,768]{2,1,0:T(8,128)(2,1)}, bf16[2,128,768]{2,1,0:T(8,128)(2,1)S(1)}, u32[]{:S(2)}) copy-start(bf16[2,128,768]{2,1,0:T(8,128)(2,1)S(1)} %collective-permute-done.11.refs_4_) | copy-start | bytes 1179652
  49.2 2.6 %collective-permute-start.14 = (bf16[384,1152]{1,0:T(8,128)(2,1)S(1)}, bf16[384,1152]{1,0:T(8,128)(2,1)S(1)}, u32[]{:S(2)}, u32[]{:S(2)}) collective-permute-start(bf16[384,1152]{1,0:T(8,128)(2,1)S(1)} %collective-permute-done.9.refs_1_), channel_id=1, source_target_pairs={{0,2},{1,3},{2,0},{3,1},{4,6},{5,7},{6,4},{7,5},{8,10},{9,11},{10,... | collective-permute-start | bytes 2654216 | tf_op jit(solution)/shard_map/ppermute | solution.py:39
  49.8 20.0 %collective-permute-start.16 = (bf16[192,1536]{1,0:T(8,128)(2,1)S(1)}, bf16[192,1536]{1,0:T(8,128)(2,1)S(1)}, u32[]{:S(2)}, u32[]{:S(2)}) collective-permute-start(bf16[192,1536]{1,0:T(8,128)(2,1)S(1)} %pad_maximum_fusion.4), channel_id=1, source_target_pairs={{0,8},{1,9},{2,18},{3,19},{4,12},{5,13},{6,22},{7,23},{8,0},{9,1},... | collective-permute-start | bytes 1769480 | tf_op jit(solution)/shard_map/ppermute | solution.py:39
  49.8 11.5 %collective-permute-start.15 = (bf16[192,1920]{1,0:T(8,128)(2,1)S(1)}, bf16[192,1920]{1,0:T(8,128)(2,1)S(1)}, u32[]{:S(2)}, u32[]{:S(2)}) collective-permute-start(bf16[192,1920]{1,0:T(8,128)(2,1)S(1)} %pad_maximum_fusion.3), channel_id=1, source_target_pairs={{0,1},{1,0},{2,6},{3,7},{4,5},{5,4},{6,2},{7,3},{8,9},{9,8},{10,14... | collective-permute-start | bytes 2211848 | tf_op jit(solution)/shard_map/ppermute | solution.py:39
  61.5 19.4 %collective-permute-start.17 = (bf16[384,1920]{1,0:T(8,128)(2,1)S(1)}, bf16[384,1920]{1,0:T(8,128)(2,1)S(1)}, u32[]{:S(2)}, u32[]{:S(2)}) collective-permute-start(bf16[384,1920]{1,0:T(8,128)(2,1)S(1)} %constant_dynamic-update-slice_fusion.refs_0_), channel_id=1, source_target_pairs={{0,4},{1,5},{2,3},{3,2},{4,0},{5,1},{6,7},{7,6},{8,12},{9,13},{10,... | collective-permute-start | bytes 4423688 | tf_op jit(solution)/shard_map/ppermute | solution.py:39
  63.1 7.1 %slice-start = ((bf16[2,128,768]{2,1,0:T(8,128)(2,1)}), bf16[1,128,768]{2,1,0:T(8,128)(2,1)S(1)}, s32[]{:S(2)}) async-start(bf16[2,128,768]{2,1,0:T(8,128)(2,1)} %copy-done.2), calls=%async_computation | async-start | bytes 393216 | tf_op jit(solution)/shard_map/slice | solution.py:924
  69.7 11.2 %collective-permute-start.18 = (bf16[384,1920]{1,0:T(8,128)(2,1)S(1)}, bf16[384,1920]{1,0:T(8,128)(2,1)S(1)}, u32[]{:S(2)}, u32[]{:S(2)}) collective-permute-start(bf16[384,1920]{1,0:T(8,128)(2,1)S(1)} %constant_dynamic-update-slice_fusion.refs_0_), channel_id=1, source_target_pairs={{0,2},{1,3},{2,0},{3,1},{4,6},{5,7},{6,4},{7,5},{8,10},{9,11},{10,... | collective-permute-start | bytes 4423688 | tf_op jit(solution)/shard_map/ppermute | solution.py:39
  80.9 3.3 %collective-permute-start.19 = (bf16[384,1920]{1,0:T(8,128)(2,1)S(1)}, bf16[384,1920]{1,0:T(8,128)(2,1)S(1)}, u32[]{:S(2)}, u32[]{:S(2)}) collective-permute-start(bf16[384,1920]{1,0:T(8,128)(2,1)S(1)} %collective-permute-done.17.refs_1_), channel_id=1, source_target_pairs={{0,2},{1,3},{2,0},{3,1},{4,6},{5,7},{6,4},{7,5},{8,10},{9,11},{10,... | collective-permute-start | bytes 4423688 | tf_op jit(solution)/shard_map/ppermute | solution.py:39
  80.9 13.2 %collective-permute-start.21 = (bf16[384,1536]{1,0:T(8,128)(2,1)S(1)}, bf16[384,1536]{1,0:T(8,128)(2,1)S(1)}, u32[]{:S(2)}, u32[]{:S(2)}) collective-permute-start(bf16[384,1536]{1,0:T(8,128)(2,1)S(1)} %constant_dynamic-update-slice_fusion.2.refs_0_), channel_id=1, source_target_pairs={{0,2},{1,3},{2,0},{3,1},{4,6},{5,7},{6,4},{7,5},{8,10},{9,11},{10,... | collective-permute-start | bytes 3538952 | tf_op jit(solution)/shard_map/ppermute | solution.py:39
  81.4 16.2 %collective-permute-start.20 = (bf16[384,1536]{1,0:T(8,128)(2,1)S(1)}, bf16[384,1536]{1,0:T(8,128)(2,1)S(1)}, u32[]{:S(2)}, u32[]{:S(2)}) collective-permute-start(bf16[384,1536]{1,0:T(8,128)(2,1)S(1)} %constant_dynamic-update-slice_fusion.2.refs_0_), channel_id=1, source_target_pairs={{0,1},{1,0},{2,10},{3,11},{4,5},{5,4},{6,14},{7,15},{8,9},{9,8},{1... | collective-permute-start | bytes 3538952 | tf_op jit(solution)/shard_map/ppermute | solution.py:39
  81.9 15.7 %collective-permute-start.22 = (bf16[2,128,768]{2,1,0:T(8,128)(2,1)S(1)}, bf16[2,128,768]{2,1,0:T(8,128)(2,1)S(1)}, u32[]{:S(2)}, u32[]{:S(2)}) collective-permute-start(bf16[2,128,768]{2,1,0:T(8,128)(2,1)S(1)} %pad_maximum_fusion.8), channel_id=1, source_target_pairs={{0,4},{1,5},{2,6},{3,7},{4,0},{5,1},{6,2},{7,3},{8,12},{9,13},{10,... | collective-permute-start | bytes 1179656 | tf_op jit(solution)/shard_map/ppermute | solution.py:39
  97.6 4.5 %copy-start.3 = (bf16[2,128,768]{2,1,0:T(8,128)(2,1)S(1)}, bf16[2,128,768]{2,1,0:T(8,128)(2,1)}, u32[]{:S(2)}) copy-start(bf16[2,128,768]{2,1,0:T(8,128)(2,1)} %copy-done.2) | copy-start | bytes 1179652
  97.6 2.8 %collective-permute-start.23 = (bf16[384,1536]{1,0:T(8,128)(2,1)S(1)}, bf16[384,1536]{1,0:T(8,128)(2,1)S(1)}, u32[]{:S(2)}, u32[]{:S(2)}) collective-permute-start(bf16[384,1536]{1,0:T(8,128)(2,1)S(1)} %collective-permute-done.20.refs_1_), channel_id=1, source_target_pairs={{0,2},{1,3},{2,0},{3,1},{4,6},{5,7},{6,4},{7,5},{8,10},{9,11},{10,... | collective-permute-start | bytes 3538952 | tf_op jit(solution)/shard_map/ppermute | solution.py:39
  110.3 5.2 %collective-permute-start.24 = (bf16[768,1536]{1,0:T(8,128)(2,1)S(1)}, bf16[768,1536]{1,0:T(8,128)(2,1)S(1)}, u32[]{:S(2)}, u32[]{:S(2)}) collective-permute-start(bf16[768,1536]{1,0:T(8,128)(2,1)S(1)} %get-tuple-element.253), channel_id=1, source_target_pairs={{0,2},{1,3},{2,0},{3,1},{4,6},{5,7},{6,4},{7,5},{8,10},{9,11},{10,... | collective-permute-start | bytes 7077896 | tf_op jit(solution)/shard_map/ppermute | solution.py:39
  110.5 4.9 %collective-permute-start.25 = (bf16[2,128,768]{2,1,0:T(8,128)(2,1)S(1)}, bf16[2,128,768]{2,1,0:T(8,128)(2,1)S(1)}, u32[]{:S(2)}, u32[]{:S(2)}) collective-permute-start(bf16[2,128,768]{2,1,0:T(8,128)(2,1)S(1)} %slice.34), channel_id=1, source_target_pairs={{0,2},{1,3},{2,0},{3,1},{4,6},{5,7},{6,4},{7,5},{8,10},{9,11},{10,... | collective-permute-start | bytes 1179656 | tf_op jit(solution)/shard_map/ppermute | solution.py:39
  115.8 12.3 %collective-permute-start.27 = (bf16[2,128,768]{2,1,0:T(8,128)(2,1)S(1)}, bf16[2,128,768]{2,1,0:T(8,128)(2,1)S(1)}, u32[]{:S(2)}, u32[]{:S(2)}) collective-permute-start(bf16[2,128,768]{2,1,0:T(8,128)(2,1)S(1)} %pad_maximum_fusion.9), channel_id=1, source_target_pairs={{0,4},{1,5},{2,6},{3,7},{4,0},{5,1},{6,2},{7,3},{8,12},{9,13},{10,... | collective-permute-start | bytes 1179656 | tf_op jit(solution)/shard_map/ppermute | solution.py:39
  117.4 16.2 %collective-permute-start.26 = (bf16[384,1536]{1,0:T(8,128)(2,1)S(1)}, bf16[384,1536]{1,0:T(8,128)(2,1)S(1)}, u32[]{:S(2)}, u32[]{:S(2)}) collective-permute-start(bf16[384,1536]{1,0:T(8,128)(2,1)S(1)} %add.53), channel_id=1, source_target_pairs={{0,1},{1,0},{2,10},{3,11},{4,5},{5,4},{6,14},{7,15},{8,9},{9,8},{1... | collective-permute-start | bytes 3538952 | tf_op jit(solution)/shard_map/ppermute | solution.py:39
  133.6 6.7 %collective-permute-start.28 = (bf16[768,1920]{1,0:T(8,128)(2,1)S(1)}, bf16[768,1920]{1,0:T(8,128)(2,1)S(1)}, u32[]{:S(2)}, u32[]{:S(2)}) collective-permute-start(bf16[768,1920]{1,0:T(8,128)(2,1)S(1)} %get-tuple-element.273), channel_id=1, source_target_pairs={{0,2},{1,3},{2,0},{3,1},{4,6},{5,7},{6,4},{7,5},{8,10},{9,11},{10,... | collective-permute-start | bytes 8847368 | tf_op jit(solution)/shard_map/ppermute | solution.py:39
  133.9 13.9 %collective-permute-start.29 = (bf16[192,1536]{1,0:T(8,128)(2,1)S(1)}, bf16[192,1536]{1,0:T(8,128)(2,1)S(1)}, u32[]{:S(2)}, u32[]{:S(2)}) collective-permute-start(bf16[192,1536]{1,0:T(8,128)(2,1)S(1)} %add.54), channel_id=1, source_target_pairs={{0,4},{1,5},{2,18},{3,19},{4,0},{5,1},{6,22},{7,23},{8,12},{9,13},... | collective-permute-start | bytes 1769480 | tf_op jit(solution)/shard_map/ppermute | solution.py:39
  134.4 18.7 %collective-permute-start.30 = (bf16[4,128,768]{2,1,0:T(8,128)(2,1)S(1)}, bf16[4,128,768]{2,1,0:T(8,128)(2,1)S(1)}, u32[]{:S(2)}, u32[]{:S(2)}) collective-permute-start(bf16[4,128,768]{2,1,0:T(8,128)(2,1)S(1)} %pad_maximum_fusion.1), channel_id=1, source_target_pairs={{0,1},{1,0},{2,3},{3,2},{4,5},{5,4},{6,7},{7,6},{8,9},{9,8},{10,11... | collective-permute-start | bytes 2359304 | tf_op jit(solution)/shard_map/ppermute | solution.py:39
  140.7 19.4 %collective-permute-start.31 = (bf16[384,1920]{1,0:T(8,128)(2,1)S(1)}, bf16[384,1920]{1,0:T(8,128)(2,1)S(1)}, u32[]{:S(2)}, u32[]{:S(2)}) collective-permute-start(bf16[384,1920]{1,0:T(8,128)(2,1)S(1)} %add.55), channel_id=1, source_target_pairs={{0,4},{1,5},{2,10},{3,11},{4,0},{5,1},{6,14},{7,15},{8,12},{9,13},... | collective-permute-start | bytes 4423688 | tf_op jit(solution)/shard_map/ppermute | solution.py:39
  153.2 8.6 %collective-permute-start.33 = (bf16[2,128,768]{2,1,0:T(8,128)(2,1)S(1)}, bf16[2,128,768]{2,1,0:T(8,128)(2,1)S(1)}, u32[]{:S(2)}, u32[]{:S(2)}) collective-permute-start(bf16[2,128,768]{2,1,0:T(8,128)(2,1)S(1)} %slice.39), channel_id=1, source_target_pairs={{0,2},{1,3},{2,0},{3,1},{4,6},{5,7},{6,4},{7,5},{8,10},{9,11},{10,... | collective-permute-start | bytes 1179656 | tf_op jit(solution)/shard_map/ppermute | solution.py:39
  158.0 3.8 %collective-permute-start.32 = (bf16[776,1152]{1,0:T(8,128)(2,1)S(1)}, bf16[776,1152]{1,0:T(8,128)(2,1)S(1)}, u32[]{:S(2)}, u32[]{:S(2)}) collective-permute-start(bf16[776,1152]{1,0:T(8,128)(2,1)S(1)} %get-tuple-element.299), channel_id=1, source_target_pairs={{0,2},{1,3},{2,0},{3,1},{4,6},{5,7},{6,4},{7,5},{8,10},{9,11},{10,... | collective-permute-start | bytes 5363720 | tf_op jit(solution)/shard_map/ppermute | solution.py:39
  162.0 16.5 %collective-permute-start.34 = (bf16[392,1152]{1,0:T(8,128)(2,1)S(1)}, bf16[392,1152]{1,0:T(8,128)(2,1)S(1)}, u32[]{:S(2)}, u32[]{:S(2)}) collective-permute-start(bf16[392,1152]{1,0:T(8,128)(2,1)S(1)} %add.58.refs_3_), channel_id=1, source_target_pairs={{0,4},{1,5},{2,3},{3,2},{4,0},{5,1},{6,7},{7,6},{8,12},{9,13},{10,... | collective-permute-start | bytes 2709512 | tf_op jit(solution)/shard_map/ppermute | solution.py:39
  163.6 17.2 %collective-permute-start.37 = (bf16[192,1920]{1,0:T(8,128)(2,1)S(1)}, bf16[192,1920]{1,0:T(8,128)(2,1)S(1)}, u32[]{:S(2)}, u32[]{:S(2)}) collective-permute-start(bf16[192,1920]{1,0:T(8,128)(2,1)S(1)} %add.57), channel_id=1, source_target_pairs={{0,1},{1,0},{2,18},{3,19},{4,5},{5,4},{6,22},{7,23},{8,9},{9,8},{1... | collective-permute-start | bytes 2211848 | tf_op jit(solution)/shard_map/ppermute | solution.py:39
  164.1 15.2 %collective-permute-start.36 = (bf16[96,1536]{1,0:T(8,128)(2,1)S(1)}, bf16[96,1536]{1,0:T(8,128)(2,1)S(1)}, u32[]{:S(2)}, u32[]{:S(2)}) collective-permute-start(bf16[96,1536]{1,0:T(8,128)(2,1)S(1)} %add.56), channel_id=1, source_target_pairs={{0,8},{1,9},{2,6},{3,7},{4,12},{5,13},{6,2},{7,3},{8,0},{9,1},{10,... | collective-permute-start | bytes 884744 | tf_op jit(solution)/shard_map/ppermute | solution.py:39
  178.6 11.0 %collective-permute-start.35 = (bf16[200,1152]{1,0:T(8,128)(2,1)S(1)}, bf16[200,1152]{1,0:T(8,128)(2,1)S(1)}, u32[]{:S(2)}, u32[]{:S(2)}) collective-permute-start(bf16[200,1152]{1,0:T(8,128)(2,1)S(1)} %add.59.refs_4_), channel_id=1, source_target_pairs={{0,1},{1,0},{2,6},{3,7},{4,5},{5,4},{6,2},{7,3},{8,9},{9,8},{10,14... | collective-permute-start | bytes 1382408 | tf_op jit(solution)/shard_map/ppermute | solution.py:39
  179.2 11.6 %collective-permute-start.40 = (bf16[2,128,768]{2,1,0:T(8,128)(2,1)S(1)}, bf16[2,128,768]{2,1,0:T(8,128)(2,1)S(1)}, u32[]{:S(2)}, u32[]{:S(2)}) collective-permute-start(bf16[2,128,768]{2,1,0:T(8,128)(2,1)S(1)} %pad_maximum_fusion.10), channel_id=1, source_target_pairs={{0,4},{1,5},{2,6},{3,7},{4,0},{5,1},{6,2},{7,3},{8,12},{9,13},{10,... | collective-permute-start | bytes 1179656 | tf_op jit(solution)/shard_map/ppermute | solution.py:39
  181.0 11.5 %collective-permute-start.41 = (bf16[96,1920]{1,0:T(8,128)(2,1)S(1)}, bf16[96,1920]{1,0:T(8,128)(2,1)S(1)}, u32[]{:S(2)}, u32[]{:S(2)}) collective-permute-start(bf16[96,1920]{1,0:T(8,128)(2,1)S(1)} %add.61), channel_id=1, source_target_pairs={{0,8},{1,9},{2,3},{3,2},{4,12},{5,13},{6,7},{7,6},{8,0},{9,1},{10,... | collective-permute-start | bytes 1105928 | tf_op jit(solution)/shard_map/ppermute | solution.py:39
  182.8 8.0 %collective-permute-start.39 = (bf16[48,1536]{1,0:T(8,128)(2,1)S(1)}, bf16[48,1536]{1,0:T(8,128)(2,1)S(1)}, u32[]{:S(2)}, u32[]{:S(2)}) collective-permute-start(bf16[48,1536]{1,0:T(8,128)(2,1)S(1)} %add.60), channel_id=1, source_target_pairs={{0,16},{1,17},{2,3},{3,2},{4,20},{5,21},{6,7},{7,6},{8,24},{9,25},... | collective-permute-start | bytes 442376 | tf_op jit(solution)/shard_map/ppermute | solution.py:39
  189.8 7.4 %collective-permute-start.38 = (bf16[104,1152]{1,0:T(8,128)(2,1)S(1)}, bf16[104,1152]{1,0:T(8,128)(2,1)S(1)}, u32[]{:S(2)}, u32[]{:S(2)}) collective-permute-start(bf16[104,1152]{1,0:T(8,128)(2,1)S(1)} %add.62.refs_5_), channel_id=1, source_target_pairs={{0,8},{1,9},{2,18},{3,19},{4,12},{5,13},{6,22},{7,23},{8,0},{9,1},... | collective-permute-start | bytes 718856 | tf_op jit(solution)/shard_map/ppermute | solution.py:39
  191.0 7.3 %collective-permute-start.43 = (bf16[48,1536]{1,0:T(8,128)(2,1)S(1)}, bf16[48,1536]{1,0:T(8,128)(2,1)S(1)}, u32[]{:S(2)}, u32[]{:S(2)}) collective-permute-start(bf16[48,1536]{1,0:T(8,128)(2,1)S(1)} %add.63), channel_id=1, source_target_pairs={{0,4},{1,5},{2,6},{3,7},{4,0},{5,1},{6,2},{7,3},{8,12},{9,13},{10,... | collective-permute-start | bytes 442376 | tf_op jit(solution)/shard_map/ppermute | solution.py:39
  192.6 13.0 %collective-permute-start.44 = (bf16[48,1920]{1,0:T(8,128)(2,1)S(1)}, bf16[48,1920]{1,0:T(8,128)(2,1)S(1)}, u32[]{:S(2)}, u32[]{:S(2)}) collective-permute-start(bf16[48,1920]{1,0:T(8,128)(2,1)S(1)} %add.64), channel_id=1, source_target_pairs={{0,16},{1,17},{2,6},{3,7},{4,20},{5,21},{6,2},{7,3},{8,24},{9,25},... | collective-permute-start | bytes 552968 | tf_op jit(solution)/shard_map/ppermute | solution.py:39
  197.0 19.8 %collective-permute-start.47 = (bf16[4,128,768]{2,1,0:T(8,128)(2,1)S(1)}, bf16[4,128,768]{2,1,0:T(8,128)(2,1)S(1)}, u32[]{:S(2)}, u32[]{:S(2)}) collective-permute-start(bf16[4,128,768]{2,1,0:T(8,128)(2,1)S(1)} %pad_maximum_fusion.2), channel_id=1, source_target_pairs={{0,1},{1,0},{2,3},{3,2},{4,5},{5,4},{6,7},{7,6},{8,9},{9,8},{10,11... | collective-permute-start | bytes 2359304 | tf_op jit(solution)/shard_map/ppermute | solution.py:39
  197.3 12.3 %collective-permute-start.42 = (bf16[56,1152]{1,0:T(8,128)(2,1)S(1)}, bf16[56,1152]{1,0:T(8,128)(2,1)S(1)}, u32[]{:S(2)}, u32[]{:S(2)}) collective-permute-start(bf16[56,1152]{1,0:T(8,128)(2,1)S(1)} %add.65.refs_0_), channel_id=1, source_target_pairs={{0,16},{1,17},{2,10},{3,11},{4,20},{5,21},{6,14},{7,15},{8,24},{9,... | collective-permute-start | bytes 387080 | tf_op jit(solution)/shard_map/ppermute | solution.py:39
  205.8 10.7 %collective-permute-start.46 = (bf16[48,1920]{1,0:T(8,128)(2,1)S(1)}, bf16[48,1920]{1,0:T(8,128)(2,1)S(1)}, u32[]{:S(2)}, u32[]{:S(2)}) collective-permute-start(bf16[48,1920]{1,0:T(8,128)(2,1)S(1)} %add.66), channel_id=1, source_target_pairs={{0,4},{1,5},{2,6},{3,7},{4,0},{5,1},{6,2},{7,3},{8,12},{9,13},{10,... | collective-permute-start | bytes 552968 | tf_op jit(solution)/shard_map/ppermute | solution.py:39
  206.5 7.3 %collective-permute-start.45 = (bf16[96,1536]{1,0:T(8,128)(2,1)S(1)}, bf16[96,1536]{1,0:T(8,128)(2,1)S(1)}, u32[]{:S(2)}, u32[]{:S(2)}) collective-permute-start(bf16[96,1536]{1,0:T(8,128)(2,1)S(1)} %constant_dynamic-update-slice_fusion.4.refs_0_), channel_id=1, source_target_pairs={{0,2},{1,3},{2,0},{3,1},{4,6},{5,7},{6,4},{7,5},{8,10},{9,11},{10,... | collective-permute-start | bytes 884744 | tf_op jit(solution)/shard_map/ppermute | solution.py:39
  209.7 8.3 %collective-permute-start.50 = (bf16[48,1152]{1,0:T(8,128)(2,1)S(1)}, bf16[48,1152]{1,0:T(8,128)(2,1)S(1)}, u32[]{:S(2)}, u32[]{:S(2)}) collective-permute-start(bf16[48,1152]{1,0:T(8,128)(2,1)S(1)} %add.67.refs_0_), channel_id=1, source_target_pairs={{0,6},{1,7},{2,4},{3,5},{4,2},{5,3},{6,0},{7,1},{8,14},{9,15},{10,... | collective-permute-start | bytes 331784 | tf_op jit(solution)/shard_map/ppermute | solution.py:39
  213.1 4.9 %collective-permute-start.49 = (bf16[48,1152]{1,0:T(8,128)(2,1)S(1)}, bf16[48,1152]{1,0:T(8,128)(2,1)S(1)}, u32[]{:S(2)}, u32[]{:S(2)}) collective-permute-start(bf16[48,1152]{1,0:T(8,128)(2,1)S(1)} %add.67.refs_0_), channel_id=1, source_target_pairs={{0,2},{1,3},{2,0},{3,1},{4,6},{5,7},{6,4},{7,5},{8,10},{9,11},{10,... | collective-permute-start | bytes 331784 | tf_op jit(solution)/shard_map/ppermute | solution.py:39
  213.8 5.8 %collective-permute-start.48 = (bf16[48,1152]{1,0:T(8,128)(2,1)S(1)}, bf16[48,1152]{1,0:T(8,128)(2,1)S(1)}, u32[]{:S(2)}, u32[]{:S(2)}) collective-permute-start(bf16[48,1152]{1,0:T(8,128)(2,1)S(1)} %add.67.refs_0_), channel_id=1, source_target_pairs={{0,4},{1,5},{2,6},{3,7},{4,0},{5,1},{6,2},{7,3},{8,12},{9,13},{10,... | collective-permute-start | bytes 331784 | tf_op jit(solution)/shard_map/ppermute | solution.py:39
  216.5 4.2 %collective-permute-start.51 = (bf16[96,1920]{1,0:T(8,128)(2,1)S(1)}, bf16[96,1920]{1,0:T(8,128)(2,1)S(1)}, u32[]{:S(2)}, u32[]{:S(2)}) collective-permute-start(bf16[96,1920]{1,0:T(8,128)(2,1)S(1)} %constant_dynamic-update-slice_fusion.6.refs_0_), channel_id=1, source_target_pairs={{0,2},{1,3},{2,0},{3,1},{4,6},{5,7},{6,4},{7,5},{8,10},{9,11},{10,... | collective-permute-start | bytes 1105928 | tf_op jit(solution)/shard_map/ppermute | solution.py:39
  (3 other events, 4.1 us)

commit v10 on v9

--- a/solution.py
+++ b/solution.py
@@ -1034,12 +1034,13 @@
         pair1 = joined(pair1, got)
         up = up + [got2]
         pair2 = add_up(up, 0, rows)
-        got1, got2 = exchange(pair1, CORE, sizes), exchange(pair2, X, sizes)
+        got2 = exchange(pair2, X, sizes)
         got3, pair1, pair2 = phase(got3, pair1, pair2)
         qkv = qkv + [got3]
         sent_last = got3
         piece = add_up(qkv, 0, rows)
         got3 = [exchange(piece, dims, sizes) for dims in (X, CORE, FAR)]
+        got1 = exchange(after(pair1, piece), CORE, sizes)
         vec = vectors(after(send3, piece), sent_last, local_width, local_units)
         piece, got1, bup = phase(piece, got1, vec[1])
         vec = (vec[0], bup) + tuple(vec[2:])

time: 223 us -> 223 us (level)
  transfers between devices with their start and end apart: 52 -> 52, of which waited for: 22 -> 24; matrix products, arithmetic and copies ran while one was open for 2% -> 2% of each run, Pallas kernels for 29% -> 29%
where the time goes in v10:
time: 223 us
  waiting for transfers between devices  85.2 us (38%)
  Pallas kernels  76.7 us (34%)
  starting transfers between devices  53 us (24%)
  local copies, waits for them, and re-layouts  5.45 us (2%)
    ppermute x52, waiting for transfers between devices, exchange(): return lax.ppermute(value, AXES, pairs)  85.2 us
    pallas_call x36, Pallas kernels, call(): pl.pallas_call(kernel, name=name, out_shape=outs, in_specs=specs, out_spe...  76.7 us
    ppermute x52, starting transfers between devices, exchange(): return lax.ppermute(value, AXES, pairs)  53 us
  transfers between devices with their start and end apart: 52, of which 24 were waited for; matrix products, arithmetic and copies ran while one was open for 2% of the time, Pallas kernels for 29%

profile of v10, /device:TPU:0, one launch (start us, length us, event | category | flops | bytes accessed | tf_op | source)
XLA Modules:
  0.0 223.2 jit_solution(9915171415858950661)
XLA Ops:
  0.7 1.0 dynamic-slice_bitcast_fusion.3
  1.7 4.1 %collective-permute-start = (bf16[48,1152]{1,0:T(8,128)(2,1)S(1)}, bf16[48,1152]{1,0:T(8,128)(2,1)S(1)}, u32[]{:S(2)}, u32[]{:S(2)}) collective-permute-start(bf16[48,1152]{1,0:T(8,128)(2,1)S(1)} %bitcast.15), channel_id=1, source_target_pairs={{0,16},{1,17},{2,10},{3,11},{4,20},{5,21},{6,14},{7,15},{8,24},{9,... | collective-permute-start | bytes 331784 | tf_op jit(solution)/shard_map/ppermute | solution.py:39
  6.8 1.6 collective-permute-start.1
  10.2 1.2 dynamic-slice_bitcast_fusion
  12.1 2.4 %collective-permute-start.2 = (bf16[96,1152]{1,0:T(8,128)(2,1)S(1)}, bf16[96,1152]{1,0:T(8,128)(2,1)S(1)}, u32[]{:S(2)}, u32[]{:S(2)}) collective-permute-start(bf16[96,1152]{1,0:T(8,128)(2,1)S(1)} %pad_maximum_fusion.14), channel_id=1, source_target_pairs={{0,8},{1,9},{2,18},{3,19},{4,12},{5,13},{6,22},{7,23},{8,0},{9,1},... | collective-permute-start | bytes 663560 | tf_op jit(solution)/shard_map/ppermute | solution.py:39
  14.5 1.5 collective-permute-start.5
  16.3 6.1 %collective-permute-done.5 = bf16[1,136,768]{2,1,0:T(8,128)(2,1)S(1)} collective-permute-done((bf16[1,136,768]{2,1,0:T(8,128)(2,1)S(1)}, bf16[1,136,768]{2,1,0:T(8,128)(2,1)S(1)}, u32[]{:S(2)}, u32[]{:S(2)}) %collective-permute-start.5) | collective-permute-done | bytes 208928 | tf_op jit(solution)/shard_map/ppermute | solution.py:39
  22.4 3.7 %collective-permute-done.6 = bf16[1,136,768]{2,1,0:T(8,128)(2,1)S(1)} collective-permute-done((bf16[1,136,768]{2,1,0:T(8,128)(2,1)S(1)}, bf16[1,136,768]{2,1,0:T(8,128)(2,1)S(1)}, u32[]{:S(2)}, u32[]{:S(2)}) %collective-permute-start.6) | collective-permute-done | bytes 208928 | tf_op jit(solution)/shard_map/ppermute | solution.py:39
  26.3 1.6 collective-permute-start.7
  28.0 2.9 %collective-permute-start.8 = (bf16[48,1920]{1,0:T(8,128)(2,1)S(1)}, bf16[48,1920]{1,0:T(8,128)(2,1)S(1)}, u32[]{:S(2)}, u32[]{:S(2)}) collective-permute-start(bf16[48,1920]{1,0:T(8,128)(2,1)S(1)} %fusion.2), channel_id=1, source_target_pairs={{0,16},{1,17},{2,10},{3,11},{4,20},{5,21},{6,14},{7,15},{8,24},{9,... | collective-permute-start | bytes 552968 | tf_op jit(solution)/shard_map/ppermute | solution.py:39
  31.1 4.8 %collective-permute-done.8 = bf16[48,1920]{1,0:T(8,128)(2,1)S(1)} collective-permute-done((bf16[48,1920]{1,0:T(8,128)(2,1)S(1)}, bf16[48,1920]{1,0:T(8,128)(2,1)S(1)}, u32[]{:S(2)}, u32[]{:S(2)}) %collective-permute-start.8) | collective-permute-done | bytes 184352 | tf_op jit(solution)/shard_map/ppermute | solution.py:39
  36.0 1.8 collective-permute-start.9
  38.4 3.5 %collective-permute-done.12 = f32[1,2304]{1,0:T(1,128)S(1)} collective-permute-done((f32[1,2304]{1,0:T(1,128)S(1)}, f32[1,2304]{1,0:T(1,128)S(1)}, u32[]{:S(2)}, u32[]{:S(2)}) %collective-permute-start.12) | collective-permute-done | bytes 9248 | tf_op jit(solution)/shard_map/ppermute | solution.py:39
  42.0 6.2 %collective-permute-done.10 = bf16[96,1920]{1,0:T(8,128)(2,1)S(1)} collective-permute-done((bf16[96,1920]{1,0:T(8,128)(2,1)S(1)}, bf16[96,1920]{1,0:T(8,128)(2,1)S(1)}, u32[]{:S(2)}, u32[]{:S(2)}) %collective-permute-start.10) | collective-permute-done | bytes 368672 | tf_op jit(solution)/shard_map/ppermute | solution.py:39
  48.2 0.9 collective-permute-done.9.refs_1_
  50.6 1.2 collective-permute-done.14.refs_3_
  51.8 1.4 unpack.3.refs_0_
  53.2 2.6 %project.1 = (bf16[512,2304]{1,0:T(8,128)(2,1)S(1)}, bf16[512,768]{1,0:T(8,128)(2,1)S(1)}, f32[512,512]{1,0:T(8,128)S(1)}) custom-call(bf16[768,2304]{1,0:T(8,128)(2,1)S(1)} %unpack.3.refs_0_, bf16[1,136,768]{2,1,0:T(8,128)(2,1)S(1)} %get-tuple-element.352.refs_1_, bf16[1,136,768]{2,1,0:T(8,128)(2,1)S(1)} %collective-permute-done.4.refs_2_, ...), custom_call_target="tpu_custom_call" | custom-call | flops 5000000000 | bytes 1000000 | tf_op jit(solution)/shard_map/project/pallas_call | solution.py:148
  55.8 5.6 %collective-permute-done.15 = bf16[192,1920]{1,0:T(8,128)(2,1)S(1)} collective-permute-done((bf16[192,1920]{1,0:T(8,128)(2,1)S(1)}, bf16[192,1920]{1,0:T(8,128)(2,1)S(1)}, u32[]{:S(2)}, u32[]{:S(2)}) %collective-permute-start.15) | collective-permute-done | bytes 737312 | tf_op jit(solution)/shard_map/ppermute | solution.py:39
  61.5 1.6 collective-permute-start.17
  63.1 6.7 %attend.2 = (bf16[512,384]{1,0:T(8,128)(2,1)S(1)}, bf16[6,512,512]{2,1,0:T(8,128)(2,1)S(1)}) custom-call(bf16[512,2304]{1,0:T(8,128)(2,1)S(1)} %get-tuple-element.228.refs_0_, f32[512,512]{1,0:T(8,128)S(1)} %get-tuple-element.222.refs_1_), custom_call_target="tpu_custom_call" | custom-call | flops 12000000000 | bytes 1000000 | tf_op jit(solution)/shard_map/attend/pallas_call | solution.py:148
  70.3 6.6 %attend.3 = (bf16[512,384]{1,0:T(8,128)(2,1)S(1)}, bf16[6,512,512]{2,1,0:T(8,128)(2,1)S(1)}) custom-call(bf16[512,2304]{1,0:T(8,128)(2,1)S(1)} %get-tuple-element.228.refs_0_, f32[512,512]{1,0:T(8,128)S(1)} %get-tuple-element.222.refs_1_), custom_call_target="tpu_custom_call" | custom-call | flops 12000000000 | bytes 1000000 | tf_op jit(solution)/shard_map/attend/pallas_call | solution.py:148
  76.9 4.0 %collective-permute-done.17.refs_1_ = bf16[384,1920]{1,0:T(8,128)(2,1)S(1)} collective-permute-done((bf16[384,1920]{1,0:T(8,128)(2,1)S(1)}, bf16[384,1920]{1,0:T(8,128)(2,1)S(1)}, u32[]{:S(2)}, u32[]{:S(2)}) %collective-permute-start.17) | collective-permute-done | bytes 1474592 | tf_op jit(solution)/shard_map/ppermute | solution.py:39
  81.9 1.5 collective-permute-start.22
  84.2 2.4 %unpack.4 = (bf16[768,768]{1,0:T(8,128)(2,1)S(1)}, bf16[768,3072]{1,0:T(8,128)(2,1)S(1)}) custom-call(bf16[384,1920]{1,0:T(8,128)(2,1)S(1)} %constant_dynamic-update-slice_fusion.refs_0_, bf16[384,1920]{1,0:T(8,128)(2,1)S(1)} %collective-permute-done.17.refs_1_, bf16[384,1920]{1,0:T(8,128)(2,1)S(1)} %collective-permute-done.18.refs_2_, ...), custom_call_target="tpu_custom_call" | custom-call | flops 5000000000 | bytes 1000000 | tf_op jit(solution)/shard_map/unpack/pallas_call | solution.py:148
  86.6 7.5 %middle.1 = (f32[512,768]{1,0:T(8,128)S(1)}, f32[512,1]{1,0:T(8,128)S(1)}, bf16[512,768]{1,0:T(8,128)(2,1)S(1)}, bf16[512,3072]{1,0:T(8,128)(2,1)S(1)}, bf16[512,3072]{1,0:T(8,128)(2,1)S(1)}) custom-call(bf16[768,768]{1,0:T(8,128)(2,1)S(1)} %get-tuple-element.235.w_out.refs_0_, bf16[768,3072]{1,0:T(8,128)(2,1)S(1)} %get-tuple-element.236.w_up.refs_1_, ...), custom_call_target="tpu_custom_call" | custom-call | flops 12000000000 | bytes 1000000 | tf_op jit(solution)/shard_map/middle/pallas_call | solution.py:148
  94.1 3.5 %collective-permute-done.20.refs_1_ = bf16[384,1536]{1,0:T(8,128)(2,1)S(1)} collective-permute-done((bf16[384,1536]{1,0:T(8,128)(2,1)S(1)}, bf16[384,1536]{1,0:T(8,128)(2,1)S(1)}, u32[]{:S(2)}, u32[]{:S(2)}) %collective-permute-start.20) | collective-permute-done | bytes 1179680 | tf_op jit(solution)/shard_map/ppermute | solution.py:39
  97.6 2.8 %collective-permute-done.23.refs_3_ = bf16[384,1536]{1,0:T(8,128)(2,1)S(1)} collective-permute-done((bf16[384,1536]{1,0:T(8,128)(2,1)S(1)}, bf16[384,1536]{1,0:T(8,128)(2,1)S(1)}, u32[]{:S(2)}, u32[]{:S(2)}) %collective-permute-start.23) | collective-permute-done | bytes 1179680 | tf_op jit(solution)/shard_map/ppermute | solution.py:39
  100.5 1.7 unpack.5.refs_0_.weight_ref
  102.1 8.1 %turn.1 = (bf16[4,128,768]{2,1,0:T(8,128)(2,1)S(1)}, f32[512,768]{1,0:T(8,128)S(1)}, bf16[512,768]{1,0:T(8,128)(2,1)S(1)}, f32[8,768]{1,0:T(8,128)S(1)}, bf16[76...) custom-call(bf16[768,3072]{1,0:T(8,128)(2,1)S(1)} %unpack.5.refs_0_.weight_ref, ...), custom_call_target="tpu_custom_call" | custom-call | flops 14000000000 | bytes 1000000 | tf_op jit(solution)/shard_map/turn/pallas_call | solution.py:148
  110.9 3.8 %hidden_back.1 = (bf16[512,3072]{1,0:T(8,128)(2,1)S(1)}, f32[1,3072]{1,0:T(1,128)S(1)}) custom-call(bf16[768,3072]{1,0:T(8,128)(2,1)S(1)} %unpack.5.refs_0_.weight_ref, bf16[512,768]{1,0:T(8,128)(2,1)S(1)} %get-tuple-element.251.gzb_ref, bf16[512,3072]{1,0:T(8,128)(2,1)S(1)} %get-tuple-element.252.slope_ref), custom_call_target="tpu_custom_call" | custom-call | flops 12000000000 | bytes 1000000 | tf_op jit(solution)/shard_map/hidden_back/pallas_call | solution.py:148
  115.8 1.6 collective-permute-start.27
  117.8 10.2 %first_back.1 = (f32[512,768]{1,0:T(8,128)S(1)}, bf16[512,768]{1,0:T(8,128)(2,1)S(1)}, f32[8,768]{1,0:T(8,128)S(1)}, bf16[768,1920]{1,0:T(8,128)(2,1)S(1)}, bf16[768,1920]{1,0:T(8,128)(2,1)S(1)}) custom-call(bf16[768,768]{1,0:T(8,128)(2,1)S(1)} %get-tuple-element.235.w_out.refs_0_, bf16[768,3072]{1,0:T(8,128)(2,1)S(1)} %get-tuple-element.236.w_up.refs_1_, ...), custom_call_target="tpu_custom_call" | custom-call | flops 20000000000 | bytes 1000000 | tf_op jit(solution)/shard_map/first_back/pallas_call | solution.py:148
  128.1 5.5 %collective-permute-done.26.refs_2_ = bf16[384,1536]{1,0:T(8,128)(2,1)S(1)} collective-permute-done((bf16[384,1536]{1,0:T(8,128)(2,1)S(1)}, bf16[384,1536]{1,0:T(8,128)(2,1)S(1)}, u32[]{:S(2)}, u32[]{:S(2)}) %collective-permute-start.26) | collective-permute-done | bytes 1179680 | tf_op jit(solution)/shard_map/ppermute | solution.py:39
  135.0 5.3 %attend_back.2 = (bf16[512,384]{1,0:T(8,128)(2,1)S(1)}, bf16[512,384]{1,0:T(8,128)(2,1)S(1)}, bf16[512,384]{1,0:T(8,128)(2,1)S(1)}) custom-call(bf16[512,2304]{1,0:T(8,128)(2,1)S(1)} %get-tuple-element.228.refs_0_, bf16[6,512,512]{2,1,0:T(8,128)(2,1)S(1)} %get-tuple-element.264.refs_1_, bf16[512,768]{1,0:T(8,128)(2,1)S(1)} %get-tuple-element.282.refs_2_), custom_call_target="tpu_custom_call" | custom-call | flops 1000000000 | bytes 1000000 | tf_op jit(solution)/shard_map/attend_back/pallas_call | solution.py:148
  140.7 1.5 collective-permute-start.31
  142.2 5.6 %attend_back.3 = (bf16[512,384]{1,0:T(8,128)(2,1)S(1)}, bf16[512,384]{1,0:T(8,128)(2,1)S(1)}, bf16[512,384]{1,0:T(8,128)(2,1)S(1)}) custom-call(bf16[512,2304]{1,0:T(8,128)(2,1)S(1)} %get-tuple-element.228.refs_0_, bf16[6,512,512]{2,1,0:T(8,128)(2,1)S(1)} %get-tuple-element.278.refs_1_, bf16[512,768]{1,0:T(8,128)(2,1)S(1)} %get-tuple-element.282.refs_2_), custom_call_target="tpu_custom_call" | custom-call | flops 1000000000 | bytes 1000000 | tf_op jit(solution)/shard_map/attend_back/pallas_call | solution.py:148
  148.0 2.7 %input_back.1.own_ref = bf16[4,128,768]{2,1,0:T(8,128)(2,1)S(1)} custom-call(bf16[768,2304]{1,0:T(8,128)(2,1)S(1)} %unpack.3.refs_0_, f32[512,768]{1,0:T(8,128)S(1)} %get-tuple-element.263.refs_1_, bf16[512,384]{1,0:T(8,128)(2,1)S(1)} %get-tuple-element.295.refs_2_.refs_4_, bf16[512,384]{1,0:T(8,128)(2,1)S(1)} %get-tuple-element.276.refs_3_.refs_5_, ...), custom_call_target="tpu_custom_call" | custom-call | flops 2000000000 | bytes 1000000 | tf_op jit(solution)/shard_map/input_back/pallas_call | solution.py:148
  150.7 2.5 %collective-permute-done.30.y_ref = bf16[4,128,768]{2,1,0:T(8,128)(2,1)S(1)} collective-permute-done((bf16[4,128,768]{2,1,0:T(8,128)(2,1)S(1)}, bf16[4,128,768]{2,1,0:T(8,128)(2,1)S(1)}, u32[]{:S(2)}, u32[]{:S(2)}) %collective-permute-start.30) | collective-permute-done | bytes 786464 | tf_op jit(solution)/shard_map/ppermute | solution.py:39
  153.2 1.9 collective-permute-start.33
  155.1 2.9 %last.1 = (bf16[776,1152]{1,0:T(8,128)(2,1)S(1)}, bf16[776,1152]{1,0:T(8,128)(2,1)S(1)}) custom-call(bf16[512,768]{1,0:T(8,128)(2,1)S(1)} %get-tuple-element.238.x_ref.refs_0_, f32[8,768]{1,0:T(8,128)S(1)} %get-tuple-element.292.refs_1_, f32[8,768]{1,0:T(8,128)S(1)} %get-tuple-element.293.refs_2_, f32[1,3072]{1,0:T(1,128)S(1)} %get-tuple-element.294.refs_3_, ...), custom_call_target="tpu_custom_call" | custom-call | flops 10000000000 | bytes 1000000 | tf_op jit(solution)/shard_map/last/pallas_call | solution.py:148
  158.1 2.0 collective-permute-done.31.refs_2_
  160.4 1.4 collective-permute-done.32.refs_1_
  162.0 1.6 collective-permute-start.34
  164.1 1.7 collective-permute-start.36
  165.9 12.6 %collective-permute-done.34.refs_2_ = bf16[392,1152]{1,0:T(8,128)(2,1)S(1)} collective-permute-done((bf16[392,1152]{1,0:T(8,128)(2,1)S(1)}, bf16[392,1152]{1,0:T(8,128)(2,1)S(1)}, u32[]{:S(2)}, u32[]{:S(2)}) %collective-permute-start.34) | collective-permute-done | bytes 903200 | tf_op jit(solution)/shard_map/ppermute | solution.py:39
  179.2 1.5 collective-permute-start.40
  181.0 1.8 collective-permute-start.41
  182.8 1.1 collective-permute-start.39
  184.0 5.7 %collective-permute-done.35.refs_3_ = bf16[200,1152]{1,0:T(8,128)(2,1)S(1)} collective-permute-done((bf16[200,1152]{1,0:T(8,128)(2,1)S(1)}, bf16[200,1152]{1,0:T(8,128)(2,1)S(1)}, u32[]{:S(2)}, u32[]{:S(2)}) %collective-permute-start.35) | collective-permute-done | bytes 460832 | tf_op jit(solution)/shard_map/ppermute | solution.py:39
  189.8 1.1 collective-permute-start.38
  191.0 1.5 collective-permute-start.43
  192.6 3.0 %collective-permute-start.44 = (bf16[48,1920]{1,0:T(8,128)(2,1)S(1)}, bf16[48,1920]{1,0:T(8,128)(2,1)S(1)}, u32[]{:S(2)}, u32[]{:S(2)}) collective-permute-start(bf16[48,1920]{1,0:T(8,128)(2,1)S(1)} %add.64), channel_id=1, source_target_pairs={{0,16},{1,17},{2,6},{3,7},{4,20},{5,21},{6,2},{7,3},{8,24},{9,25},... | collective-permute-start | bytes 552968 | tf_op jit(solution)/shard_map/ppermute | solution.py:39
  195.6 1.3 deliver.2
  197.3 1.0 collective-permute-start.42
  198.3 7.3 %collective-permute-done.44.refs_5_ = bf16[48,1920]{1,0:T(8,128)(2,1)S(1)} collective-permute-done((bf16[48,1920]{1,0:T(8,128)(2,1)S(1)}, bf16[48,1920]{1,0:T(8,128)(2,1)S(1)}, u32[]{:S(2)}, u32[]{:S(2)}) %collective-permute-start.44) | collective-permute-done | bytes 184352 | tf_op jit(solution)/shard_map/ppermute | solution.py:39
  206.5 1.9 collective-permute-done.42.refs_5_.refs_1_
  208.5 4.7 %collective-permute-start.50 = (bf16[48,1152]{1,0:T(8,128)(2,1)S(1)}, bf16[48,1152]{1,0:T(8,128)(2,1)S(1)}, u32[]{:S(2)}, u32[]{:S(2)}) collective-permute-start(bf16[48,1152]{1,0:T(8,128)(2,1)S(1)} %add.67.refs_0_), channel_id=1, source_target_pairs={{0,6},{1,7},{2,4},{3,5},{4,2},{5,3},{6,0},{7,1},{8,14},{9,15},{10,... | collective-permute-start | bytes 331784 | tf_op jit(solution)/shard_map/ppermute | solution.py:39
  214.9 1.4 collective-permute-start.48
  216.3 1.2 settle.3
  217.6 1.3 deliver.3
  218.9 1.3 collective-permute-done.48.refs_1_
  220.2 1.0 settle.4
  221.2 1.2 settle.5
  (143 shorter events, 19.3 us)
Async XLA Ops:
  0.6 8.4 %copy-start = (bf16[4,2,128,768]{3,2,1,0:T(8,128)(2,1)S(1)}, bf16[4,2,128,768]{3,2,1,0:T(8,128)(2,1)}, u32[]{:S(2)}) copy-start(bf16[4,2,128,768]{3,2,1,0:T(8,128)(2,1)} %param.15) | copy-start | bytes 4718596
  1.7 9.7 %collective-permute-start = (bf16[48,1152]{1,0:T(8,128)(2,1)S(1)}, bf16[48,1152]{1,0:T(8,128)(2,1)S(1)}, u32[]{:S(2)}, u32[]{:S(2)}) collective-permute-start(bf16[48,1152]{1,0:T(8,128)(2,1)S(1)} %bitcast.15), channel_id=1, source_target_pairs={{0,16},{1,17},{2,10},{3,11},{4,20},{5,21},{6,14},{7,15},{8,24},{9,... | collective-permute-start | bytes 331784 | tf_op jit(solution)/shard_map/ppermute | solution.py:39
  6.8 5.2 %collective-permute-start.1 = (bf16[48,1536]{1,0:T(8,128)(2,1)S(1)}, bf16[48,1536]{1,0:T(8,128)(2,1)S(1)}, u32[]{:S(2)}, u32[]{:S(2)}) collective-permute-start(bf16[48,1536]{1,0:T(8,128)(2,1)S(1)} %dynamic-slice_bitcast_fusion.2), channel_id=1, source_target_pairs={{0,4},{1,5},{2,3},{3,2},{4,0},{5,1},{6,7},{7,6},{8,12},{9,13},{10,... | collective-permute-start | bytes 442376 | tf_op jit(solution)/shard_map/ppermute | solution.py:39
  12.0 14.1 %collective-permute-start.3 = (bf16[96,1536]{1,0:T(8,128)(2,1)S(1)}, bf16[96,1536]{1,0:T(8,128)(2,1)S(1)}, u32[]{:S(2)}, u32[]{:S(2)}) collective-permute-start(bf16[96,1536]{1,0:T(8,128)(2,1)S(1)} %pad_maximum_fusion.12), channel_id=1, source_target_pairs={{0,16},{1,17},{2,6},{3,7},{4,20},{5,21},{6,2},{7,3},{8,24},{9,25},... | collective-permute-start | bytes 884744 | tf_op jit(solution)/shard_map/ppermute | solution.py:39
  12.1 14.0 %collective-permute-start.2 = (bf16[96,1152]{1,0:T(8,128)(2,1)S(1)}, bf16[96,1152]{1,0:T(8,128)(2,1)S(1)}, u32[]{:S(2)}, u32[]{:S(2)}) collective-permute-start(bf16[96,1152]{1,0:T(8,128)(2,1)S(1)} %pad_maximum_fusion.14), channel_id=1, source_target_pairs={{0,8},{1,9},{2,18},{3,19},{4,12},{5,13},{6,22},{7,23},{8,0},{9,1},... | collective-permute-start | bytes 663560 | tf_op jit(solution)/shard_map/ppermute | solution.py:39
  14.5 1.9 collective-permute-start.4
  14.5 8.0 %collective-permute-start.5 = (bf16[1,136,768]{2,1,0:T(8,128)(2,1)S(1)}, bf16[1,136,768]{2,1,0:T(8,128)(2,1)S(1)}, u32[]{:S(2)}, u32[]{:S(2)}) collective-permute-start(bf16[1,136,768]{2,1,0:T(8,128)(2,1)S(1)} %get-tuple-element.188), channel_id=1, source_target_pairs={{0,4},{1,5},{2,6},{3,7},{4,0},{5,1},{6,2},{7,3},{8,12},{9,13},{10,... | collective-permute-start | bytes 626696 | tf_op jit(solution)/shard_map/ppermute | solution.py:39
  15.9 10.2 %collective-permute-start.6 = (bf16[1,136,768]{2,1,0:T(8,128)(2,1)S(1)}, bf16[1,136,768]{2,1,0:T(8,128)(2,1)S(1)}, u32[]{:S(2)}, u32[]{:S(2)}) collective-permute-start(bf16[1,136,768]{2,1,0:T(8,128)(2,1)S(1)} %get-tuple-element.189), channel_id=1, source_target_pairs={{0,6},{1,7},{2,4},{3,5},{4,2},{5,3},{6,0},{7,1},{8,14},{9,15},{10,... | collective-permute-start | bytes 626696 | tf_op jit(solution)/shard_map/ppermute | solution.py:39
  26.2 4.8 %copy-start.4 = (f32[1536]{0:T(1024)S(1)}, f32[1536]{0:T(1024)}, u32[]{:S(2)}) copy-start(f32[1536]{0:T(1024)} %up_ref) | copy-start | bytes 18436
  26.2 4.8 %copy-start.5 = (f32[768]{0:T(1024)S(1)}, f32[768]{0:T(1024)}, u32[]{:S(2)}) copy-start(f32[768]{0:T(1024)} %refs_0_.1) | copy-start | bytes 9220
  26.2 4.8 %copy-start.6 = (f32[768]{0:T(1024)S(1)}, f32[768]{0:T(1024)}, u32[]{:S(2)}) copy-start(f32[768]{0:T(1024)} %refs_1_.1) | copy-start | bytes 9220
  26.2 4.8 %copy-start.7 = (f32[768]{0:T(1024)S(1)}, f32[768]{0:T(1024)}, u32[]{:S(2)}) copy-start(f32[768]{0:T(1024)} %refs_2_.1) | copy-start | bytes 9220
  26.2 4.7 %copy-start.8 = (f32[768]{0:T(1024)S(1)}, f32[768]{0:T(1024)}, u32[]{:S(2)}) copy-start(f32[768]{0:T(1024)} %refs_3_.1) | copy-start | bytes 9220
  26.2 4.7 %copy-start.9 = (f32[768]{0:T(1024)S(1)}, f32[768]{0:T(1024)}, u32[]{:S(2)}) copy-start(f32[768]{0:T(1024)} %refs_4_.1) | copy-start | bytes 9220
  26.2 4.7 %copy-start.10 = (f32[768]{0:T(1024)S(1)}, f32[768]{0:T(1024)}, u32[]{:S(2)}) copy-start(f32[768]{0:T(1024)} %refs_5_.1) | copy-start | bytes 9220
  26.3 4.7 %copy-start.11 = (f32[2,384]{1,0:T(2,128)S(1)}, f32[2,384]{1,0:T(2,128)}, u32[]{:S(2)}) copy-start(f32[2,384]{1,0:T(2,128)} %qv_ref.1) | copy-start | bytes 9220
  26.3 9.5 %collective-permute-start.7 = (bf16[192,1152]{1,0:T(8,128)(2,1)S(1)}, bf16[192,1152]{1,0:T(8,128)(2,1)S(1)}, u32[]{:S(2)}, u32[]{:S(2)}) collective-permute-start(bf16[192,1152]{1,0:T(8,128)(2,1)S(1)} %pad_maximum_fusion.5), channel_id=1, source_target_pairs={{0,1},{1,0},{2,6},{3,7},{4,5},{5,4},{6,2},{7,3},{8,9},{9,8},{10,14... | collective-permute-start | bytes 1327112 | tf_op jit(solution)/shard_map/ppermute | solution.py:39
  28.0 7.9 %collective-permute-start.8 = (bf16[48,1920]{1,0:T(8,128)(2,1)S(1)}, bf16[48,1920]{1,0:T(8,128)(2,1)S(1)}, u32[]{:S(2)}, u32[]{:S(2)}) collective-permute-start(bf16[48,1920]{1,0:T(8,128)(2,1)S(1)} %fusion.2), channel_id=1, source_target_pairs={{0,16},{1,17},{2,10},{3,11},{4,20},{5,21},{6,14},{7,15},{8,24},{9,... | collective-permute-start | bytes 552968 | tf_op jit(solution)/shard_map/ppermute | solution.py:39
  36.0 12.3 %collective-permute-start.13 = (bf16[384,1152]{1,0:T(8,128)(2,1)S(1)}, bf16[384,1152]{1,0:T(8,128)(2,1)S(1)}, u32[]{:S(2)}, u32[]{:S(2)}) collective-permute-start(bf16[384,1152]{1,0:T(8,128)(2,1)S(1)} %pad_maximum_fusion.refs_0_), channel_id=1, source_target_pairs={{0,2},{1,3},{2,0},{3,1},{4,6},{5,7},{6,4},{7,5},{8,10},{9,11},{10,... | collective-permute-start | bytes 2654216 | tf_op jit(solution)/shard_map/ppermute | solution.py:39
  36.0 13.1 %collective-permute-start.9 = (bf16[384,1152]{1,0:T(8,128)(2,1)S(1)}, bf16[384,1152]{1,0:T(8,128)(2,1)S(1)}, u32[]{:S(2)}, u32[]{:S(2)}) collective-permute-start(bf16[384,1152]{1,0:T(8,128)(2,1)S(1)} %pad_maximum_fusion.refs_0_), channel_id=1, source_target_pairs={{0,4},{1,5},{2,3},{3,2},{4,0},{5,1},{6,7},{7,6},{8,12},{9,13},{10,... | collective-permute-start | bytes 2654216 | tf_op jit(solution)/shard_map/ppermute | solution.py:39
  37.9 10.4 %collective-permute-start.11 = (bf16[2,128,768]{2,1,0:T(8,128)(2,1)S(1)}, bf16[2,128,768]{2,1,0:T(8,128)(2,1)S(1)}, u32[]{:S(2)}, u32[]{:S(2)}) collective-permute-start(bf16[2,128,768]{2,1,0:T(8,128)(2,1)S(1)} %pad_maximum_fusion.7), channel_id=1, source_target_pairs={{0,2},{1,3},{2,0},{3,1},{4,6},{5,7},{6,4},{7,5},{8,10},{9,11},{10,... | collective-permute-start | bytes 1179656 | tf_op jit(solution)/shard_map/ppermute | solution.py:39
  37.9 10.3 %collective-permute-start.10 = (bf16[96,1920]{1,0:T(8,128)(2,1)S(1)}, bf16[96,1920]{1,0:T(8,128)(2,1)S(1)}, u32[]{:S(2)}, u32[]{:S(2)}) collective-permute-start(bf16[96,1920]{1,0:T(8,128)(2,1)S(1)} %pad_maximum_fusion.11), channel_id=1, source_target_pairs={{0,8},{1,9},{2,18},{3,19},{4,12},{5,13},{6,22},{7,23},{8,0},{9,1},... | collective-permute-start | bytes 1105928 | tf_op jit(solution)/shard_map/ppermute | solution.py:39
  38.2 3.8 %collective-permute-start.12 = (f32[1,2304]{1,0:T(1,128)S(1)}, f32[1,2304]{1,0:T(1,128)S(1)}, u32[]{:S(2)}, u32[]{:S(2)}) collective-permute-start(f32[1,2304]{1,0:T(1,128)S(1)} %get-tuple-element.206), channel_id=1, source_target_pairs={{0,1},{1,0},{2,3},{3,2},{4,5},{5,4},{6,7},{7,6},{8,9},{9,8},{10,11... | collective-permute-start | bytes 27656 | tf_op jit(solution)/shard_map/ppermute | solution.py:39
  48.2 14.9 %copy-start.2 = (bf16[2,128,768]{2,1,0:T(8,128)(2,1)}, bf16[2,128,768]{2,1,0:T(8,128)(2,1)S(1)}, u32[]{:S(2)}) copy-start(bf16[2,128,768]{2,1,0:T(8,128)(2,1)S(1)} %collective-permute-done.11.refs_4_) | copy-start | bytes 1179652
  49.2 2.6 %collective-permute-start.14 = (bf16[384,1152]{1,0:T(8,128)(2,1)S(1)}, bf16[384,1152]{1,0:T(8,128)(2,1)S(1)}, u32[]{:S(2)}, u32[]{:S(2)}) collective-permute-start(bf16[384,1152]{1,0:T(8,128)(2,1)S(1)} %collective-permute-done.9.refs_1_), channel_id=1, source_target_pairs={{0,2},{1,3},{2,0},{3,1},{4,6},{5,7},{6,4},{7,5},{8,10},{9,11},{10,... | collective-permute-start | bytes 2654216 | tf_op jit(solution)/shard_map/ppermute | solution.py:39
  49.8 20.0 %collective-permute-start.16 = (bf16[192,1536]{1,0:T(8,128)(2,1)S(1)}, bf16[192,1536]{1,0:T(8,128)(2,1)S(1)}, u32[]{:S(2)}, u32[]{:S(2)}) collective-permute-start(bf16[192,1536]{1,0:T(8,128)(2,1)S(1)} %pad_maximum_fusion.4), channel_id=1, source_target_pairs={{0,8},{1,9},{2,18},{3,19},{4,12},{5,13},{6,22},{7,23},{8,0},{9,1},... | collective-permute-start | bytes 1769480 | tf_op jit(solution)/shard_map/ppermute | solution.py:39
  49.8 11.5 %collective-permute-start.15 = (bf16[192,1920]{1,0:T(8,128)(2,1)S(1)}, bf16[192,1920]{1,0:T(8,128)(2,1)S(1)}, u32[]{:S(2)}, u32[]{:S(2)}) collective-permute-start(bf16[192,1920]{1,0:T(8,128)(2,1)S(1)} %pad_maximum_fusion.3), channel_id=1, source_target_pairs={{0,1},{1,0},{2,6},{3,7},{4,5},{5,4},{6,2},{7,3},{8,9},{9,8},{10,14... | collective-permute-start | bytes 2211848 | tf_op jit(solution)/shard_map/ppermute | solution.py:39
  61.5 19.4 %collective-permute-start.17 = (bf16[384,1920]{1,0:T(8,128)(2,1)S(1)}, bf16[384,1920]{1,0:T(8,128)(2,1)S(1)}, u32[]{:S(2)}, u32[]{:S(2)}) collective-permute-start(bf16[384,1920]{1,0:T(8,128)(2,1)S(1)} %constant_dynamic-update-slice_fusion.refs_0_), channel_id=1, source_target_pairs={{0,4},{1,5},{2,3},{3,2},{4,0},{5,1},{6,7},{7,6},{8,12},{9,13},{10,... | collective-permute-start | bytes 4423688 | tf_op jit(solution)/shard_map/ppermute | solution.py:39
  63.1 7.1 %slice-start = ((bf16[2,128,768]{2,1,0:T(8,128)(2,1)}), bf16[1,128,768]{2,1,0:T(8,128)(2,1)S(1)}, s32[]{:S(2)}) async-start(bf16[2,128,768]{2,1,0:T(8,128)(2,1)} %copy-done.2), calls=%async_computation | async-start | bytes 393216 | tf_op jit(solution)/shard_map/slice | solution.py:924
  69.7 11.2 %collective-permute-start.18 = (bf16[384,1920]{1,0:T(8,128)(2,1)S(1)}, bf16[384,1920]{1,0:T(8,128)(2,1)S(1)}, u32[]{:S(2)}, u32[]{:S(2)}) collective-permute-start(bf16[384,1920]{1,0:T(8,128)(2,1)S(1)} %constant_dynamic-update-slice_fusion.refs_0_), channel_id=1, source_target_pairs={{0,2},{1,3},{2,0},{3,1},{4,6},{5,7},{6,4},{7,5},{8,10},{9,11},{10,... | collective-permute-start | bytes 4423688 | tf_op jit(solution)/shard_map/ppermute | solution.py:39
  80.9 3.3 %collective-permute-start.19 = (bf16[384,1920]{1,0:T(8,128)(2,1)S(1)}, bf16[384,1920]{1,0:T(8,128)(2,1)S(1)}, u32[]{:S(2)}, u32[]{:S(2)}) collective-permute-start(bf16[384,1920]{1,0:T(8,128)(2,1)S(1)} %collective-permute-done.17.refs_1_), channel_id=1, source_target_pairs={{0,2},{1,3},{2,0},{3,1},{4,6},{5,7},{6,4},{7,5},{8,10},{9,11},{10,... | collective-permute-start | bytes 4423688 | tf_op jit(solution)/shard_map/ppermute | solution.py:39
  80.9 13.2 %collective-permute-start.21 = (bf16[384,1536]{1,0:T(8,128)(2,1)S(1)}, bf16[384,1536]{1,0:T(8,128)(2,1)S(1)}, u32[]{:S(2)}, u32[]{:S(2)}) collective-permute-start(bf16[384,1536]{1,0:T(8,128)(2,1)S(1)} %constant_dynamic-update-slice_fusion.2.refs_0_), channel_id=1, source_target_pairs={{0,2},{1,3},{2,0},{3,1},{4,6},{5,7},{6,4},{7,5},{8,10},{9,11},{10,... | collective-permute-start | bytes 3538952 | tf_op jit(solution)/shard_map/ppermute | solution.py:39
  81.4 16.2 %collective-permute-start.20 = (bf16[384,1536]{1,0:T(8,128)(2,1)S(1)}, bf16[384,1536]{1,0:T(8,128)(2,1)S(1)}, u32[]{:S(2)}, u32[]{:S(2)}) collective-permute-start(bf16[384,1536]{1,0:T(8,128)(2,1)S(1)} %constant_dynamic-update-slice_fusion.2.refs_0_), channel_id=1, source_target_pairs={{0,1},{1,0},{2,10},{3,11},{4,5},{5,4},{6,14},{7,15},{8,9},{9,8},{1... | collective-permute-start | bytes 3538952 | tf_op jit(solution)/shard_map/ppermute | solution.py:39
  81.9 15.7 %collective-permute-start.22 = (bf16[2,128,768]{2,1,0:T(8,128)(2,1)S(1)}, bf16[2,128,768]{2,1,0:T(8,128)(2,1)S(1)}, u32[]{:S(2)}, u32[]{:S(2)}) collective-permute-start(bf16[2,128,768]{2,1,0:T(8,128)(2,1)S(1)} %pad_maximum_fusion.8), channel_id=1, source_target_pairs={{0,4},{1,5},{2,6},{3,7},{4,0},{5,1},{6,2},{7,3},{8,12},{9,13},{10,... | collective-permute-start | bytes 1179656 | tf_op jit(solution)/shard_map/ppermute | solution.py:39
  97.6 4.5 %copy-start.3 = (bf16[2,128,768]{2,1,0:T(8,128)(2,1)S(1)}, bf16[2,128,768]{2,1,0:T(8,128)(2,1)}, u32[]{:S(2)}) copy-start(bf16[2,128,768]{2,1,0:T(8,128)(2,1)} %copy-done.2) | copy-start | bytes 1179652
  97.6 2.8 %collective-permute-start.23 = (bf16[384,1536]{1,0:T(8,128)(2,1)S(1)}, bf16[384,1536]{1,0:T(8,128)(2,1)S(1)}, u32[]{:S(2)}, u32[]{:S(2)}) collective-permute-start(bf16[384,1536]{1,0:T(8,128)(2,1)S(1)} %collective-permute-done.20.refs_1_), channel_id=1, source_target_pairs={{0,2},{1,3},{2,0},{3,1},{4,6},{5,7},{6,4},{7,5},{8,10},{9,11},{10,... | collective-permute-start | bytes 3538952 | tf_op jit(solution)/shard_map/ppermute | solution.py:39
  110.3 5.2 %collective-permute-start.24 = (bf16[768,1536]{1,0:T(8,128)(2,1)S(1)}, bf16[768,1536]{1,0:T(8,128)(2,1)S(1)}, u32[]{:S(2)}, u32[]{:S(2)}) collective-permute-start(bf16[768,1536]{1,0:T(8,128)(2,1)S(1)} %get-tuple-element.254), channel_id=1, source_target_pairs={{0,2},{1,3},{2,0},{3,1},{4,6},{5,7},{6,4},{7,5},{8,10},{9,11},{10,... | collective-permute-start | bytes 7077896 | tf_op jit(solution)/shard_map/ppermute | solution.py:39
  110.5 4.9 %collective-permute-start.25 = (bf16[2,128,768]{2,1,0:T(8,128)(2,1)S(1)}, bf16[2,128,768]{2,1,0:T(8,128)(2,1)S(1)}, u32[]{:S(2)}, u32[]{:S(2)}) collective-permute-start(bf16[2,128,768]{2,1,0:T(8,128)(2,1)S(1)} %slice.34), channel_id=1, source_target_pairs={{0,2},{1,3},{2,0},{3,1},{4,6},{5,7},{6,4},{7,5},{8,10},{9,11},{10,... | collective-permute-start | bytes 1179656 | tf_op jit(solution)/shard_map/ppermute | solution.py:39
  115.8 12.3 %collective-permute-start.27 = (bf16[2,128,768]{2,1,0:T(8,128)(2,1)S(1)}, bf16[2,128,768]{2,1,0:T(8,128)(2,1)S(1)}, u32[]{:S(2)}, u32[]{:S(2)}) collective-permute-start(bf16[2,128,768]{2,1,0:T(8,128)(2,1)S(1)} %pad_maximum_fusion.9), channel_id=1, source_target_pairs={{0,4},{1,5},{2,6},{3,7},{4,0},{5,1},{6,2},{7,3},{8,12},{9,13},{10,... | collective-permute-start | bytes 1179656 | tf_op jit(solution)/shard_map/ppermute | solution.py:39
  117.4 16.2 %collective-permute-start.26 = (bf16[384,1536]{1,0:T(8,128)(2,1)S(1)}, bf16[384,1536]{1,0:T(8,128)(2,1)S(1)}, u32[]{:S(2)}, u32[]{:S(2)}) collective-permute-start(bf16[384,1536]{1,0:T(8,128)(2,1)S(1)} %add.53), channel_id=1, source_target_pairs={{0,1},{1,0},{2,10},{3,11},{4,5},{5,4},{6,14},{7,15},{8,9},{9,8},{1... | collective-permute-start | bytes 3538952 | tf_op jit(solution)/shard_map/ppermute | solution.py:39
  133.6 6.7 %collective-permute-start.28 = (bf16[768,1920]{1,0:T(8,128)(2,1)S(1)}, bf16[768,1920]{1,0:T(8,128)(2,1)S(1)}, u32[]{:S(2)}, u32[]{:S(2)}) collective-permute-start(bf16[768,1920]{1,0:T(8,128)(2,1)S(1)} %get-tuple-element.274), channel_id=1, source_target_pairs={{0,2},{1,3},{2,0},{3,1},{4,6},{5,7},{6,4},{7,5},{8,10},{9,11},{10,... | collective-permute-start | bytes 8847368 | tf_op jit(solution)/shard_map/ppermute | solution.py:39
  133.9 13.9 %collective-permute-start.29 = (bf16[192,1536]{1,0:T(8,128)(2,1)S(1)}, bf16[192,1536]{1,0:T(8,128)(2,1)S(1)}, u32[]{:S(2)}, u32[]{:S(2)}) collective-permute-start(bf16[192,1536]{1,0:T(8,128)(2,1)S(1)} %add.54), channel_id=1, source_target_pairs={{0,4},{1,5},{2,18},{3,19},{4,0},{5,1},{6,22},{7,23},{8,12},{9,13},... | collective-permute-start | bytes 1769480 | tf_op jit(solution)/shard_map/ppermute | solution.py:39
  134.4 18.7 %collective-permute-start.30 = (bf16[4,128,768]{2,1,0:T(8,128)(2,1)S(1)}, bf16[4,128,768]{2,1,0:T(8,128)(2,1)S(1)}, u32[]{:S(2)}, u32[]{:S(2)}) collective-permute-start(bf16[4,128,768]{2,1,0:T(8,128)(2,1)S(1)} %pad_maximum_fusion.1), channel_id=1, source_target_pairs={{0,1},{1,0},{2,3},{3,2},{4,5},{5,4},{6,7},{7,6},{8,9},{9,8},{10,11... | collective-permute-start | bytes 2359304 | tf_op jit(solution)/shard_map/ppermute | solution.py:39
  140.7 19.4 %collective-permute-start.31 = (bf16[384,1920]{1,0:T(8,128)(2,1)S(1)}, bf16[384,1920]{1,0:T(8,128)(2,1)S(1)}, u32[]{:S(2)}, u32[]{:S(2)}) collective-permute-start(bf16[384,1920]{1,0:T(8,128)(2,1)S(1)} %add.55), channel_id=1, source_target_pairs={{0,4},{1,5},{2,10},{3,11},{4,0},{5,1},{6,14},{7,15},{8,12},{9,13},... | collective-permute-start | bytes 4423688 | tf_op jit(solution)/shard_map/ppermute | solution.py:39
  153.2 8.6 %collective-permute-start.33 = (bf16[2,128,768]{2,1,0:T(8,128)(2,1)S(1)}, bf16[2,128,768]{2,1,0:T(8,128)(2,1)S(1)}, u32[]{:S(2)}, u32[]{:S(2)}) collective-permute-start(bf16[2,128,768]{2,1,0:T(8,128)(2,1)S(1)} %slice.39), channel_id=1, source_target_pairs={{0,2},{1,3},{2,0},{3,1},{4,6},{5,7},{6,4},{7,5},{8,10},{9,11},{10,... | collective-permute-start | bytes 1179656 | tf_op jit(solution)/shard_map/ppermute | solution.py:39
  158.0 3.8 %collective-permute-start.32 = (bf16[776,1152]{1,0:T(8,128)(2,1)S(1)}, bf16[776,1152]{1,0:T(8,128)(2,1)S(1)}, u32[]{:S(2)}, u32[]{:S(2)}) collective-permute-start(bf16[776,1152]{1,0:T(8,128)(2,1)S(1)} %get-tuple-element.300), channel_id=1, source_target_pairs={{0,2},{1,3},{2,0},{3,1},{4,6},{5,7},{6,4},{7,5},{8,10},{9,11},{10,... | collective-permute-start | bytes 5363720 | tf_op jit(solution)/shard_map/ppermute | solution.py:39
  162.0 16.5 %collective-permute-start.34 = (bf16[392,1152]{1,0:T(8,128)(2,1)S(1)}, bf16[392,1152]{1,0:T(8,128)(2,1)S(1)}, u32[]{:S(2)}, u32[]{:S(2)}) collective-permute-start(bf16[392,1152]{1,0:T(8,128)(2,1)S(1)} %add.58.refs_3_), channel_id=1, source_target_pairs={{0,4},{1,5},{2,3},{3,2},{4,0},{5,1},{6,7},{7,6},{8,12},{9,13},{10,... | collective-permute-start | bytes 2709512 | tf_op jit(solution)/shard_map/ppermute | solution.py:39
  163.6 17.2 %collective-permute-start.37 = (bf16[192,1920]{1,0:T(8,128)(2,1)S(1)}, bf16[192,1920]{1,0:T(8,128)(2,1)S(1)}, u32[]{:S(2)}, u32[]{:S(2)}) collective-permute-start(bf16[192,1920]{1,0:T(8,128)(2,1)S(1)} %add.57), channel_id=1, source_target_pairs={{0,1},{1,0},{2,18},{3,19},{4,5},{5,4},{6,22},{7,23},{8,9},{9,8},{1... | collective-permute-start | bytes 2211848 | tf_op jit(solution)/shard_map/ppermute | solution.py:39
  164.1 15.2 %collective-permute-start.36 = (bf16[96,1536]{1,0:T(8,128)(2,1)S(1)}, bf16[96,1536]{1,0:T(8,128)(2,1)S(1)}, u32[]{:S(2)}, u32[]{:S(2)}) collective-permute-start(bf16[96,1536]{1,0:T(8,128)(2,1)S(1)} %add.56), channel_id=1, source_target_pairs={{0,8},{1,9},{2,6},{3,7},{4,12},{5,13},{6,2},{7,3},{8,0},{9,1},{10,... | collective-permute-start | bytes 884744 | tf_op jit(solution)/shard_map/ppermute | solution.py:39
  178.6 11.0 %collective-permute-start.35 = (bf16[200,1152]{1,0:T(8,128)(2,1)S(1)}, bf16[200,1152]{1,0:T(8,128)(2,1)S(1)}, u32[]{:S(2)}, u32[]{:S(2)}) collective-permute-start(bf16[200,1152]{1,0:T(8,128)(2,1)S(1)} %add.59.refs_4_), channel_id=1, source_target_pairs={{0,1},{1,0},{2,6},{3,7},{4,5},{5,4},{6,2},{7,3},{8,9},{9,8},{10,14... | collective-permute-start | bytes 1382408 | tf_op jit(solution)/shard_map/ppermute | solution.py:39
  179.2 11.6 %collective-permute-start.40 = (bf16[2,128,768]{2,1,0:T(8,128)(2,1)S(1)}, bf16[2,128,768]{2,1,0:T(8,128)(2,1)S(1)}, u32[]{:S(2)}, u32[]{:S(2)}) collective-permute-start(bf16[2,128,768]{2,1,0:T(8,128)(2,1)S(1)} %pad_maximum_fusion.10), channel_id=1, source_target_pairs={{0,4},{1,5},{2,6},{3,7},{4,0},{5,1},{6,2},{7,3},{8,12},{9,13},{10,... | collective-permute-start | bytes 1179656 | tf_op jit(solution)/shard_map/ppermute | solution.py:39
  181.0 11.5 %collective-permute-start.41 = (bf16[96,1920]{1,0:T(8,128)(2,1)S(1)}, bf16[96,1920]{1,0:T(8,128)(2,1)S(1)}, u32[]{:S(2)}, u32[]{:S(2)}) collective-permute-start(bf16[96,1920]{1,0:T(8,128)(2,1)S(1)} %add.61), channel_id=1, source_target_pairs={{0,8},{1,9},{2,3},{3,2},{4,12},{5,13},{6,7},{7,6},{8,0},{9,1},{10,... | collective-permute-start | bytes 1105928 | tf_op jit(solution)/shard_map/ppermute | solution.py:39
  182.8 8.0 %collective-permute-start.39 = (bf16[48,1536]{1,0:T(8,128)(2,1)S(1)}, bf16[48,1536]{1,0:T(8,128)(2,1)S(1)}, u32[]{:S(2)}, u32[]{:S(2)}) collective-permute-start(bf16[48,1536]{1,0:T(8,128)(2,1)S(1)} %add.60), channel_id=1, source_target_pairs={{0,16},{1,17},{2,3},{3,2},{4,20},{5,21},{6,7},{7,6},{8,24},{9,25},... | collective-permute-start | bytes 442376 | tf_op jit(solution)/shard_map/ppermute | solution.py:39
  189.8 7.4 %collective-permute-start.38 = (bf16[104,1152]{1,0:T(8,128)(2,1)S(1)}, bf16[104,1152]{1,0:T(8,128)(2,1)S(1)}, u32[]{:S(2)}, u32[]{:S(2)}) collective-permute-start(bf16[104,1152]{1,0:T(8,128)(2,1)S(1)} %add.62.refs_5_), channel_id=1, source_target_pairs={{0,8},{1,9},{2,18},{3,19},{4,12},{5,13},{6,22},{7,23},{8,0},{9,1},... | collective-permute-start | bytes 718856 | tf_op jit(solution)/shard_map/ppermute | solution.py:39
  191.0 7.3 %collective-permute-start.43 = (bf16[48,1536]{1,0:T(8,128)(2,1)S(1)}, bf16[48,1536]{1,0:T(8,128)(2,1)S(1)}, u32[]{:S(2)}, u32[]{:S(2)}) collective-permute-start(bf16[48,1536]{1,0:T(8,128)(2,1)S(1)} %add.63), channel_id=1, source_target_pairs={{0,4},{1,5},{2,6},{3,7},{4,0},{5,1},{6,2},{7,3},{8,12},{9,13},{10,... | collective-permute-start | bytes 442376 | tf_op jit(solution)/shard_map/ppermute | solution.py:39
  192.6 13.0 %collective-permute-start.44 = (bf16[48,1920]{1,0:T(8,128)(2,1)S(1)}, bf16[48,1920]{1,0:T(8,128)(2,1)S(1)}, u32[]{:S(2)}, u32[]{:S(2)}) collective-permute-start(bf16[48,1920]{1,0:T(8,128)(2,1)S(1)} %add.64), channel_id=1, source_target_pairs={{0,16},{1,17},{2,6},{3,7},{4,20},{5,21},{6,2},{7,3},{8,24},{9,25},... | collective-permute-start | bytes 552968 | tf_op jit(solution)/shard_map/ppermute | solution.py:39
  196.9 20.7 %collective-permute-start.47 = (bf16[4,128,768]{2,1,0:T(8,128)(2,1)S(1)}, bf16[4,128,768]{2,1,0:T(8,128)(2,1)S(1)}, u32[]{:S(2)}, u32[]{:S(2)}) collective-permute-start(bf16[4,128,768]{2,1,0:T(8,128)(2,1)S(1)} %pad_maximum_fusion.2), channel_id=1, source_target_pairs={{0,1},{1,0},{2,3},{3,2},{4,5},{5,4},{6,7},{7,6},{8,9},{9,8},{10,11... | collective-permute-start | bytes 2359304 | tf_op jit(solution)/shard_map/ppermute | solution.py:39
  197.3 11.1 %collective-permute-start.42 = (bf16[56,1152]{1,0:T(8,128)(2,1)S(1)}, bf16[56,1152]{1,0:T(8,128)(2,1)S(1)}, u32[]{:S(2)}, u32[]{:S(2)}) collective-permute-start(bf16[56,1152]{1,0:T(8,128)(2,1)S(1)} %add.65.refs_0_), channel_id=1, source_target_pairs={{0,16},{1,17},{2,10},{3,11},{4,20},{5,21},{6,14},{7,15},{8,24},{9,... | collective-permute-start | bytes 387080 | tf_op jit(solution)/shard_map/ppermute | solution.py:39
  205.8 11.7 %collective-permute-start.46 = (bf16[48,1920]{1,0:T(8,128)(2,1)S(1)}, bf16[48,1920]{1,0:T(8,128)(2,1)S(1)}, u32[]{:S(2)}, u32[]{:S(2)}) collective-permute-start(bf16[48,1920]{1,0:T(8,128)(2,1)S(1)} %add.66), channel_id=1, source_target_pairs={{0,4},{1,5},{2,6},{3,7},{4,0},{5,1},{6,2},{7,3},{8,12},{9,13},{10,... | collective-permute-start | bytes 552968 | tf_op jit(solution)/shard_map/ppermute | solution.py:39
  208.5 10.4 %collective-permute-start.50 = (bf16[48,1152]{1,0:T(8,128)(2,1)S(1)}, bf16[48,1152]{1,0:T(8,128)(2,1)S(1)}, u32[]{:S(2)}, u32[]{:S(2)}) collective-permute-start(bf16[48,1152]{1,0:T(8,128)(2,1)S(1)} %add.67.refs_0_), channel_id=1, source_target_pairs={{0,6},{1,7},{2,4},{3,5},{4,2},{5,3},{6,0},{7,1},{8,14},{9,15},{10,... | collective-permute-start | bytes 331784 | tf_op jit(solution)/shard_map/ppermute | solution.py:39
  213.1 5.8 %collective-permute-start.49 = (bf16[48,1152]{1,0:T(8,128)(2,1)S(1)}, bf16[48,1152]{1,0:T(8,128)(2,1)S(1)}, u32[]{:S(2)}, u32[]{:S(2)}) collective-permute-start(bf16[48,1152]{1,0:T(8,128)(2,1)S(1)} %add.67.refs_0_), channel_id=1, source_target_pairs={{0,2},{1,3},{2,0},{3,1},{4,6},{5,7},{6,4},{7,5},{8,10},{9,11},{10,... | collective-permute-start | bytes 331784 | tf_op jit(solution)/shard_map/ppermute | solution.py:39
  213.2 1.7 collective-permute-start.45
  214.9 5.3 %collective-permute-start.48 = (bf16[48,1152]{1,0:T(8,128)(2,1)S(1)}, bf16[48,1152]{1,0:T(8,128)(2,1)S(1)}, u32[]{:S(2)}, u32[]{:S(2)}) collective-permute-start(bf16[48,1152]{1,0:T(8,128)(2,1)S(1)} %add.67.refs_0_), channel_id=1, source_target_pairs={{0,4},{1,5},{2,6},{3,7},{4,0},{5,1},{6,2},{7,3},{8,12},{9,13},{10,... | collective-permute-start | bytes 331784 | tf_op jit(solution)/shard_map/ppermute | solution.py:39
  217.5 3.8 %collective-permute-start.51 = (bf16[96,1920]{1,0:T(8,128)(2,1)S(1)}, bf16[96,1920]{1,0:T(8,128)(2,1)S(1)}, u32[]{:S(2)}, u32[]{:S(2)}) collective-permute-start(bf16[96,1920]{1,0:T(8,128)(2,1)S(1)} %constant_dynamic-update-slice_fusion.4.refs_0_), channel_id=1, source_target_pairs={{0,2},{1,3},{2,0},{3,1},{4,6},{5,7},{6,4},{7,5},{8,10},{9,11},{10,... | collective-permute-start | bytes 1105928 | tf_op jit(solution)/shard_map/ppermute | solution.py:39
  (3 other events, 4.1 us)
